TPU v7x, 512 devices: a whole 4x4x16 slice. The times are simulated.
512 devices in a mesh: ctx: 32 (over x_hi, z), tp: 16 (over x_lo, y, core).
Axes of the slice: x: 4 (x_hi: 2, x_lo: 2; x = x_hi * 2 + x_lo), y: 4, z: 16, core: 2. Of those that a mesh axis runs over, the one named last changes fastest.
Arguments:
- hidden_in: bfloat16 [16384, 4096], P('ctx', 'tp'), may hold values from -6 to 6
- norm_gain: bfloat16 [1, 4096], P(None, 'ctx'), may hold values from 0.25 to 1.75
- w_qkv: bfloat16 [1, 3, 4096, 2048], P(None, None, 'ctx', 'tp'), may hold values from -0.09375 to 0.09375
- w_out: bfloat16 [1, 2048, 4096], P(None, 'tp', 'ctx'), may hold values from -1 to 1
Outputs:
- hidden_out: bfloat16 [16384, 4096], P('ctx', 'tp')
All inputs are finite; a program needn't handle non-finite values.
Results may differ from a plain program's by a relative error of at most 0.015.
Values may be sent and summed in bfloat16 or wider, within the bound.
No kernel may reach another device: no remote copies, remote signals or barrier semaphores. Data moves between devices by JAX's collectives and lax.ppermute only.
A program may use at most 64 MiB of HBM per device.

v0:
```python
import math

import jax
import jax.numpy as jnp
from jax import lax
from jax.experimental import pallas as pl
from jax.experimental.pallas import tpu as pltpu
from jax.sharding import PartitionSpec as P


INTERPRET = False
AXES = ("ctx", "tp")
BF = jnp.bfloat16
F32 = jnp.float32
REV = [int(f"{p:04b}"[::-1], 2) for p in range(16)]


def pairs_of(target):
    pairs = []
    for src in range(512):
        ctx, tp = divmod(src, 16)
        a, z, b, y, k = ctx // 16, ctx % 16, tp // 8, tp // 2 % 4, tp % 2
        to = target(a, z, b, y, k)
        if to is not None:
            a, z, b, y, k = to
            pairs.append((src, (a * 16 + z % 16) * 16 + b * 8 + y % 4 * 2 + k))
    return pairs


def permute(value, target):
    return lax.ppermute(value, AXES, pairs_of(target))


def call(body, outs, scratch=(), flops=0, nbytes=1 << 20, vmem=24 << 20, scalars=True):
    def run(*args):
        specs = [pl.BlockSpec(memory_space=pltpu.VMEM) for _ in args]
        if scalars:
            specs[0] = pl.BlockSpec(memory_space=pltpu.SMEM)
        return pl.pallas_call(
            body,
            out_shape=outs,
            in_specs=specs,
            out_specs=jax.tree.map(lambda _: pl.BlockSpec(memory_space=pltpu.VMEM), outs),
            scratch_shapes=list(scratch),
            compiler_params=pltpu.CompilerParams(vmem_limit_bytes=vmem),
            cost_estimate=pl.CostEstimate(flops=flops, bytes_accessed=nbytes, transcendentals=0),
            interpret=INTERPRET,
        )(*args)

    return run


def shape(dims, dtype):
    return jax.ShapeDtypeStruct(dims, dtype)


def sign_of(k):
    return 1 - 2 * k


def gather_z(chunk):
    held = chunk
    for by in (8, 4, 2, 1):
        got = permute(held, lambda a, z, b, y, k: (a, z + sign_of(k) * by, b, y, k))
        if by > 1:
            held = jnp.concatenate([held, got], axis=0)
    return held, got


def source_z(z, k, p):
    return (z - sign_of(k) * REV[p] + 16) % 16


def project_body(pos, *refs):
    blocks, (w_lo, w_hi, own_ref, ssq_ref, send_ref, out_w_ref, w_nat) = refs[:8], refs[8:]
    z, y, k = pos[1], pos[3], pos[4]
    rows = w_nat.shape[0] // 16
    wide = own_ref.shape[1]
    for p in range(16):
        at = pl.multiple_of(source_z(z, k, p) * rows, rows)
        half = w_lo if p < 8 else w_hi
        w_nat[pl.ds(at, rows), :] = half[(p % 8) * rows : (p % 8 + 1) * rows, :wide]
        out_w_ref[pl.ds(at, rows), :] = half[(p % 8) * rows : (p % 8 + 1) * rows, wide:]
    seg = own_ref.shape[0]
    tile = min(seg, 256)
    for r in range(2 * seg // tile):
        acc = jnp.zeros((tile, wide), F32)
        ssq = jnp.zeros((tile, 1), F32)
        for i in range(8):
            yy = (y + i // 2) % 4
            kk = k if i % 2 == 0 else 1 - k
            at = pl.multiple_of((yy * 2 + kk) * 2 * rows, 2 * rows)
            block = blocks[i][r * tile : (r + 1) * tile, :]
            acc += jnp.dot(block, w_nat[pl.ds(at, 2 * rows), :], preferred_element_type=F32)
            wider = block.astype(F32)
            ssq += jnp.sum(wider * wider, axis=1, keepdims=True)
        at = r * tile % seg
        if r * tile < seg:
            own_ref[at : at + tile, :] = acc
            ssq_ref[at : at + tile, :] = jnp.broadcast_to(ssq, (tile, ssq_ref.shape[1]))
        else:
            send_ref[at : at + tile, :wide] = acc.astype(BF)
            lanes = send_ref.shape[1] - wide
            high = ssq.astype(BF).astype(F32)
            lane = lax.broadcasted_iota(jnp.int32, (tile, lanes), 1)
            both = jnp.where(lane < lanes // 2, high, ssq - high)
            send_ref[at : at + tile, wide:] = both.astype(BF)


def combine_body(own_ref, ssq_ref, got_ref, q_ref, kv_ref, *, features):
    hd = q_ref.shape[1]
    wide = 3 * hd
    lanes = got_ref.shape[1] - wide
    half = got_ref[:, wide:].astype(F32)
    ssq = ssq_ref[:, :1] + half[:, :1] + half[:, lanes // 2 : lanes // 2 + 1]
    scale = lax.rsqrt(ssq * (1.0 / features) + 1e-06)
    total = (own_ref[...] + got_ref[:, :wide].astype(F32)) * scale
    q_ref[...] = total[:, :hd].astype(BF)
    kv_ref[...] = total[:, hd:].astype(BF)


def scores_of(q, keys):
    hd = q.shape[1]
    return lax.dot_general(
        q, keys, (((1,), (1,)), ((), ())), preferred_element_type=F32
    ) * (1.0 / math.sqrt(hd))


def own_body(q_ref, kv_ref, e_ref, sum_ref):
    hd = q_ref.shape[1]
    scores = scores_of(q_ref[...], kv_ref[:, :hd])
    row = lax.broadcasted_iota(jnp.int32, scores.shape, 0)
    col = lax.broadcasted_iota(jnp.int32, scores.shape, 1)
    e = jnp.where(col <= row, jnp.exp(scores), 0.0)
    e_ref[...] = e
    sum_ref[...] = jnp.broadcast_to(jnp.sum(e, axis=1, keepdims=True), sum_ref.shape)


def attend_body(pos, q_ref, kv_ref, prev_ref, e_ref, sum_ref, out_ref):
    hd = q_ref.shape[1]
    e = jnp.exp(scores_of(q_ref[...], prev_ref[:, :hd]))
    first = pos[0] * 16 + pos[1] == 0
    e = jnp.where(jnp.full(e.shape, first), 0.0, e)
    total = sum_ref[:, :1] + jnp.sum(e, axis=1, keepdims=True)
    inverse = 1.0 / total
    out = jnp.dot((e_ref[...] * inverse).astype(BF), kv_ref[:, hd:], preferred_element_type=F32)
    out += jnp.dot((e * inverse).astype(BF), prev_ref[:, hd:], preferred_element_type=F32)
    out_ref[...] = out.astype(BF)


def output_body(pos, *refs):
    pieces, (w_own, w_other, hidden_ref, out_ref, w_nat) = refs[:8], refs[8:]
    a, b, y, k = pos[0], pos[2], pos[3], pos[4]
    hd = w_nat.shape[2]
    w_nat[a] = w_own[...]
    w_nat[1 - a] = w_other[...]
    total = hidden_ref[...].astype(F32)
    for i in range(8):
        yy = (y + i // 2) % 4
        kk = k if i % 2 == 0 else 1 - k
        at = pl.multiple_of((yy * 2 + kk + 2 * y + k) % 8 * 2 * hd, 2 * hd)
        rows = []
        for head_b in (b, 1 - b):
            both = w_nat[head_b, pl.ds(at, 2 * hd), :]
            rows.append(jnp.concatenate([both[:hd], both[hd:]], axis=1))
        total += jnp.dot(pieces[i][...], jnp.concatenate(rows, axis=0), preferred_element_type=F32)
    out_ref[...] = total.astype(BF)


def swap_hi(a, z, b, y, k):
    return 1 - a, z, b, y, k


def swap_core(a, z, b, y, k):
    return a, z, b, y, 1 - k


def around(value):
    pieces = []
    for by in range(4):
        piece = value
        if by:
            piece = permute(value, lambda a, z, b, y, k: (a, z, b, y - by, k))
        pieces += [piece, permute(piece, swap_core)]
    return pieces


def layer(hidden, norm_gain, w_qkv, w_out):
    seg, feats = hidden.shape
    hd = w_out.shape[1]
    ctx, tp = lax.axis_index("ctx"), lax.axis_index("tp")
    a, z, b, y, k = ctx // 16, ctx % 16, tp // 8, tp // 2 % 4, tp % 2
    pos = jnp.stack([a, z, b, y, k]).astype(jnp.int32)

    corner = {(0, 0): (0, 1), (0, 1): (1, 1), (1, 1): (1, 0), (1, 0): (0, 0)}
    turn = permute(hidden, lambda a, z, b, y, k: (*_at(corner, a, b, z), y, k))
    cross = permute(hidden, lambda a, z, b, y, k: (b, z, a, y, k) if a != b else None)
    own = jnp.where(a == b, hidden, turn)
    other = jnp.where(a == b, turn, cross)
    blocks = around(jnp.concatenate([own, other], axis=0))

    piece = permute(w_out[0], lambda a, z, b, y, k: (b, z + 2 * (2 * y + k), a, z // 4, z // 2 % 2))
    folded = (w_qkv[0].astype(F32) * norm_gain[0].astype(F32)[None, :, None]).astype(BF)
    chunk = jnp.concatenate([folded[0], folded[1], folded[2], piece], axis=1)
    w_lo, w_hi = gather_z(chunk)

    own_part, own_ssq, send, out_w = call(
        project_body,
        (
            shape((seg, 3 * hd), F32),
            shape((seg, hd), F32),
            shape((seg, 4 * hd), BF),
            shape((16 * hd, hd), BF),
        ),
        [pltpu.VMEM((16 * hd, 3 * hd), BF)],
        flops=4 * seg * 8 * feats * 3 * hd,
        nbytes=8 << 20,
    )(pos, *blocks, w_lo, w_hi)
    got = permute(send, swap_hi)
    q, kv = call(
        lambda *refs: combine_body(*refs, features=16 * feats),
        (shape((seg, hd), BF), shape((seg, 2 * hd), BF)),
        nbytes=2 << 20,
        scalars=False,
    )(own_part, own_ssq, got)
    prev = lax.ppermute(kv, "ctx", [(i, i + 1) for i in range(31)])
    out_w_other = permute(out_w, swap_hi)
    e_own, sum_own = call(
        own_body,
        (shape((seg, seg), F32), shape((seg, hd), F32)),
        flops=2 * seg * seg * hd,
        nbytes=2 << 20,
        scalars=False,
    )(q, kv)
    attended = call(
        attend_body, shape((seg, hd), BF), flops=6 * seg * seg * hd, nbytes=2 << 20
    )(pos, q, kv, prev, e_own, sum_own)

    facing = permute(attended, lambda a, z, b, y, k: (a, z, 1 - b, y, k))
    pieces = around(jnp.concatenate([attended, facing], axis=1))
    return call(
        output_body,
        shape((seg, feats), BF),
        [pltpu.VMEM((2, 16 * hd, hd), BF)],
        flops=2 * seg * feats * 16 * hd,
        nbytes=4 << 20,
    )(pos, *pieces, out_w, out_w_other, hidden)


def _at(corner, a, b, z):
    to = corner[a, b]
    return to[0], z, to[1]


def solution(mesh):
    placed = (P("ctx", "tp"), P(None, "ctx"), P(None, None, "ctx", "tp"), P(None, "tp", "ctx"))
    return jax.shard_map(
        layer, mesh=mesh, in_specs=placed, out_specs=P("ctx", "tp"), check_vma=False
    )
```

profile of v0, /device:TPU:1, one launch (start us, length us, event | category | flops | bytes accessed | tf_op | source)
XLA Modules:
  0.0 172.3 jit_solution(12826777417690159841)
XLA Ops:
  0.0 6.4 %collective-permute-start.9 = (bf16[128,128]{1,0:T(8,128)(2,1)}, bf16[128,128]{1,0:T(8,128)(2,1)S(1)}, u32[]{:S(2)}, u32[]{:S(2)}) collective-permute-start(bf16[128,128]{1,0:T(8,128)(2,1)} %bitcast.18), channel_id=1, source_target_pairs={{0,0},{1,32},{2,64},{3,96},{4,128},{5,160},{6,192},{7,224},{8,256}... | collective-permute-start | bytes 98312 | tf_op jit(solution)/shard_map/ppermute | solution.py:31
  9.8 19.4 %collective-permute-start.10 = (bf16[128,512]{1,0:T(8,128)(2,1)S(1)}, bf16[128,512]{1,0:T(8,128)(2,1)S(1)}, u32[]{:S(2)}, u32[]{:S(2)}) collective-permute-start(bf16[128,512]{1,0:T(8,128)(2,1)S(1)} %pad_maximum_fusion.5), channel_id=1, source_target_pairs={{0,128},{1,129},{2,130},{3,131},{4,132},{5,133},{6,134},{7,135},{8... | collective-permute-start | bytes 393224 | tf_op jit(solution)/shard_map/ppermute | solution.py:31
  29.3 2.4 %collective-permute-done.10 = bf16[128,512]{1,0:T(8,128)(2,1)S(1)} collective-permute-done((bf16[128,512]{1,0:T(8,128)(2,1)S(1)}, bf16[128,512]{1,0:T(8,128)(2,1)S(1)}, u32[]{:S(2)}, u32[]{:S(2)}) %collective-permute-start.10) | collective-permute-done | bytes 131104 | tf_op jit(solution)/shard_map/ppermute | solution.py:31
  31.7 10.7 %collective-permute-start.11 = (bf16[256,512]{1,0:T(8,128)(2,1)S(1)}, bf16[256,512]{1,0:T(8,128)(2,1)S(1)}, u32[]{:S(2)}, u32[]{:S(2)}) collective-permute-start(bf16[256,512]{1,0:T(8,128)(2,1)S(1)} %pad_maximum_fusion.3), channel_id=1, source_target_pairs={{0,64},{1,193},{2,66},{3,195},{4,68},{5,197},{6,70},{7,199},{8,72}... | collective-permute-start | bytes 786440 | tf_op jit(solution)/shard_map/ppermute | solution.py:31
  42.4 4.0 %collective-permute-start = (bf16[512,256]{1,0:T(8,128)(2,1)S(1)}, bf16[512,256]{1,0:T(8,128)(2,1)S(1)}, u32[]{:S(2)}, u32[]{:S(2)}) collective-permute-start(bf16[512,256]{1,0:T(8,128)(2,1)S(1)} %copy-done), channel_id=1, source_target_pairs={{0,8},{1,9},{2,10},{3,11},{4,12},{5,13},{6,14},{7,15},{8,264},{9,2... | collective-permute-start | bytes 786440 | tf_op jit(solution)/shard_map/ppermute | solution.py:31
  47.1 7.1 %collective-permute-done.11 = bf16[256,512]{1,0:T(8,128)(2,1)S(1)} collective-permute-done((bf16[256,512]{1,0:T(8,128)(2,1)S(1)}, bf16[256,512]{1,0:T(8,128)(2,1)S(1)}, u32[]{:S(2)}, u32[]{:S(2)}) %collective-permute-start.11) | collective-permute-done | bytes 262176 | tf_op jit(solution)/shard_map/ppermute | solution.py:31
  54.2 3.9 %collective-permute-start.12 = (bf16[512,512]{1,0:T(8,128)(2,1)S(1)}, bf16[512,512]{1,0:T(8,128)(2,1)}, u32[]{:S(2)}, u32[]{:S(2)}) collective-permute-start(bf16[512,512]{1,0:T(8,128)(2,1)S(1)} %pad_maximum_fusion.2), channel_id=1, source_target_pairs={{0,32},{1,225},{2,34},{3,227},{4,36},{5,229},{6,38},{7,231},{8,40}... | collective-permute-start | bytes 1572872 | tf_op jit(solution)/shard_map/ppermute | solution.py:31
  58.3 6.3 %collective-permute-start.7 = (bf16[1024,256]{1,0:T(8,128)(2,1)S(1)}, bf16[1024,256]{1,0:T(8,128)(2,1)S(1)}, u32[]{:S(2)}, u32[]{:S(2)}) collective-permute-start(bf16[1024,256]{1,0:T(8,128)(2,1)S(1)} %pad_maximum_fusion.1.refs_0_), channel_id=1, source_target_pairs={{0,2},{1,3},{2,4},{3,5},{4,6},{5,7},{6,0},{7,1},{8,10},{9,11},{10,... | collective-permute-start | bytes 1572872 | tf_op jit(solution)/shard_map/ppermute | solution.py:31
  64.6 3.0 %collective-permute-start.5 = (bf16[1024,256]{1,0:T(8,128)(2,1)S(1)}, bf16[1024,256]{1,0:T(8,128)(2,1)}, u32[]{:S(2)}, u32[]{:S(2)}) collective-permute-start(bf16[1024,256]{1,0:T(8,128)(2,1)S(1)} %pad_maximum_fusion.1.refs_0_), channel_id=1, source_target_pairs={{0,4},{1,5},{2,6},{3,7},{4,0},{5,1},{6,2},{7,3},{8,12},{9,13},{10,... | collective-permute-start | bytes 1572872 | tf_op jit(solution)/shard_map/ppermute | solution.py:31
  67.6 3.3 %collective-permute-start.3 = (bf16[1024,256]{1,0:T(8,128)(2,1)S(1)}, bf16[1024,256]{1,0:T(8,128)(2,1)}, u32[]{:S(2)}, u32[]{:S(2)}) collective-permute-start(bf16[1024,256]{1,0:T(8,128)(2,1)S(1)} %pad_maximum_fusion.1.refs_0_), channel_id=1, source_target_pairs={{0,6},{1,7},{2,0},{3,1},{4,2},{5,3},{6,4},{7,5},{8,14},{9,15},{10,... | collective-permute-start | bytes 1572872 | tf_op jit(solution)/shard_map/ppermute | solution.py:31
  72.0 6.1 %collective-permute-start.13 = (bf16[1024,512]{1,0:T(8,128)(2,1)S(1)}, bf16[1024,512]{1,0:T(8,128)(2,1)S(1)}, u32[]{:S(2)}, u32[]{:S(2)}) collective-permute-start(bf16[1024,512]{1,0:T(8,128)(2,1)S(1)} %pad_maximum_fusion.refs_8_), channel_id=1, source_target_pairs={{0,16},{1,241},{2,18},{3,243},{4,20},{5,245},{6,22},{7,247},{8,24}... | collective-permute-start | bytes 3145736 | tf_op jit(solution)/shard_map/ppermute | solution.py:31
  78.0 3.9 %collective-permute-start.2 = (bf16[1024,256]{1,0:T(8,128)(2,1)S(1)}, bf16[1024,256]{1,0:T(8,128)(2,1)}, u32[]{:S(2)}, u32[]{:S(2)}) collective-permute-start(bf16[1024,256]{1,0:T(8,128)(2,1)S(1)} %pad_maximum_fusion.1.refs_0_), channel_id=1, source_target_pairs={{0,1},{1,0},{2,3},{3,2},{4,5},{5,4},{6,7},{7,6},{8,9},{9,8},{10,11... | collective-permute-start | bytes 1572872 | tf_op jit(solution)/shard_map/ppermute | solution.py:31
  81.9 1.9 %collective-permute-start.8 = (bf16[1024,256]{1,0:T(8,128)(2,1)S(1)}, bf16[1024,256]{1,0:T(8,128)(2,1)}, u32[]{:S(2)}, u32[]{:S(2)}) collective-permute-start(bf16[1024,256]{1,0:T(8,128)(2,1)S(1)} %collective-permute-done.7.refs_6_), channel_id=1, source_target_pairs={{0,1},{1,0},{2,3},{3,2},{4,5},{5,4},{6,7},{7,6},{8,9},{9,8},{10,11... | collective-permute-start | bytes 1572872 | tf_op jit(solution)/shard_map/ppermute | solution.py:31
  83.9 2.9 %collective-permute-done.5.refs_4_ = bf16[1024,256]{1,0:T(8,128)(2,1)} collective-permute-done((bf16[1024,256]{1,0:T(8,128)(2,1)S(1)}, bf16[1024,256]{1,0:T(8,128)(2,1)}, u32[]{:S(2)}, u32[]{:S(2)}) %collective-permute-start.5) | collective-permute-done | bytes 524320 | tf_op jit(solution)/shard_map/ppermute | solution.py:31
  86.7 5.0 %collective-permute-start.6 = (bf16[1024,256]{1,0:T(8,128)(2,1)}, bf16[1024,256]{1,0:T(8,128)(2,1)}, u32[]{:S(2)}, u32[]{:S(2)}) collective-permute-start(bf16[1024,256]{1,0:T(8,128)(2,1)} %collective-permute-done.5.refs_4_), channel_id=1, source_target_pairs={{0,1},{1,0},{2,3},{3,2},{4,5},{5,4},{6,7},{7,6},{8,9},{9,8},{10,11... | collective-permute-start | bytes 1572872 | tf_op jit(solution)/shard_map/ppermute | solution.py:31
  91.8 1.9 %collective-permute-start.4 = (bf16[1024,256]{1,0:T(8,128)(2,1)}, bf16[1024,256]{1,0:T(8,128)(2,1)}, u32[]{:S(2)}, u32[]{:S(2)}) collective-permute-start(bf16[1024,256]{1,0:T(8,128)(2,1)} %collective-permute-done.3.refs_2_), channel_id=1, source_target_pairs={{0,1},{1,0},{2,3},{3,2},{4,5},{5,4},{6,7},{7,6},{8,9},{9,8},{10,11... | collective-permute-start | bytes 1572872 | tf_op jit(solution)/shard_map/ppermute | solution.py:31
  93.9 2.1 %collective-permute-done.4.refs_3_ = bf16[1024,256]{1,0:T(8,128)(2,1)} collective-permute-done((bf16[1024,256]{1,0:T(8,128)(2,1)}, bf16[1024,256]{1,0:T(8,128)(2,1)}, u32[]{:S(2)}, u32[]{:S(2)}) %collective-permute-start.4) | collective-permute-done | bytes 524320 | tf_op jit(solution)/shard_map/ppermute | solution.py:31
  95.9 4.5 %shard_map.46 = (f32[512,384]{1,0:T(8,128)S(1)}, f32[512,128]{1,0:T(8,128)S(1)}, bf16[512,512]{1,0:T(8,128)(2,1)S(1)}, bf16[2048,128]{1,0:T(8,128)(2,1)S(1)}) custom-call(s32[5]{0:T(128)S(1)} %stack.23.pos, bf16[1024,256]{1,0:T(8,128)(2,1)S(1)} %pad_maximum_fusion.1.refs_0_, bf16[1024,256]{1,0:T(8,128)(2,1)} %collective-permute-done.2.refs_1_, ...), custom_call_target="tpu_custom_call" | custom-call | flops 1610612736 | bytes 8388608 | tf_op jit(solution)/shard_map/pallas_call | solution.py:39
  100.4 8.1 %collective-permute-start.14 = (bf16[512,512]{1,0:T(8,128)(2,1)S(1)}, bf16[512,512]{1,0:T(8,128)(2,1)S(1)}, u32[]{:S(2)}, u32[]{:S(2)}) collective-permute-start(bf16[512,512]{1,0:T(8,128)(2,1)S(1)} %get-tuple-element.15), channel_id=1, source_target_pairs={{0,256},{1,257},{2,258},{3,259},{4,260},{5,261},{6,262},{7,263},{8... | collective-permute-start | bytes 1572872 | tf_op jit(solution)/shard_map/ppermute | solution.py:31
  108.5 11.9 %collective-permute-done.14.refs_2_ = bf16[512,512]{1,0:T(8,128)(2,1)S(1)} collective-permute-done((bf16[512,512]{1,0:T(8,128)(2,1)S(1)}, bf16[512,512]{1,0:T(8,128)(2,1)S(1)}, u32[]{:S(2)}, u32[]{:S(2)}) %collective-permute-start.14) | collective-permute-done | bytes 524320 | tf_op jit(solution)/shard_map/ppermute | solution.py:31
  120.7 2.7 %collective-permute-start.15 = (bf16[512,256]{1,0:T(8,128)(2,1)S(1)}, bf16[512,256]{1,0:T(8,128)(2,1)S(1)}, u32[]{:S(2)}, u32[]{:S(2)}) collective-permute-start(bf16[512,256]{1,0:T(8,128)(2,1)S(1)} %get-tuple-element.17.kv_ref), channel_id=1, source_target_pairs={{0,16},{16,32},{32,48},{48,64},{64,80},{80,96},{96,112},{112,128},... | collective-permute-start | bytes 786440 | tf_op jit(solution)/shard_map/ppermute | solution.py:226
  123.8 4.0 %collective-permute-done.15.prev_ref = bf16[512,256]{1,0:T(8,128)(2,1)S(1)} collective-permute-done((bf16[512,256]{1,0:T(8,128)(2,1)S(1)}, bf16[512,256]{1,0:T(8,128)(2,1)S(1)}, u32[]{:S(2)}, u32[]{:S(2)}) %collective-permute-start.15) | collective-permute-done | bytes 262176 | tf_op jit(solution)/shard_map/ppermute | solution.py:226
  129.6 4.0 %collective-permute-start.16 = (bf16[512,128]{1,0:T(8,128)(2,1)S(1)}, bf16[512,128]{1,0:T(8,128)(2,1)S(1)}, u32[]{:S(2)}, u32[]{:S(2)}) collective-permute-start(bf16[512,128]{1,0:T(8,128)(2,1)S(1)} %shard_map.49), channel_id=1, source_target_pairs={{0,8},{1,9},{2,10},{3,11},{4,12},{5,13},{6,14},{7,15},{8,0},{9,1},... | collective-permute-start | bytes 393224 | tf_op jit(solution)/shard_map/ppermute | solution.py:31
  133.7 2.3 %collective-permute-done.16 = bf16[512,128]{1,0:T(8,128)(2,1)S(1)} collective-permute-done((bf16[512,128]{1,0:T(8,128)(2,1)S(1)}, bf16[512,128]{1,0:T(8,128)(2,1)S(1)}, u32[]{:S(2)}, u32[]{:S(2)}) %collective-permute-start.16) | collective-permute-done | bytes 131104 | tf_op jit(solution)/shard_map/ppermute | solution.py:31
  136.0 4.7 %collective-permute-start.22 = (bf16[512,256]{1,0:T(8,128)(2,1)S(1)}, bf16[512,256]{1,0:T(8,128)(2,1)S(1)}, u32[]{:S(2)}, u32[]{:S(2)}) collective-permute-start(bf16[512,256]{1,0:T(8,128)(2,1)S(1)} %pad_maximum_fusion.4.refs_0_), channel_id=1, source_target_pairs={{0,2},{1,3},{2,4},{3,5},{4,6},{5,7},{6,0},{7,1},{8,10},{9,11},{10,... | collective-permute-start | bytes 786440 | tf_op jit(solution)/shard_map/ppermute | solution.py:31
  140.8 8.7 %collective-permute-start.24 = (bf16[2048,128]{1,0:T(8,128)(2,1)S(1)}, bf16[2048,128]{1,0:T(8,128)(2,1)S(1)}, u32[]{:S(2)}, u32[]{:S(2)}) collective-permute-start(bf16[2048,128]{1,0:T(8,128)(2,1)S(1)} %get-tuple-element.20.refs_8_), channel_id=1, source_target_pairs={{0,256},{1,257},{2,258},{3,259},{4,260},{5,261},{6,262},{7,263},{8... | collective-permute-start | bytes 1572872 | tf_op jit(solution)/shard_map/ppermute | solution.py:31
  149.5 2.8 %collective-permute-start.20 = (bf16[512,256]{1,0:T(8,128)(2,1)S(1)}, bf16[512,256]{1,0:T(8,128)(2,1)S(1)}, u32[]{:S(2)}, u32[]{:S(2)}) collective-permute-start(bf16[512,256]{1,0:T(8,128)(2,1)S(1)} %pad_maximum_fusion.4.refs_0_), channel_id=1, source_target_pairs={{0,4},{1,5},{2,6},{3,7},{4,0},{5,1},{6,2},{7,3},{8,12},{9,13},{10,... | collective-permute-start | bytes 786440 | tf_op jit(solution)/shard_map/ppermute | solution.py:31
  152.4 4.0 %collective-permute-start.18 = (bf16[512,256]{1,0:T(8,128)(2,1)S(1)}, bf16[512,256]{1,0:T(8,128)(2,1)S(1)}, u32[]{:S(2)}, u32[]{:S(2)}) collective-permute-start(bf16[512,256]{1,0:T(8,128)(2,1)S(1)} %pad_maximum_fusion.4.refs_0_), channel_id=1, source_target_pairs={{0,6},{1,7},{2,0},{3,1},{4,2},{5,3},{6,4},{7,5},{8,14},{9,15},{10,... | collective-permute-start | bytes 786440 | tf_op jit(solution)/shard_map/ppermute | solution.py:31
  156.3 6.1 %collective-permute-start.17 = (bf16[512,256]{1,0:T(8,128)(2,1)S(1)}, bf16[512,256]{1,0:T(8,128)(2,1)S(1)}, u32[]{:S(2)}, u32[]{:S(2)}) collective-permute-start(bf16[512,256]{1,0:T(8,128)(2,1)S(1)} %pad_maximum_fusion.4.refs_0_), channel_id=1, source_target_pairs={{0,1},{1,0},{2,3},{3,2},{4,5},{5,4},{6,7},{7,6},{8,9},{9,8},{10,11... | collective-permute-start | bytes 786440 | tf_op jit(solution)/shard_map/ppermute | solution.py:31
  162.5 1.9 %collective-permute-start.23 = (bf16[512,256]{1,0:T(8,128)(2,1)S(1)}, bf16[512,256]{1,0:T(8,128)(2,1)S(1)}, u32[]{:S(2)}, u32[]{:S(2)}) collective-permute-start(bf16[512,256]{1,0:T(8,128)(2,1)S(1)} %collective-permute-done.22.refs_6_), channel_id=1, source_target_pairs={{0,1},{1,0},{2,3},{3,2},{4,5},{5,4},{6,7},{7,6},{8,9},{9,8},{10,11... | collective-permute-start | bytes 786440 | tf_op jit(solution)/shard_map/ppermute | solution.py:31
  164.4 2.4 %collective-permute-start.21 = (bf16[512,256]{1,0:T(8,128)(2,1)S(1)}, bf16[512,256]{1,0:T(8,128)(2,1)S(1)}, u32[]{:S(2)}, u32[]{:S(2)}) collective-permute-start(bf16[512,256]{1,0:T(8,128)(2,1)S(1)} %collective-permute-done.20.refs_4_), channel_id=1, source_target_pairs={{0,1},{1,0},{2,3},{3,2},{4,5},{5,4},{6,7},{7,6},{8,9},{9,8},{10,11... | collective-permute-start | bytes 786440 | tf_op jit(solution)/shard_map/ppermute | solution.py:31
  170.3 2.0 %shard_map.50 = bf16[512,256]{1,0:T(8,128)(2,1)} custom-call(s32[5]{0:T(128)S(1)} %stack.23.pos, bf16[512,256]{1,0:T(8,128)(2,1)S(1)} %pad_maximum_fusion.4.refs_0_, bf16[512,256]{1,0:T(8,128)(2,1)S(1)} %collective-permute-done.17.refs_1_, bf16[512,256]{1,0:T(8,128)(2,1)S(1)} %collective-permute-done.18.refs_2_, ...), custom_call_target="tpu_custom_call" | custom-call | flops 536870912 | bytes 4194304 | tf_op jit(solution)/shard_map/pallas_call | solution.py:39
  (36 shorter events, 11.3 us)
Async XLA Ops:
  0.0 42.4 %copy-start = (bf16[512,256]{1,0:T(8,128)(2,1)S(1)}, bf16[512,256]{1,0:T(8,128)(2,1)}, u32[]{:S(2)}) copy-start(bf16[512,256]{1,0:T(8,128)(2,1)} %refs_10_.1) | copy-start | bytes 786436
  0.0 9.8 %collective-permute-start.9 = (bf16[128,128]{1,0:T(8,128)(2,1)}, bf16[128,128]{1,0:T(8,128)(2,1)S(1)}, u32[]{:S(2)}, u32[]{:S(2)}) collective-permute-start(bf16[128,128]{1,0:T(8,128)(2,1)} %bitcast.18), channel_id=1, source_target_pairs={{0,0},{1,32},{2,64},{3,96},{4,128},{5,160},{6,192},{7,224},{8,256}... | collective-permute-start | bytes 98312 | tf_op jit(solution)/shard_map/ppermute | solution.py:31
  9.8 21.9 %collective-permute-start.10 = (bf16[128,512]{1,0:T(8,128)(2,1)S(1)}, bf16[128,512]{1,0:T(8,128)(2,1)S(1)}, u32[]{:S(2)}, u32[]{:S(2)}) collective-permute-start(bf16[128,512]{1,0:T(8,128)(2,1)S(1)} %pad_maximum_fusion.5), channel_id=1, source_target_pairs={{0,128},{1,129},{2,130},{3,131},{4,132},{5,133},{6,134},{7,135},{8... | collective-permute-start | bytes 393224 | tf_op jit(solution)/shard_map/ppermute | solution.py:31
  31.7 22.5 %collective-permute-start.11 = (bf16[256,512]{1,0:T(8,128)(2,1)S(1)}, bf16[256,512]{1,0:T(8,128)(2,1)S(1)}, u32[]{:S(2)}, u32[]{:S(2)}) collective-permute-start(bf16[256,512]{1,0:T(8,128)(2,1)S(1)} %pad_maximum_fusion.3), channel_id=1, source_target_pairs={{0,64},{1,193},{2,66},{3,195},{4,68},{5,197},{6,70},{7,199},{8,72}... | collective-permute-start | bytes 786440 | tf_op jit(solution)/shard_map/ppermute | solution.py:31
  42.4 15.8 %collective-permute-start = (bf16[512,256]{1,0:T(8,128)(2,1)S(1)}, bf16[512,256]{1,0:T(8,128)(2,1)S(1)}, u32[]{:S(2)}, u32[]{:S(2)}) collective-permute-start(bf16[512,256]{1,0:T(8,128)(2,1)S(1)} %copy-done), channel_id=1, source_target_pairs={{0,8},{1,9},{2,10},{3,11},{4,12},{5,13},{6,14},{7,15},{8,264},{9,2... | collective-permute-start | bytes 786440 | tf_op jit(solution)/shard_map/ppermute | solution.py:31
  46.4 11.8 %collective-permute-start.1 = (bf16[512,256]{1,0:T(8,128)(2,1)S(1)}, bf16[512,256]{1,0:T(8,128)(2,1)S(1)}, u32[]{:S(2)}, u32[]{:S(2)}) collective-permute-start(bf16[512,256]{1,0:T(8,128)(2,1)S(1)} %copy-done), channel_id=1, source_target_pairs={{8,256},{9,257},{10,258},{11,259},{12,260},{13,261},{14,262},{15,2... | collective-permute-start | bytes 786440 | tf_op jit(solution)/shard_map/ppermute | solution.py:31
  54.2 16.6 %collective-permute-start.12 = (bf16[512,512]{1,0:T(8,128)(2,1)S(1)}, bf16[512,512]{1,0:T(8,128)(2,1)}, u32[]{:S(2)}, u32[]{:S(2)}) collective-permute-start(bf16[512,512]{1,0:T(8,128)(2,1)S(1)} %pad_maximum_fusion.2), channel_id=1, source_target_pairs={{0,32},{1,225},{2,34},{3,227},{4,36},{5,229},{6,38},{7,231},{8,40}... | collective-permute-start | bytes 1572872 | tf_op jit(solution)/shard_map/ppermute | solution.py:31
  58.3 23.6 %collective-permute-start.7 = (bf16[1024,256]{1,0:T(8,128)(2,1)S(1)}, bf16[1024,256]{1,0:T(8,128)(2,1)S(1)}, u32[]{:S(2)}, u32[]{:S(2)}) collective-permute-start(bf16[1024,256]{1,0:T(8,128)(2,1)S(1)} %pad_maximum_fusion.1.refs_0_), channel_id=1, source_target_pairs={{0,2},{1,3},{2,4},{3,5},{4,6},{5,7},{6,0},{7,1},{8,10},{9,11},{10,... | collective-permute-start | bytes 1572872 | tf_op jit(solution)/shard_map/ppermute | solution.py:31
  64.6 22.1 %collective-permute-start.5 = (bf16[1024,256]{1,0:T(8,128)(2,1)S(1)}, bf16[1024,256]{1,0:T(8,128)(2,1)}, u32[]{:S(2)}, u32[]{:S(2)}) collective-permute-start(bf16[1024,256]{1,0:T(8,128)(2,1)S(1)} %pad_maximum_fusion.1.refs_0_), channel_id=1, source_target_pairs={{0,4},{1,5},{2,6},{3,7},{4,0},{5,1},{6,2},{7,3},{8,12},{9,13},{10,... | collective-permute-start | bytes 1572872 | tf_op jit(solution)/shard_map/ppermute | solution.py:31
  67.6 24.2 %collective-permute-start.3 = (bf16[1024,256]{1,0:T(8,128)(2,1)S(1)}, bf16[1024,256]{1,0:T(8,128)(2,1)}, u32[]{:S(2)}, u32[]{:S(2)}) collective-permute-start(bf16[1024,256]{1,0:T(8,128)(2,1)S(1)} %pad_maximum_fusion.1.refs_0_), channel_id=1, source_target_pairs={{0,6},{1,7},{2,0},{3,1},{4,2},{5,3},{6,4},{7,5},{8,14},{9,15},{10,... | collective-permute-start | bytes 1572872 | tf_op jit(solution)/shard_map/ppermute | solution.py:31
  72.0 23.9 %collective-permute-start.13 = (bf16[1024,512]{1,0:T(8,128)(2,1)S(1)}, bf16[1024,512]{1,0:T(8,128)(2,1)S(1)}, u32[]{:S(2)}, u32[]{:S(2)}) collective-permute-start(bf16[1024,512]{1,0:T(8,128)(2,1)S(1)} %pad_maximum_fusion.refs_8_), channel_id=1, source_target_pairs={{0,16},{1,241},{2,18},{3,243},{4,20},{5,245},{6,22},{7,247},{8,24}... | collective-permute-start | bytes 3145736 | tf_op jit(solution)/shard_map/ppermute | solution.py:31
  78.0 15.8 %collective-permute-start.2 = (bf16[1024,256]{1,0:T(8,128)(2,1)S(1)}, bf16[1024,256]{1,0:T(8,128)(2,1)}, u32[]{:S(2)}, u32[]{:S(2)}) collective-permute-start(bf16[1024,256]{1,0:T(8,128)(2,1)S(1)} %pad_maximum_fusion.1.refs_0_), channel_id=1, source_target_pairs={{0,1},{1,0},{2,3},{3,2},{4,5},{5,4},{6,7},{7,6},{8,9},{9,8},{10,11... | collective-permute-start | bytes 1572872 | tf_op jit(solution)/shard_map/ppermute | solution.py:31
  81.9 11.9 %collective-permute-start.8 = (bf16[1024,256]{1,0:T(8,128)(2,1)S(1)}, bf16[1024,256]{1,0:T(8,128)(2,1)}, u32[]{:S(2)}, u32[]{:S(2)}) collective-permute-start(bf16[1024,256]{1,0:T(8,128)(2,1)S(1)} %collective-permute-done.7.refs_6_), channel_id=1, source_target_pairs={{0,1},{1,0},{2,3},{3,2},{4,5},{5,4},{6,7},{7,6},{8,9},{9,8},{10,11... | collective-permute-start | bytes 1572872 | tf_op jit(solution)/shard_map/ppermute | solution.py:31
  86.7 7.1 %collective-permute-start.6 = (bf16[1024,256]{1,0:T(8,128)(2,1)}, bf16[1024,256]{1,0:T(8,128)(2,1)}, u32[]{:S(2)}, u32[]{:S(2)}) collective-permute-start(bf16[1024,256]{1,0:T(8,128)(2,1)} %collective-permute-done.5.refs_4_), channel_id=1, source_target_pairs={{0,1},{1,0},{2,3},{3,2},{4,5},{5,4},{6,7},{7,6},{8,9},{9,8},{10,11... | collective-permute-start | bytes 1572872 | tf_op jit(solution)/shard_map/ppermute | solution.py:31
  91.8 4.1 %collective-permute-start.4 = (bf16[1024,256]{1,0:T(8,128)(2,1)}, bf16[1024,256]{1,0:T(8,128)(2,1)}, u32[]{:S(2)}, u32[]{:S(2)}) collective-permute-start(bf16[1024,256]{1,0:T(8,128)(2,1)} %collective-permute-done.3.refs_2_), channel_id=1, source_target_pairs={{0,1},{1,0},{2,3},{3,2},{4,5},{5,4},{6,7},{7,6},{8,9},{9,8},{10,11... | collective-permute-start | bytes 1572872 | tf_op jit(solution)/shard_map/ppermute | solution.py:31
  100.4 20.0 %collective-permute-start.14 = (bf16[512,512]{1,0:T(8,128)(2,1)S(1)}, bf16[512,512]{1,0:T(8,128)(2,1)S(1)}, u32[]{:S(2)}, u32[]{:S(2)}) collective-permute-start(bf16[512,512]{1,0:T(8,128)(2,1)S(1)} %get-tuple-element.15), channel_id=1, source_target_pairs={{0,256},{1,257},{2,258},{3,259},{4,260},{5,261},{6,262},{7,263},{8... | collective-permute-start | bytes 1572872 | tf_op jit(solution)/shard_map/ppermute | solution.py:31
  120.7 7.1 %collective-permute-start.15 = (bf16[512,256]{1,0:T(8,128)(2,1)S(1)}, bf16[512,256]{1,0:T(8,128)(2,1)S(1)}, u32[]{:S(2)}, u32[]{:S(2)}) collective-permute-start(bf16[512,256]{1,0:T(8,128)(2,1)S(1)} %get-tuple-element.17.kv_ref), channel_id=1, source_target_pairs={{0,16},{16,32},{32,48},{48,64},{64,80},{80,96},{96,112},{112,128},... | collective-permute-start | bytes 786440 | tf_op jit(solution)/shard_map/ppermute | solution.py:226
  129.6 6.4 %collective-permute-start.16 = (bf16[512,128]{1,0:T(8,128)(2,1)S(1)}, bf16[512,128]{1,0:T(8,128)(2,1)S(1)}, u32[]{:S(2)}, u32[]{:S(2)}) collective-permute-start(bf16[512,128]{1,0:T(8,128)(2,1)S(1)} %shard_map.49), channel_id=1, source_target_pairs={{0,8},{1,9},{2,10},{3,11},{4,12},{5,13},{6,14},{7,15},{8,0},{9,1},... | collective-permute-start | bytes 393224 | tf_op jit(solution)/shard_map/ppermute | solution.py:31
  136.0 26.4 %collective-permute-start.22 = (bf16[512,256]{1,0:T(8,128)(2,1)S(1)}, bf16[512,256]{1,0:T(8,128)(2,1)S(1)}, u32[]{:S(2)}, u32[]{:S(2)}) collective-permute-start(bf16[512,256]{1,0:T(8,128)(2,1)S(1)} %pad_maximum_fusion.4.refs_0_), channel_id=1, source_target_pairs={{0,2},{1,3},{2,4},{3,5},{4,6},{5,7},{6,0},{7,1},{8,10},{9,11},{10,... | collective-permute-start | bytes 786440 | tf_op jit(solution)/shard_map/ppermute | solution.py:31
  140.8 28.0 %collective-permute-start.24 = (bf16[2048,128]{1,0:T(8,128)(2,1)S(1)}, bf16[2048,128]{1,0:T(8,128)(2,1)S(1)}, u32[]{:S(2)}, u32[]{:S(2)}) collective-permute-start(bf16[2048,128]{1,0:T(8,128)(2,1)S(1)} %get-tuple-element.20.refs_8_), channel_id=1, source_target_pairs={{0,256},{1,257},{2,258},{3,259},{4,260},{5,261},{6,262},{7,263},{8... | collective-permute-start | bytes 1572872 | tf_op jit(solution)/shard_map/ppermute | solution.py:31
  149.5 14.9 %collective-permute-start.20 = (bf16[512,256]{1,0:T(8,128)(2,1)S(1)}, bf16[512,256]{1,0:T(8,128)(2,1)S(1)}, u32[]{:S(2)}, u32[]{:S(2)}) collective-permute-start(bf16[512,256]{1,0:T(8,128)(2,1)S(1)} %pad_maximum_fusion.4.refs_0_), channel_id=1, source_target_pairs={{0,4},{1,5},{2,6},{3,7},{4,0},{5,1},{6,2},{7,3},{8,12},{9,13},{10,... | collective-permute-start | bytes 786440 | tf_op jit(solution)/shard_map/ppermute | solution.py:31
  152.4 14.5 %collective-permute-start.18 = (bf16[512,256]{1,0:T(8,128)(2,1)S(1)}, bf16[512,256]{1,0:T(8,128)(2,1)S(1)}, u32[]{:S(2)}, u32[]{:S(2)}) collective-permute-start(bf16[512,256]{1,0:T(8,128)(2,1)S(1)} %pad_maximum_fusion.4.refs_0_), channel_id=1, source_target_pairs={{0,6},{1,7},{2,0},{3,1},{4,2},{5,3},{6,4},{7,5},{8,14},{9,15},{10,... | collective-permute-start | bytes 786440 | tf_op jit(solution)/shard_map/ppermute | solution.py:31
  156.3 12.4 %collective-permute-start.17 = (bf16[512,256]{1,0:T(8,128)(2,1)S(1)}, bf16[512,256]{1,0:T(8,128)(2,1)S(1)}, u32[]{:S(2)}, u32[]{:S(2)}) collective-permute-start(bf16[512,256]{1,0:T(8,128)(2,1)S(1)} %pad_maximum_fusion.4.refs_0_), channel_id=1, source_target_pairs={{0,1},{1,0},{2,3},{3,2},{4,5},{5,4},{6,7},{7,6},{8,9},{9,8},{10,11... | collective-permute-start | bytes 786440 | tf_op jit(solution)/shard_map/ppermute | solution.py:31
  162.5 6.3 %collective-permute-start.23 = (bf16[512,256]{1,0:T(8,128)(2,1)S(1)}, bf16[512,256]{1,0:T(8,128)(2,1)S(1)}, u32[]{:S(2)}, u32[]{:S(2)}) collective-permute-start(bf16[512,256]{1,0:T(8,128)(2,1)S(1)} %collective-permute-done.22.refs_6_), channel_id=1, source_target_pairs={{0,1},{1,0},{2,3},{3,2},{4,5},{5,4},{6,7},{7,6},{8,9},{9,8},{10,11... | collective-permute-start | bytes 786440 | tf_op jit(solution)/shard_map/ppermute | solution.py:31
  164.4 4.4 %collective-permute-start.21 = (bf16[512,256]{1,0:T(8,128)(2,1)S(1)}, bf16[512,256]{1,0:T(8,128)(2,1)S(1)}, u32[]{:S(2)}, u32[]{:S(2)}) collective-permute-start(bf16[512,256]{1,0:T(8,128)(2,1)S(1)} %collective-permute-done.20.refs_4_), channel_id=1, source_target_pairs={{0,1},{1,0},{2,3},{3,2},{4,5},{5,4},{6,7},{7,6},{8,9},{9,8},{10,11... | collective-permute-start | bytes 786440 | tf_op jit(solution)/shard_map/ppermute | solution.py:31
  166.8 3.4 %collective-permute-start.19 = (bf16[512,256]{1,0:T(8,128)(2,1)S(1)}, bf16[512,256]{1,0:T(8,128)(2,1)S(1)}, u32[]{:S(2)}, u32[]{:S(2)}) collective-permute-start(bf16[512,256]{1,0:T(8,128)(2,1)S(1)} %collective-permute-done.18.refs_2_), channel_id=1, source_target_pairs={{0,1},{1,0},{2,3},{3,2},{4,5},{5,4},{6,7},{7,6},{8,9},{9,8},{10,11... | collective-permute-start | bytes 786440 | tf_op jit(solution)/shard_map/ppermute | solution.py:31
where the time goes:
time: 173 us; the launch traced here: 172 us
  starting transfers between devices  124 us (72%)
  waiting for transfers between devices  35.9 us (21%)
  Pallas kernels  8.92 us (5%)
  other arithmetic  2.95 us (2%)
    ppermute x24, starting transfers between devices, permute(): return lax.ppermute(value, AXES, pairs_of(target))  121 us
    ppermute x24, waiting for transfers between devices, permute(): return lax.ppermute(value, AXES, pairs_of(target))  31.9 us
    pallas_call x5, Pallas kernels, run(): pl.pallas_call(body, out_shape=outs, in_specs=specs, out_specs=jax.tree.m...  8.92 us
    ppermute x1, waiting for transfers between devices, layer(): prev = lax.ppermute(kv, 'ctx', [(i, i + 1) for i in range(31)])  4.02 us
  transfers between devices with their start and end apart: 25, of which 9 were waited for; matrix products, arithmetic and copies ran while one was open for 2% of the time, Pallas kernels for 0%

commit v1 on v0

v1 whole, which is shorter than its diff:
```python
import math

import jax
import jax.numpy as jnp
from jax import lax
from jax.experimental import pallas as pl
from jax.experimental.pallas import tpu as pltpu
from jax.sharding import PartitionSpec as P


INTERPRET = False
AXES = ("ctx", "tp")
BF = jnp.bfloat16
F32 = jnp.float32
STEPS = ((0, -4, 4, 8), (2, 6), (-2, -6), (1, -3, 5, 9), (-1, -5, 3, 7))


def pairs_of(target):
    pairs = []
    for src in range(512):
        ctx, tp = divmod(src, 16)
        a, z, b, y, k = ctx // 16, ctx % 16, tp // 8, tp // 2 % 4, tp % 2
        to = target(a, z, b, y, k)
        if to is not None:
            a, z, b, y, k = to
            pairs.append((src, (a * 16 + z % 16) * 16 + b * 8 + y % 4 * 2 + k))
    return pairs


def permute(value, target):
    return lax.ppermute(value, AXES, pairs_of(target))


def call(body, outs, scratch=(), flops=0, nbytes=1 << 20, vmem=24 << 20, scalars=True):
    def run(*args):
        specs = [pl.BlockSpec(memory_space=pltpu.VMEM) for _ in args]
        if scalars:
            specs[0] = pl.BlockSpec(memory_space=pltpu.SMEM)
        return pl.pallas_call(
            body,
            out_shape=outs,
            in_specs=specs,
            out_specs=jax.tree.map(lambda _: pl.BlockSpec(memory_space=pltpu.VMEM), outs),
            scratch_shapes=list(scratch),
            compiler_params=pltpu.CompilerParams(vmem_limit_bytes=vmem),
            cost_estimate=pl.CostEstimate(flops=flops, bytes_accessed=nbytes, transcendentals=0),
            interpret=INTERPRET,
        )(*args)

    return run


def shape(dims, dtype):
    return jax.ShapeDtypeStruct(dims, dtype)


def place(pos):
    ctx, tp = pos[0], pos[1]
    return ctx >> 4, ctx & 15, tp >> 3, (tp >> 1) & 3, tp & 1


def gather_z(chunk, core):
    def move(value, by):
        return permute(value, lambda a, z, b, y, k: (a, z + by, b, y, k))

    up4 = move(chunk, 4)
    down4 = move(chunk, -4)
    relay = permute(
        jnp.where(core == 0, down4, up4), lambda a, z, b, y, k: (a, z + (4 if k else 12), b, y, k)
    )
    down2 = move(jnp.concatenate([chunk, down4], axis=0), -2)
    up2 = move(jnp.concatenate([chunk, up4], axis=0), 2)
    held = jnp.concatenate([chunk, up4, down4, relay], axis=0)
    down1 = move(held, -1)
    up1 = move(held, 1)
    return held, down2, up2, down1, up1


def project_rows(pos, blocks, weights, first, seg):
    _, _, _, y, k = place(pos)
    rows = weights.shape[0] // 16
    tile = min(seg, 256)
    for r in range(0, seg, tile):
        acc = jnp.zeros((tile, weights.shape[1]), F32)
        ssq = jnp.zeros((tile, 1), F32)
        for i in range(8):
            yy = (y + i // 2) & 3
            kk = k if i % 2 == 0 else 1 - k
            at = pl.multiple_of((yy * 2 + kk) * 2 * rows, 2 * rows)
            block = blocks[i][first + r : first + r + tile, :]
            acc += jnp.dot(block, weights[pl.ds(at, 2 * rows), :], preferred_element_type=F32)
            wider = block.astype(F32)
            ssq += jnp.sum(wider * wider, axis=1, keepdims=True)
        yield slice(r, r + tile), acc, ssq


def project_other_body(pos, *refs):
    blocks, parts, (send_ref, w_ref, out_w_ref) = refs[:8], refs[8:13], refs[13:]
    _, z, _, _, _ = place(pos)
    rows = w_ref.shape[0] // 16
    seg = send_ref.shape[0]
    wide = w_ref.shape[1]
    for part, steps in zip(parts, STEPS):
        for i, step in enumerate(steps):
            at = pl.multiple_of(((z + step + 16) & 15) * rows, rows)
            w_ref[pl.ds(at, rows), :] = part[i * rows : (i + 1) * rows, :wide]
            out_w_ref[pl.ds(at, rows), :] = part[i * rows : (i + 1) * rows, wide:]
    lanes = send_ref.shape[1] - wide
    for at, acc, ssq in project_rows(pos, blocks, w_ref, seg, seg):
        send_ref[at, :wide] = acc.astype(BF)
        high = ssq.astype(BF).astype(F32)
        lane = lax.broadcasted_iota(jnp.int32, (ssq.shape[0], lanes), 1)
        send_ref[at, wide:] = jnp.where(lane < lanes // 2, high, ssq - high).astype(BF)


def project_own_body(pos, *refs):
    blocks, (w_ref, own_ref, ssq_ref) = refs[:8], refs[8:]
    for at, acc, ssq in project_rows(pos, blocks, w_ref, 0, own_ref.shape[0]):
        own_ref[at, :] = acc
        ssq_ref[at, :] = jnp.broadcast_to(ssq, (ssq.shape[0], ssq_ref.shape[1]))


def combine_body(own_ref, ssq_ref, got_ref, q_ref, kv_ref, *, features):
    hd = q_ref.shape[1]
    wide = 3 * hd
    lanes = got_ref.shape[1] - wide
    half = got_ref[:, wide:].astype(F32)
    ssq = ssq_ref[:, :1] + half[:, :1] + half[:, lanes // 2 : lanes // 2 + 1]
    scale = lax.rsqrt(ssq * (1.0 / features) + 1e-06)
    total = (own_ref[...] + got_ref[:, :wide].astype(F32)) * scale
    q_ref[...] = total[:, :hd].astype(BF)
    kv_ref[...] = total[:, hd:].astype(BF)


def scores_of(q, keys):
    hd = q.shape[1]
    return lax.dot_general(
        q, keys, (((1,), (1,)), ((), ())), preferred_element_type=F32
    ) * (1.0 / math.sqrt(hd))


def own_body(q_ref, kv_ref, e_ref, sum_ref):
    hd = q_ref.shape[1]
    scores = scores_of(q_ref[...], kv_ref[:, :hd])
    row = lax.broadcasted_iota(jnp.int32, scores.shape, 0)
    col = lax.broadcasted_iota(jnp.int32, scores.shape, 1)
    e = jnp.where(col <= row, jnp.exp(scores), 0.0)
    e_ref[...] = e
    sum_ref[...] = jnp.broadcast_to(jnp.sum(e, axis=1, keepdims=True), sum_ref.shape)


def attend_body(pos, q_ref, kv_ref, prev_ref, e_ref, sum_ref, out_ref):
    hd = q_ref.shape[1]
    e = jnp.exp(scores_of(q_ref[...], prev_ref[:, :hd]))
    first = pos[0] == 0
    e = jnp.where(jnp.full(e.shape, first), 0.0, e)
    total = sum_ref[:, :1] + jnp.sum(e, axis=1, keepdims=True)
    inverse = 1.0 / total
    out = jnp.dot((e_ref[...] * inverse).astype(BF), kv_ref[:, hd:], preferred_element_type=F32)
    out += jnp.dot((e * inverse).astype(BF), prev_ref[:, hd:], preferred_element_type=F32)
    out_ref[...] = out.astype(BF)


def output_of(pos, pieces, w_own, w_other, core):
    a, _, b, y, _ = place(pos)
    hd = w_own.shape[1]
    total = None
    for i in range(4):
        yy = (y + i) & 3
        at = pl.multiple_of(((core + 2 * yy + 2 * y) & 7) * 2 * hd, 2 * hd)
        own = w_own[pl.ds(at, 2 * hd), :]
        other = w_other[pl.ds(at, 2 * hd), :]
        same = jnp.full(own.shape, a == b)
        rows = []
        for both in (jnp.where(same, own, other), jnp.where(same, other, own)):
            rows.append(jnp.concatenate([both[:hd], both[hd:]], axis=1))
        part = jnp.dot(pieces[i][...], jnp.concatenate(rows, axis=0), preferred_element_type=F32)
        total = part if total is None else total + part
    return total


def output_other_body(pos, *refs):
    pieces, (w_own, w_other, send_ref) = refs[:4], refs[4:]
    core = 1 - place(pos)[4]
    send_ref[...] = output_of(pos, pieces, w_own, w_other, core).astype(BF)


def output_own_body(pos, *refs):
    pieces, (w_own, w_other, hidden_ref, out_ref) = refs[:4], refs[4:]
    core = place(pos)[4]
    out_ref[...] = hidden_ref[...].astype(F32) + output_of(pos, pieces, w_own, w_other, core)


def add_body(own_ref, got_ref, out_ref):
    out_ref[...] = (own_ref[...] + got_ref[...].astype(F32)).astype(BF)


def swap_hi(a, z, b, y, k):
    return 1 - a, z, b, y, k


def swap_core(a, z, b, y, k):
    return a, z, b, y, 1 - k


def around(value):
    pieces = [value]
    for by in (1, 2, 3):
        pieces.append(permute(value, lambda a, z, b, y, k: (a, z, b, y - by, k)))
    return pieces


def layer(hidden, norm_gain, w_qkv, w_out):
    seg, feats = hidden.shape
    hd = w_out.shape[1]
    ctx, tp = lax.axis_index("ctx"), lax.axis_index("tp")
    pos = jnp.stack([ctx, tp]).astype(jnp.int32)
    same = (ctx >> 4) == (tp >> 3)

    piece = permute(w_out[0], lambda a, z, b, y, k: (b, z + 4 * y, a, z // 4, k))
    folded = (w_qkv[0].astype(F32) * norm_gain[0].astype(F32)[None, :, None]).astype(BF)
    chunk = jnp.concatenate([folded[0], folded[1], folded[2], piece], axis=1)
    parts = gather_z(chunk, tp & 1)

    corner = {(0, 0): (0, 1), (0, 1): (1, 1), (1, 1): (1, 0), (1, 0): (0, 0)}
    turn = permute(hidden, lambda a, z, b, y, k: (*_at(corner, a, b, z), y, k))
    cross = permute(hidden, lambda a, z, b, y, k: (b, z, a, y, k) if a != b else None)
    own = jnp.where(same, hidden, turn)
    other = jnp.where(same, turn, cross)
    blocks = []
    for block in around(jnp.concatenate([own, other], axis=0)):
        blocks += [block, permute(block, swap_core)]

    send, weights, out_w = call(
        project_other_body,
        (
            shape((seg, 4 * hd), BF),
            shape((16 * hd, 3 * hd), BF),
            shape((16 * hd, hd), BF),
        ),
        flops=2 * seg * 8 * feats * 3 * hd,
        nbytes=8 << 20,
    )(pos, *blocks, *parts)
    got = permute(send, swap_hi)
    own_part, own_ssq = call(
        project_own_body,
        (shape((seg, 3 * hd), F32), shape((seg, hd), F32)),
        flops=2 * seg * 8 * feats * 3 * hd,
        nbytes=8 << 20,
    )(pos, *blocks, weights)
    q, kv = call(
        lambda *refs: combine_body(*refs, features=16 * feats),
        (shape((seg, hd), BF), shape((seg, 2 * hd), BF)),
        nbytes=2 << 20,
        scalars=False,
    )(own_part, own_ssq, got)
    prev = lax.ppermute(kv, "ctx", [(i, i + 1) for i in range(31)])
    e_own, sum_own = call(
        own_body,
        (shape((seg, seg), F32), shape((seg, hd), F32)),
        flops=2 * seg * seg * hd,
        nbytes=2 << 20,
        scalars=False,
    )(q, kv)
    attended = call(
        attend_body, shape((seg, hd), BF), flops=6 * seg * seg * hd, nbytes=2 << 20
    )(pos, q, kv, prev, e_own, sum_own)

    facing = permute(attended, lambda a, z, b, y, k: (a, z, 1 - b, y, k))
    out_w_other = permute(out_w, swap_hi)
    pieces = around(jnp.concatenate([attended, facing], axis=1))
    sizes = dict(flops=2 * seg * feats * 8 * hd, nbytes=3 << 20)
    out_send = call(output_other_body, shape((seg, feats), BF), **sizes)(
        pos, *pieces, out_w, out_w_other
    )
    out_got = permute(out_send, swap_core)
    out_own = call(output_own_body, shape((seg, feats), F32), **sizes)(
        pos, *pieces, out_w, out_w_other, hidden
    )
    return call(add_body, shape((seg, feats), BF), scalars=False)(out_own, out_got)


def _at(corner, a, b, z):
    to = corner[a, b]
    return to[0], z, to[1]


def solution(mesh):
    placed = (P("ctx", "tp"), P(None, "ctx"), P(None, None, "ctx", "tp"), P(None, "tp", "ctx"))
    return jax.shard_map(
        layer, mesh=mesh, in_specs=placed, out_specs=P("ctx", "tp"), check_vma=False
    )
```

time: 173 us -> 176 us (1.017)
  the two profiles are of different devices: /device:TPU:1 before, /device:TPU:11 now
where the time goes in v1:
time: 176 us; the launch traced here: 175 us
  starting transfers between devices  106 us (60%)
  waiting for transfers between devices  58 us (33%)
  Pallas kernels  9.2 us (5%)
  other arithmetic  1.94 us (1%)
    ppermute x24, starting transfers between devices, permute(): return lax.ppermute(value, AXES, pairs_of(target))  104 us
    ppermute x24, waiting for transfers between devices, permute(): return lax.ppermute(value, AXES, pairs_of(target))  58 us
    pallas_call x8, Pallas kernels, run(): pl.pallas_call(body, out_shape=outs, in_specs=specs, out_specs=jax.tree.m...  9.2 us
  transfers between devices with their start and end apart: 25, of which 10 were waited for; matrix products, arithmetic and copies ran while one was open for 1% of the time, Pallas kernels for 3%

profile of v1, /device:TPU:11, one launch (start us, length us, event | category | flops | bytes accessed | tf_op | source)
XLA Modules:
  0.0 175.3 jit_solution(1995267559664651788)
XLA Ops:
  0.0 9.8 %collective-permute-start.9 = (bf16[128,128]{1,0:T(8,128)(2,1)}, bf16[128,128]{1,0:T(8,128)(2,1)S(1)}, u32[]{:S(2)}, u32[]{:S(2)}) collective-permute-start(bf16[128,128]{1,0:T(8,128)(2,1)} %bitcast.15), channel_id=1, source_target_pairs={{0,0},{1,1},{2,64},{3,65},{4,128},{5,129},{6,192},{7,193},{8,256},... | collective-permute-start | bytes 98312 | tf_op jit(solution)/shard_map/ppermute | solution.py:31
  13.1 14.9 %collective-permute-start.11 = (bf16[128,512]{1,0:T(8,128)(2,1)S(1)}, bf16[128,512]{1,0:T(8,128)(2,1)S(1)}, u32[]{:S(2)}, u32[]{:S(2)}) collective-permute-start(bf16[128,512]{1,0:T(8,128)(2,1)S(1)} %pad_maximum_fusion.6), channel_id=1, source_target_pairs={{0,192},{1,193},{2,194},{3,195},{4,196},{5,197},{6,198},{7,199},{8... | collective-permute-start | bytes 393224 | tf_op jit(solution)/shard_map/ppermute | solution.py:31
  28.0 1.9 %collective-permute-start.10 = (bf16[128,512]{1,0:T(8,128)(2,1)S(1)}, bf16[128,512]{1,0:T(8,128)(2,1)S(1)}, u32[]{:S(2)}, u32[]{:S(2)}) collective-permute-start(bf16[128,512]{1,0:T(8,128)(2,1)S(1)} %pad_maximum_fusion.6), channel_id=1, source_target_pairs={{0,64},{1,65},{2,66},{3,67},{4,68},{5,69},{6,70},{7,71},{8,72},{9,... | collective-permute-start | bytes 393224 | tf_op jit(solution)/shard_map/ppermute | solution.py:31
  29.9 2.9 %collective-permute-start = (bf16[512,256]{1,0:T(8,128)(2,1)}, bf16[512,256]{1,0:T(8,128)(2,1)S(1)}, u32[]{:S(2)}, u32[]{:S(2)}) collective-permute-start(bf16[512,256]{1,0:T(8,128)(2,1)} %refs_6_.1), channel_id=1, source_target_pairs={{0,8},{1,9},{2,10},{3,11},{4,12},{5,13},{6,14},{7,15},{8,264},{9,2... | collective-permute-start | bytes 786440 | tf_op jit(solution)/shard_map/ppermute | solution.py:31
  32.8 2.2 %collective-permute-start.1 = (bf16[512,256]{1,0:T(8,128)(2,1)}, bf16[512,256]{1,0:T(8,128)(2,1)S(1)}, u32[]{:S(2)}, u32[]{:S(2)}) collective-permute-start(bf16[512,256]{1,0:T(8,128)(2,1)} %refs_6_.1), channel_id=1, source_target_pairs={{8,256},{9,257},{10,258},{11,259},{12,260},{13,261},{14,262},{15,2... | collective-permute-start | bytes 786440 | tf_op jit(solution)/shard_map/ppermute | solution.py:31
  35.0 3.0 %collective-permute-done.10 = bf16[128,512]{1,0:T(8,128)(2,1)S(1)} collective-permute-done((bf16[128,512]{1,0:T(8,128)(2,1)S(1)}, bf16[128,512]{1,0:T(8,128)(2,1)S(1)}, u32[]{:S(2)}, u32[]{:S(2)}) %collective-permute-start.10) | collective-permute-done | bytes 131104 | tf_op jit(solution)/shard_map/ppermute | solution.py:31
  38.0 2.5 %collective-permute-start.12 = (bf16[128,512]{1,0:T(8,128)(2,1)S(1)}, bf16[128,512]{1,0:T(8,128)(2,1)S(1)}, u32[]{:S(2)}, u32[]{:S(2)}) collective-permute-start(bf16[128,512]{1,0:T(8,128)(2,1)S(1)} %broadcast_select_fusion.2), channel_id=1, source_target_pairs={{0,192},{1,65},{2,194},{3,67},{4,196},{5,69},{6,198},{7,71},{8,200... | collective-permute-start | bytes 393224 | tf_op jit(solution)/shard_map/ppermute | solution.py:31
  40.6 9.2 %collective-permute-start.14 = (bf16[256,512]{1,0:T(8,128)(2,1)S(1)}, bf16[256,512]{1,0:T(8,128)(2,1)S(1)}, u32[]{:S(2)}, u32[]{:S(2)}) collective-permute-start(bf16[256,512]{1,0:T(8,128)(2,1)S(1)} %get-tuple-element.25), channel_id=1, source_target_pairs={{0,32},{1,33},{2,34},{3,35},{4,36},{5,37},{6,38},{7,39},{8,40},{9,... | collective-permute-start | bytes 786440 | tf_op jit(solution)/shard_map/ppermute | solution.py:31
  49.9 1.9 %collective-permute-start.7 = (bf16[1024,256]{1,0:T(8,128)(2,1)S(1)}, bf16[1024,256]{1,0:T(8,128)(2,1)S(1)}, u32[]{:S(2)}, u32[]{:S(2)}) collective-permute-start(bf16[1024,256]{1,0:T(8,128)(2,1)S(1)} %pad_maximum_fusion.refs_0_), channel_id=1, source_target_pairs={{0,2},{1,3},{2,4},{3,5},{4,6},{5,7},{6,0},{7,1},{8,10},{9,11},{10,... | collective-permute-start | bytes 1572872 | tf_op jit(solution)/shard_map/ppermute | solution.py:31
  51.9 4.9 %collective-permute-start.5 = (bf16[1024,256]{1,0:T(8,128)(2,1)S(1)}, bf16[1024,256]{1,0:T(8,128)(2,1)S(1)}, u32[]{:S(2)}, u32[]{:S(2)}) collective-permute-start(bf16[1024,256]{1,0:T(8,128)(2,1)S(1)} %pad_maximum_fusion.refs_0_), channel_id=1, source_target_pairs={{0,4},{1,5},{2,6},{3,7},{4,0},{5,1},{6,2},{7,3},{8,12},{9,13},{10,... | collective-permute-start | bytes 1572872 | tf_op jit(solution)/shard_map/ppermute | solution.py:31
  56.8 4.0 %collective-permute-start.3 = (bf16[1024,256]{1,0:T(8,128)(2,1)S(1)}, bf16[1024,256]{1,0:T(8,128)(2,1)S(1)}, u32[]{:S(2)}, u32[]{:S(2)}) collective-permute-start(bf16[1024,256]{1,0:T(8,128)(2,1)S(1)} %pad_maximum_fusion.refs_0_), channel_id=1, source_target_pairs={{0,6},{1,7},{2,0},{3,1},{4,2},{5,3},{6,4},{7,5},{8,14},{9,15},{10,... | collective-permute-start | bytes 1572872 | tf_op jit(solution)/shard_map/ppermute | solution.py:31
  60.8 8.1 %collective-permute-start.2 = (bf16[1024,256]{1,0:T(8,128)(2,1)S(1)}, bf16[1024,256]{1,0:T(8,128)(2,1)S(1)}, u32[]{:S(2)}, u32[]{:S(2)}) collective-permute-start(bf16[1024,256]{1,0:T(8,128)(2,1)S(1)} %pad_maximum_fusion.refs_0_), channel_id=1, source_target_pairs={{0,1},{1,0},{2,3},{3,2},{4,5},{5,4},{6,7},{7,6},{8,9},{9,8},{10,11... | collective-permute-start | bytes 1572872 | tf_op jit(solution)/shard_map/ppermute | solution.py:31
  68.8 1.9 %collective-permute-start.13 = (bf16[256,512]{1,0:T(8,128)(2,1)S(1)}, bf16[256,512]{1,0:T(8,128)(2,1)S(1)}, u32[]{:S(2)}, u32[]{:S(2)}) collective-permute-start(bf16[256,512]{1,0:T(8,128)(2,1)S(1)} %get-tuple-element.26), channel_id=1, source_target_pairs={{0,224},{1,225},{2,226},{3,227},{4,228},{5,229},{6,230},{7,231},{8... | collective-permute-start | bytes 786440 | tf_op jit(solution)/shard_map/ppermute | solution.py:31
  70.8 12.3 %collective-permute-done.13.refs_9_ = bf16[256,512]{1,0:T(8,128)(2,1)S(1)} collective-permute-done((bf16[256,512]{1,0:T(8,128)(2,1)S(1)}, bf16[256,512]{1,0:T(8,128)(2,1)S(1)}, u32[]{:S(2)}, u32[]{:S(2)}) %collective-permute-start.13) | collective-permute-done | bytes 262176 | tf_op jit(solution)/shard_map/ppermute | solution.py:31
  83.1 4.4 %collective-permute-start.16 = (bf16[512,512]{1,0:T(8,128)(2,1)S(1)}, bf16[512,512]{1,0:T(8,128)(2,1)S(1)}, u32[]{:S(2)}, u32[]{:S(2)}) collective-permute-start(bf16[512,512]{1,0:T(8,128)(2,1)S(1)} %pad_maximum_fusion.1.refs_8_), channel_id=1, source_target_pairs={{0,16},{1,17},{2,18},{3,19},{4,20},{5,21},{6,22},{7,23},{8,24},{9,... | collective-permute-start | bytes 1572872 | tf_op jit(solution)/shard_map/ppermute | solution.py:31
  87.6 4.0 %collective-permute-start.15 = (bf16[512,512]{1,0:T(8,128)(2,1)S(1)}, bf16[512,512]{1,0:T(8,128)(2,1)S(1)}, u32[]{:S(2)}, u32[]{:S(2)}) collective-permute-start(bf16[512,512]{1,0:T(8,128)(2,1)S(1)} %pad_maximum_fusion.1.refs_8_), channel_id=1, source_target_pairs={{0,240},{1,241},{2,242},{3,243},{4,244},{5,245},{6,246},{7,247},{8... | collective-permute-start | bytes 1572872 | tf_op jit(solution)/shard_map/ppermute | solution.py:31
  91.6 3.4 %collective-permute-start.8 = (bf16[1024,256]{1,0:T(8,128)(2,1)S(1)}, bf16[1024,256]{1,0:T(8,128)(2,1)S(1)}, u32[]{:S(2)}, u32[]{:S(2)}) collective-permute-start(bf16[1024,256]{1,0:T(8,128)(2,1)S(1)} %collective-permute-done.7.refs_6_), channel_id=1, source_target_pairs={{0,1},{1,0},{2,3},{3,2},{4,5},{5,4},{6,7},{7,6},{8,9},{9,8},{10,11... | collective-permute-start | bytes 1572872 | tf_op jit(solution)/shard_map/ppermute | solution.py:31
  95.0 1.9 %collective-permute-start.6 = (bf16[1024,256]{1,0:T(8,128)(2,1)S(1)}, bf16[1024,256]{1,0:T(8,128)(2,1)S(1)}, u32[]{:S(2)}, u32[]{:S(2)}) collective-permute-start(bf16[1024,256]{1,0:T(8,128)(2,1)S(1)} %collective-permute-done.5.refs_4_), channel_id=1, source_target_pairs={{0,1},{1,0},{2,3},{3,2},{4,5},{5,4},{6,7},{7,6},{8,9},{9,8},{10,11... | collective-permute-start | bytes 1572872 | tf_op jit(solution)/shard_map/ppermute | solution.py:31
  96.9 2.4 %collective-permute-start.4 = (bf16[1024,256]{1,0:T(8,128)(2,1)S(1)}, bf16[1024,256]{1,0:T(8,128)(2,1)S(1)}, u32[]{:S(2)}, u32[]{:S(2)}) collective-permute-start(bf16[1024,256]{1,0:T(8,128)(2,1)S(1)} %collective-permute-done.3.refs_2_), channel_id=1, source_target_pairs={{0,1},{1,0},{2,3},{3,2},{4,5},{5,4},{6,7},{7,6},{8,9},{9,8},{10,11... | collective-permute-start | bytes 1572872 | tf_op jit(solution)/shard_map/ppermute | solution.py:31
  102.2 2.1 %shard_map.46 = (bf16[512,512]{1,0:T(8,128)(2,1)S(1)}, bf16[2048,384]{1,0:T(8,128)(2,1)S(1)}, bf16[2048,128]{1,0:T(8,128)(2,1)S(1)}) custom-call(s32[2]{0:T(128)S(1)} %pad_add_fusion.pos, bf16[1024,256]{1,0:T(8,128)(2,1)S(1)} %pad_maximum_fusion.refs_0_, bf16[1024,256]{1,0:T(8,128)(2,1)S(1)} %collective-permute-done.2.refs_1_, ...), custom_call_target="tpu_custom_call" | custom-call | flops 805306368 | bytes 8388608 | tf_op jit(solution)/shard_map/pallas_call | solution.py:39
  104.3 2.8 %collective-permute-start.17 = (bf16[512,512]{1,0:T(8,128)(2,1)S(1)}, bf16[512,512]{1,0:T(8,128)(2,1)S(1)}, u32[]{:S(2)}, u32[]{:S(2)}) collective-permute-start(bf16[512,512]{1,0:T(8,128)(2,1)S(1)} %get-tuple-element.17), channel_id=1, source_target_pairs={{0,256},{1,257},{2,258},{3,259},{4,260},{5,261},{6,262},{7,263},{8... | collective-permute-start | bytes 1572872 | tf_op jit(solution)/shard_map/ppermute | solution.py:31
  107.1 1.9 %shard_map.47 = (f32[512,384]{1,0:T(8,128)S(1)}, f32[512,128]{1,0:T(8,128)S(1)}) custom-call(s32[2]{0:T(128)S(1)} %pad_add_fusion.pos, bf16[1024,256]{1,0:T(8,128)(2,1)S(1)} %pad_maximum_fusion.refs_0_, bf16[1024,256]{1,0:T(8,128)(2,1)S(1)} %collective-permute-done.2.refs_1_, bf16[1024,256]{1,0:T(8,128)(2,1)S(1)} %collective-permute-done.3.refs_2_, ...), custom_call_target="tpu_custom_call" | custom-call | flops 805306368 | bytes 8388608 | tf_op jit(solution)/shard_map/pallas_call | solution.py:39
  109.0 10.6 %collective-permute-done.17.refs_2_ = bf16[512,512]{1,0:T(8,128)(2,1)S(1)} collective-permute-done((bf16[512,512]{1,0:T(8,128)(2,1)S(1)}, bf16[512,512]{1,0:T(8,128)(2,1)S(1)}, u32[]{:S(2)}, u32[]{:S(2)}) %collective-permute-start.17) | collective-permute-done | bytes 524320 | tf_op jit(solution)/shard_map/ppermute | solution.py:31
  121.4 3.1 %collective-permute-start.23 = (bf16[2048,128]{1,0:T(8,128)(2,1)S(1)}, bf16[2048,128]{1,0:T(8,128)(2,1)S(1)}, u32[]{:S(2)}, u32[]{:S(2)}) collective-permute-start(bf16[2048,128]{1,0:T(8,128)(2,1)S(1)} %get-tuple-element.22.refs_4_), channel_id=1, source_target_pairs={{0,256},{1,257},{2,258},{3,259},{4,260},{5,261},{6,262},{7,263},{8... | collective-permute-start | bytes 1572872 | tf_op jit(solution)/shard_map/ppermute | solution.py:31
  126.8 5.8 %collective-permute-start.19 = (bf16[512,128]{1,0:T(8,128)(2,1)S(1)}, bf16[512,128]{1,0:T(8,128)(2,1)S(1)}, u32[]{:S(2)}, u32[]{:S(2)}) collective-permute-start(bf16[512,128]{1,0:T(8,128)(2,1)S(1)} %shard_map.50), channel_id=1, source_target_pairs={{0,8},{1,9},{2,10},{3,11},{4,12},{5,13},{6,14},{7,15},{8,0},{9,1},... | collective-permute-start | bytes 393224 | tf_op jit(solution)/shard_map/ppermute | solution.py:31
  132.5 15.9 %collective-permute-done.19 = bf16[512,128]{1,0:T(8,128)(2,1)S(1)} collective-permute-done((bf16[512,128]{1,0:T(8,128)(2,1)S(1)}, bf16[512,128]{1,0:T(8,128)(2,1)S(1)}, u32[]{:S(2)}, u32[]{:S(2)}) %collective-permute-start.19) | collective-permute-done | bytes 131104 | tf_op jit(solution)/shard_map/ppermute | solution.py:31
  148.5 4.2 %collective-permute-start.22 = (bf16[512,256]{1,0:T(8,128)(2,1)S(1)}, bf16[512,256]{1,0:T(8,128)(2,1)S(1)}, u32[]{:S(2)}, u32[]{:S(2)}) collective-permute-start(bf16[512,256]{1,0:T(8,128)(2,1)S(1)} %pad_maximum_fusion.5.refs_0_), channel_id=1, source_target_pairs={{0,2},{1,3},{2,4},{3,5},{4,6},{5,7},{6,0},{7,1},{8,10},{9,11},{10,... | collective-permute-start | bytes 786440 | tf_op jit(solution)/shard_map/ppermute | solution.py:31
  152.8 3.1 %collective-permute-start.21 = (bf16[512,256]{1,0:T(8,128)(2,1)S(1)}, bf16[512,256]{1,0:T(8,128)(2,1)S(1)}, u32[]{:S(2)}, u32[]{:S(2)}) collective-permute-start(bf16[512,256]{1,0:T(8,128)(2,1)S(1)} %pad_maximum_fusion.5.refs_0_), channel_id=1, source_target_pairs={{0,4},{1,5},{2,6},{3,7},{4,0},{5,1},{6,2},{7,3},{8,12},{9,13},{10,... | collective-permute-start | bytes 786440 | tf_op jit(solution)/shard_map/ppermute | solution.py:31
  155.8 2.6 %collective-permute-start.20 = (bf16[512,256]{1,0:T(8,128)(2,1)S(1)}, bf16[512,256]{1,0:T(8,128)(2,1)S(1)}, u32[]{:S(2)}, u32[]{:S(2)}) collective-permute-start(bf16[512,256]{1,0:T(8,128)(2,1)S(1)} %pad_maximum_fusion.5.refs_0_), channel_id=1, source_target_pairs={{0,6},{1,7},{2,0},{3,1},{4,2},{5,3},{6,4},{7,5},{8,14},{9,15},{10,... | collective-permute-start | bytes 786440 | tf_op jit(solution)/shard_map/ppermute | solution.py:31
  158.4 4.9 %collective-permute-done.21.refs_2_ = bf16[512,256]{1,0:T(8,128)(2,1)S(1)} collective-permute-done((bf16[512,256]{1,0:T(8,128)(2,1)S(1)}, bf16[512,256]{1,0:T(8,128)(2,1)S(1)}, u32[]{:S(2)}, u32[]{:S(2)}) %collective-permute-start.21) | collective-permute-done | bytes 262176 | tf_op jit(solution)/shard_map/ppermute | solution.py:31
  163.3 6.7 %collective-permute-done.20.refs_1_ = bf16[512,256]{1,0:T(8,128)(2,1)S(1)} collective-permute-done((bf16[512,256]{1,0:T(8,128)(2,1)S(1)}, bf16[512,256]{1,0:T(8,128)(2,1)S(1)}, u32[]{:S(2)}, u32[]{:S(2)}) %collective-permute-start.20) | collective-permute-done | bytes 262176 | tf_op jit(solution)/shard_map/ppermute | solution.py:31
  171.0 2.4 %collective-permute-start.24 = (bf16[512,256]{1,0:T(8,128)(2,1)S(1)}, bf16[512,256]{1,0:T(8,128)(2,1)S(1)}, u32[]{:S(2)}, u32[]{:S(2)}) collective-permute-start(bf16[512,256]{1,0:T(8,128)(2,1)S(1)} %shard_map.52), channel_id=1, source_target_pairs={{0,1},{1,0},{2,3},{3,2},{4,5},{5,4},{6,7},{7,6},{8,9},{9,8},{10,11... | collective-permute-start | bytes 786440 | tf_op jit(solution)/shard_map/ppermute | solution.py:31
  (39 shorter events, 13.4 us)
Async XLA Ops:
  0.0 49.8 %copy-start = (bf16[512,256]{1,0:T(8,128)(2,1)S(1)}, bf16[512,256]{1,0:T(8,128)(2,1)}, u32[]{:S(2)}) copy-start(bf16[512,256]{1,0:T(8,128)(2,1)} %refs_6_.1) | copy-start | bytes 786436
  0.0 13.1 %collective-permute-start.9 = (bf16[128,128]{1,0:T(8,128)(2,1)}, bf16[128,128]{1,0:T(8,128)(2,1)S(1)}, u32[]{:S(2)}, u32[]{:S(2)}) collective-permute-start(bf16[128,128]{1,0:T(8,128)(2,1)} %bitcast.15), channel_id=1, source_target_pairs={{0,0},{1,1},{2,64},{3,65},{4,128},{5,129},{6,192},{7,193},{8,256},... | collective-permute-start | bytes 98312 | tf_op jit(solution)/shard_map/ppermute | solution.py:31
  13.1 21.9 %collective-permute-start.11 = (bf16[128,512]{1,0:T(8,128)(2,1)S(1)}, bf16[128,512]{1,0:T(8,128)(2,1)S(1)}, u32[]{:S(2)}, u32[]{:S(2)}) collective-permute-start(bf16[128,512]{1,0:T(8,128)(2,1)S(1)} %pad_maximum_fusion.6), channel_id=1, source_target_pairs={{0,192},{1,193},{2,194},{3,195},{4,196},{5,197},{6,198},{7,199},{8... | collective-permute-start | bytes 393224 | tf_op jit(solution)/shard_map/ppermute | solution.py:31
  28.0 10.0 %collective-permute-start.10 = (bf16[128,512]{1,0:T(8,128)(2,1)S(1)}, bf16[128,512]{1,0:T(8,128)(2,1)S(1)}, u32[]{:S(2)}, u32[]{:S(2)}) collective-permute-start(bf16[128,512]{1,0:T(8,128)(2,1)S(1)} %pad_maximum_fusion.6), channel_id=1, source_target_pairs={{0,64},{1,65},{2,66},{3,67},{4,68},{5,69},{6,70},{7,71},{8,72},{9,... | collective-permute-start | bytes 393224 | tf_op jit(solution)/shard_map/ppermute | solution.py:31
  29.9 19.9 %collective-permute-start = (bf16[512,256]{1,0:T(8,128)(2,1)}, bf16[512,256]{1,0:T(8,128)(2,1)S(1)}, u32[]{:S(2)}, u32[]{:S(2)}) collective-permute-start(bf16[512,256]{1,0:T(8,128)(2,1)} %refs_6_.1), channel_id=1, source_target_pairs={{0,8},{1,9},{2,10},{3,11},{4,12},{5,13},{6,14},{7,15},{8,264},{9,2... | collective-permute-start | bytes 786440 | tf_op jit(solution)/shard_map/ppermute | solution.py:31
  32.8 17.0 %collective-permute-start.1 = (bf16[512,256]{1,0:T(8,128)(2,1)}, bf16[512,256]{1,0:T(8,128)(2,1)S(1)}, u32[]{:S(2)}, u32[]{:S(2)}) collective-permute-start(bf16[512,256]{1,0:T(8,128)(2,1)} %refs_6_.1), channel_id=1, source_target_pairs={{8,256},{9,257},{10,258},{11,259},{12,260},{13,261},{14,262},{15,2... | collective-permute-start | bytes 786440 | tf_op jit(solution)/shard_map/ppermute | solution.py:31
  38.0 22.8 %collective-permute-start.12 = (bf16[128,512]{1,0:T(8,128)(2,1)S(1)}, bf16[128,512]{1,0:T(8,128)(2,1)S(1)}, u32[]{:S(2)}, u32[]{:S(2)}) collective-permute-start(bf16[128,512]{1,0:T(8,128)(2,1)S(1)} %broadcast_select_fusion.2), channel_id=1, source_target_pairs={{0,192},{1,65},{2,194},{3,67},{4,196},{5,69},{6,198},{7,71},{8,200... | collective-permute-start | bytes 393224 | tf_op jit(solution)/shard_map/ppermute | solution.py:31
  40.6 28.2 %collective-permute-start.14 = (bf16[256,512]{1,0:T(8,128)(2,1)S(1)}, bf16[256,512]{1,0:T(8,128)(2,1)S(1)}, u32[]{:S(2)}, u32[]{:S(2)}) collective-permute-start(bf16[256,512]{1,0:T(8,128)(2,1)S(1)} %get-tuple-element.25), channel_id=1, source_target_pairs={{0,32},{1,33},{2,34},{3,35},{4,36},{5,37},{6,38},{7,39},{8,40},{9,... | collective-permute-start | bytes 786440 | tf_op jit(solution)/shard_map/ppermute | solution.py:31
  49.9 37.6 %collective-permute-start.7 = (bf16[1024,256]{1,0:T(8,128)(2,1)S(1)}, bf16[1024,256]{1,0:T(8,128)(2,1)S(1)}, u32[]{:S(2)}, u32[]{:S(2)}) collective-permute-start(bf16[1024,256]{1,0:T(8,128)(2,1)S(1)} %pad_maximum_fusion.refs_0_), channel_id=1, source_target_pairs={{0,2},{1,3},{2,4},{3,5},{4,6},{5,7},{6,0},{7,1},{8,10},{9,11},{10,... | collective-permute-start | bytes 1572872 | tf_op jit(solution)/shard_map/ppermute | solution.py:31
  51.9 39.7 %collective-permute-start.5 = (bf16[1024,256]{1,0:T(8,128)(2,1)S(1)}, bf16[1024,256]{1,0:T(8,128)(2,1)S(1)}, u32[]{:S(2)}, u32[]{:S(2)}) collective-permute-start(bf16[1024,256]{1,0:T(8,128)(2,1)S(1)} %pad_maximum_fusion.refs_0_), channel_id=1, source_target_pairs={{0,4},{1,5},{2,6},{3,7},{4,0},{5,1},{6,2},{7,3},{8,12},{9,13},{10,... | collective-permute-start | bytes 1572872 | tf_op jit(solution)/shard_map/ppermute | solution.py:31
  56.8 38.2 %collective-permute-start.3 = (bf16[1024,256]{1,0:T(8,128)(2,1)S(1)}, bf16[1024,256]{1,0:T(8,128)(2,1)S(1)}, u32[]{:S(2)}, u32[]{:S(2)}) collective-permute-start(bf16[1024,256]{1,0:T(8,128)(2,1)S(1)} %pad_maximum_fusion.refs_0_), channel_id=1, source_target_pairs={{0,6},{1,7},{2,0},{3,1},{4,2},{5,3},{6,4},{7,5},{8,14},{9,15},{10,... | collective-permute-start | bytes 1572872 | tf_op jit(solution)/shard_map/ppermute | solution.py:31
  60.8 36.2 %collective-permute-start.2 = (bf16[1024,256]{1,0:T(8,128)(2,1)S(1)}, bf16[1024,256]{1,0:T(8,128)(2,1)S(1)}, u32[]{:S(2)}, u32[]{:S(2)}) collective-permute-start(bf16[1024,256]{1,0:T(8,128)(2,1)S(1)} %pad_maximum_fusion.refs_0_), channel_id=1, source_target_pairs={{0,1},{1,0},{2,3},{3,2},{4,5},{5,4},{6,7},{7,6},{8,9},{9,8},{10,11... | collective-permute-start | bytes 1572872 | tf_op jit(solution)/shard_map/ppermute | solution.py:31
  68.8 14.3 %collective-permute-start.13 = (bf16[256,512]{1,0:T(8,128)(2,1)S(1)}, bf16[256,512]{1,0:T(8,128)(2,1)S(1)}, u32[]{:S(2)}, u32[]{:S(2)}) collective-permute-start(bf16[256,512]{1,0:T(8,128)(2,1)S(1)} %get-tuple-element.26), channel_id=1, source_target_pairs={{0,224},{1,225},{2,226},{3,227},{4,228},{5,229},{6,230},{7,231},{8... | collective-permute-start | bytes 786440 | tf_op jit(solution)/shard_map/ppermute | solution.py:31
  83.1 17.6 %collective-permute-start.16 = (bf16[512,512]{1,0:T(8,128)(2,1)S(1)}, bf16[512,512]{1,0:T(8,128)(2,1)S(1)}, u32[]{:S(2)}, u32[]{:S(2)}) collective-permute-start(bf16[512,512]{1,0:T(8,128)(2,1)S(1)} %pad_maximum_fusion.1.refs_8_), channel_id=1, source_target_pairs={{0,16},{1,17},{2,18},{3,19},{4,20},{5,21},{6,22},{7,23},{8,24},{9,... | collective-permute-start | bytes 1572872 | tf_op jit(solution)/shard_map/ppermute | solution.py:31
  87.6 14.6 %collective-permute-start.15 = (bf16[512,512]{1,0:T(8,128)(2,1)S(1)}, bf16[512,512]{1,0:T(8,128)(2,1)S(1)}, u32[]{:S(2)}, u32[]{:S(2)}) collective-permute-start(bf16[512,512]{1,0:T(8,128)(2,1)S(1)} %pad_maximum_fusion.1.refs_8_), channel_id=1, source_target_pairs={{0,240},{1,241},{2,242},{3,243},{4,244},{5,245},{6,246},{7,247},{8... | collective-permute-start | bytes 1572872 | tf_op jit(solution)/shard_map/ppermute | solution.py:31
  91.6 10.6 %collective-permute-start.8 = (bf16[1024,256]{1,0:T(8,128)(2,1)S(1)}, bf16[1024,256]{1,0:T(8,128)(2,1)S(1)}, u32[]{:S(2)}, u32[]{:S(2)}) collective-permute-start(bf16[1024,256]{1,0:T(8,128)(2,1)S(1)} %collective-permute-done.7.refs_6_), channel_id=1, source_target_pairs={{0,1},{1,0},{2,3},{3,2},{4,5},{5,4},{6,7},{7,6},{8,9},{9,8},{10,11... | collective-permute-start | bytes 1572872 | tf_op jit(solution)/shard_map/ppermute | solution.py:31
  95.0 7.2 %collective-permute-start.6 = (bf16[1024,256]{1,0:T(8,128)(2,1)S(1)}, bf16[1024,256]{1,0:T(8,128)(2,1)S(1)}, u32[]{:S(2)}, u32[]{:S(2)}) collective-permute-start(bf16[1024,256]{1,0:T(8,128)(2,1)S(1)} %collective-permute-done.5.refs_4_), channel_id=1, source_target_pairs={{0,1},{1,0},{2,3},{3,2},{4,5},{5,4},{6,7},{7,6},{8,9},{9,8},{10,11... | collective-permute-start | bytes 1572872 | tf_op jit(solution)/shard_map/ppermute | solution.py:31
  96.9 5.2 %collective-permute-start.4 = (bf16[1024,256]{1,0:T(8,128)(2,1)S(1)}, bf16[1024,256]{1,0:T(8,128)(2,1)S(1)}, u32[]{:S(2)}, u32[]{:S(2)}) collective-permute-start(bf16[1024,256]{1,0:T(8,128)(2,1)S(1)} %collective-permute-done.3.refs_2_), channel_id=1, source_target_pairs={{0,1},{1,0},{2,3},{3,2},{4,5},{5,4},{6,7},{7,6},{8,9},{9,8},{10,11... | collective-permute-start | bytes 1572872 | tf_op jit(solution)/shard_map/ppermute | solution.py:31
  104.3 15.3 %collective-permute-start.17 = (bf16[512,512]{1,0:T(8,128)(2,1)S(1)}, bf16[512,512]{1,0:T(8,128)(2,1)S(1)}, u32[]{:S(2)}, u32[]{:S(2)}) collective-permute-start(bf16[512,512]{1,0:T(8,128)(2,1)S(1)} %get-tuple-element.17), channel_id=1, source_target_pairs={{0,256},{1,257},{2,258},{3,259},{4,260},{5,261},{6,262},{7,263},{8... | collective-permute-start | bytes 1572872 | tf_op jit(solution)/shard_map/ppermute | solution.py:31
  119.8 5.1 %collective-permute-start.18 = (bf16[512,256]{1,0:T(8,128)(2,1)S(1)}, bf16[512,256]{1,0:T(8,128)(2,1)S(1)}, u32[]{:S(2)}, u32[]{:S(2)}) collective-permute-start(bf16[512,256]{1,0:T(8,128)(2,1)S(1)} %get-tuple-element.19.kv_ref), channel_id=1, source_target_pairs={{0,16},{16,32},{32,48},{48,64},{64,80},{80,96},{96,112},{112,128},... | collective-permute-start | bytes 786440 | tf_op jit(solution)/shard_map/ppermute | solution.py:257
  121.4 37.0 %collective-permute-start.23 = (bf16[2048,128]{1,0:T(8,128)(2,1)S(1)}, bf16[2048,128]{1,0:T(8,128)(2,1)S(1)}, u32[]{:S(2)}, u32[]{:S(2)}) collective-permute-start(bf16[2048,128]{1,0:T(8,128)(2,1)S(1)} %get-tuple-element.22.refs_4_), channel_id=1, source_target_pairs={{0,256},{1,257},{2,258},{3,259},{4,260},{5,261},{6,262},{7,263},{8... | collective-permute-start | bytes 1572872 | tf_op jit(solution)/shard_map/ppermute | solution.py:31
  126.8 21.7 %collective-permute-start.19 = (bf16[512,128]{1,0:T(8,128)(2,1)S(1)}, bf16[512,128]{1,0:T(8,128)(2,1)S(1)}, u32[]{:S(2)}, u32[]{:S(2)}) collective-permute-start(bf16[512,128]{1,0:T(8,128)(2,1)S(1)} %shard_map.50), channel_id=1, source_target_pairs={{0,8},{1,9},{2,10},{3,11},{4,12},{5,13},{6,14},{7,15},{8,0},{9,1},... | collective-permute-start | bytes 393224 | tf_op jit(solution)/shard_map/ppermute | solution.py:31
  148.5 9.9 %collective-permute-start.22 = (bf16[512,256]{1,0:T(8,128)(2,1)S(1)}, bf16[512,256]{1,0:T(8,128)(2,1)S(1)}, u32[]{:S(2)}, u32[]{:S(2)}) collective-permute-start(bf16[512,256]{1,0:T(8,128)(2,1)S(1)} %pad_maximum_fusion.5.refs_0_), channel_id=1, source_target_pairs={{0,2},{1,3},{2,4},{3,5},{4,6},{5,7},{6,0},{7,1},{8,10},{9,11},{10,... | collective-permute-start | bytes 786440 | tf_op jit(solution)/shard_map/ppermute | solution.py:31
  152.8 10.5 %collective-permute-start.21 = (bf16[512,256]{1,0:T(8,128)(2,1)S(1)}, bf16[512,256]{1,0:T(8,128)(2,1)S(1)}, u32[]{:S(2)}, u32[]{:S(2)}) collective-permute-start(bf16[512,256]{1,0:T(8,128)(2,1)S(1)} %pad_maximum_fusion.5.refs_0_), channel_id=1, source_target_pairs={{0,4},{1,5},{2,6},{3,7},{4,0},{5,1},{6,2},{7,3},{8,12},{9,13},{10,... | collective-permute-start | bytes 786440 | tf_op jit(solution)/shard_map/ppermute | solution.py:31
  155.8 14.2 %collective-permute-start.20 = (bf16[512,256]{1,0:T(8,128)(2,1)S(1)}, bf16[512,256]{1,0:T(8,128)(2,1)S(1)}, u32[]{:S(2)}, u32[]{:S(2)}) collective-permute-start(bf16[512,256]{1,0:T(8,128)(2,1)S(1)} %pad_maximum_fusion.5.refs_0_), channel_id=1, source_target_pairs={{0,6},{1,7},{2,0},{3,1},{4,2},{5,3},{6,4},{7,5},{8,14},{9,15},{10,... | collective-permute-start | bytes 786440 | tf_op jit(solution)/shard_map/ppermute | solution.py:31
  171.0 3.6 %collective-permute-start.24 = (bf16[512,256]{1,0:T(8,128)(2,1)S(1)}, bf16[512,256]{1,0:T(8,128)(2,1)S(1)}, u32[]{:S(2)}, u32[]{:S(2)}) collective-permute-start(bf16[512,256]{1,0:T(8,128)(2,1)S(1)} %shard_map.52), channel_id=1, source_target_pairs={{0,1},{1,0},{2,3},{3,2},{4,5},{5,4},{6,7},{7,6},{8,9},{9,8},{10,11... | collective-permute-start | bytes 786440 | tf_op jit(solution)/shard_map/ppermute | solution.py:31

commit v2 on v1

--- a/solution.py
+++ b/solution.py
@@ -76,58 +76,69 @@
     return held, down2, up2, down1, up1
 
 
+def squares_body(*refs):
+    blocks, (own_ref, other_ref) = refs[:8], refs[8:]
+    seg = own_ref.shape[1]
+    ones = jnp.ones((own_ref.shape[0], blocks[0].shape[1]), BF)
+    for first, ref in ((0, own_ref), (seg, other_ref)):
+        total = jnp.zeros(ref.shape, F32)
+        for block in blocks:
+            wider = block[first : first + seg, :].astype(F32)
+            total += lax.dot_general(
+                ones,
+                (wider * wider).astype(BF),
+                (((1,), (1,)), ((), ())),
+                preferred_element_type=F32,
+            )
+        ref[...] = total
+
+
 def project_rows(pos, blocks, weights, first, seg):
     _, _, _, y, k = place(pos)
     rows = weights.shape[0] // 16
     tile = min(seg, 256)
     for r in range(0, seg, tile):
         acc = jnp.zeros((tile, weights.shape[1]), F32)
-        ssq = jnp.zeros((tile, 1), F32)
         for i in range(8):
             yy = (y + i // 2) & 3
             kk = k if i % 2 == 0 else 1 - k
             at = pl.multiple_of((yy * 2 + kk) * 2 * rows, 2 * rows)
             block = blocks[i][first + r : first + r + tile, :]
             acc += jnp.dot(block, weights[pl.ds(at, 2 * rows), :], preferred_element_type=F32)
-            wider = block.astype(F32)
-            ssq += jnp.sum(wider * wider, axis=1, keepdims=True)
-        yield slice(r, r + tile), acc, ssq
+        yield slice(r, r + tile), acc
 
 
 def project_other_body(pos, *refs):
     blocks, parts, (send_ref, w_ref, out_w_ref) = refs[:8], refs[8:13], refs[13:]
     _, z, _, _, _ = place(pos)
     rows = w_ref.shape[0] // 16
-    seg = send_ref.shape[0]
-    wide = w_ref.shape[1]
+    seg, wide = send_ref.shape
     for part, steps in zip(parts, STEPS):
         for i, step in enumerate(steps):
             at = pl.multiple_of(((z + step + 16) & 15) * rows, rows)
             w_ref[pl.ds(at, rows), :] = part[i * rows : (i + 1) * rows, :wide]
             out_w_ref[pl.ds(at, rows), :] = part[i * rows : (i + 1) * rows, wide:]
-    lanes = send_ref.shape[1] - wide
-    for at, acc, ssq in project_rows(pos, blocks, w_ref, seg, seg):
-        send_ref[at, :wide] = acc.astype(BF)
-        high = ssq.astype(BF).astype(F32)
-        lane = lax.broadcasted_iota(jnp.int32, (ssq.shape[0], lanes), 1)
-        send_ref[at, wide:] = jnp.where(lane < lanes // 2, high, ssq - high).astype(BF)
+    for at, acc in project_rows(pos, blocks, w_ref, seg, seg):
+        send_ref[at, :] = acc.astype(BF)
 
 
 def project_own_body(pos, *refs):
-    blocks, (w_ref, own_ref, ssq_ref) = refs[:8], refs[8:]
-    for at, acc, ssq in project_rows(pos, blocks, w_ref, 0, own_ref.shape[0]):
+    blocks, (w_ref, own_ref) = refs[:8], refs[8:]
+    for at, acc in project_rows(pos, blocks, w_ref, 0, own_ref.shape[0]):
         own_ref[at, :] = acc
-        ssq_ref[at, :] = jnp.broadcast_to(ssq, (ssq.shape[0], ssq_ref.shape[1]))
-
-
-def combine_body(own_ref, ssq_ref, got_ref, q_ref, kv_ref, *, features):
+
+
+def combine_body(own_ref, got_ref, ssq_ref, ssq_got_ref, q_ref, kv_ref, *, features):
     hd = q_ref.shape[1]
-    wide = 3 * hd
-    lanes = got_ref.shape[1] - wide
-    half = got_ref[:, wide:].astype(F32)
-    ssq = ssq_ref[:, :1] + half[:, :1] + half[:, lanes // 2 : lanes // 2 + 1]
-    scale = lax.rsqrt(ssq * (1.0 / features) + 1e-06)
-    total = (own_ref[...] + got_ref[:, :wide].astype(F32)) * scale
+    scale = lax.rsqrt((ssq_ref[...] + ssq_got_ref[...]) * (1.0 / features) + 1e-06)
+    column = lax.dot_general(
+        scale,
+        jnp.full((scale.shape[0], 3 * hd), 1.0 / scale.shape[0], F32),
+        (((0,), (0,)), ((), ())),
+        precision=lax.Precision.HIGHEST,
+        preferred_element_type=F32,
+    )
+    total = (own_ref[...] + got_ref[...].astype(F32)) * column
     q_ref[...] = total[:, :hd].astype(BF)
     kv_ref[...] = total[:, hd:].astype(BF)
 
@@ -231,10 +242,18 @@
     for block in around(jnp.concatenate([own, other], axis=0)):
         blocks += [block, permute(block, swap_core)]
 
+    ssq, ssq_send = call(
+        squares_body,
+        (shape((8, seg), F32), shape((8, seg), F32)),
+        flops=4 * seg * 8 * feats * 8,
+        nbytes=4 << 20,
+        scalars=False,
+    )(*blocks)
+    ssq_got = permute(ssq_send, swap_hi)
     send, weights, out_w = call(
         project_other_body,
         (
-            shape((seg, 4 * hd), BF),
+            shape((seg, 3 * hd), BF),
             shape((16 * hd, 3 * hd), BF),
             shape((16 * hd, hd), BF),
         ),
@@ -242,9 +261,9 @@
         nbytes=8 << 20,
     )(pos, *blocks, *parts)
     got = permute(send, swap_hi)
-    own_part, own_ssq = call(
+    own_part = call(
         project_own_body,
-        (shape((seg, 3 * hd), F32), shape((seg, hd), F32)),
+        shape((seg, 3 * hd), F32),
         flops=2 * seg * 8 * feats * 3 * hd,
         nbytes=8 << 20,
     )(pos, *blocks, weights)
@@ -253,7 +272,7 @@
         (shape((seg, hd), BF), shape((seg, 2 * hd), BF)),
         nbytes=2 << 20,
         scalars=False,
-    )(own_part, own_ssq, got)
+    )(own_part, got, ssq, ssq_got)
     prev = lax.ppermute(kv, "ctx", [(i, i + 1) for i in range(31)])
     e_own, sum_own = call(
         own_body,

time: 176 us -> 170 us (0.966)
  the two profiles are of different devices: /device:TPU:11 before, /device:TPU:3 now
where the time goes in v2:
time: 170 us; the launch traced here: 169 us
  starting transfers between devices  113 us (66%)
  waiting for transfers between devices  42.7 us (25%)
  Pallas kernels  10.8 us (6%)
  other arithmetic  1.94 us (1%)
    ppermute x25, starting transfers between devices, permute(): return lax.ppermute(value, AXES, pairs_of(target))  112 us
    ppermute x25, waiting for transfers between devices, permute(): return lax.ppermute(value, AXES, pairs_of(target))  42.7 us
    pallas_call x9, Pallas kernels, run(): pl.pallas_call(body, out_shape=outs, in_specs=specs, out_specs=jax.tree.m...  10.8 us
  transfers between devices with their start and end apart: 26, of which 11 were waited for; matrix products, arithmetic and copies ran while one was open for 1% of the time, Pallas kernels for 4%

profile of v2, /device:TPU:3, one launch (start us, length us, event | category | flops | bytes accessed | tf_op | source)
XLA Modules:
  0.0 169.2 jit_solution(7006453664740911465)
XLA Ops:
  0.0 3.2 %collective-permute-start.9 = (bf16[128,128]{1,0:T(8,128)(2,1)}, bf16[128,128]{1,0:T(8,128)(2,1)S(1)}, u32[]{:S(2)}, u32[]{:S(2)}) collective-permute-start(bf16[128,128]{1,0:T(8,128)(2,1)} %bitcast.15), channel_id=1, source_target_pairs={{0,0},{1,1},{2,64},{3,65},{4,128},{5,129},{6,192},{7,193},{8,256},... | collective-permute-start | bytes 98312 | tf_op jit(solution)/shard_map/ppermute | solution.py:31
  5.0 19.5 %collective-permute-start.11 = (bf16[128,512]{1,0:T(8,128)(2,1)S(1)}, bf16[128,512]{1,0:T(8,128)(2,1)S(1)}, u32[]{:S(2)}, u32[]{:S(2)}) collective-permute-start(bf16[128,512]{1,0:T(8,128)(2,1)S(1)} %pad_maximum_fusion.6), channel_id=1, source_target_pairs={{0,192},{1,193},{2,194},{3,195},{4,196},{5,197},{6,198},{7,199},{8... | collective-permute-start | bytes 393224 | tf_op jit(solution)/shard_map/ppermute | solution.py:31
  24.5 1.9 %collective-permute-start.10 = (bf16[128,512]{1,0:T(8,128)(2,1)S(1)}, bf16[128,512]{1,0:T(8,128)(2,1)S(1)}, u32[]{:S(2)}, u32[]{:S(2)}) collective-permute-start(bf16[128,512]{1,0:T(8,128)(2,1)S(1)} %pad_maximum_fusion.6), channel_id=1, source_target_pairs={{0,64},{1,65},{2,66},{3,67},{4,68},{5,69},{6,70},{7,71},{8,72},{9,... | collective-permute-start | bytes 393224 | tf_op jit(solution)/shard_map/ppermute | solution.py:31
  26.5 2.9 %collective-permute-start = (bf16[512,256]{1,0:T(8,128)(2,1)}, bf16[512,256]{1,0:T(8,128)(2,1)S(1)}, u32[]{:S(2)}, u32[]{:S(2)}) collective-permute-start(bf16[512,256]{1,0:T(8,128)(2,1)} %refs_6_.1), channel_id=1, source_target_pairs={{0,8},{1,9},{2,10},{3,11},{4,12},{5,13},{6,14},{7,15},{8,264},{9,2... | collective-permute-start | bytes 786440 | tf_op jit(solution)/shard_map/ppermute | solution.py:31
  29.3 2.2 %collective-permute-start.1 = (bf16[512,256]{1,0:T(8,128)(2,1)}, bf16[512,256]{1,0:T(8,128)(2,1)S(1)}, u32[]{:S(2)}, u32[]{:S(2)}) collective-permute-start(bf16[512,256]{1,0:T(8,128)(2,1)} %refs_6_.1), channel_id=1, source_target_pairs={{8,256},{9,257},{10,258},{11,259},{12,260},{13,261},{14,262},{15,2... | collective-permute-start | bytes 786440 | tf_op jit(solution)/shard_map/ppermute | solution.py:31
  31.5 4.2 %collective-permute-done.11 = bf16[128,512]{1,0:T(8,128)(2,1)S(1)} collective-permute-done((bf16[128,512]{1,0:T(8,128)(2,1)S(1)}, bf16[128,512]{1,0:T(8,128)(2,1)S(1)}, u32[]{:S(2)}, u32[]{:S(2)}) %collective-permute-start.11) | collective-permute-done | bytes 131104 | tf_op jit(solution)/shard_map/ppermute | solution.py:31
  35.7 2.2 %collective-permute-done.10 = bf16[128,512]{1,0:T(8,128)(2,1)S(1)} collective-permute-done((bf16[128,512]{1,0:T(8,128)(2,1)S(1)}, bf16[128,512]{1,0:T(8,128)(2,1)S(1)}, u32[]{:S(2)}, u32[]{:S(2)}) %collective-permute-start.10) | collective-permute-done | bytes 131104 | tf_op jit(solution)/shard_map/ppermute | solution.py:31
  37.9 9.6 %collective-permute-start.12 = (bf16[128,512]{1,0:T(8,128)(2,1)S(1)}, bf16[128,512]{1,0:T(8,128)(2,1)S(1)}, u32[]{:S(2)}, u32[]{:S(2)}) collective-permute-start(bf16[128,512]{1,0:T(8,128)(2,1)S(1)} %broadcast_select_fusion.2), channel_id=1, source_target_pairs={{0,192},{1,65},{2,194},{3,67},{4,196},{5,69},{6,198},{7,71},{8,200... | collective-permute-start | bytes 393224 | tf_op jit(solution)/shard_map/ppermute | solution.py:31
  47.6 5.0 %collective-permute-start.13 = (bf16[256,512]{1,0:T(8,128)(2,1)S(1)}, bf16[256,512]{1,0:T(8,128)(2,1)S(1)}, u32[]{:S(2)}, u32[]{:S(2)}) collective-permute-start(bf16[256,512]{1,0:T(8,128)(2,1)S(1)} %get-tuple-element.26), channel_id=1, source_target_pairs={{0,224},{1,225},{2,226},{3,227},{4,228},{5,229},{6,230},{7,231},{8... | collective-permute-start | bytes 786440 | tf_op jit(solution)/shard_map/ppermute | solution.py:31
  52.7 5.5 %collective-permute-start.2 = (bf16[1024,256]{1,0:T(8,128)(2,1)S(1)}, bf16[1024,256]{1,0:T(8,128)(2,1)S(1)}, u32[]{:S(2)}, u32[]{:S(2)}) collective-permute-start(bf16[1024,256]{1,0:T(8,128)(2,1)S(1)} %pad_maximum_fusion.refs_0_), channel_id=1, source_target_pairs={{0,1},{1,0},{2,3},{3,2},{4,5},{5,4},{6,7},{7,6},{8,9},{9,8},{10,11... | collective-permute-start | bytes 1572872 | tf_op jit(solution)/shard_map/ppermute | solution.py:31
  58.3 3.4 %collective-permute-start.3 = (bf16[1024,256]{1,0:T(8,128)(2,1)S(1)}, bf16[1024,256]{1,0:T(8,128)(2,1)S(1)}, u32[]{:S(2)}, u32[]{:S(2)}) collective-permute-start(bf16[1024,256]{1,0:T(8,128)(2,1)S(1)} %pad_maximum_fusion.refs_0_), channel_id=1, source_target_pairs={{0,6},{1,7},{2,0},{3,1},{4,2},{5,3},{6,4},{7,5},{8,14},{9,15},{10,... | collective-permute-start | bytes 1572872 | tf_op jit(solution)/shard_map/ppermute | solution.py:31
  61.7 1.9 %collective-permute-start.5 = (bf16[1024,256]{1,0:T(8,128)(2,1)S(1)}, bf16[1024,256]{1,0:T(8,128)(2,1)S(1)}, u32[]{:S(2)}, u32[]{:S(2)}) collective-permute-start(bf16[1024,256]{1,0:T(8,128)(2,1)S(1)} %pad_maximum_fusion.refs_0_), channel_id=1, source_target_pairs={{0,4},{1,5},{2,6},{3,7},{4,0},{5,1},{6,2},{7,3},{8,12},{9,13},{10,... | collective-permute-start | bytes 1572872 | tf_op jit(solution)/shard_map/ppermute | solution.py:31
  63.6 2.5 %collective-permute-start.7 = (bf16[1024,256]{1,0:T(8,128)(2,1)S(1)}, bf16[1024,256]{1,0:T(8,128)(2,1)S(1)}, u32[]{:S(2)}, u32[]{:S(2)}) collective-permute-start(bf16[1024,256]{1,0:T(8,128)(2,1)S(1)} %pad_maximum_fusion.refs_0_), channel_id=1, source_target_pairs={{0,2},{1,3},{2,4},{3,5},{4,6},{5,7},{6,0},{7,1},{8,10},{9,11},{10,... | collective-permute-start | bytes 1572872 | tf_op jit(solution)/shard_map/ppermute | solution.py:31
  66.2 3.3 %collective-permute-start.14 = (bf16[256,512]{1,0:T(8,128)(2,1)S(1)}, bf16[256,512]{1,0:T(8,128)(2,1)S(1)}, u32[]{:S(2)}, u32[]{:S(2)}) collective-permute-start(bf16[256,512]{1,0:T(8,128)(2,1)S(1)} %get-tuple-element.25), channel_id=1, source_target_pairs={{0,32},{1,33},{2,34},{3,35},{4,36},{5,37},{6,38},{7,39},{8,40},{9,... | collective-permute-start | bytes 786440 | tf_op jit(solution)/shard_map/ppermute | solution.py:31
  69.5 6.2 %collective-permute-done.14.refs_10_ = bf16[256,512]{1,0:T(8,128)(2,1)S(1)} collective-permute-done((bf16[256,512]{1,0:T(8,128)(2,1)S(1)}, bf16[256,512]{1,0:T(8,128)(2,1)S(1)}, u32[]{:S(2)}, u32[]{:S(2)}) %collective-permute-start.14) | collective-permute-done | bytes 262176 | tf_op jit(solution)/shard_map/ppermute | solution.py:31
  75.7 6.3 %collective-permute-start.15 = (bf16[512,512]{1,0:T(8,128)(2,1)S(1)}, bf16[512,512]{1,0:T(8,128)(2,1)S(1)}, u32[]{:S(2)}, u32[]{:S(2)}) collective-permute-start(bf16[512,512]{1,0:T(8,128)(2,1)S(1)} %pad_maximum_fusion.1.refs_8_), channel_id=1, source_target_pairs={{0,240},{1,241},{2,242},{3,243},{4,244},{5,245},{6,246},{7,247},{8... | collective-permute-start | bytes 1572872 | tf_op jit(solution)/shard_map/ppermute | solution.py:31
  82.0 3.9 %collective-permute-start.16 = (bf16[512,512]{1,0:T(8,128)(2,1)S(1)}, bf16[512,512]{1,0:T(8,128)(2,1)S(1)}, u32[]{:S(2)}, u32[]{:S(2)}) collective-permute-start(bf16[512,512]{1,0:T(8,128)(2,1)S(1)} %pad_maximum_fusion.1.refs_8_), channel_id=1, source_target_pairs={{0,16},{1,17},{2,18},{3,19},{4,20},{5,21},{6,22},{7,23},{8,24},{9,... | collective-permute-start | bytes 1572872 | tf_op jit(solution)/shard_map/ppermute | solution.py:31
  85.9 7.0 %collective-permute-start.4 = (bf16[1024,256]{1,0:T(8,128)(2,1)S(1)}, bf16[1024,256]{1,0:T(8,128)(2,1)S(1)}, u32[]{:S(2)}, u32[]{:S(2)}) collective-permute-start(bf16[1024,256]{1,0:T(8,128)(2,1)S(1)} %collective-permute-done.3.refs_2_), channel_id=1, source_target_pairs={{0,1},{1,0},{2,3},{3,2},{4,5},{5,4},{6,7},{7,6},{8,9},{9,8},{10,11... | collective-permute-start | bytes 1572872 | tf_op jit(solution)/shard_map/ppermute | solution.py:31
  92.9 1.9 %collective-permute-start.6 = (bf16[1024,256]{1,0:T(8,128)(2,1)S(1)}, bf16[1024,256]{1,0:T(8,128)(2,1)S(1)}, u32[]{:S(2)}, u32[]{:S(2)}) collective-permute-start(bf16[1024,256]{1,0:T(8,128)(2,1)S(1)} %collective-permute-done.5.refs_4_), channel_id=1, source_target_pairs={{0,1},{1,0},{2,3},{3,2},{4,5},{5,4},{6,7},{7,6},{8,9},{9,8},{10,11... | collective-permute-start | bytes 1572872 | tf_op jit(solution)/shard_map/ppermute | solution.py:31
  94.8 2.4 %collective-permute-start.8 = (bf16[1024,256]{1,0:T(8,128)(2,1)S(1)}, bf16[1024,256]{1,0:T(8,128)(2,1)S(1)}, u32[]{:S(2)}, u32[]{:S(2)}) collective-permute-start(bf16[1024,256]{1,0:T(8,128)(2,1)S(1)} %collective-permute-done.7.refs_6_), channel_id=1, source_target_pairs={{0,1},{1,0},{2,3},{3,2},{4,5},{5,4},{6,7},{7,6},{8,9},{9,8},{10,11... | collective-permute-start | bytes 1572872 | tf_op jit(solution)/shard_map/ppermute | solution.py:31
  98.8 2.0 %shard_map.46 = (bf16[512,384]{1,0:T(8,128)(2,1)S(1)}, bf16[2048,384]{1,0:T(8,128)(2,1)S(1)}, bf16[2048,128]{1,0:T(8,128)(2,1)S(1)}) custom-call(s32[2]{0:T(128)S(1)} %pad_add_fusion.pos, bf16[1024,256]{1,0:T(8,128)(2,1)S(1)} %pad_maximum_fusion.refs_0_, bf16[1024,256]{1,0:T(8,128)(2,1)S(1)} %collective-permute-done.2.refs_1_, ...), custom_call_target="tpu_custom_call" | custom-call | flops 805306368 | bytes 8388608 | tf_op jit(solution)/shard_map/pallas_call | solution.py:39
  100.8 2.8 %collective-permute-start.17 = (bf16[512,384]{1,0:T(8,128)(2,1)S(1)}, bf16[512,384]{1,0:T(8,128)(2,1)S(1)}, u32[]{:S(2)}, u32[]{:S(2)}) collective-permute-start(bf16[512,384]{1,0:T(8,128)(2,1)S(1)} %get-tuple-element.15), channel_id=1, source_target_pairs={{0,256},{1,257},{2,258},{3,259},{4,260},{5,261},{6,262},{7,263},{8... | collective-permute-start | bytes 1179656 | tf_op jit(solution)/shard_map/ppermute | solution.py:31
  104.8 4.0 %collective-permute-start.18 = (f32[8,512]{1,0:T(8,128)S(1)}, f32[8,512]{1,0:T(8,128)S(1)}, u32[]{:S(2)}, u32[]{:S(2)}) collective-permute-start(f32[8,512]{1,0:T(8,128)S(1)} %get-tuple-element.17), channel_id=1, source_target_pairs={{0,256},{1,257},{2,258},{3,259},{4,260},{5,261},{6,262},{7,263},{8... | collective-permute-start | bytes 49160 | tf_op jit(solution)/shard_map/ppermute | solution.py:31
  110.6 2.9 %collective-permute-done.18.refs_3_ = f32[8,512]{1,0:T(8,128)S(1)} collective-permute-done((f32[8,512]{1,0:T(8,128)S(1)}, f32[8,512]{1,0:T(8,128)S(1)}, u32[]{:S(2)}, u32[]{:S(2)}) %collective-permute-start.18) | collective-permute-done | bytes 16416 | tf_op jit(solution)/shard_map/ppermute | solution.py:31
  115.9 3.1 %collective-permute-start.24 = (bf16[2048,128]{1,0:T(8,128)(2,1)S(1)}, bf16[2048,128]{1,0:T(8,128)(2,1)S(1)}, u32[]{:S(2)}, u32[]{:S(2)}) collective-permute-start(bf16[2048,128]{1,0:T(8,128)(2,1)S(1)} %get-tuple-element.22.refs_4_), channel_id=1, source_target_pairs={{0,256},{1,257},{2,258},{3,259},{4,260},{5,261},{6,262},{7,263},{8... | collective-permute-start | bytes 1572872 | tf_op jit(solution)/shard_map/ppermute | solution.py:31
  121.2 8.0 %collective-permute-start.20 = (bf16[512,128]{1,0:T(8,128)(2,1)S(1)}, bf16[512,128]{1,0:T(8,128)(2,1)S(1)}, u32[]{:S(2)}, u32[]{:S(2)}) collective-permute-start(bf16[512,128]{1,0:T(8,128)(2,1)S(1)} %shard_map.51), channel_id=1, source_target_pairs={{0,8},{1,9},{2,10},{3,11},{4,12},{5,13},{6,14},{7,15},{8,0},{9,1},... | collective-permute-start | bytes 393224 | tf_op jit(solution)/shard_map/ppermute | solution.py:31
  129.3 12.8 %collective-permute-done.20 = bf16[512,128]{1,0:T(8,128)(2,1)S(1)} collective-permute-done((bf16[512,128]{1,0:T(8,128)(2,1)S(1)}, bf16[512,128]{1,0:T(8,128)(2,1)S(1)}, u32[]{:S(2)}, u32[]{:S(2)}) %collective-permute-start.20) | collective-permute-done | bytes 131104 | tf_op jit(solution)/shard_map/ppermute | solution.py:31
  142.1 4.6 %collective-permute-start.21 = (bf16[512,256]{1,0:T(8,128)(2,1)S(1)}, bf16[512,256]{1,0:T(8,128)(2,1)S(1)}, u32[]{:S(2)}, u32[]{:S(2)}) collective-permute-start(bf16[512,256]{1,0:T(8,128)(2,1)S(1)} %pad_maximum_fusion.5.refs_0_), channel_id=1, source_target_pairs={{0,6},{1,7},{2,0},{3,1},{4,2},{5,3},{6,4},{7,5},{8,14},{9,15},{10,... | collective-permute-start | bytes 786440 | tf_op jit(solution)/shard_map/ppermute | solution.py:31
  148.6 2.5 %collective-permute-start.23 = (bf16[512,256]{1,0:T(8,128)(2,1)S(1)}, bf16[512,256]{1,0:T(8,128)(2,1)S(1)}, u32[]{:S(2)}, u32[]{:S(2)}) collective-permute-start(bf16[512,256]{1,0:T(8,128)(2,1)S(1)} %pad_maximum_fusion.5.refs_0_), channel_id=1, source_target_pairs={{0,2},{1,3},{2,4},{3,5},{4,6},{5,7},{6,0},{7,1},{8,10},{9,11},{10,... | collective-permute-start | bytes 786440 | tf_op jit(solution)/shard_map/ppermute | solution.py:31
  152.2 4.2 %collective-permute-done.22.refs_2_ = bf16[512,256]{1,0:T(8,128)(2,1)S(1)} collective-permute-done((bf16[512,256]{1,0:T(8,128)(2,1)S(1)}, bf16[512,256]{1,0:T(8,128)(2,1)S(1)}, u32[]{:S(2)}, u32[]{:S(2)}) %collective-permute-start.22) | collective-permute-done | bytes 262176 | tf_op jit(solution)/shard_map/ppermute | solution.py:31
  156.4 7.5 %collective-permute-done.23.refs_3_ = bf16[512,256]{1,0:T(8,128)(2,1)S(1)} collective-permute-done((bf16[512,256]{1,0:T(8,128)(2,1)S(1)}, bf16[512,256]{1,0:T(8,128)(2,1)S(1)}, u32[]{:S(2)}, u32[]{:S(2)}) %collective-permute-start.23) | collective-permute-done | bytes 262176 | tf_op jit(solution)/shard_map/ppermute | solution.py:31
  164.9 2.4 %collective-permute-start.25 = (bf16[512,256]{1,0:T(8,128)(2,1)S(1)}, bf16[512,256]{1,0:T(8,128)(2,1)S(1)}, u32[]{:S(2)}, u32[]{:S(2)}) collective-permute-start(bf16[512,256]{1,0:T(8,128)(2,1)S(1)} %shard_map.53), channel_id=1, source_target_pairs={{0,1},{1,0},{2,3},{3,2},{4,5},{5,4},{6,7},{7,6},{8,9},{9,8},{10,11... | collective-permute-start | bytes 786440 | tf_op jit(solution)/shard_map/ppermute | solution.py:31
  (42 shorter events, 17.0 us)
Async XLA Ops:
  0.0 52.6 %copy-start = (bf16[512,256]{1,0:T(8,128)(2,1)S(1)}, bf16[512,256]{1,0:T(8,128)(2,1)}, u32[]{:S(2)}) copy-start(bf16[512,256]{1,0:T(8,128)(2,1)} %refs_6_.1) | copy-start | bytes 786436
  0.0 5.0 %collective-permute-start.9 = (bf16[128,128]{1,0:T(8,128)(2,1)}, bf16[128,128]{1,0:T(8,128)(2,1)S(1)}, u32[]{:S(2)}, u32[]{:S(2)}) collective-permute-start(bf16[128,128]{1,0:T(8,128)(2,1)} %bitcast.15), channel_id=1, source_target_pairs={{0,0},{1,1},{2,64},{3,65},{4,128},{5,129},{6,192},{7,193},{8,256},... | collective-permute-start | bytes 98312 | tf_op jit(solution)/shard_map/ppermute | solution.py:31
  5.0 30.7 %collective-permute-start.11 = (bf16[128,512]{1,0:T(8,128)(2,1)S(1)}, bf16[128,512]{1,0:T(8,128)(2,1)S(1)}, u32[]{:S(2)}, u32[]{:S(2)}) collective-permute-start(bf16[128,512]{1,0:T(8,128)(2,1)S(1)} %pad_maximum_fusion.6), channel_id=1, source_target_pairs={{0,192},{1,193},{2,194},{3,195},{4,196},{5,197},{6,198},{7,199},{8... | collective-permute-start | bytes 393224 | tf_op jit(solution)/shard_map/ppermute | solution.py:31
  24.5 13.3 %collective-permute-start.10 = (bf16[128,512]{1,0:T(8,128)(2,1)S(1)}, bf16[128,512]{1,0:T(8,128)(2,1)S(1)}, u32[]{:S(2)}, u32[]{:S(2)}) collective-permute-start(bf16[128,512]{1,0:T(8,128)(2,1)S(1)} %pad_maximum_fusion.6), channel_id=1, source_target_pairs={{0,64},{1,65},{2,66},{3,67},{4,68},{5,69},{6,70},{7,71},{8,72},{9,... | collective-permute-start | bytes 393224 | tf_op jit(solution)/shard_map/ppermute | solution.py:31
  26.5 26.2 %collective-permute-start = (bf16[512,256]{1,0:T(8,128)(2,1)}, bf16[512,256]{1,0:T(8,128)(2,1)S(1)}, u32[]{:S(2)}, u32[]{:S(2)}) collective-permute-start(bf16[512,256]{1,0:T(8,128)(2,1)} %refs_6_.1), channel_id=1, source_target_pairs={{0,8},{1,9},{2,10},{3,11},{4,12},{5,13},{6,14},{7,15},{8,264},{9,2... | collective-permute-start | bytes 786440 | tf_op jit(solution)/shard_map/ppermute | solution.py:31
  29.3 23.3 %collective-permute-start.1 = (bf16[512,256]{1,0:T(8,128)(2,1)}, bf16[512,256]{1,0:T(8,128)(2,1)S(1)}, u32[]{:S(2)}, u32[]{:S(2)}) collective-permute-start(bf16[512,256]{1,0:T(8,128)(2,1)} %refs_6_.1), channel_id=1, source_target_pairs={{8,256},{9,257},{10,258},{11,259},{12,260},{13,261},{14,262},{15,2... | collective-permute-start | bytes 786440 | tf_op jit(solution)/shard_map/ppermute | solution.py:31
  37.9 25.8 %collective-permute-start.12 = (bf16[128,512]{1,0:T(8,128)(2,1)S(1)}, bf16[128,512]{1,0:T(8,128)(2,1)S(1)}, u32[]{:S(2)}, u32[]{:S(2)}) collective-permute-start(bf16[128,512]{1,0:T(8,128)(2,1)S(1)} %broadcast_select_fusion.2), channel_id=1, source_target_pairs={{0,192},{1,65},{2,194},{3,67},{4,196},{5,69},{6,198},{7,71},{8,200... | collective-permute-start | bytes 393224 | tf_op jit(solution)/shard_map/ppermute | solution.py:31
  47.6 18.6 %collective-permute-start.13 = (bf16[256,512]{1,0:T(8,128)(2,1)S(1)}, bf16[256,512]{1,0:T(8,128)(2,1)S(1)}, u32[]{:S(2)}, u32[]{:S(2)}) collective-permute-start(bf16[256,512]{1,0:T(8,128)(2,1)S(1)} %get-tuple-element.26), channel_id=1, source_target_pairs={{0,224},{1,225},{2,226},{3,227},{4,228},{5,229},{6,230},{7,231},{8... | collective-permute-start | bytes 786440 | tf_op jit(solution)/shard_map/ppermute | solution.py:31
  52.7 29.3 %collective-permute-start.2 = (bf16[1024,256]{1,0:T(8,128)(2,1)S(1)}, bf16[1024,256]{1,0:T(8,128)(2,1)S(1)}, u32[]{:S(2)}, u32[]{:S(2)}) collective-permute-start(bf16[1024,256]{1,0:T(8,128)(2,1)S(1)} %pad_maximum_fusion.refs_0_), channel_id=1, source_target_pairs={{0,1},{1,0},{2,3},{3,2},{4,5},{5,4},{6,7},{7,6},{8,9},{9,8},{10,11... | collective-permute-start | bytes 1572872 | tf_op jit(solution)/shard_map/ppermute | solution.py:31
  58.3 27.6 %collective-permute-start.3 = (bf16[1024,256]{1,0:T(8,128)(2,1)S(1)}, bf16[1024,256]{1,0:T(8,128)(2,1)S(1)}, u32[]{:S(2)}, u32[]{:S(2)}) collective-permute-start(bf16[1024,256]{1,0:T(8,128)(2,1)S(1)} %pad_maximum_fusion.refs_0_), channel_id=1, source_target_pairs={{0,6},{1,7},{2,0},{3,1},{4,2},{5,3},{6,4},{7,5},{8,14},{9,15},{10,... | collective-permute-start | bytes 1572872 | tf_op jit(solution)/shard_map/ppermute | solution.py:31
  61.7 31.2 %collective-permute-start.5 = (bf16[1024,256]{1,0:T(8,128)(2,1)S(1)}, bf16[1024,256]{1,0:T(8,128)(2,1)S(1)}, u32[]{:S(2)}, u32[]{:S(2)}) collective-permute-start(bf16[1024,256]{1,0:T(8,128)(2,1)S(1)} %pad_maximum_fusion.refs_0_), channel_id=1, source_target_pairs={{0,4},{1,5},{2,6},{3,7},{4,0},{5,1},{6,2},{7,3},{8,12},{9,13},{10,... | collective-permute-start | bytes 1572872 | tf_op jit(solution)/shard_map/ppermute | solution.py:31
  63.6 31.2 %collective-permute-start.7 = (bf16[1024,256]{1,0:T(8,128)(2,1)S(1)}, bf16[1024,256]{1,0:T(8,128)(2,1)S(1)}, u32[]{:S(2)}, u32[]{:S(2)}) collective-permute-start(bf16[1024,256]{1,0:T(8,128)(2,1)S(1)} %pad_maximum_fusion.refs_0_), channel_id=1, source_target_pairs={{0,2},{1,3},{2,4},{3,5},{4,6},{5,7},{6,0},{7,1},{8,10},{9,11},{10,... | collective-permute-start | bytes 1572872 | tf_op jit(solution)/shard_map/ppermute | solution.py:31
  66.2 9.5 %collective-permute-start.14 = (bf16[256,512]{1,0:T(8,128)(2,1)S(1)}, bf16[256,512]{1,0:T(8,128)(2,1)S(1)}, u32[]{:S(2)}, u32[]{:S(2)}) collective-permute-start(bf16[256,512]{1,0:T(8,128)(2,1)S(1)} %get-tuple-element.25), channel_id=1, source_target_pairs={{0,32},{1,33},{2,34},{3,35},{4,36},{5,37},{6,38},{7,39},{8,40},{9,... | collective-permute-start | bytes 786440 | tf_op jit(solution)/shard_map/ppermute | solution.py:31
  75.7 21.7 %collective-permute-start.15 = (bf16[512,512]{1,0:T(8,128)(2,1)S(1)}, bf16[512,512]{1,0:T(8,128)(2,1)S(1)}, u32[]{:S(2)}, u32[]{:S(2)}) collective-permute-start(bf16[512,512]{1,0:T(8,128)(2,1)S(1)} %pad_maximum_fusion.1.refs_8_), channel_id=1, source_target_pairs={{0,240},{1,241},{2,242},{3,243},{4,244},{5,245},{6,246},{7,247},{8... | collective-permute-start | bytes 1572872 | tf_op jit(solution)/shard_map/ppermute | solution.py:31
  82.0 15.4 %collective-permute-start.16 = (bf16[512,512]{1,0:T(8,128)(2,1)S(1)}, bf16[512,512]{1,0:T(8,128)(2,1)S(1)}, u32[]{:S(2)}, u32[]{:S(2)}) collective-permute-start(bf16[512,512]{1,0:T(8,128)(2,1)S(1)} %pad_maximum_fusion.1.refs_8_), channel_id=1, source_target_pairs={{0,16},{1,17},{2,18},{3,19},{4,20},{5,21},{6,22},{7,23},{8,24},{9,... | collective-permute-start | bytes 1572872 | tf_op jit(solution)/shard_map/ppermute | solution.py:31
  85.9 11.4 %collective-permute-start.4 = (bf16[1024,256]{1,0:T(8,128)(2,1)S(1)}, bf16[1024,256]{1,0:T(8,128)(2,1)S(1)}, u32[]{:S(2)}, u32[]{:S(2)}) collective-permute-start(bf16[1024,256]{1,0:T(8,128)(2,1)S(1)} %collective-permute-done.3.refs_2_), channel_id=1, source_target_pairs={{0,1},{1,0},{2,3},{3,2},{4,5},{5,4},{6,7},{7,6},{8,9},{9,8},{10,11... | collective-permute-start | bytes 1572872 | tf_op jit(solution)/shard_map/ppermute | solution.py:31
  92.9 4.4 %collective-permute-start.6 = (bf16[1024,256]{1,0:T(8,128)(2,1)S(1)}, bf16[1024,256]{1,0:T(8,128)(2,1)S(1)}, u32[]{:S(2)}, u32[]{:S(2)}) collective-permute-start(bf16[1024,256]{1,0:T(8,128)(2,1)S(1)} %collective-permute-done.5.refs_4_), channel_id=1, source_target_pairs={{0,1},{1,0},{2,3},{3,2},{4,5},{5,4},{6,7},{7,6},{8,9},{9,8},{10,11... | collective-permute-start | bytes 1572872 | tf_op jit(solution)/shard_map/ppermute | solution.py:31
  94.8 3.9 %collective-permute-start.8 = (bf16[1024,256]{1,0:T(8,128)(2,1)S(1)}, bf16[1024,256]{1,0:T(8,128)(2,1)S(1)}, u32[]{:S(2)}, u32[]{:S(2)}) collective-permute-start(bf16[1024,256]{1,0:T(8,128)(2,1)S(1)} %collective-permute-done.7.refs_6_), channel_id=1, source_target_pairs={{0,1},{1,0},{2,3},{3,2},{4,5},{5,4},{6,7},{7,6},{8,9},{9,8},{10,11... | collective-permute-start | bytes 1572872 | tf_op jit(solution)/shard_map/ppermute | solution.py:31
  100.8 12.7 %collective-permute-start.17 = (bf16[512,384]{1,0:T(8,128)(2,1)S(1)}, bf16[512,384]{1,0:T(8,128)(2,1)S(1)}, u32[]{:S(2)}, u32[]{:S(2)}) collective-permute-start(bf16[512,384]{1,0:T(8,128)(2,1)S(1)} %get-tuple-element.15), channel_id=1, source_target_pairs={{0,256},{1,257},{2,258},{3,259},{4,260},{5,261},{6,262},{7,263},{8... | collective-permute-start | bytes 1179656 | tf_op jit(solution)/shard_map/ppermute | solution.py:31
  104.8 8.7 %collective-permute-start.18 = (f32[8,512]{1,0:T(8,128)S(1)}, f32[8,512]{1,0:T(8,128)S(1)}, u32[]{:S(2)}, u32[]{:S(2)}) collective-permute-start(f32[8,512]{1,0:T(8,128)S(1)} %get-tuple-element.17), channel_id=1, source_target_pairs={{0,256},{1,257},{2,258},{3,259},{4,260},{5,261},{6,262},{7,263},{8... | collective-permute-start | bytes 49160 | tf_op jit(solution)/shard_map/ppermute | solution.py:31
  114.3 5.1 %collective-permute-start.19 = (bf16[512,256]{1,0:T(8,128)(2,1)S(1)}, bf16[512,256]{1,0:T(8,128)(2,1)S(1)}, u32[]{:S(2)}, u32[]{:S(2)}) collective-permute-start(bf16[512,256]{1,0:T(8,128)(2,1)S(1)} %get-tuple-element.19.kv_ref), channel_id=1, source_target_pairs={{0,16},{16,32},{32,48},{48,64},{64,80},{80,96},{96,112},{112,128},... | collective-permute-start | bytes 786440 | tf_op jit(solution)/shard_map/ppermute | solution.py:276
  115.9 35.2 %collective-permute-start.24 = (bf16[2048,128]{1,0:T(8,128)(2,1)S(1)}, bf16[2048,128]{1,0:T(8,128)(2,1)S(1)}, u32[]{:S(2)}, u32[]{:S(2)}) collective-permute-start(bf16[2048,128]{1,0:T(8,128)(2,1)S(1)} %get-tuple-element.22.refs_4_), channel_id=1, source_target_pairs={{0,256},{1,257},{2,258},{3,259},{4,260},{5,261},{6,262},{7,263},{8... | collective-permute-start | bytes 1572872 | tf_op jit(solution)/shard_map/ppermute | solution.py:31
  121.2 20.8 %collective-permute-start.20 = (bf16[512,128]{1,0:T(8,128)(2,1)S(1)}, bf16[512,128]{1,0:T(8,128)(2,1)S(1)}, u32[]{:S(2)}, u32[]{:S(2)}) collective-permute-start(bf16[512,128]{1,0:T(8,128)(2,1)S(1)} %shard_map.51), channel_id=1, source_target_pairs={{0,8},{1,9},{2,10},{3,11},{4,12},{5,13},{6,14},{7,15},{8,0},{9,1},... | collective-permute-start | bytes 393224 | tf_op jit(solution)/shard_map/ppermute | solution.py:31
  142.1 10.2 %collective-permute-start.21 = (bf16[512,256]{1,0:T(8,128)(2,1)S(1)}, bf16[512,256]{1,0:T(8,128)(2,1)S(1)}, u32[]{:S(2)}, u32[]{:S(2)}) collective-permute-start(bf16[512,256]{1,0:T(8,128)(2,1)S(1)} %pad_maximum_fusion.5.refs_0_), channel_id=1, source_target_pairs={{0,6},{1,7},{2,0},{3,1},{4,2},{5,3},{6,4},{7,5},{8,14},{9,15},{10,... | collective-permute-start | bytes 786440 | tf_op jit(solution)/shard_map/ppermute | solution.py:31
  146.6 9.8 %collective-permute-start.22 = (bf16[512,256]{1,0:T(8,128)(2,1)S(1)}, bf16[512,256]{1,0:T(8,128)(2,1)S(1)}, u32[]{:S(2)}, u32[]{:S(2)}) collective-permute-start(bf16[512,256]{1,0:T(8,128)(2,1)S(1)} %pad_maximum_fusion.5.refs_0_), channel_id=1, source_target_pairs={{0,4},{1,5},{2,6},{3,7},{4,0},{5,1},{6,2},{7,3},{8,12},{9,13},{10,... | collective-permute-start | bytes 786440 | tf_op jit(solution)/shard_map/ppermute | solution.py:31
  148.6 15.3 %collective-permute-start.23 = (bf16[512,256]{1,0:T(8,128)(2,1)S(1)}, bf16[512,256]{1,0:T(8,128)(2,1)S(1)}, u32[]{:S(2)}, u32[]{:S(2)}) collective-permute-start(bf16[512,256]{1,0:T(8,128)(2,1)S(1)} %pad_maximum_fusion.5.refs_0_), channel_id=1, source_target_pairs={{0,2},{1,3},{2,4},{3,5},{4,6},{5,7},{6,0},{7,1},{8,10},{9,11},{10,... | collective-permute-start | bytes 786440 | tf_op jit(solution)/shard_map/ppermute | solution.py:31
  164.9 3.6 %collective-permute-start.25 = (bf16[512,256]{1,0:T(8,128)(2,1)S(1)}, bf16[512,256]{1,0:T(8,128)(2,1)S(1)}, u32[]{:S(2)}, u32[]{:S(2)}) collective-permute-start(bf16[512,256]{1,0:T(8,128)(2,1)S(1)} %shard_map.53), channel_id=1, source_target_pairs={{0,1},{1,0},{2,3},{3,2},{4,5},{5,4},{6,7},{7,6},{8,9},{9,8},{10,11... | collective-permute-start | bytes 786440 | tf_op jit(solution)/shard_map/ppermute | solution.py:31

commit v3 on v2

--- a/solution.py
+++ b/solution.py
@@ -12,6 +12,7 @@
 AXES = ("ctx", "tp")
 BF = jnp.bfloat16
 F32 = jnp.float32
+REV = [int(f"{p:04b}"[::-1], 2) for p in range(16)]
 STEPS = ((0, -4, 4, 8), (2, 6), (-2, -6), (1, -3, 5, 9), (-1, -5, 3, 7))
 
 
@@ -93,6 +94,15 @@
         ref[...] = total
 
 
+def double_z(chunk):
+    held = chunk
+    for by in (8, 4, 2, 1):
+        got = permute(held, lambda a, z, b, y, k: (a, z + (16 - by if k else by), b, y, k))
+        if by > 1:
+            held = jnp.concatenate([held, got], axis=0)
+    return held, got
+
+
 def project_rows(pos, blocks, weights, first, seg):
     _, _, _, y, k = place(pos)
     rows = weights.shape[0] // 16
@@ -109,17 +119,17 @@
 
 
 def project_other_body(pos, *refs):
-    blocks, parts, (send_ref, w_ref, out_w_ref) = refs[:8], refs[8:13], refs[13:]
+    blocks, parts, (kv_ref, q_ref, w_ref) = refs[:8], refs[8:13], refs[13:]
     _, z, _, _, _ = place(pos)
     rows = w_ref.shape[0] // 16
-    seg, wide = send_ref.shape
+    seg, hd = q_ref.shape
     for part, steps in zip(parts, STEPS):
         for i, step in enumerate(steps):
             at = pl.multiple_of(((z + step + 16) & 15) * rows, rows)
-            w_ref[pl.ds(at, rows), :] = part[i * rows : (i + 1) * rows, :wide]
-            out_w_ref[pl.ds(at, rows), :] = part[i * rows : (i + 1) * rows, wide:]
+            w_ref[pl.ds(at, rows), :] = part[i * rows : (i + 1) * rows, :]
     for at, acc in project_rows(pos, blocks, w_ref, seg, seg):
-        send_ref[at, :] = acc.astype(BF)
+        q_ref[at, :] = acc[:, :hd].astype(BF)
+        kv_ref[at, :] = acc[:, hd:].astype(BF)
 
 
 def project_own_body(pos, *refs):
@@ -128,19 +138,18 @@
         own_ref[at, :] = acc
 
 
-def combine_body(own_ref, got_ref, ssq_ref, ssq_got_ref, q_ref, kv_ref, *, features):
-    hd = q_ref.shape[1]
+def combine_body(own_ref, got_ref, ssq_ref, ssq_got_ref, out_ref, *, features, first):
+    wide = out_ref.shape[1]
     scale = lax.rsqrt((ssq_ref[...] + ssq_got_ref[...]) * (1.0 / features) + 1e-06)
     column = lax.dot_general(
         scale,
-        jnp.full((scale.shape[0], 3 * hd), 1.0 / scale.shape[0], F32),
+        jnp.full((scale.shape[0], wide), 1.0 / scale.shape[0], F32),
         (((0,), (0,)), ((), ())),
         precision=lax.Precision.HIGHEST,
         preferred_element_type=F32,
     )
-    total = (own_ref[...] + got_ref[...].astype(F32)) * column
-    q_ref[...] = total[:, :hd].astype(BF)
-    kv_ref[...] = total[:, hd:].astype(BF)
+    own = own_ref[:, first : first + wide]
+    out_ref[...] = ((own + got_ref[...].astype(F32)) * column).astype(BF)
 
 
 def scores_of(q, keys):
@@ -172,34 +181,39 @@
     out_ref[...] = out.astype(BF)
 
 
-def output_of(pos, pieces, w_own, w_other, core):
+def output_of(pos, pieces, w_ref, core):
     a, _, b, y, _ = place(pos)
-    hd = w_own.shape[1]
+    hd = w_ref.shape[1] // 2
     total = None
     for i in range(4):
         yy = (y + i) & 3
         at = pl.multiple_of(((core + 2 * yy + 2 * y) & 7) * 2 * hd, 2 * hd)
-        own = w_own[pl.ds(at, 2 * hd), :]
-        other = w_other[pl.ds(at, 2 * hd), :]
+        both = w_ref[pl.ds(at, 2 * hd), :]
+        own, other = both[:, :hd], both[:, hd:]
         same = jnp.full(own.shape, a == b)
         rows = []
-        for both in (jnp.where(same, own, other), jnp.where(same, other, own)):
-            rows.append(jnp.concatenate([both[:hd], both[hd:]], axis=1))
+        for half in (jnp.where(same, own, other), jnp.where(same, other, own)):
+            rows.append(jnp.concatenate([half[:hd], half[hd:]], axis=1))
         part = jnp.dot(pieces[i][...], jnp.concatenate(rows, axis=0), preferred_element_type=F32)
         total = part if total is None else total + part
     return total
 
 
 def output_other_body(pos, *refs):
-    pieces, (w_own, w_other, send_ref) = refs[:4], refs[4:]
-    core = 1 - place(pos)[4]
-    send_ref[...] = output_of(pos, pieces, w_own, w_other, core).astype(BF)
+    pieces, (w_lo, w_hi, send_ref, w_ref) = refs[:4], refs[4:]
+    _, z, _, _, k = place(pos)
+    rows = w_ref.shape[0] // 16
+    for p in range(16):
+        at = pl.multiple_of(((z - (1 - 2 * k) * REV[p] + 16) & 15) * rows, rows)
+        half = w_lo if p < 8 else w_hi
+        w_ref[pl.ds(at, rows), :] = half[p % 8 * rows : (p % 8 + 1) * rows, :]
+    send_ref[...] = output_of(pos, pieces, w_ref, 1 - k).astype(BF)
 
 
 def output_own_body(pos, *refs):
-    pieces, (w_own, w_other, hidden_ref, out_ref) = refs[:4], refs[4:]
+    pieces, (w_ref, hidden_ref, out_ref) = refs[:4], refs[4:]
     core = place(pos)[4]
-    out_ref[...] = hidden_ref[...].astype(F32) + output_of(pos, pieces, w_own, w_other, core)
+    out_ref[...] = hidden_ref[...].astype(F32) + output_of(pos, pieces, w_ref, core)
 
 
 def add_body(own_ref, got_ref, out_ref):
@@ -228,9 +242,8 @@
     pos = jnp.stack([ctx, tp]).astype(jnp.int32)
     same = (ctx >> 4) == (tp >> 3)
 
-    piece = permute(w_out[0], lambda a, z, b, y, k: (b, z + 4 * y, a, z // 4, k))
     folded = (w_qkv[0].astype(F32) * norm_gain[0].astype(F32)[None, :, None]).astype(BF)
-    chunk = jnp.concatenate([folded[0], folded[1], folded[2], piece], axis=1)
+    chunk = jnp.concatenate([folded[0], folded[1], folded[2]], axis=1)
     parts = gather_z(chunk, tp & 1)
 
     corner = {(0, 0): (0, 1), (0, 1): (1, 1), (1, 1): (1, 0), (1, 0): (0, 0)}
@@ -242,6 +255,10 @@
     for block in around(jnp.concatenate([own, other], axis=0)):
         blocks += [block, permute(block, swap_core)]
 
+    piece_a = permute(w_out[0], lambda a, z, b, y, k: (b, z + 4 * y, a, z // 4, k))
+    piece_b = permute(w_out[0], lambda a, z, b, y, k: (1 - b, z + 4 * y, a, z // 4, k))
+    o_lo, o_hi = double_z(jnp.concatenate([piece_a, piece_b], axis=1))
+
     ssq, ssq_send = call(
         squares_body,
         (shape((8, seg), F32), shape((8, seg), F32)),
@@ -250,29 +267,31 @@
         scalars=False,
     )(*blocks)
     ssq_got = permute(ssq_send, swap_hi)
-    send, weights, out_w = call(
+    kv_send, q_send, weights = call(
         project_other_body,
-        (
-            shape((seg, 3 * hd), BF),
-            shape((16 * hd, 3 * hd), BF),
-            shape((16 * hd, hd), BF),
-        ),
+        (shape((seg, 2 * hd), BF), shape((seg, hd), BF), shape((16 * hd, 3 * hd), BF)),
         flops=2 * seg * 8 * feats * 3 * hd,
         nbytes=8 << 20,
     )(pos, *blocks, *parts)
-    got = permute(send, swap_hi)
+    kv_got = permute(kv_send, swap_hi)
+    q_got = permute(q_send, swap_hi)
     own_part = call(
         project_own_body,
         shape((seg, 3 * hd), F32),
         flops=2 * seg * 8 * feats * 3 * hd,
         nbytes=8 << 20,
     )(pos, *blocks, weights)
-    q, kv = call(
-        lambda *refs: combine_body(*refs, features=16 * feats),
-        (shape((seg, hd), BF), shape((seg, 2 * hd), BF)),
-        nbytes=2 << 20,
-        scalars=False,
-    )(own_part, got, ssq, ssq_got)
+
+    def combine(got, first):
+        return call(
+            lambda *refs: combine_body(*refs, features=16 * feats, first=first),
+            shape(got.shape, BF),
+            nbytes=1 << 20,
+            scalars=False,
+        )(own_part, got, ssq, ssq_got)
+
+    kv = combine(kv_got, hd)
+    q = combine(q_got, 0)
     prev = lax.ppermute(kv, "ctx", [(i, i + 1) for i in range(31)])
     e_own, sum_own = call(
         own_body,
@@ -286,15 +305,14 @@
     )(pos, q, kv, prev, e_own, sum_own)
 
     facing = permute(attended, lambda a, z, b, y, k: (a, z, 1 - b, y, k))
-    out_w_other = permute(out_w, swap_hi)
     pieces = around(jnp.concatenate([attended, facing], axis=1))
     sizes = dict(flops=2 * seg * feats * 8 * hd, nbytes=3 << 20)
-    out_send = call(output_other_body, shape((seg, feats), BF), **sizes)(
-        pos, *pieces, out_w, out_w_other
-    )
+    out_send, out_w = call(
+        output_other_body, (shape((seg, feats), BF), shape((16 * hd, 2 * hd), BF)), **sizes
+    )(pos, *pieces, o_lo, o_hi)
     out_got = permute(out_send, swap_core)
     out_own = call(output_own_body, shape((seg, feats), F32), **sizes)(
-        pos, *pieces, out_w, out_w_other, hidden
+        pos, *pieces, out_w, hidden
     )
     return call(add_body, shape((seg, feats), BF), scalars=False)(out_own, out_got)
 

time: 170 us -> 193 us (1.14)
  the two profiles are of different devices: /device:TPU:3 before, /device:TPU:1 now
where the time goes in v3:
time: 193 us; the launch traced here: 192 us
  starting transfers between devices  141 us (73%)
  waiting for transfers between devices  36.3 us (19%)
  Pallas kernels  11 us (6%)
  other arithmetic  2.97 us (2%)
    ppermute x30, starting transfers between devices, permute(): return lax.ppermute(value, AXES, pairs_of(target))  140 us
    ppermute x30, waiting for transfers between devices, permute(): return lax.ppermute(value, AXES, pairs_of(target))  36.2 us
    pallas_call x10, Pallas kernels, run(): pl.pallas_call(body, out_shape=outs, in_specs=specs, out_specs=jax.tree.m...  11 us
  transfers between devices with their start and end apart: 31, of which 10 were waited for; matrix products, arithmetic and copies ran while one was open for 2% of the time, Pallas kernels for 5%

profile of v3, /device:TPU:1, one launch (start us, length us, event | category | flops | bytes accessed | tf_op | source)
XLA Modules:
  0.0 191.8 jit_solution(16451087688987705683)
XLA Ops:
  0.0 3.9 %collective-permute-start = (bf16[512,256]{1,0:T(8,128)(2,1)}, bf16[512,256]{1,0:T(8,128)(2,1)S(1)}, u32[]{:S(2)}, u32[]{:S(2)}) collective-permute-start(bf16[512,256]{1,0:T(8,128)(2,1)} %refs_5_.1), channel_id=1, source_target_pairs={{0,8},{1,9},{2,10},{3,11},{4,12},{5,13},{6,14},{7,15},{8,264},{9,2... | collective-permute-start | bytes 786440 | tf_op jit(solution)/shard_map/ppermute | solution.py:32
  7.7 15.7 %collective-permute-start.10 = (bf16[128,384]{1,0:T(8,128)(2,1)S(1)}, bf16[128,384]{1,0:T(8,128)(2,1)S(1)}, u32[]{:S(2)}, u32[]{:S(2)}) collective-permute-start(bf16[128,384]{1,0:T(8,128)(2,1)S(1)} %pad_maximum_fusion.9), channel_id=1, source_target_pairs={{0,192},{1,193},{2,194},{3,195},{4,196},{5,197},{6,198},{7,199},{8... | collective-permute-start | bytes 294920 | tf_op jit(solution)/shard_map/ppermute | solution.py:32
  23.4 1.9 %collective-permute-start.9 = (bf16[128,384]{1,0:T(8,128)(2,1)S(1)}, bf16[128,384]{1,0:T(8,128)(2,1)S(1)}, u32[]{:S(2)}, u32[]{:S(2)}) collective-permute-start(bf16[128,384]{1,0:T(8,128)(2,1)S(1)} %pad_maximum_fusion.9), channel_id=1, source_target_pairs={{0,64},{1,65},{2,66},{3,67},{4,68},{5,69},{6,70},{7,71},{8,72},{9,... | collective-permute-start | bytes 294920 | tf_op jit(solution)/shard_map/ppermute | solution.py:32
  25.4 6.5 %collective-permute-start.25 = (bf16[128,128]{1,0:T(8,128)(2,1)}, bf16[128,128]{1,0:T(8,128)(2,1)S(1)}, u32[]{:S(2)}, u32[]{:S(2)}) collective-permute-start(bf16[128,128]{1,0:T(8,128)(2,1)} %bitcast.16), channel_id=1, source_target_pairs={{0,256},{1,257},{2,320},{3,321},{4,384},{5,385},{6,448},{7,449},{8... | collective-permute-start | bytes 98312 | tf_op jit(solution)/shard_map/ppermute | solution.py:32
  33.2 27.2 %collective-permute-start.26 = (bf16[128,256]{1,0:T(8,128)(2,1)S(1)}, bf16[128,256]{1,0:T(8,128)(2,1)S(1)}, u32[]{:S(2)}, u32[]{:S(2)}) collective-permute-start(bf16[128,256]{1,0:T(8,128)(2,1)S(1)} %constant_dynamic-update-slice_fusion), channel_id=1, source_target_pairs={{0,128},{1,129},{2,130},{3,131},{4,132},{5,133},{6,134},{7,135},{8... | collective-permute-start | bytes 196616 | tf_op jit(solution)/shard_map/ppermute | solution.py:32
  60.5 1.9 %collective-permute-start.11 = (bf16[128,384]{1,0:T(8,128)(2,1)S(1)}, bf16[128,384]{1,0:T(8,128)(2,1)S(1)}, u32[]{:S(2)}, u32[]{:S(2)}) collective-permute-start(bf16[128,384]{1,0:T(8,128)(2,1)S(1)} %broadcast_select_fusion.2), channel_id=1, source_target_pairs={{0,192},{1,65},{2,194},{3,67},{4,196},{5,69},{6,198},{7,71},{8,200... | collective-permute-start | bytes 294920 | tf_op jit(solution)/shard_map/ppermute | solution.py:32
  63.5 1.9 %collective-permute-start.3 = (bf16[1024,256]{1,0:T(8,128)(2,1)S(1)}, bf16[1024,256]{1,0:T(8,128)(2,1)S(1)}, u32[]{:S(2)}, u32[]{:S(2)}) collective-permute-start(bf16[1024,256]{1,0:T(8,128)(2,1)S(1)} %pad_maximum_fusion.refs_0_), channel_id=1, source_target_pairs={{0,6},{1,7},{2,0},{3,1},{4,2},{5,3},{6,4},{7,5},{8,14},{9,15},{10,... | collective-permute-start | bytes 1572872 | tf_op jit(solution)/shard_map/ppermute | solution.py:32
  65.4 1.9 %collective-permute-start.5 = (bf16[1024,256]{1,0:T(8,128)(2,1)S(1)}, bf16[1024,256]{1,0:T(8,128)(2,1)S(1)}, u32[]{:S(2)}, u32[]{:S(2)}) collective-permute-start(bf16[1024,256]{1,0:T(8,128)(2,1)S(1)} %pad_maximum_fusion.refs_0_), channel_id=1, source_target_pairs={{0,4},{1,5},{2,6},{3,7},{4,0},{5,1},{6,2},{7,3},{8,12},{9,13},{10,... | collective-permute-start | bytes 1572872 | tf_op jit(solution)/shard_map/ppermute | solution.py:32
  67.3 3.4 %collective-permute-start.7 = (bf16[1024,256]{1,0:T(8,128)(2,1)S(1)}, bf16[1024,256]{1,0:T(8,128)(2,1)S(1)}, u32[]{:S(2)}, u32[]{:S(2)}) collective-permute-start(bf16[1024,256]{1,0:T(8,128)(2,1)S(1)} %pad_maximum_fusion.refs_0_), channel_id=1, source_target_pairs={{0,2},{1,3},{2,4},{3,5},{4,6},{5,7},{6,0},{7,1},{8,10},{9,11},{10,... | collective-permute-start | bytes 1572872 | tf_op jit(solution)/shard_map/ppermute | solution.py:32
  70.8 4.5 %collective-permute-start.12 = (bf16[256,384]{1,0:T(8,128)(2,1)S(1)}, bf16[256,384]{1,0:T(8,128)(2,1)S(1)}, u32[]{:S(2)}, u32[]{:S(2)}) collective-permute-start(bf16[256,384]{1,0:T(8,128)(2,1)S(1)} %get-tuple-element.26), channel_id=1, source_target_pairs={{0,224},{1,225},{2,226},{3,227},{4,228},{5,229},{6,230},{7,231},{8... | collective-permute-start | bytes 589832 | tf_op jit(solution)/shard_map/ppermute | solution.py:32
  75.3 1.9 %collective-permute-start.14 = (bf16[512,384]{1,0:T(8,128)(2,1)S(1)}, bf16[512,384]{1,0:T(8,128)(2,1)S(1)}, u32[]{:S(2)}, u32[]{:S(2)}) collective-permute-start(bf16[512,384]{1,0:T(8,128)(2,1)S(1)} %pad_maximum_fusion.2.refs_8_), channel_id=1, source_target_pairs={{0,240},{1,241},{2,242},{3,243},{4,244},{5,245},{6,246},{7,247},{8... | collective-permute-start | bytes 1179656 | tf_op jit(solution)/shard_map/ppermute | solution.py:32
  77.2 5.0 %collective-permute-done.12.refs_9_ = bf16[256,384]{1,0:T(8,128)(2,1)S(1)} collective-permute-done((bf16[256,384]{1,0:T(8,128)(2,1)S(1)}, bf16[256,384]{1,0:T(8,128)(2,1)S(1)}, u32[]{:S(2)}, u32[]{:S(2)}) %collective-permute-start.12) | collective-permute-done | bytes 196640 | tf_op jit(solution)/shard_map/ppermute | solution.py:32
  82.3 4.9 %collective-permute-start.13 = (bf16[256,384]{1,0:T(8,128)(2,1)S(1)}, bf16[256,384]{1,0:T(8,128)(2,1)S(1)}, u32[]{:S(2)}, u32[]{:S(2)}) collective-permute-start(bf16[256,384]{1,0:T(8,128)(2,1)S(1)} %get-tuple-element.25), channel_id=1, source_target_pairs={{0,32},{1,33},{2,34},{3,35},{4,36},{5,37},{6,38},{7,39},{8,40},{9,... | collective-permute-start | bytes 589832 | tf_op jit(solution)/shard_map/ppermute | solution.py:32
  87.1 4.2 %collective-permute-done.13.refs_10_ = bf16[256,384]{1,0:T(8,128)(2,1)S(1)} collective-permute-done((bf16[256,384]{1,0:T(8,128)(2,1)S(1)}, bf16[256,384]{1,0:T(8,128)(2,1)S(1)}, u32[]{:S(2)}, u32[]{:S(2)}) %collective-permute-start.13) | collective-permute-done | bytes 196640 | tf_op jit(solution)/shard_map/ppermute | solution.py:32
  91.4 6.9 %collective-permute-start.2 = (bf16[1024,256]{1,0:T(8,128)(2,1)S(1)}, bf16[1024,256]{1,0:T(8,128)(2,1)S(1)}, u32[]{:S(2)}, u32[]{:S(2)}) collective-permute-start(bf16[1024,256]{1,0:T(8,128)(2,1)S(1)} %pad_maximum_fusion.refs_0_), channel_id=1, source_target_pairs={{0,1},{1,0},{2,3},{3,2},{4,5},{5,4},{6,7},{7,6},{8,9},{9,8},{10,11... | collective-permute-start | bytes 1572872 | tf_op jit(solution)/shard_map/ppermute | solution.py:32
  100.2 2.4 %collective-permute-start.6 = (bf16[1024,256]{1,0:T(8,128)(2,1)S(1)}, bf16[1024,256]{1,0:T(8,128)(2,1)S(1)}, u32[]{:S(2)}, u32[]{:S(2)}) collective-permute-start(bf16[1024,256]{1,0:T(8,128)(2,1)S(1)} %collective-permute-done.5.refs_4_), channel_id=1, source_target_pairs={{0,1},{1,0},{2,3},{3,2},{4,5},{5,4},{6,7},{7,6},{8,9},{9,8},{10,11... | collective-permute-start | bytes 1572872 | tf_op jit(solution)/shard_map/ppermute | solution.py:32
  104.5 2.6 %collective-permute-start.15 = (bf16[512,384]{1,0:T(8,128)(2,1)S(1)}, bf16[512,384]{1,0:T(8,128)(2,1)S(1)}, u32[]{:S(2)}, u32[]{:S(2)}) collective-permute-start(bf16[512,384]{1,0:T(8,128)(2,1)S(1)} %pad_maximum_fusion.2.refs_8_), channel_id=1, source_target_pairs={{0,16},{1,17},{2,18},{3,19},{4,20},{5,21},{6,22},{7,23},{8,24},{9,... | collective-permute-start | bytes 1179656 | tf_op jit(solution)/shard_map/ppermute | solution.py:32
  107.1 10.7 %collective-permute-done.15.refs_12_ = bf16[512,384]{1,0:T(8,128)(2,1)S(1)} collective-permute-done((bf16[512,384]{1,0:T(8,128)(2,1)S(1)}, bf16[512,384]{1,0:T(8,128)(2,1)S(1)}, u32[]{:S(2)}, u32[]{:S(2)}) %collective-permute-start.15) | collective-permute-done | bytes 393248 | tf_op jit(solution)/shard_map/ppermute | solution.py:32
  117.8 5.8 %collective-permute-start.27 = (bf16[256,256]{1,0:T(8,128)(2,1)S(1)}, bf16[256,256]{1,0:T(8,128)(2,1)S(1)}, u32[]{:S(2)}, u32[]{:S(2)}) collective-permute-start(bf16[256,256]{1,0:T(8,128)(2,1)S(1)} %pad_maximum_fusion.8), channel_id=1, source_target_pairs={{0,64},{1,193},{2,66},{3,195},{4,68},{5,197},{6,70},{7,199},{8,72}... | collective-permute-start | bytes 393224 | tf_op jit(solution)/shard_map/ppermute | solution.py:32
  123.7 1.9 %shard_map.46 = (bf16[512,256]{1,0:T(8,128)(2,1)S(1)}, bf16[512,128]{1,0:T(8,128)(2,1)S(1)}, bf16[2048,384]{1,0:T(8,128)(2,1)S(1)}) custom-call(s32[2]{0:T(128)S(1)} %pad_add_fusion.pos, bf16[1024,256]{1,0:T(8,128)(2,1)S(1)} %pad_maximum_fusion.refs_0_, bf16[1024,256]{1,0:T(8,128)(2,1)S(1)} %collective-permute-done.2.refs_1_, ...), custom_call_target="tpu_custom_call" | custom-call | flops 805306368 | bytes 8388608 | tf_op jit(solution)/shard_map/pallas_call | solution.py:40
  125.7 5.4 %collective-permute-start.18 = (bf16[512,256]{1,0:T(8,128)(2,1)S(1)}, bf16[512,256]{1,0:T(8,128)(2,1)S(1)}, u32[]{:S(2)}, u32[]{:S(2)}) collective-permute-start(bf16[512,256]{1,0:T(8,128)(2,1)S(1)} %get-tuple-element.18), channel_id=1, source_target_pairs={{0,256},{1,257},{2,258},{3,259},{4,260},{5,261},{6,262},{7,263},{8... | collective-permute-start | bytes 786440 | tf_op jit(solution)/shard_map/ppermute | solution.py:32
  131.6 2.0 %collective-permute-start.28 = (bf16[512,256]{1,0:T(8,128)(2,1)S(1)}, bf16[512,256]{1,0:T(8,128)(2,1)S(1)}, u32[]{:S(2)}, u32[]{:S(2)}) collective-permute-start(bf16[512,256]{1,0:T(8,128)(2,1)S(1)} %pad_maximum_fusion.4), channel_id=1, source_target_pairs={{0,32},{1,225},{2,34},{3,227},{4,36},{5,229},{6,38},{7,231},{8,40}... | collective-permute-start | bytes 786440 | tf_op jit(solution)/shard_map/ppermute | solution.py:32
  134.9 6.8 %collective-permute-start.17 = (f32[8,512]{1,0:T(8,128)S(1)}, f32[8,512]{1,0:T(8,128)S(1)}, u32[]{:S(2)}, u32[]{:S(2)}) collective-permute-start(f32[8,512]{1,0:T(8,128)S(1)} %get-tuple-element.17), channel_id=1, source_target_pairs={{0,256},{1,257},{2,258},{3,259},{4,260},{5,261},{6,262},{7,263},{8... | collective-permute-start | bytes 49160 | tf_op jit(solution)/shard_map/ppermute | solution.py:32
  145.4 4.8 %collective-permute-start.16 = (bf16[512,128]{1,0:T(8,128)(2,1)S(1)}, bf16[512,128]{1,0:T(8,128)(2,1)S(1)}, u32[]{:S(2)}, u32[]{:S(2)}) collective-permute-start(bf16[512,128]{1,0:T(8,128)(2,1)S(1)} %get-tuple-element.15), channel_id=1, source_target_pairs={{0,256},{1,257},{2,258},{3,259},{4,260},{5,261},{6,262},{7,263},{8... | collective-permute-start | bytes 393224 | tf_op jit(solution)/shard_map/ppermute | solution.py:32
  150.2 4.3 %collective-permute-start.29 = (bf16[1024,256]{1,0:T(8,128)(2,1)S(1)}, bf16[1024,256]{1,0:T(8,128)(2,1)S(1)}, u32[]{:S(2)}, u32[]{:S(2)}) collective-permute-start(bf16[1024,256]{1,0:T(8,128)(2,1)S(1)} %pad_maximum_fusion.1.refs_4_), channel_id=1, source_target_pairs={{0,16},{1,241},{2,18},{3,243},{4,20},{5,245},{6,22},{7,247},{8,24}... | collective-permute-start | bytes 1572872 | tf_op jit(solution)/shard_map/ppermute | solution.py:32
  154.6 3.4 %collective-permute-done.16.refs_1_ = bf16[512,128]{1,0:T(8,128)(2,1)S(1)} collective-permute-done((bf16[512,128]{1,0:T(8,128)(2,1)S(1)}, bf16[512,128]{1,0:T(8,128)(2,1)S(1)}, u32[]{:S(2)}, u32[]{:S(2)}) %collective-permute-start.16) | collective-permute-done | bytes 131104 | tf_op jit(solution)/shard_map/ppermute | solution.py:32
  160.7 2.1 %collective-permute-start.20 = (bf16[512,128]{1,0:T(8,128)(2,1)S(1)}, bf16[512,128]{1,0:T(8,128)(2,1)S(1)}, u32[]{:S(2)}, u32[]{:S(2)}) collective-permute-start(bf16[512,128]{1,0:T(8,128)(2,1)S(1)} %shard_map.52), channel_id=1, source_target_pairs={{0,8},{1,9},{2,10},{3,11},{4,12},{5,13},{6,14},{7,15},{8,0},{9,1},... | collective-permute-start | bytes 393224 | tf_op jit(solution)/shard_map/ppermute | solution.py:32
  162.8 3.7 %collective-permute-done.20 = bf16[512,128]{1,0:T(8,128)(2,1)S(1)} collective-permute-done((bf16[512,128]{1,0:T(8,128)(2,1)S(1)}, bf16[512,128]{1,0:T(8,128)(2,1)S(1)}, u32[]{:S(2)}, u32[]{:S(2)}) %collective-permute-start.20) | collective-permute-done | bytes 131104 | tf_op jit(solution)/shard_map/ppermute | solution.py:32
  170.4 3.4 %collective-permute-start.23 = (bf16[512,256]{1,0:T(8,128)(2,1)S(1)}, bf16[512,256]{1,0:T(8,128)(2,1)S(1)}, u32[]{:S(2)}, u32[]{:S(2)}) collective-permute-start(bf16[512,256]{1,0:T(8,128)(2,1)S(1)} %pad_maximum_fusion.3.refs_0_), channel_id=1, source_target_pairs={{0,2},{1,3},{2,4},{3,5},{4,6},{5,7},{6,0},{7,1},{8,10},{9,11},{10,... | collective-permute-start | bytes 786440 | tf_op jit(solution)/shard_map/ppermute | solution.py:32
  173.8 3.3 %collective-permute-done.22.refs_2_ = bf16[512,256]{1,0:T(8,128)(2,1)S(1)} collective-permute-done((bf16[512,256]{1,0:T(8,128)(2,1)S(1)}, bf16[512,256]{1,0:T(8,128)(2,1)S(1)}, u32[]{:S(2)}, u32[]{:S(2)}) %collective-permute-start.22) | collective-permute-done | bytes 262176 | tf_op jit(solution)/shard_map/ppermute | solution.py:32
  177.1 3.8 %collective-permute-done.23.refs_3_ = bf16[512,256]{1,0:T(8,128)(2,1)S(1)} collective-permute-done((bf16[512,256]{1,0:T(8,128)(2,1)S(1)}, bf16[512,256]{1,0:T(8,128)(2,1)S(1)}, u32[]{:S(2)}, u32[]{:S(2)}) %collective-permute-start.23) | collective-permute-done | bytes 262176 | tf_op jit(solution)/shard_map/ppermute | solution.py:32
  181.9 8.0 %collective-permute-start.30 = (bf16[512,256]{1,0:T(8,128)(2,1)S(1)}, bf16[512,256]{1,0:T(8,128)(2,1)S(1)}, u32[]{:S(2)}, u32[]{:S(2)}) collective-permute-start(bf16[512,256]{1,0:T(8,128)(2,1)S(1)} %get-tuple-element.22), channel_id=1, source_target_pairs={{0,1},{1,0},{2,3},{3,2},{4,5},{5,4},{6,7},{7,6},{8,9},{9,8},{10,11... | collective-permute-start | bytes 786440 | tf_op jit(solution)/shard_map/ppermute | solution.py:32
  (58 shorter events, 25.2 us)
Async XLA Ops:
  0.0 62.4 %collective-permute-start = (bf16[512,256]{1,0:T(8,128)(2,1)}, bf16[512,256]{1,0:T(8,128)(2,1)S(1)}, u32[]{:S(2)}, u32[]{:S(2)}) collective-permute-start(bf16[512,256]{1,0:T(8,128)(2,1)} %refs_5_.1), channel_id=1, source_target_pairs={{0,8},{1,9},{2,10},{3,11},{4,12},{5,13},{6,14},{7,15},{8,264},{9,2... | collective-permute-start | bytes 786440 | tf_op jit(solution)/shard_map/ppermute | solution.py:32
  3.9 58.5 %collective-permute-start.1 = (bf16[512,256]{1,0:T(8,128)(2,1)}, bf16[512,256]{1,0:T(8,128)(2,1)S(1)}, u32[]{:S(2)}, u32[]{:S(2)}) collective-permute-start(bf16[512,256]{1,0:T(8,128)(2,1)} %refs_5_.1), channel_id=1, source_target_pairs={{8,256},{9,257},{10,258},{11,259},{12,260},{13,261},{14,262},{15,2... | collective-permute-start | bytes 786440 | tf_op jit(solution)/shard_map/ppermute | solution.py:32
  4.6 20.7 %collective-permute-start.24 = (bf16[128,128]{1,0:T(8,128)(2,1)}, bf16[128,128]{1,0:T(8,128)(2,1)S(1)}, u32[]{:S(2)}, u32[]{:S(2)}) collective-permute-start(bf16[128,128]{1,0:T(8,128)(2,1)} %bitcast.15), channel_id=1, source_target_pairs={{0,0},{1,1},{2,64},{3,65},{4,128},{5,129},{6,192},{7,193},{8,256},... | collective-permute-start | bytes 98312 | tf_op jit(solution)/shard_map/ppermute | solution.py:32
  7.7 52.7 %collective-permute-start.10 = (bf16[128,384]{1,0:T(8,128)(2,1)S(1)}, bf16[128,384]{1,0:T(8,128)(2,1)S(1)}, u32[]{:S(2)}, u32[]{:S(2)}) collective-permute-start(bf16[128,384]{1,0:T(8,128)(2,1)S(1)} %pad_maximum_fusion.9), channel_id=1, source_target_pairs={{0,192},{1,193},{2,194},{3,195},{4,196},{5,197},{6,198},{7,199},{8... | collective-permute-start | bytes 294920 | tf_op jit(solution)/shard_map/ppermute | solution.py:32
  23.4 37.0 %collective-permute-start.9 = (bf16[128,384]{1,0:T(8,128)(2,1)S(1)}, bf16[128,384]{1,0:T(8,128)(2,1)S(1)}, u32[]{:S(2)}, u32[]{:S(2)}) collective-permute-start(bf16[128,384]{1,0:T(8,128)(2,1)S(1)} %pad_maximum_fusion.9), channel_id=1, source_target_pairs={{0,64},{1,65},{2,66},{3,67},{4,68},{5,69},{6,70},{7,71},{8,72},{9,... | collective-permute-start | bytes 294920 | tf_op jit(solution)/shard_map/ppermute | solution.py:32
  25.4 7.8 %collective-permute-start.25 = (bf16[128,128]{1,0:T(8,128)(2,1)}, bf16[128,128]{1,0:T(8,128)(2,1)S(1)}, u32[]{:S(2)}, u32[]{:S(2)}) collective-permute-start(bf16[128,128]{1,0:T(8,128)(2,1)} %bitcast.16), channel_id=1, source_target_pairs={{0,256},{1,257},{2,320},{3,321},{4,384},{5,385},{6,448},{7,449},{8... | collective-permute-start | bytes 98312 | tf_op jit(solution)/shard_map/ppermute | solution.py:32
  33.2 42.1 %collective-permute-start.26 = (bf16[128,256]{1,0:T(8,128)(2,1)S(1)}, bf16[128,256]{1,0:T(8,128)(2,1)S(1)}, u32[]{:S(2)}, u32[]{:S(2)}) collective-permute-start(bf16[128,256]{1,0:T(8,128)(2,1)S(1)} %constant_dynamic-update-slice_fusion), channel_id=1, source_target_pairs={{0,128},{1,129},{2,130},{3,131},{4,132},{5,133},{6,134},{7,135},{8... | collective-permute-start | bytes 196616 | tf_op jit(solution)/shard_map/ppermute | solution.py:32
  60.5 10.3 %collective-permute-start.11 = (bf16[128,384]{1,0:T(8,128)(2,1)S(1)}, bf16[128,384]{1,0:T(8,128)(2,1)S(1)}, u32[]{:S(2)}, u32[]{:S(2)}) collective-permute-start(bf16[128,384]{1,0:T(8,128)(2,1)S(1)} %broadcast_select_fusion.2), channel_id=1, source_target_pairs={{0,192},{1,65},{2,194},{3,67},{4,196},{5,69},{6,198},{7,71},{8,200... | collective-permute-start | bytes 294920 | tf_op jit(solution)/shard_map/ppermute | solution.py:32
  63.5 34.8 %collective-permute-start.3 = (bf16[1024,256]{1,0:T(8,128)(2,1)S(1)}, bf16[1024,256]{1,0:T(8,128)(2,1)S(1)}, u32[]{:S(2)}, u32[]{:S(2)}) collective-permute-start(bf16[1024,256]{1,0:T(8,128)(2,1)S(1)} %pad_maximum_fusion.refs_0_), channel_id=1, source_target_pairs={{0,6},{1,7},{2,0},{3,1},{4,2},{5,3},{6,4},{7,5},{8,14},{9,15},{10,... | collective-permute-start | bytes 1572872 | tf_op jit(solution)/shard_map/ppermute | solution.py:32
  65.4 34.8 %collective-permute-start.5 = (bf16[1024,256]{1,0:T(8,128)(2,1)S(1)}, bf16[1024,256]{1,0:T(8,128)(2,1)S(1)}, u32[]{:S(2)}, u32[]{:S(2)}) collective-permute-start(bf16[1024,256]{1,0:T(8,128)(2,1)S(1)} %pad_maximum_fusion.refs_0_), channel_id=1, source_target_pairs={{0,4},{1,5},{2,6},{3,7},{4,0},{5,1},{6,2},{7,3},{8,12},{9,13},{10,... | collective-permute-start | bytes 1572872 | tf_op jit(solution)/shard_map/ppermute | solution.py:32
  67.3 35.3 %collective-permute-start.7 = (bf16[1024,256]{1,0:T(8,128)(2,1)S(1)}, bf16[1024,256]{1,0:T(8,128)(2,1)S(1)}, u32[]{:S(2)}, u32[]{:S(2)}) collective-permute-start(bf16[1024,256]{1,0:T(8,128)(2,1)S(1)} %pad_maximum_fusion.refs_0_), channel_id=1, source_target_pairs={{0,2},{1,3},{2,4},{3,5},{4,6},{5,7},{6,0},{7,1},{8,10},{9,11},{10,... | collective-permute-start | bytes 1572872 | tf_op jit(solution)/shard_map/ppermute | solution.py:32
  70.8 11.5 %collective-permute-start.12 = (bf16[256,384]{1,0:T(8,128)(2,1)S(1)}, bf16[256,384]{1,0:T(8,128)(2,1)S(1)}, u32[]{:S(2)}, u32[]{:S(2)}) collective-permute-start(bf16[256,384]{1,0:T(8,128)(2,1)S(1)} %get-tuple-element.26), channel_id=1, source_target_pairs={{0,224},{1,225},{2,226},{3,227},{4,228},{5,229},{6,230},{7,231},{8... | collective-permute-start | bytes 589832 | tf_op jit(solution)/shard_map/ppermute | solution.py:32
  75.3 29.2 %collective-permute-start.14 = (bf16[512,384]{1,0:T(8,128)(2,1)S(1)}, bf16[512,384]{1,0:T(8,128)(2,1)S(1)}, u32[]{:S(2)}, u32[]{:S(2)}) collective-permute-start(bf16[512,384]{1,0:T(8,128)(2,1)S(1)} %pad_maximum_fusion.2.refs_8_), channel_id=1, source_target_pairs={{0,240},{1,241},{2,242},{3,243},{4,244},{5,245},{6,246},{7,247},{8... | collective-permute-start | bytes 1179656 | tf_op jit(solution)/shard_map/ppermute | solution.py:32
  82.3 9.1 %collective-permute-start.13 = (bf16[256,384]{1,0:T(8,128)(2,1)S(1)}, bf16[256,384]{1,0:T(8,128)(2,1)S(1)}, u32[]{:S(2)}, u32[]{:S(2)}) collective-permute-start(bf16[256,384]{1,0:T(8,128)(2,1)S(1)} %get-tuple-element.25), channel_id=1, source_target_pairs={{0,32},{1,33},{2,34},{3,35},{4,36},{5,37},{6,38},{7,39},{8,40},{9,... | collective-permute-start | bytes 589832 | tf_op jit(solution)/shard_map/ppermute | solution.py:32
  91.4 32.3 %collective-permute-start.2 = (bf16[1024,256]{1,0:T(8,128)(2,1)S(1)}, bf16[1024,256]{1,0:T(8,128)(2,1)S(1)}, u32[]{:S(2)}, u32[]{:S(2)}) collective-permute-start(bf16[1024,256]{1,0:T(8,128)(2,1)S(1)} %pad_maximum_fusion.refs_0_), channel_id=1, source_target_pairs={{0,1},{1,0},{2,3},{3,2},{4,5},{5,4},{6,7},{7,6},{8,9},{9,8},{10,11... | collective-permute-start | bytes 1572872 | tf_op jit(solution)/shard_map/ppermute | solution.py:32
  98.2 25.5 %collective-permute-start.4 = (bf16[1024,256]{1,0:T(8,128)(2,1)S(1)}, bf16[1024,256]{1,0:T(8,128)(2,1)S(1)}, u32[]{:S(2)}, u32[]{:S(2)}) collective-permute-start(bf16[1024,256]{1,0:T(8,128)(2,1)S(1)} %collective-permute-done.3.refs_2_), channel_id=1, source_target_pairs={{0,1},{1,0},{2,3},{3,2},{4,5},{5,4},{6,7},{7,6},{8,9},{9,8},{10,11... | collective-permute-start | bytes 1572872 | tf_op jit(solution)/shard_map/ppermute | solution.py:32
  100.2 23.5 %collective-permute-start.6 = (bf16[1024,256]{1,0:T(8,128)(2,1)S(1)}, bf16[1024,256]{1,0:T(8,128)(2,1)S(1)}, u32[]{:S(2)}, u32[]{:S(2)}) collective-permute-start(bf16[1024,256]{1,0:T(8,128)(2,1)S(1)} %collective-permute-done.5.refs_4_), channel_id=1, source_target_pairs={{0,1},{1,0},{2,3},{3,2},{4,5},{5,4},{6,7},{7,6},{8,9},{9,8},{10,11... | collective-permute-start | bytes 1572872 | tf_op jit(solution)/shard_map/ppermute | solution.py:32
  102.6 21.1 %collective-permute-start.8 = (bf16[1024,256]{1,0:T(8,128)(2,1)S(1)}, bf16[1024,256]{1,0:T(8,128)(2,1)S(1)}, u32[]{:S(2)}, u32[]{:S(2)}) collective-permute-start(bf16[1024,256]{1,0:T(8,128)(2,1)S(1)} %collective-permute-done.7.refs_6_), channel_id=1, source_target_pairs={{0,1},{1,0},{2,3},{3,2},{4,5},{5,4},{6,7},{7,6},{8,9},{9,8},{10,11... | collective-permute-start | bytes 1572872 | tf_op jit(solution)/shard_map/ppermute | solution.py:32
  104.5 13.3 %collective-permute-start.15 = (bf16[512,384]{1,0:T(8,128)(2,1)S(1)}, bf16[512,384]{1,0:T(8,128)(2,1)S(1)}, u32[]{:S(2)}, u32[]{:S(2)}) collective-permute-start(bf16[512,384]{1,0:T(8,128)(2,1)S(1)} %pad_maximum_fusion.2.refs_8_), channel_id=1, source_target_pairs={{0,16},{1,17},{2,18},{3,19},{4,20},{5,21},{6,22},{7,23},{8,24},{9,... | collective-permute-start | bytes 1179656 | tf_op jit(solution)/shard_map/ppermute | solution.py:32
  117.8 13.8 %collective-permute-start.27 = (bf16[256,256]{1,0:T(8,128)(2,1)S(1)}, bf16[256,256]{1,0:T(8,128)(2,1)S(1)}, u32[]{:S(2)}, u32[]{:S(2)}) collective-permute-start(bf16[256,256]{1,0:T(8,128)(2,1)S(1)} %pad_maximum_fusion.8), channel_id=1, source_target_pairs={{0,64},{1,193},{2,66},{3,195},{4,68},{5,197},{6,70},{7,199},{8,72}... | collective-permute-start | bytes 393224 | tf_op jit(solution)/shard_map/ppermute | solution.py:32
  125.7 17.9 %collective-permute-start.18 = (bf16[512,256]{1,0:T(8,128)(2,1)S(1)}, bf16[512,256]{1,0:T(8,128)(2,1)S(1)}, u32[]{:S(2)}, u32[]{:S(2)}) collective-permute-start(bf16[512,256]{1,0:T(8,128)(2,1)S(1)} %get-tuple-element.18), channel_id=1, source_target_pairs={{0,256},{1,257},{2,258},{3,259},{4,260},{5,261},{6,262},{7,263},{8... | collective-permute-start | bytes 786440 | tf_op jit(solution)/shard_map/ppermute | solution.py:32
  131.6 18.5 %collective-permute-start.28 = (bf16[512,256]{1,0:T(8,128)(2,1)S(1)}, bf16[512,256]{1,0:T(8,128)(2,1)S(1)}, u32[]{:S(2)}, u32[]{:S(2)}) collective-permute-start(bf16[512,256]{1,0:T(8,128)(2,1)S(1)} %pad_maximum_fusion.4), channel_id=1, source_target_pairs={{0,32},{1,225},{2,34},{3,227},{4,36},{5,229},{6,38},{7,231},{8,40}... | collective-permute-start | bytes 786440 | tf_op jit(solution)/shard_map/ppermute | solution.py:32
  134.9 8.6 %collective-permute-start.17 = (f32[8,512]{1,0:T(8,128)S(1)}, f32[8,512]{1,0:T(8,128)S(1)}, u32[]{:S(2)}, u32[]{:S(2)}) collective-permute-start(f32[8,512]{1,0:T(8,128)S(1)} %get-tuple-element.17), channel_id=1, source_target_pairs={{0,256},{1,257},{2,258},{3,259},{4,260},{5,261},{6,262},{7,263},{8... | collective-permute-start | bytes 49160 | tf_op jit(solution)/shard_map/ppermute | solution.py:32
  144.1 14.7 %collective-permute-start.19 = (bf16[512,256]{1,0:T(8,128)(2,1)S(1)}, bf16[512,256]{1,0:T(8,128)(2,1)S(1)}, u32[]{:S(2)}, u32[]{:S(2)}) collective-permute-start(bf16[512,256]{1,0:T(8,128)(2,1)S(1)} %shard_map.50.kv_ref), channel_id=1, source_target_pairs={{0,16},{16,32},{32,48},{48,64},{64,80},{80,96},{96,112},{112,128},... | collective-permute-start | bytes 786440 | tf_op jit(solution)/shard_map/ppermute | solution.py:295
  145.4 12.6 %collective-permute-start.16 = (bf16[512,128]{1,0:T(8,128)(2,1)S(1)}, bf16[512,128]{1,0:T(8,128)(2,1)S(1)}, u32[]{:S(2)}, u32[]{:S(2)}) collective-permute-start(bf16[512,128]{1,0:T(8,128)(2,1)S(1)} %get-tuple-element.15), channel_id=1, source_target_pairs={{0,256},{1,257},{2,258},{3,259},{4,260},{5,261},{6,262},{7,263},{8... | collective-permute-start | bytes 393224 | tf_op jit(solution)/shard_map/ppermute | solution.py:32
  150.2 23.5 %collective-permute-start.29 = (bf16[1024,256]{1,0:T(8,128)(2,1)S(1)}, bf16[1024,256]{1,0:T(8,128)(2,1)S(1)}, u32[]{:S(2)}, u32[]{:S(2)}) collective-permute-start(bf16[1024,256]{1,0:T(8,128)(2,1)S(1)} %pad_maximum_fusion.1.refs_4_), channel_id=1, source_target_pairs={{0,16},{1,241},{2,18},{3,243},{4,20},{5,245},{6,22},{7,247},{8,24}... | collective-permute-start | bytes 1572872 | tf_op jit(solution)/shard_map/ppermute | solution.py:32
  160.6 29.3 %copy-start = (bf16[512,256]{1,0:T(8,128)(2,1)S(1)}, bf16[512,256]{1,0:T(8,128)(2,1)}, u32[]{:S(2)}) copy-start(bf16[512,256]{1,0:T(8,128)(2,1)} %refs_5_.1) | copy-start | bytes 786436
  160.7 5.8 %collective-permute-start.20 = (bf16[512,128]{1,0:T(8,128)(2,1)S(1)}, bf16[512,128]{1,0:T(8,128)(2,1)S(1)}, u32[]{:S(2)}, u32[]{:S(2)}) collective-permute-start(bf16[512,128]{1,0:T(8,128)(2,1)S(1)} %shard_map.52), channel_id=1, source_target_pairs={{0,8},{1,9},{2,10},{3,11},{4,12},{5,13},{6,14},{7,15},{8,0},{9,1},... | collective-permute-start | bytes 393224 | tf_op jit(solution)/shard_map/ppermute | solution.py:32
  166.5 7.2 %collective-permute-start.21 = (bf16[512,256]{1,0:T(8,128)(2,1)S(1)}, bf16[512,256]{1,0:T(8,128)(2,1)S(1)}, u32[]{:S(2)}, u32[]{:S(2)}) collective-permute-start(bf16[512,256]{1,0:T(8,128)(2,1)S(1)} %pad_maximum_fusion.3.refs_0_), channel_id=1, source_target_pairs={{0,6},{1,7},{2,0},{3,1},{4,2},{5,3},{6,4},{7,5},{8,14},{9,15},{10,... | collective-permute-start | bytes 786440 | tf_op jit(solution)/shard_map/ppermute | solution.py:32
  168.5 8.6 %collective-permute-start.22 = (bf16[512,256]{1,0:T(8,128)(2,1)S(1)}, bf16[512,256]{1,0:T(8,128)(2,1)S(1)}, u32[]{:S(2)}, u32[]{:S(2)}) collective-permute-start(bf16[512,256]{1,0:T(8,128)(2,1)S(1)} %pad_maximum_fusion.3.refs_0_), channel_id=1, source_target_pairs={{0,4},{1,5},{2,6},{3,7},{4,0},{5,1},{6,2},{7,3},{8,12},{9,13},{10,... | collective-permute-start | bytes 786440 | tf_op jit(solution)/shard_map/ppermute | solution.py:32
  170.4 10.5 %collective-permute-start.23 = (bf16[512,256]{1,0:T(8,128)(2,1)S(1)}, bf16[512,256]{1,0:T(8,128)(2,1)S(1)}, u32[]{:S(2)}, u32[]{:S(2)}) collective-permute-start(bf16[512,256]{1,0:T(8,128)(2,1)S(1)} %pad_maximum_fusion.3.refs_0_), channel_id=1, source_target_pairs={{0,2},{1,3},{2,4},{3,5},{4,6},{5,7},{6,0},{7,1},{8,10},{9,11},{10,... | collective-permute-start | bytes 786440 | tf_op jit(solution)/shard_map/ppermute | solution.py:32
  181.9 9.1 %collective-permute-start.30 = (bf16[512,256]{1,0:T(8,128)(2,1)S(1)}, bf16[512,256]{1,0:T(8,128)(2,1)S(1)}, u32[]{:S(2)}, u32[]{:S(2)}) collective-permute-start(bf16[512,256]{1,0:T(8,128)(2,1)S(1)} %get-tuple-element.22), channel_id=1, source_target_pairs={{0,1},{1,0},{2,3},{3,2},{4,5},{5,4},{6,7},{7,6},{8,9},{9,8},{10,11... | collective-permute-start | bytes 786440 | tf_op jit(solution)/shard_map/ppermute | solution.py:32

commit v4 on v2

--- a/solution.py
+++ b/solution.py
@@ -12,7 +12,7 @@
 AXES = ("ctx", "tp")
 BF = jnp.bfloat16
 F32 = jnp.float32
-STEPS = ((0, -4, 4, 8), (2, 6), (-2, -6), (1, -3, 5, 9), (-1, -5, 3, 7))
+HELD = (0, -4, 4, 8)
 
 
 def pairs_of(target):
@@ -68,22 +68,26 @@
     relay = permute(
         jnp.where(core == 0, down4, up4), lambda a, z, b, y, k: (a, z + (4 if k else 12), b, y, k)
     )
-    down2 = move(jnp.concatenate([chunk, down4], axis=0), -2)
-    up2 = move(jnp.concatenate([chunk, up4], axis=0), 2)
     held = jnp.concatenate([chunk, up4, down4, relay], axis=0)
-    down1 = move(held, -1)
-    up1 = move(held, 1)
-    return held, down2, up2, down1, up1
+    two = permute(held, lambda a, z, b, y, k: (a, z + (2 if k else 14), b, y, k))
+    return held, two, move(held, -1), move(held, 1)
+
+
+def columns_of(blocks, i, first, size):
+    if i % 2 == 0:
+        return blocks[i // 2][first : first + size, :]
+    first += i // 2 * blocks[0].shape[0]
+    return blocks[4][first : first + size, :]
 
 
 def squares_body(*refs):
-    blocks, (own_ref, other_ref) = refs[:8], refs[8:]
+    blocks, (own_ref, other_ref) = refs[:5], refs[5:]
     seg = own_ref.shape[1]
     ones = jnp.ones((own_ref.shape[0], blocks[0].shape[1]), BF)
     for first, ref in ((0, own_ref), (seg, other_ref)):
         total = jnp.zeros(ref.shape, F32)
-        for block in blocks:
-            wider = block[first : first + seg, :].astype(F32)
+        for i in range(8):
+            wider = columns_of(blocks, i, first, seg).astype(F32)
             total += lax.dot_general(
                 ones,
                 (wider * wider).astype(BF),
@@ -103,44 +107,45 @@
             yy = (y + i // 2) & 3
             kk = k if i % 2 == 0 else 1 - k
             at = pl.multiple_of((yy * 2 + kk) * 2 * rows, 2 * rows)
-            block = blocks[i][first + r : first + r + tile, :]
+            block = columns_of(blocks, i, first + r, tile)
             acc += jnp.dot(block, weights[pl.ds(at, 2 * rows), :], preferred_element_type=F32)
         yield slice(r, r + tile), acc
 
 
 def project_other_body(pos, *refs):
-    blocks, parts, (send_ref, w_ref, out_w_ref) = refs[:8], refs[8:13], refs[13:]
-    _, z, _, _, _ = place(pos)
+    blocks, parts, (kv_ref, q_ref, w_ref, out_w_ref) = refs[:5], refs[5:9], refs[9:]
+    _, z, _, _, k = place(pos)
     rows = w_ref.shape[0] // 16
-    seg, wide = send_ref.shape
-    for part, steps in zip(parts, STEPS):
-        for i, step in enumerate(steps):
-            at = pl.multiple_of(((z + step + 16) & 15) * rows, rows)
+    seg, hd = q_ref.shape
+    wide = w_ref.shape[1]
+    for part, base in zip(parts, (0, 2 - 4 * k, 1, -1)):
+        for i, step in enumerate(HELD):
+            at = pl.multiple_of(((z + base + step + 16) & 15) * rows, rows)
             w_ref[pl.ds(at, rows), :] = part[i * rows : (i + 1) * rows, :wide]
             out_w_ref[pl.ds(at, rows), :] = part[i * rows : (i + 1) * rows, wide:]
     for at, acc in project_rows(pos, blocks, w_ref, seg, seg):
-        send_ref[at, :] = acc.astype(BF)
+        q_ref[at, :] = acc[:, :hd].astype(BF)
+        kv_ref[at, :] = acc[:, hd:].astype(BF)
 
 
 def project_own_body(pos, *refs):
-    blocks, (w_ref, own_ref) = refs[:8], refs[8:]
+    blocks, (w_ref, own_ref) = refs[:5], refs[5:]
     for at, acc in project_rows(pos, blocks, w_ref, 0, own_ref.shape[0]):
         own_ref[at, :] = acc
 
 
-def combine_body(own_ref, got_ref, ssq_ref, ssq_got_ref, q_ref, kv_ref, *, features):
-    hd = q_ref.shape[1]
+def combine_body(own_ref, got_ref, ssq_ref, ssq_got_ref, out_ref, *, features, first):
+    wide = out_ref.shape[1]
     scale = lax.rsqrt((ssq_ref[...] + ssq_got_ref[...]) * (1.0 / features) + 1e-06)
     column = lax.dot_general(
         scale,
-        jnp.full((scale.shape[0], 3 * hd), 1.0 / scale.shape[0], F32),
+        jnp.full((scale.shape[0], wide), 1.0 / scale.shape[0], F32),
         (((0,), (0,)), ((), ())),
         precision=lax.Precision.HIGHEST,
         preferred_element_type=F32,
     )
-    total = (own_ref[...] + got_ref[...].astype(F32)) * column
-    q_ref[...] = total[:, :hd].astype(BF)
-    kv_ref[...] = total[:, hd:].astype(BF)
+    own = own_ref[:, first : first + wide]
+    out_ref[...] = ((own + got_ref[...].astype(F32)) * column).astype(BF)
 
 
 def scores_of(q, keys):
@@ -238,9 +243,8 @@
     cross = permute(hidden, lambda a, z, b, y, k: (b, z, a, y, k) if a != b else None)
     own = jnp.where(same, hidden, turn)
     other = jnp.where(same, turn, cross)
-    blocks = []
-    for block in around(jnp.concatenate([own, other], axis=0)):
-        blocks += [block, permute(block, swap_core)]
+    blocks = around(jnp.concatenate([own, other], axis=0))
+    blocks.append(permute(jnp.concatenate(blocks, axis=0), swap_core))
 
     ssq, ssq_send = call(
         squares_body,
@@ -250,29 +254,36 @@
         scalars=False,
     )(*blocks)
     ssq_got = permute(ssq_send, swap_hi)
-    send, weights, out_w = call(
+    kv_send, q_send, weights, out_w = call(
         project_other_body,
         (
-            shape((seg, 3 * hd), BF),
+            shape((seg, 2 * hd), BF),
+            shape((seg, hd), BF),
             shape((16 * hd, 3 * hd), BF),
             shape((16 * hd, hd), BF),
         ),
         flops=2 * seg * 8 * feats * 3 * hd,
         nbytes=8 << 20,
     )(pos, *blocks, *parts)
-    got = permute(send, swap_hi)
+    kv_got = permute(kv_send, swap_hi)
+    q_got = permute(q_send, swap_hi)
     own_part = call(
         project_own_body,
         shape((seg, 3 * hd), F32),
         flops=2 * seg * 8 * feats * 3 * hd,
         nbytes=8 << 20,
     )(pos, *blocks, weights)
-    q, kv = call(
-        lambda *refs: combine_body(*refs, features=16 * feats),
-        (shape((seg, hd), BF), shape((seg, 2 * hd), BF)),
-        nbytes=2 << 20,
-        scalars=False,
-    )(own_part, got, ssq, ssq_got)
+
+    def combine(got, first):
+        return call(
+            lambda *refs: combine_body(*refs, features=16 * feats, first=first),
+            shape(got.shape, BF),
+            nbytes=1 << 20,
+            scalars=False,
+        )(own_part, got, ssq, ssq_got)
+
+    kv = combine(kv_got, hd)
+    q = combine(q_got, 0)
     prev = lax.ppermute(kv, "ctx", [(i, i + 1) for i in range(31)])
     e_own, sum_own = call(
         own_body,

time: 170 us -> 202 us (1.19)
  the two profiles are of different devices: /device:TPU:3 before, /device:TPU:7 now
where the time goes in v4:
time: 202 us; the launch traced here: 201 us
  starting transfers between devices  102 us (50%)
  waiting for transfers between devices  78.9 us (39%)
  Pallas kernels  11 us (5%)
  local copies, waits for them, and re-layouts  4.81 us (2%)
  other arithmetic  3.43 us (2%)
    ppermute x22, starting transfers between devices, permute(): return lax.ppermute(value, AXES, pairs_of(target))  96.3 us
    ppermute x22, waiting for transfers between devices, permute(): return lax.ppermute(value, AXES, pairs_of(target))  78.9 us
    pallas_call x10, Pallas kernels, run(): pl.pallas_call(body, out_shape=outs, in_specs=specs, out_specs=jax.tree.m...  11 us
    ppermute x1, starting transfers between devices, layer(): prev = lax.ppermute(kv, 'ctx', [(i, i + 1) for i in range(31)])  6.17 us
  transfers between devices with their start and end apart: 23, of which 15 were waited for; matrix products, arithmetic and copies ran while one was open for 2% of the time, Pallas kernels for 3%

profile of v4, /device:TPU:7, one launch (start us, length us, event | category | flops | bytes accessed | tf_op | source)
XLA Modules:
  0.0 201.0 jit_solution(10332853127117887275)
XLA Ops:
  0.0 2.4 %collective-permute-start = (bf16[512,256]{1,0:T(8,128)(2,1)}, bf16[512,256]{1,0:T(8,128)(2,1)S(1)}, u32[]{:S(2)}, u32[]{:S(2)}) collective-permute-start(bf16[512,256]{1,0:T(8,128)(2,1)} %refs_6_.1), channel_id=1, source_target_pairs={{0,8},{1,9},{2,10},{3,11},{4,12},{5,13},{6,14},{7,15},{8,264},{9,2... | collective-permute-start | bytes 786440 | tf_op jit(solution)/shard_map/ppermute | solution.py:31
  3.2 7.6 %collective-permute-done = bf16[512,256]{1,0:T(8,128)(2,1)S(1)} collective-permute-done((bf16[512,256]{1,0:T(8,128)(2,1)}, bf16[512,256]{1,0:T(8,128)(2,1)S(1)}, u32[]{:S(2)}, u32[]{:S(2)}) %collective-permute-start) | collective-permute-done | bytes 262176 | tf_op jit(solution)/shard_map/ppermute | solution.py:31
  13.3 4.8 %collective-permute-start.2 = (bf16[1024,256]{1,0:T(8,128)(2,1)S(1)}, bf16[1024,256]{1,0:T(8,128)(2,1)S(1)}, u32[]{:S(2)}, u32[]{:S(2)}) collective-permute-start(bf16[1024,256]{1,0:T(8,128)(2,1)S(1)} %pad_maximum_fusion.refs_0_), channel_id=1, source_target_pairs={{0,6},{1,7},{2,0},{3,1},{4,2},{5,3},{6,4},{7,5},{8,14},{9,15},{10,... | collective-permute-start | bytes 1572872 | tf_op jit(solution)/shard_map/ppermute | solution.py:31
  18.1 2.3 %collective-permute-start.3 = (bf16[1024,256]{1,0:T(8,128)(2,1)S(1)}, bf16[1024,256]{1,0:T(8,128)(2,1)S(1)}, u32[]{:S(2)}, u32[]{:S(2)}) collective-permute-start(bf16[1024,256]{1,0:T(8,128)(2,1)S(1)} %pad_maximum_fusion.refs_0_), channel_id=1, source_target_pairs={{0,4},{1,5},{2,6},{3,7},{4,0},{5,1},{6,2},{7,3},{8,12},{9,13},{10,... | collective-permute-start | bytes 1572872 | tf_op jit(solution)/shard_map/ppermute | solution.py:31
  20.4 2.6 %collective-permute-start.4 = (bf16[1024,256]{1,0:T(8,128)(2,1)S(1)}, bf16[1024,256]{1,0:T(8,128)(2,1)S(1)}, u32[]{:S(2)}, u32[]{:S(2)}) collective-permute-start(bf16[1024,256]{1,0:T(8,128)(2,1)S(1)} %pad_maximum_fusion.refs_0_), channel_id=1, source_target_pairs={{0,2},{1,3},{2,4},{3,5},{4,6},{5,7},{6,0},{7,1},{8,10},{9,11},{10,... | collective-permute-start | bytes 1572872 | tf_op jit(solution)/shard_map/ppermute | solution.py:31
  23.0 5.9 %collective-permute-done.2.refs_1_ = bf16[1024,256]{1,0:T(8,128)(2,1)S(1)} collective-permute-done((bf16[1024,256]{1,0:T(8,128)(2,1)S(1)}, bf16[1024,256]{1,0:T(8,128)(2,1)S(1)}, u32[]{:S(2)}, u32[]{:S(2)}) %collective-permute-start.2) | collective-permute-done | bytes 524320 | tf_op jit(solution)/shard_map/ppermute | solution.py:31
  29.7 3.5 %collective-permute-done.3.refs_2_ = bf16[1024,256]{1,0:T(8,128)(2,1)S(1)} collective-permute-done((bf16[1024,256]{1,0:T(8,128)(2,1)S(1)}, bf16[1024,256]{1,0:T(8,128)(2,1)S(1)}, u32[]{:S(2)}, u32[]{:S(2)}) %collective-permute-start.3) | collective-permute-done | bytes 524320 | tf_op jit(solution)/shard_map/ppermute | solution.py:31
  34.1 12.5 %collective-permute-done.4.refs_3_ = bf16[1024,256]{1,0:T(8,128)(2,1)S(1)} collective-permute-done((bf16[1024,256]{1,0:T(8,128)(2,1)S(1)}, bf16[1024,256]{1,0:T(8,128)(2,1)S(1)}, u32[]{:S(2)}, u32[]{:S(2)}) %collective-permute-start.4) | collective-permute-done | bytes 524320 | tf_op jit(solution)/shard_map/ppermute | solution.py:31
  47.6 2.4 %collective-permute-start.5 = (bf16[4096,256]{1,0:T(8,128)(2,1)}, bf16[4096,256]{1,0:T(8,128)(2,1)S(1)}, u32[]{:S(2)}, u32[]{:S(2)}) collective-permute-start(bf16[4096,256]{1,0:T(8,128)(2,1)} %constant_dynamic-update-slice_fusion), channel_id=1, source_target_pairs={{0,1},{1,0},{2,3},{3,2},{4,5},{5,4},{6,7},{7,6},{8,9},{9,8},{10,11... | collective-permute-start | bytes 6291464 | tf_op jit(solution)/shard_map/ppermute | solution.py:31
  51.5 22.3 %collective-permute-start.8 = (bf16[128,512]{1,0:T(8,128)(2,1)}, bf16[128,512]{1,0:T(8,128)(2,1)S(1)}, u32[]{:S(2)}, u32[]{:S(2)}) collective-permute-start(bf16[128,512]{1,0:T(8,128)(2,1)} %pad_maximum_fusion.3), channel_id=1, source_target_pairs={{0,192},{1,193},{2,194},{3,195},{4,196},{5,197},{6,198},{7,199},{8... | collective-permute-start | bytes 393224 | tf_op jit(solution)/shard_map/ppermute | solution.py:31
  75.7 7.5 %collective-permute-done.8 = bf16[128,512]{1,0:T(8,128)(2,1)S(1)} collective-permute-done((bf16[128,512]{1,0:T(8,128)(2,1)}, bf16[128,512]{1,0:T(8,128)(2,1)S(1)}, u32[]{:S(2)}, u32[]{:S(2)}) %collective-permute-start.8) | collective-permute-done | bytes 131104 | tf_op jit(solution)/shard_map/ppermute | solution.py:31
  83.2 3.7 %collective-permute-done.7 = bf16[128,512]{1,0:T(8,128)(2,1)S(1)} collective-permute-done((bf16[128,512]{1,0:T(8,128)(2,1)}, bf16[128,512]{1,0:T(8,128)(2,1)S(1)}, u32[]{:S(2)}, u32[]{:S(2)}) %collective-permute-start.7) | collective-permute-done | bytes 131104 | tf_op jit(solution)/shard_map/ppermute | solution.py:31
  86.8 2.2 %collective-permute-start.9 = (bf16[128,512]{1,0:T(8,128)(2,1)S(1)}, bf16[128,512]{1,0:T(8,128)(2,1)S(1)}, u32[]{:S(2)}, u32[]{:S(2)}) collective-permute-start(bf16[128,512]{1,0:T(8,128)(2,1)S(1)} %broadcast_select_fusion.2), channel_id=1, source_target_pairs={{0,192},{1,65},{2,194},{3,67},{4,196},{5,69},{6,198},{7,71},{8,200... | collective-permute-start | bytes 393224 | tf_op jit(solution)/shard_map/ppermute | solution.py:31
  89.0 12.1 %collective-permute-done.9 = bf16[128,512]{1,0:T(8,128)(2,1)S(1)} collective-permute-done((bf16[128,512]{1,0:T(8,128)(2,1)S(1)}, bf16[128,512]{1,0:T(8,128)(2,1)S(1)}, u32[]{:S(2)}, u32[]{:S(2)}) %collective-permute-start.9) | collective-permute-done | bytes 131104 | tf_op jit(solution)/shard_map/ppermute | solution.py:31
  101.1 6.3 %collective-permute-start.10 = (bf16[512,512]{1,0:T(8,128)(2,1)S(1)}, bf16[512,512]{1,0:T(8,128)(2,1)S(1)}, u32[]{:S(2)}, u32[]{:S(2)}) collective-permute-start(bf16[512,512]{1,0:T(8,128)(2,1)S(1)} %pad_maximum_fusion.1.refs_5_), channel_id=1, source_target_pairs={{0,224},{1,33},{2,226},{3,35},{4,228},{5,37},{6,230},{7,39},{8,232... | collective-permute-start | bytes 1572872 | tf_op jit(solution)/shard_map/ppermute | solution.py:31
  107.5 7.0 %collective-permute-start.11 = (bf16[512,512]{1,0:T(8,128)(2,1)S(1)}, bf16[512,512]{1,0:T(8,128)(2,1)S(1)}, u32[]{:S(2)}, u32[]{:S(2)}) collective-permute-start(bf16[512,512]{1,0:T(8,128)(2,1)S(1)} %pad_maximum_fusion.1.refs_5_), channel_id=1, source_target_pairs={{0,240},{1,241},{2,242},{3,243},{4,244},{5,245},{6,246},{7,247},{8... | collective-permute-start | bytes 1572872 | tf_op jit(solution)/shard_map/ppermute | solution.py:31
  114.5 1.9 collective-permute-start.12
  116.5 2.7 %collective-permute-done.10.refs_6_ = bf16[512,512]{1,0:T(8,128)(2,1)S(1)} collective-permute-done((bf16[512,512]{1,0:T(8,128)(2,1)S(1)}, bf16[512,512]{1,0:T(8,128)(2,1)S(1)}, u32[]{:S(2)}, u32[]{:S(2)}) %collective-permute-start.10) | collective-permute-done | bytes 524320 | tf_op jit(solution)/shard_map/ppermute | solution.py:31
  119.2 10.8 %collective-permute-done.11.refs_7_ = bf16[512,512]{1,0:T(8,128)(2,1)S(1)} collective-permute-done((bf16[512,512]{1,0:T(8,128)(2,1)S(1)}, bf16[512,512]{1,0:T(8,128)(2,1)S(1)}, u32[]{:S(2)}, u32[]{:S(2)}) %collective-permute-start.11) | collective-permute-done | bytes 524320 | tf_op jit(solution)/shard_map/ppermute | solution.py:31
  132.1 2.0 %shard_map.46 = (bf16[512,256]{1,0:T(8,128)(2,1)S(1)}, bf16[512,128]{1,0:T(8,128)(2,1)S(1)}, bf16[2048,384]{1,0:T(8,128)(2,1)S(1)}, bf16[2048,128]{1,0:T(8,128)(2,1)S(1)}) custom-call(s32[2]{0:T(128)S(1)} %pad_add_fusion.pos, bf16[1024,256]{1,0:T(8,128)(2,1)S(1)} %pad_maximum_fusion.refs_0_, bf16[1024,256]{1,0:T(8,128)(2,1)S(1)} %collective-permute-done.2.refs_1_, ...), custom_call_target="tpu_custom_call" | custom-call | flops 805306368 | bytes 8388608 | tf_op jit(solution)/shard_map/pallas_call | solution.py:39
  134.1 3.8 %collective-permute-start.15 = (bf16[512,256]{1,0:T(8,128)(2,1)S(1)}, bf16[512,256]{1,0:T(8,128)(2,1)S(1)}, u32[]{:S(2)}, u32[]{:S(2)}) collective-permute-start(bf16[512,256]{1,0:T(8,128)(2,1)S(1)} %get-tuple-element.17), channel_id=1, source_target_pairs={{0,256},{1,257},{2,258},{3,259},{4,260},{5,261},{6,262},{7,263},{8... | collective-permute-start | bytes 786440 | tf_op jit(solution)/shard_map/ppermute | solution.py:31
  139.1 3.0 %collective-permute-start.14 = (f32[8,512]{1,0:T(8,128)S(1)}, f32[8,512]{1,0:T(8,128)S(1)}, u32[]{:S(2)}, u32[]{:S(2)}) collective-permute-start(f32[8,512]{1,0:T(8,128)S(1)} %get-tuple-element.16), channel_id=1, source_target_pairs={{0,256},{1,257},{2,258},{3,259},{4,260},{5,261},{6,262},{7,263},{8... | collective-permute-start | bytes 49160 | tf_op jit(solution)/shard_map/ppermute | solution.py:31
  145.6 6.2 %collective-permute-start.16 = (bf16[512,256]{1,0:T(8,128)(2,1)S(1)}, bf16[512,256]{1,0:T(8,128)(2,1)S(1)}, u32[]{:S(2)}, u32[]{:S(2)}) collective-permute-start(bf16[512,256]{1,0:T(8,128)(2,1)S(1)} %shard_map.50.kv_ref), channel_id=1, source_target_pairs={{0,16},{16,32},{32,48},{48,64},{64,80},{80,96},{96,112},{112,128},... | collective-permute-start | bytes 786440 | tf_op jit(solution)/shard_map/ppermute | solution.py:287
  151.8 2.2 %collective-permute-start.13 = (bf16[512,128]{1,0:T(8,128)(2,1)S(1)}, bf16[512,128]{1,0:T(8,128)(2,1)S(1)}, u32[]{:S(2)}, u32[]{:S(2)}) collective-permute-start(bf16[512,128]{1,0:T(8,128)(2,1)S(1)} %get-tuple-element.14), channel_id=1, source_target_pairs={{0,256},{1,257},{2,258},{3,259},{4,260},{5,261},{6,262},{7,263},{8... | collective-permute-start | bytes 393224 | tf_op jit(solution)/shard_map/ppermute | solution.py:31
  154.0 4.6 %collective-permute-start.21 = (bf16[2048,128]{1,0:T(8,128)(2,1)S(1)}, bf16[2048,128]{1,0:T(8,128)(2,1)S(1)}, u32[]{:S(2)}, u32[]{:S(2)}) collective-permute-start(bf16[2048,128]{1,0:T(8,128)(2,1)S(1)} %get-tuple-element.20.refs_4_), channel_id=1, source_target_pairs={{0,256},{1,257},{2,258},{3,259},{4,260},{5,261},{6,262},{7,263},{8... | collective-permute-start | bytes 1572872 | tf_op jit(solution)/shard_map/ppermute | solution.py:31
  163.6 5.5 %collective-permute-done.17 = bf16[512,128]{1,0:T(8,128)(2,1)S(1)} collective-permute-done((bf16[512,128]{1,0:T(8,128)(2,1)S(1)}, bf16[512,128]{1,0:T(8,128)(2,1)S(1)}, u32[]{:S(2)}, u32[]{:S(2)}) %collective-permute-start.17) | collective-permute-done | bytes 131104 | tf_op jit(solution)/shard_map/ppermute | solution.py:31
  169.1 2.6 %collective-permute-start.18 = (bf16[512,256]{1,0:T(8,128)(2,1)S(1)}, bf16[512,256]{1,0:T(8,128)(2,1)S(1)}, u32[]{:S(2)}, u32[]{:S(2)}) collective-permute-start(bf16[512,256]{1,0:T(8,128)(2,1)S(1)} %pad_maximum_fusion.2.refs_0_), channel_id=1, source_target_pairs={{0,6},{1,7},{2,0},{3,1},{4,2},{5,3},{6,4},{7,5},{8,14},{9,15},{10,... | collective-permute-start | bytes 786440 | tf_op jit(solution)/shard_map/ppermute | solution.py:31
  171.7 3.5 %collective-permute-start.19 = (bf16[512,256]{1,0:T(8,128)(2,1)S(1)}, bf16[512,256]{1,0:T(8,128)(2,1)S(1)}, u32[]{:S(2)}, u32[]{:S(2)}) collective-permute-start(bf16[512,256]{1,0:T(8,128)(2,1)S(1)} %pad_maximum_fusion.2.refs_0_), channel_id=1, source_target_pairs={{0,4},{1,5},{2,6},{3,7},{4,0},{5,1},{6,2},{7,3},{8,12},{9,13},{10,... | collective-permute-start | bytes 786440 | tf_op jit(solution)/shard_map/ppermute | solution.py:31
  175.2 2.8 %collective-permute-start.20 = (bf16[512,256]{1,0:T(8,128)(2,1)S(1)}, bf16[512,256]{1,0:T(8,128)(2,1)S(1)}, u32[]{:S(2)}, u32[]{:S(2)}) collective-permute-start(bf16[512,256]{1,0:T(8,128)(2,1)S(1)} %pad_maximum_fusion.2.refs_0_), channel_id=1, source_target_pairs={{0,2},{1,3},{2,4},{3,5},{4,6},{5,7},{6,0},{7,1},{8,10},{9,11},{10,... | collective-permute-start | bytes 786440 | tf_op jit(solution)/shard_map/ppermute | solution.py:31
  178.0 2.3 %collective-permute-done.19.refs_2_ = bf16[512,256]{1,0:T(8,128)(2,1)S(1)} collective-permute-done((bf16[512,256]{1,0:T(8,128)(2,1)S(1)}, bf16[512,256]{1,0:T(8,128)(2,1)S(1)}, u32[]{:S(2)}, u32[]{:S(2)}) %collective-permute-start.19) | collective-permute-done | bytes 262176 | tf_op jit(solution)/shard_map/ppermute | solution.py:31
  180.4 3.2 %collective-permute-done.20.refs_3_ = bf16[512,256]{1,0:T(8,128)(2,1)S(1)} collective-permute-done((bf16[512,256]{1,0:T(8,128)(2,1)S(1)}, bf16[512,256]{1,0:T(8,128)(2,1)S(1)}, u32[]{:S(2)}, u32[]{:S(2)}) %collective-permute-start.20) | collective-permute-done | bytes 262176 | tf_op jit(solution)/shard_map/ppermute | solution.py:31
  184.6 14.5 %collective-permute-start.22 = (bf16[512,256]{1,0:T(8,128)(2,1)S(1)}, bf16[512,256]{1,0:T(8,128)(2,1)S(1)}, u32[]{:S(2)}, u32[]{:S(2)}) collective-permute-start(bf16[512,256]{1,0:T(8,128)(2,1)S(1)} %shard_map.54), channel_id=1, source_target_pairs={{0,1},{1,0},{2,3},{3,2},{4,5},{5,4},{6,7},{7,6},{8,9},{9,8},{10,11... | collective-permute-start | bytes 786440 | tf_op jit(solution)/shard_map/ppermute | solution.py:31
  (54 shorter events, 24.1 us)
Async XLA Ops:
  0.0 10.8 %collective-permute-start = (bf16[512,256]{1,0:T(8,128)(2,1)}, bf16[512,256]{1,0:T(8,128)(2,1)S(1)}, u32[]{:S(2)}, u32[]{:S(2)}) collective-permute-start(bf16[512,256]{1,0:T(8,128)(2,1)} %refs_6_.1), channel_id=1, source_target_pairs={{0,8},{1,9},{2,10},{3,11},{4,12},{5,13},{6,14},{7,15},{8,264},{9,2... | collective-permute-start | bytes 786440 | tf_op jit(solution)/shard_map/ppermute | solution.py:31
  2.5 10.0 %collective-permute-start.1 = (bf16[512,256]{1,0:T(8,128)(2,1)}, bf16[512,256]{1,0:T(8,128)(2,1)S(1)}, u32[]{:S(2)}, u32[]{:S(2)}) collective-permute-start(bf16[512,256]{1,0:T(8,128)(2,1)} %refs_6_.1), channel_id=1, source_target_pairs={{8,256},{9,257},{10,258},{11,259},{12,260},{13,261},{14,262},{15,2... | collective-permute-start | bytes 786440 | tf_op jit(solution)/shard_map/ppermute | solution.py:31
  13.3 36.7 %copy-start.6 = (bf16[1,128,128]{2,1,0:T(8,128)(2,1)S(1)}, bf16[1,128,128]{2,1,0:T(8,128)(2,1)}, u32[]{:S(2)}) copy-start(bf16[1,128,128]{2,1,0:T(8,128)(2,1)} %param.7) | copy-start | bytes 98308
  13.3 37.4 %copy-start.7 = (bf16[1,128]{1,0:T(2,128)(2,1)S(1)}, bf16[1,128]{1,0:T(2,128)(2,1)}, u32[]{:S(2)}) copy-start(bf16[1,128]{1,0:T(2,128)(2,1)} %param.5) | copy-start | bytes 772
  13.3 37.4 %copy-start.5 = (bf16[1,3,128,128]{3,2,1,0:T(8,128)(2,1)S(1)}, bf16[1,3,128,128]{3,2,1,0:T(8,128)(2,1)}, u32[]{:S(2)}) copy-start(bf16[1,3,128,128]{3,2,1,0:T(8,128)(2,1)} %param.6) | copy-start | bytes 294916
  13.3 15.6 %collective-permute-start.2 = (bf16[1024,256]{1,0:T(8,128)(2,1)S(1)}, bf16[1024,256]{1,0:T(8,128)(2,1)S(1)}, u32[]{:S(2)}, u32[]{:S(2)}) collective-permute-start(bf16[1024,256]{1,0:T(8,128)(2,1)S(1)} %pad_maximum_fusion.refs_0_), channel_id=1, source_target_pairs={{0,6},{1,7},{2,0},{3,1},{4,2},{5,3},{6,4},{7,5},{8,14},{9,15},{10,... | collective-permute-start | bytes 1572872 | tf_op jit(solution)/shard_map/ppermute | solution.py:31
  18.1 15.1 %collective-permute-start.3 = (bf16[1024,256]{1,0:T(8,128)(2,1)S(1)}, bf16[1024,256]{1,0:T(8,128)(2,1)S(1)}, u32[]{:S(2)}, u32[]{:S(2)}) collective-permute-start(bf16[1024,256]{1,0:T(8,128)(2,1)S(1)} %pad_maximum_fusion.refs_0_), channel_id=1, source_target_pairs={{0,4},{1,5},{2,6},{3,7},{4,0},{5,1},{6,2},{7,3},{8,12},{9,13},{10,... | collective-permute-start | bytes 1572872 | tf_op jit(solution)/shard_map/ppermute | solution.py:31
  20.4 26.2 %collective-permute-start.4 = (bf16[1024,256]{1,0:T(8,128)(2,1)S(1)}, bf16[1024,256]{1,0:T(8,128)(2,1)S(1)}, u32[]{:S(2)}, u32[]{:S(2)}) collective-permute-start(bf16[1024,256]{1,0:T(8,128)(2,1)S(1)} %pad_maximum_fusion.refs_0_), channel_id=1, source_target_pairs={{0,2},{1,3},{2,4},{3,5},{4,6},{5,7},{6,0},{7,1},{8,10},{9,11},{10,... | collective-permute-start | bytes 1572872 | tf_op jit(solution)/shard_map/ppermute | solution.py:31
  33.2 13.4 %copy-start = (bf16[1024,256]{1,0:T(8,128)(2,1)}, bf16[1024,256]{1,0:T(8,128)(2,1)S(1)}, u32[]{:S(2)}) copy-start(bf16[1024,256]{1,0:T(8,128)(2,1)S(1)} %collective-permute-done.3.refs_2_) | copy-start | bytes 1572868
  46.6 1.0 copy-start.2
  47.6 82.4 %collective-permute-start.5 = (bf16[4096,256]{1,0:T(8,128)(2,1)}, bf16[4096,256]{1,0:T(8,128)(2,1)S(1)}, u32[]{:S(2)}, u32[]{:S(2)}) collective-permute-start(bf16[4096,256]{1,0:T(8,128)(2,1)} %constant_dynamic-update-slice_fusion), channel_id=1, source_target_pairs={{0,1},{1,0},{2,3},{3,2},{4,5},{5,4},{6,7},{7,6},{8,9},{9,8},{10,11... | collective-permute-start | bytes 6291464 | tf_op jit(solution)/shard_map/ppermute | solution.py:31
  50.0 0.8 collective-permute-start.6
  51.5 31.7 %collective-permute-start.8 = (bf16[128,512]{1,0:T(8,128)(2,1)}, bf16[128,512]{1,0:T(8,128)(2,1)S(1)}, u32[]{:S(2)}, u32[]{:S(2)}) collective-permute-start(bf16[128,512]{1,0:T(8,128)(2,1)} %pad_maximum_fusion.3), channel_id=1, source_target_pairs={{0,192},{1,193},{2,194},{3,195},{4,196},{5,197},{6,198},{7,199},{8... | collective-permute-start | bytes 393224 | tf_op jit(solution)/shard_map/ppermute | solution.py:31
  73.8 13.1 %collective-permute-start.7 = (bf16[128,512]{1,0:T(8,128)(2,1)}, bf16[128,512]{1,0:T(8,128)(2,1)S(1)}, u32[]{:S(2)}, u32[]{:S(2)}) collective-permute-start(bf16[128,512]{1,0:T(8,128)(2,1)} %pad_maximum_fusion.3), channel_id=1, source_target_pairs={{0,64},{1,65},{2,66},{3,67},{4,68},{5,69},{6,70},{7,71},{8,72},{9,... | collective-permute-start | bytes 393224 | tf_op jit(solution)/shard_map/ppermute | solution.py:31
  86.8 14.2 %collective-permute-start.9 = (bf16[128,512]{1,0:T(8,128)(2,1)S(1)}, bf16[128,512]{1,0:T(8,128)(2,1)S(1)}, u32[]{:S(2)}, u32[]{:S(2)}) collective-permute-start(bf16[128,512]{1,0:T(8,128)(2,1)S(1)} %broadcast_select_fusion.2), channel_id=1, source_target_pairs={{0,192},{1,65},{2,194},{3,67},{4,196},{5,69},{6,198},{7,71},{8,200... | collective-permute-start | bytes 393224 | tf_op jit(solution)/shard_map/ppermute | solution.py:31
  101.1 18.1 %collective-permute-start.10 = (bf16[512,512]{1,0:T(8,128)(2,1)S(1)}, bf16[512,512]{1,0:T(8,128)(2,1)S(1)}, u32[]{:S(2)}, u32[]{:S(2)}) collective-permute-start(bf16[512,512]{1,0:T(8,128)(2,1)S(1)} %pad_maximum_fusion.1.refs_5_), channel_id=1, source_target_pairs={{0,224},{1,33},{2,226},{3,35},{4,228},{5,37},{6,230},{7,39},{8,232... | collective-permute-start | bytes 1572872 | tf_op jit(solution)/shard_map/ppermute | solution.py:31
  107.5 22.5 %collective-permute-start.11 = (bf16[512,512]{1,0:T(8,128)(2,1)S(1)}, bf16[512,512]{1,0:T(8,128)(2,1)S(1)}, u32[]{:S(2)}, u32[]{:S(2)}) collective-permute-start(bf16[512,512]{1,0:T(8,128)(2,1)S(1)} %pad_maximum_fusion.1.refs_5_), channel_id=1, source_target_pairs={{0,240},{1,241},{2,242},{3,243},{4,244},{5,245},{6,246},{7,247},{8... | collective-permute-start | bytes 1572872 | tf_op jit(solution)/shard_map/ppermute | solution.py:31
  114.5 15.5 %collective-permute-start.12 = (bf16[512,512]{1,0:T(8,128)(2,1)S(1)}, bf16[512,512]{1,0:T(8,128)(2,1)S(1)}, u32[]{:S(2)}, u32[]{:S(2)}) collective-permute-start(bf16[512,512]{1,0:T(8,128)(2,1)S(1)} %pad_maximum_fusion.1.refs_5_), channel_id=1, source_target_pairs={{0,16},{1,17},{2,18},{3,19},{4,20},{5,21},{6,22},{7,23},{8,24},{9,... | collective-permute-start | bytes 1572872 | tf_op jit(solution)/shard_map/ppermute | solution.py:31
  130.0 1.0 copy-start.1
  131.0 1.0 copy-start.3
  134.1 11.0 %collective-permute-start.15 = (bf16[512,256]{1,0:T(8,128)(2,1)S(1)}, bf16[512,256]{1,0:T(8,128)(2,1)S(1)}, u32[]{:S(2)}, u32[]{:S(2)}) collective-permute-start(bf16[512,256]{1,0:T(8,128)(2,1)S(1)} %get-tuple-element.17), channel_id=1, source_target_pairs={{0,256},{1,257},{2,258},{3,259},{4,260},{5,261},{6,262},{7,263},{8... | collective-permute-start | bytes 786440 | tf_op jit(solution)/shard_map/ppermute | solution.py:31
  139.1 6.0 %collective-permute-start.14 = (f32[8,512]{1,0:T(8,128)S(1)}, f32[8,512]{1,0:T(8,128)S(1)}, u32[]{:S(2)}, u32[]{:S(2)}) collective-permute-start(f32[8,512]{1,0:T(8,128)S(1)} %get-tuple-element.16), channel_id=1, source_target_pairs={{0,256},{1,257},{2,258},{3,259},{4,260},{5,261},{6,262},{7,263},{8... | collective-permute-start | bytes 49160 | tf_op jit(solution)/shard_map/ppermute | solution.py:31
  145.6 14.2 %collective-permute-start.16 = (bf16[512,256]{1,0:T(8,128)(2,1)S(1)}, bf16[512,256]{1,0:T(8,128)(2,1)S(1)}, u32[]{:S(2)}, u32[]{:S(2)}) collective-permute-start(bf16[512,256]{1,0:T(8,128)(2,1)S(1)} %shard_map.50.kv_ref), channel_id=1, source_target_pairs={{0,16},{16,32},{32,48},{48,64},{64,80},{80,96},{96,112},{112,128},... | collective-permute-start | bytes 786440 | tf_op jit(solution)/shard_map/ppermute | solution.py:287
  151.8 7.2 %collective-permute-start.13 = (bf16[512,128]{1,0:T(8,128)(2,1)S(1)}, bf16[512,128]{1,0:T(8,128)(2,1)S(1)}, u32[]{:S(2)}, u32[]{:S(2)}) collective-permute-start(bf16[512,128]{1,0:T(8,128)(2,1)S(1)} %get-tuple-element.14), channel_id=1, source_target_pairs={{0,256},{1,257},{2,258},{3,259},{4,260},{5,261},{6,262},{7,263},{8... | collective-permute-start | bytes 393224 | tf_op jit(solution)/shard_map/ppermute | solution.py:31
  154.0 24.0 %collective-permute-start.21 = (bf16[2048,128]{1,0:T(8,128)(2,1)S(1)}, bf16[2048,128]{1,0:T(8,128)(2,1)S(1)}, u32[]{:S(2)}, u32[]{:S(2)}) collective-permute-start(bf16[2048,128]{1,0:T(8,128)(2,1)S(1)} %get-tuple-element.20.refs_4_), channel_id=1, source_target_pairs={{0,256},{1,257},{2,258},{3,259},{4,260},{5,261},{6,262},{7,263},{8... | collective-permute-start | bytes 1572872 | tf_op jit(solution)/shard_map/ppermute | solution.py:31
  159.8 39.3 %copy-start.4 = (bf16[512,256]{1,0:T(8,128)(2,1)S(1)}, bf16[512,256]{1,0:T(8,128)(2,1)}, u32[]{:S(2)}) copy-start(bf16[512,256]{1,0:T(8,128)(2,1)} %refs_6_.1) | copy-start | bytes 786436
  161.7 7.4 %collective-permute-start.17 = (bf16[512,128]{1,0:T(8,128)(2,1)S(1)}, bf16[512,128]{1,0:T(8,128)(2,1)S(1)}, u32[]{:S(2)}, u32[]{:S(2)}) collective-permute-start(bf16[512,128]{1,0:T(8,128)(2,1)S(1)} %shard_map.52), channel_id=1, source_target_pairs={{0,8},{1,9},{2,10},{3,11},{4,12},{5,13},{6,14},{7,15},{8,0},{9,1},... | collective-permute-start | bytes 393224 | tf_op jit(solution)/shard_map/ppermute | solution.py:31
  169.1 8.9 %collective-permute-start.18 = (bf16[512,256]{1,0:T(8,128)(2,1)S(1)}, bf16[512,256]{1,0:T(8,128)(2,1)S(1)}, u32[]{:S(2)}, u32[]{:S(2)}) collective-permute-start(bf16[512,256]{1,0:T(8,128)(2,1)S(1)} %pad_maximum_fusion.2.refs_0_), channel_id=1, source_target_pairs={{0,6},{1,7},{2,0},{3,1},{4,2},{5,3},{6,4},{7,5},{8,14},{9,15},{10,... | collective-permute-start | bytes 786440 | tf_op jit(solution)/shard_map/ppermute | solution.py:31
  171.7 8.6 %collective-permute-start.19 = (bf16[512,256]{1,0:T(8,128)(2,1)S(1)}, bf16[512,256]{1,0:T(8,128)(2,1)S(1)}, u32[]{:S(2)}, u32[]{:S(2)}) collective-permute-start(bf16[512,256]{1,0:T(8,128)(2,1)S(1)} %pad_maximum_fusion.2.refs_0_), channel_id=1, source_target_pairs={{0,4},{1,5},{2,6},{3,7},{4,0},{5,1},{6,2},{7,3},{8,12},{9,13},{10,... | collective-permute-start | bytes 786440 | tf_op jit(solution)/shard_map/ppermute | solution.py:31
  175.2 8.3 %collective-permute-start.20 = (bf16[512,256]{1,0:T(8,128)(2,1)S(1)}, bf16[512,256]{1,0:T(8,128)(2,1)S(1)}, u32[]{:S(2)}, u32[]{:S(2)}) collective-permute-start(bf16[512,256]{1,0:T(8,128)(2,1)S(1)} %pad_maximum_fusion.2.refs_0_), channel_id=1, source_target_pairs={{0,2},{1,3},{2,4},{3,5},{4,6},{5,7},{6,0},{7,1},{8,10},{9,11},{10,... | collective-permute-start | bytes 786440 | tf_op jit(solution)/shard_map/ppermute | solution.py:31
  184.6 15.6 %collective-permute-start.22 = (bf16[512,256]{1,0:T(8,128)(2,1)S(1)}, bf16[512,256]{1,0:T(8,128)(2,1)S(1)}, u32[]{:S(2)}, u32[]{:S(2)}) collective-permute-start(bf16[512,256]{1,0:T(8,128)(2,1)S(1)} %shard_map.54), channel_id=1, source_target_pairs={{0,1},{1,0},{2,3},{3,2},{4,5},{5,4},{6,7},{7,6},{8,9},{9,8},{10,11... | collective-permute-start | bytes 786440 | tf_op jit(solution)/shard_map/ppermute | solution.py:31

commit v5 on v4

--- a/solution.py
+++ b/solution.py
@@ -12,7 +12,7 @@
 AXES = ("ctx", "tp")
 BF = jnp.bfloat16
 F32 = jnp.float32
-HELD = (0, -4, 4, 8)
+STEPS = ((0, -4, 4, 8), (2, 6), (-2, -6), (1, -3, 5, 9), (-1, -5, 3, 7))
 
 
 def pairs_of(target):
@@ -68,26 +68,22 @@
     relay = permute(
         jnp.where(core == 0, down4, up4), lambda a, z, b, y, k: (a, z + (4 if k else 12), b, y, k)
     )
+    down2 = move(jnp.concatenate([chunk, down4], axis=0), -2)
+    up2 = move(jnp.concatenate([chunk, up4], axis=0), 2)
     held = jnp.concatenate([chunk, up4, down4, relay], axis=0)
-    two = permute(held, lambda a, z, b, y, k: (a, z + (2 if k else 14), b, y, k))
-    return held, two, move(held, -1), move(held, 1)
-
-
-def columns_of(blocks, i, first, size):
-    if i % 2 == 0:
-        return blocks[i // 2][first : first + size, :]
-    first += i // 2 * blocks[0].shape[0]
-    return blocks[4][first : first + size, :]
+    down1 = move(held, -1)
+    up1 = move(held, 1)
+    return held, down2, up2, down1, up1
 
 
 def squares_body(*refs):
-    blocks, (own_ref, other_ref) = refs[:5], refs[5:]
+    blocks, (own_ref, other_ref) = refs[:8], refs[8:]
     seg = own_ref.shape[1]
     ones = jnp.ones((own_ref.shape[0], blocks[0].shape[1]), BF)
     for first, ref in ((0, own_ref), (seg, other_ref)):
         total = jnp.zeros(ref.shape, F32)
-        for i in range(8):
-            wider = columns_of(blocks, i, first, seg).astype(F32)
+        for block in blocks:
+            wider = block[first : first + seg, :].astype(F32)
             total += lax.dot_general(
                 ones,
                 (wider * wider).astype(BF),
@@ -107,20 +103,20 @@
             yy = (y + i // 2) & 3
             kk = k if i % 2 == 0 else 1 - k
             at = pl.multiple_of((yy * 2 + kk) * 2 * rows, 2 * rows)
-            block = columns_of(blocks, i, first + r, tile)
+            block = blocks[i][first + r : first + r + tile, :]
             acc += jnp.dot(block, weights[pl.ds(at, 2 * rows), :], preferred_element_type=F32)
         yield slice(r, r + tile), acc
 
 
 def project_other_body(pos, *refs):
-    blocks, parts, (kv_ref, q_ref, w_ref, out_w_ref) = refs[:5], refs[5:9], refs[9:]
-    _, z, _, _, k = place(pos)
+    blocks, parts, (kv_ref, q_ref, w_ref, out_w_ref) = refs[:8], refs[8:13], refs[13:]
+    _, z, _, _, _ = place(pos)
     rows = w_ref.shape[0] // 16
     seg, hd = q_ref.shape
     wide = w_ref.shape[1]
-    for part, base in zip(parts, (0, 2 - 4 * k, 1, -1)):
-        for i, step in enumerate(HELD):
-            at = pl.multiple_of(((z + base + step + 16) & 15) * rows, rows)
+    for part, steps in zip(parts, STEPS):
+        for i, step in enumerate(steps):
+            at = pl.multiple_of(((z + step + 16) & 15) * rows, rows)
             w_ref[pl.ds(at, rows), :] = part[i * rows : (i + 1) * rows, :wide]
             out_w_ref[pl.ds(at, rows), :] = part[i * rows : (i + 1) * rows, wide:]
     for at, acc in project_rows(pos, blocks, w_ref, seg, seg):
@@ -129,7 +125,7 @@
 
 
 def project_own_body(pos, *refs):
-    blocks, (w_ref, own_ref) = refs[:5], refs[5:]
+    blocks, (w_ref, own_ref) = refs[:8], refs[8:]
     for at, acc in project_rows(pos, blocks, w_ref, 0, own_ref.shape[0]):
         own_ref[at, :] = acc
 
@@ -243,8 +239,9 @@
     cross = permute(hidden, lambda a, z, b, y, k: (b, z, a, y, k) if a != b else None)
     own = jnp.where(same, hidden, turn)
     other = jnp.where(same, turn, cross)
-    blocks = around(jnp.concatenate([own, other], axis=0))
-    blocks.append(permute(jnp.concatenate(blocks, axis=0), swap_core))
+    blocks = []
+    for block in around(jnp.concatenate([own, other], axis=0)):
+        blocks += [block, permute(block, swap_core)]
 
     ssq, ssq_send = call(
         squares_body,

time: 202 us -> 171 us (0.85)
  the two profiles are of different devices: /device:TPU:7 before, /device:TPU:1 now
where the time goes in v5:
time: 171 us; the launch traced here: 170 us
  starting transfers between devices  117 us (68%)
  waiting for transfers between devices  39.8 us (23%)
  Pallas kernels  11 us (6%)
  other arithmetic  1.94 us (1%)
    ppermute x26, starting transfers between devices, permute(): return lax.ppermute(value, AXES, pairs_of(target))  113 us
    ppermute x26, waiting for transfers between devices, permute(): return lax.ppermute(value, AXES, pairs_of(target))  39.8 us
    pallas_call x10, Pallas kernels, run(): pl.pallas_call(body, out_shape=outs, in_specs=specs, out_specs=jax.tree.m...  11 us
    ppermute x1, starting transfers between devices, layer(): prev = lax.ppermute(kv, 'ctx', [(i, i + 1) for i in range(31)])  4.12 us
  transfers between devices with their start and end apart: 27, of which 10 were waited for; matrix products, arithmetic and copies ran while one was open for 1% of the time, Pallas kernels for 4%

profile of v5, /device:TPU:1, one launch (start us, length us, event | category | flops | bytes accessed | tf_op | source)
XLA Modules:
  0.0 170.1 jit_solution(13482951723136589745)
XLA Ops:
  3.2 21.2 %collective-permute-start.11 = (bf16[128,512]{1,0:T(8,128)(2,1)S(1)}, bf16[128,512]{1,0:T(8,128)(2,1)S(1)}, u32[]{:S(2)}, u32[]{:S(2)}) collective-permute-start(bf16[128,512]{1,0:T(8,128)(2,1)S(1)} %pad_maximum_fusion.6), channel_id=1, source_target_pairs={{0,192},{1,193},{2,194},{3,195},{4,196},{5,197},{6,198},{7,199},{8... | collective-permute-start | bytes 393224 | tf_op jit(solution)/shard_map/ppermute | solution.py:31
  26.4 4.0 %collective-permute-start = (bf16[512,256]{1,0:T(8,128)(2,1)}, bf16[512,256]{1,0:T(8,128)(2,1)S(1)}, u32[]{:S(2)}, u32[]{:S(2)}) collective-permute-start(bf16[512,256]{1,0:T(8,128)(2,1)} %refs_6_.1), channel_id=1, source_target_pairs={{0,8},{1,9},{2,10},{3,11},{4,12},{5,13},{6,14},{7,15},{8,264},{9,2... | collective-permute-start | bytes 786440 | tf_op jit(solution)/shard_map/ppermute | solution.py:31
  31.1 4.5 %collective-permute-done.11 = bf16[128,512]{1,0:T(8,128)(2,1)S(1)} collective-permute-done((bf16[128,512]{1,0:T(8,128)(2,1)S(1)}, bf16[128,512]{1,0:T(8,128)(2,1)S(1)}, u32[]{:S(2)}, u32[]{:S(2)}) %collective-permute-start.11) | collective-permute-done | bytes 131104 | tf_op jit(solution)/shard_map/ppermute | solution.py:31
  35.6 2.1 %collective-permute-done.10 = bf16[128,512]{1,0:T(8,128)(2,1)S(1)} collective-permute-done((bf16[128,512]{1,0:T(8,128)(2,1)S(1)}, bf16[128,512]{1,0:T(8,128)(2,1)S(1)}, u32[]{:S(2)}, u32[]{:S(2)}) %collective-permute-start.10) | collective-permute-done | bytes 131104 | tf_op jit(solution)/shard_map/ppermute | solution.py:31
  37.8 9.7 %collective-permute-start.12 = (bf16[128,512]{1,0:T(8,128)(2,1)S(1)}, bf16[128,512]{1,0:T(8,128)(2,1)S(1)}, u32[]{:S(2)}, u32[]{:S(2)}) collective-permute-start(bf16[128,512]{1,0:T(8,128)(2,1)S(1)} %broadcast_select_fusion.2), channel_id=1, source_target_pairs={{0,192},{1,65},{2,194},{3,67},{4,196},{5,69},{6,198},{7,71},{8,200... | collective-permute-start | bytes 393224 | tf_op jit(solution)/shard_map/ppermute | solution.py:31
  47.5 5.0 %collective-permute-start.13 = (bf16[256,512]{1,0:T(8,128)(2,1)S(1)}, bf16[256,512]{1,0:T(8,128)(2,1)S(1)}, u32[]{:S(2)}, u32[]{:S(2)}) collective-permute-start(bf16[256,512]{1,0:T(8,128)(2,1)S(1)} %get-tuple-element.24), channel_id=1, source_target_pairs={{0,224},{1,225},{2,226},{3,227},{4,228},{5,229},{6,230},{7,231},{8... | collective-permute-start | bytes 786440 | tf_op jit(solution)/shard_map/ppermute | solution.py:31
  52.6 5.6 %collective-permute-start.2 = (bf16[1024,256]{1,0:T(8,128)(2,1)S(1)}, bf16[1024,256]{1,0:T(8,128)(2,1)S(1)}, u32[]{:S(2)}, u32[]{:S(2)}) collective-permute-start(bf16[1024,256]{1,0:T(8,128)(2,1)S(1)} %pad_maximum_fusion.refs_0_), channel_id=1, source_target_pairs={{0,1},{1,0},{2,3},{3,2},{4,5},{5,4},{6,7},{7,6},{8,9},{9,8},{10,11... | collective-permute-start | bytes 1572872 | tf_op jit(solution)/shard_map/ppermute | solution.py:31
  58.2 3.5 %collective-permute-start.3 = (bf16[1024,256]{1,0:T(8,128)(2,1)S(1)}, bf16[1024,256]{1,0:T(8,128)(2,1)S(1)}, u32[]{:S(2)}, u32[]{:S(2)}) collective-permute-start(bf16[1024,256]{1,0:T(8,128)(2,1)S(1)} %pad_maximum_fusion.refs_0_), channel_id=1, source_target_pairs={{0,6},{1,7},{2,0},{3,1},{4,2},{5,3},{6,4},{7,5},{8,14},{9,15},{10,... | collective-permute-start | bytes 1572872 | tf_op jit(solution)/shard_map/ppermute | solution.py:31
  61.7 1.9 %collective-permute-start.5 = (bf16[1024,256]{1,0:T(8,128)(2,1)S(1)}, bf16[1024,256]{1,0:T(8,128)(2,1)S(1)}, u32[]{:S(2)}, u32[]{:S(2)}) collective-permute-start(bf16[1024,256]{1,0:T(8,128)(2,1)S(1)} %pad_maximum_fusion.refs_0_), channel_id=1, source_target_pairs={{0,4},{1,5},{2,6},{3,7},{4,0},{5,1},{6,2},{7,3},{8,12},{9,13},{10,... | collective-permute-start | bytes 1572872 | tf_op jit(solution)/shard_map/ppermute | solution.py:31
  63.6 2.5 %collective-permute-start.7 = (bf16[1024,256]{1,0:T(8,128)(2,1)S(1)}, bf16[1024,256]{1,0:T(8,128)(2,1)S(1)}, u32[]{:S(2)}, u32[]{:S(2)}) collective-permute-start(bf16[1024,256]{1,0:T(8,128)(2,1)S(1)} %pad_maximum_fusion.refs_0_), channel_id=1, source_target_pairs={{0,2},{1,3},{2,4},{3,5},{4,6},{5,7},{6,0},{7,1},{8,10},{9,11},{10,... | collective-permute-start | bytes 1572872 | tf_op jit(solution)/shard_map/ppermute | solution.py:31
  66.1 3.2 %collective-permute-start.14 = (bf16[256,512]{1,0:T(8,128)(2,1)S(1)}, bf16[256,512]{1,0:T(8,128)(2,1)S(1)}, u32[]{:S(2)}, u32[]{:S(2)}) collective-permute-start(bf16[256,512]{1,0:T(8,128)(2,1)S(1)} %get-tuple-element.23), channel_id=1, source_target_pairs={{0,32},{1,33},{2,34},{3,35},{4,36},{5,37},{6,38},{7,39},{8,40},{9,... | collective-permute-start | bytes 786440 | tf_op jit(solution)/shard_map/ppermute | solution.py:31
  69.4 6.3 %collective-permute-done.14.refs_10_ = bf16[256,512]{1,0:T(8,128)(2,1)S(1)} collective-permute-done((bf16[256,512]{1,0:T(8,128)(2,1)S(1)}, bf16[256,512]{1,0:T(8,128)(2,1)S(1)}, u32[]{:S(2)}, u32[]{:S(2)}) %collective-permute-start.14) | collective-permute-done | bytes 262176 | tf_op jit(solution)/shard_map/ppermute | solution.py:31
  75.7 6.3 %collective-permute-start.15 = (bf16[512,512]{1,0:T(8,128)(2,1)S(1)}, bf16[512,512]{1,0:T(8,128)(2,1)S(1)}, u32[]{:S(2)}, u32[]{:S(2)}) collective-permute-start(bf16[512,512]{1,0:T(8,128)(2,1)S(1)} %pad_maximum_fusion.1.refs_8_), channel_id=1, source_target_pairs={{0,240},{1,241},{2,242},{3,243},{4,244},{5,245},{6,246},{7,247},{8... | collective-permute-start | bytes 1572872 | tf_op jit(solution)/shard_map/ppermute | solution.py:31
  82.0 4.0 %collective-permute-start.16 = (bf16[512,512]{1,0:T(8,128)(2,1)S(1)}, bf16[512,512]{1,0:T(8,128)(2,1)S(1)}, u32[]{:S(2)}, u32[]{:S(2)}) collective-permute-start(bf16[512,512]{1,0:T(8,128)(2,1)S(1)} %pad_maximum_fusion.1.refs_8_), channel_id=1, source_target_pairs={{0,16},{1,17},{2,18},{3,19},{4,20},{5,21},{6,22},{7,23},{8,24},{9,... | collective-permute-start | bytes 1572872 | tf_op jit(solution)/shard_map/ppermute | solution.py:31
  86.0 6.8 %collective-permute-start.4 = (bf16[1024,256]{1,0:T(8,128)(2,1)S(1)}, bf16[1024,256]{1,0:T(8,128)(2,1)S(1)}, u32[]{:S(2)}, u32[]{:S(2)}) collective-permute-start(bf16[1024,256]{1,0:T(8,128)(2,1)S(1)} %collective-permute-done.3.refs_2_), channel_id=1, source_target_pairs={{0,1},{1,0},{2,3},{3,2},{4,5},{5,4},{6,7},{7,6},{8,9},{9,8},{10,11... | collective-permute-start | bytes 1572872 | tf_op jit(solution)/shard_map/ppermute | solution.py:31
  92.8 1.9 %collective-permute-start.6 = (bf16[1024,256]{1,0:T(8,128)(2,1)S(1)}, bf16[1024,256]{1,0:T(8,128)(2,1)S(1)}, u32[]{:S(2)}, u32[]{:S(2)}) collective-permute-start(bf16[1024,256]{1,0:T(8,128)(2,1)S(1)} %collective-permute-done.5.refs_4_), channel_id=1, source_target_pairs={{0,1},{1,0},{2,3},{3,2},{4,5},{5,4},{6,7},{7,6},{8,9},{9,8},{10,11... | collective-permute-start | bytes 1572872 | tf_op jit(solution)/shard_map/ppermute | solution.py:31
  94.7 2.4 %collective-permute-start.8 = (bf16[1024,256]{1,0:T(8,128)(2,1)S(1)}, bf16[1024,256]{1,0:T(8,128)(2,1)S(1)}, u32[]{:S(2)}, u32[]{:S(2)}) collective-permute-start(bf16[1024,256]{1,0:T(8,128)(2,1)S(1)} %collective-permute-done.7.refs_6_), channel_id=1, source_target_pairs={{0,1},{1,0},{2,3},{3,2},{4,5},{5,4},{6,7},{7,6},{8,9},{9,8},{10,11... | collective-permute-start | bytes 1572872 | tf_op jit(solution)/shard_map/ppermute | solution.py:31
  98.7 2.0 %shard_map.46 = (bf16[512,256]{1,0:T(8,128)(2,1)S(1)}, bf16[512,128]{1,0:T(8,128)(2,1)S(1)}, bf16[2048,384]{1,0:T(8,128)(2,1)S(1)}, bf16[2048,128]{1,0:T(8,128)(2,1)S(1)}) custom-call(s32[2]{0:T(128)S(1)} %pad_add_fusion.pos, bf16[1024,256]{1,0:T(8,128)(2,1)S(1)} %pad_maximum_fusion.refs_0_, bf16[1024,256]{1,0:T(8,128)(2,1)S(1)} %collective-permute-done.2.refs_1_, ...), custom_call_target="tpu_custom_call" | custom-call | flops 805306368 | bytes 8388608 | tf_op jit(solution)/shard_map/pallas_call | solution.py:39
  100.7 7.4 %collective-permute-start.19 = (bf16[512,256]{1,0:T(8,128)(2,1)S(1)}, bf16[512,256]{1,0:T(8,128)(2,1)S(1)}, u32[]{:S(2)}, u32[]{:S(2)}) collective-permute-start(bf16[512,256]{1,0:T(8,128)(2,1)S(1)} %get-tuple-element.17), channel_id=1, source_target_pairs={{0,256},{1,257},{2,258},{3,259},{4,260},{5,261},{6,262},{7,263},{8... | collective-permute-start | bytes 786440 | tf_op jit(solution)/shard_map/ppermute | solution.py:31
  109.3 1.9 %collective-permute-start.18 = (f32[8,512]{1,0:T(8,128)S(1)}, f32[8,512]{1,0:T(8,128)S(1)}, u32[]{:S(2)}, u32[]{:S(2)}) collective-permute-start(f32[8,512]{1,0:T(8,128)S(1)} %get-tuple-element.16), channel_id=1, source_target_pairs={{0,256},{1,257},{2,258},{3,259},{4,260},{5,261},{6,262},{7,263},{8... | collective-permute-start | bytes 49160 | tf_op jit(solution)/shard_map/ppermute | solution.py:31
  113.1 2.3 %collective-permute-done.18.refs_3_ = f32[8,512]{1,0:T(8,128)S(1)} collective-permute-done((f32[8,512]{1,0:T(8,128)S(1)}, f32[8,512]{1,0:T(8,128)S(1)}, u32[]{:S(2)}, u32[]{:S(2)}) %collective-permute-start.18) | collective-permute-done | bytes 16416 | tf_op jit(solution)/shard_map/ppermute | solution.py:31
  115.9 4.1 %collective-permute-start.20 = (bf16[512,256]{1,0:T(8,128)(2,1)S(1)}, bf16[512,256]{1,0:T(8,128)(2,1)S(1)}, u32[]{:S(2)}, u32[]{:S(2)}) collective-permute-start(bf16[512,256]{1,0:T(8,128)(2,1)S(1)} %shard_map.50.kv_ref), channel_id=1, source_target_pairs={{0,16},{16,32},{32,48},{48,64},{64,80},{80,96},{96,112},{112,128},... | collective-permute-start | bytes 786440 | tf_op jit(solution)/shard_map/ppermute | solution.py:284
  120.0 2.7 %collective-permute-start.17 = (bf16[512,128]{1,0:T(8,128)(2,1)S(1)}, bf16[512,128]{1,0:T(8,128)(2,1)S(1)}, u32[]{:S(2)}, u32[]{:S(2)}) collective-permute-start(bf16[512,128]{1,0:T(8,128)(2,1)S(1)} %get-tuple-element.14), channel_id=1, source_target_pairs={{0,256},{1,257},{2,258},{3,259},{4,260},{5,261},{6,262},{7,263},{8... | collective-permute-start | bytes 393224 | tf_op jit(solution)/shard_map/ppermute | solution.py:31
  122.7 4.1 %collective-permute-start.25 = (bf16[2048,128]{1,0:T(8,128)(2,1)S(1)}, bf16[2048,128]{1,0:T(8,128)(2,1)S(1)}, u32[]{:S(2)}, u32[]{:S(2)}) collective-permute-start(bf16[2048,128]{1,0:T(8,128)(2,1)S(1)} %get-tuple-element.20.refs_4_), channel_id=1, source_target_pairs={{0,256},{1,257},{2,258},{3,259},{4,260},{5,261},{6,262},{7,263},{8... | collective-permute-start | bytes 1572872 | tf_op jit(solution)/shard_map/ppermute | solution.py:31
  130.9 2.0 %collective-permute-start.21 = (bf16[512,128]{1,0:T(8,128)(2,1)S(1)}, bf16[512,128]{1,0:T(8,128)(2,1)S(1)}, u32[]{:S(2)}, u32[]{:S(2)}) collective-permute-start(bf16[512,128]{1,0:T(8,128)(2,1)S(1)} %shard_map.52), channel_id=1, source_target_pairs={{0,8},{1,9},{2,10},{3,11},{4,12},{5,13},{6,14},{7,15},{8,0},{9,1},... | collective-permute-start | bytes 393224 | tf_op jit(solution)/shard_map/ppermute | solution.py:31
  132.9 10.2 %collective-permute-done.21 = bf16[512,128]{1,0:T(8,128)(2,1)S(1)} collective-permute-done((bf16[512,128]{1,0:T(8,128)(2,1)S(1)}, bf16[512,128]{1,0:T(8,128)(2,1)S(1)}, u32[]{:S(2)}, u32[]{:S(2)}) %collective-permute-start.21) | collective-permute-done | bytes 131104 | tf_op jit(solution)/shard_map/ppermute | solution.py:31
  143.1 4.4 %collective-permute-start.22 = (bf16[512,256]{1,0:T(8,128)(2,1)S(1)}, bf16[512,256]{1,0:T(8,128)(2,1)S(1)}, u32[]{:S(2)}, u32[]{:S(2)}) collective-permute-start(bf16[512,256]{1,0:T(8,128)(2,1)S(1)} %pad_maximum_fusion.5.refs_0_), channel_id=1, source_target_pairs={{0,6},{1,7},{2,0},{3,1},{4,2},{5,3},{6,4},{7,5},{8,14},{9,15},{10,... | collective-permute-start | bytes 786440 | tf_op jit(solution)/shard_map/ppermute | solution.py:31
  147.6 2.8 %collective-permute-start.23 = (bf16[512,256]{1,0:T(8,128)(2,1)S(1)}, bf16[512,256]{1,0:T(8,128)(2,1)S(1)}, u32[]{:S(2)}, u32[]{:S(2)}) collective-permute-start(bf16[512,256]{1,0:T(8,128)(2,1)S(1)} %pad_maximum_fusion.5.refs_0_), channel_id=1, source_target_pairs={{0,4},{1,5},{2,6},{3,7},{4,0},{5,1},{6,2},{7,3},{8,12},{9,13},{10,... | collective-permute-start | bytes 786440 | tf_op jit(solution)/shard_map/ppermute | solution.py:31
  150.4 1.9 %collective-permute-start.24 = (bf16[512,256]{1,0:T(8,128)(2,1)S(1)}, bf16[512,256]{1,0:T(8,128)(2,1)S(1)}, u32[]{:S(2)}, u32[]{:S(2)}) collective-permute-start(bf16[512,256]{1,0:T(8,128)(2,1)S(1)} %pad_maximum_fusion.5.refs_0_), channel_id=1, source_target_pairs={{0,2},{1,3},{2,4},{3,5},{4,6},{5,7},{6,0},{7,1},{8,10},{9,11},{10,... | collective-permute-start | bytes 786440 | tf_op jit(solution)/shard_map/ppermute | solution.py:31
  152.4 4.5 %collective-permute-done.23.refs_2_ = bf16[512,256]{1,0:T(8,128)(2,1)S(1)} collective-permute-done((bf16[512,256]{1,0:T(8,128)(2,1)S(1)}, bf16[512,256]{1,0:T(8,128)(2,1)S(1)}, u32[]{:S(2)}, u32[]{:S(2)}) %collective-permute-start.23) | collective-permute-done | bytes 262176 | tf_op jit(solution)/shard_map/ppermute | solution.py:31
  156.9 6.8 %collective-permute-done.24.refs_3_ = bf16[512,256]{1,0:T(8,128)(2,1)S(1)} collective-permute-done((bf16[512,256]{1,0:T(8,128)(2,1)S(1)}, bf16[512,256]{1,0:T(8,128)(2,1)S(1)}, u32[]{:S(2)}, u32[]{:S(2)}) %collective-permute-start.24) | collective-permute-done | bytes 262176 | tf_op jit(solution)/shard_map/ppermute | solution.py:31
  164.7 3.5 %collective-permute-start.26 = (bf16[512,256]{1,0:T(8,128)(2,1)S(1)}, bf16[512,256]{1,0:T(8,128)(2,1)S(1)}, u32[]{:S(2)}, u32[]{:S(2)}) collective-permute-start(bf16[512,256]{1,0:T(8,128)(2,1)S(1)} %shard_map.54), channel_id=1, source_target_pairs={{0,1},{1,0},{2,3},{3,2},{4,5},{5,4},{6,7},{7,6},{8,9},{9,8},{10,11... | collective-permute-start | bytes 786440 | tf_op jit(solution)/shard_map/ppermute | solution.py:31
  (45 shorter events, 18.1 us)
Async XLA Ops:
  0.0 52.5 %copy-start = (bf16[512,256]{1,0:T(8,128)(2,1)S(1)}, bf16[512,256]{1,0:T(8,128)(2,1)}, u32[]{:S(2)}) copy-start(bf16[512,256]{1,0:T(8,128)(2,1)} %refs_6_.1) | copy-start | bytes 786436
  0.0 3.2 %collective-permute-start.9 = (bf16[128,128]{1,0:T(8,128)(2,1)}, bf16[128,128]{1,0:T(8,128)(2,1)S(1)}, u32[]{:S(2)}, u32[]{:S(2)}) collective-permute-start(bf16[128,128]{1,0:T(8,128)(2,1)} %bitcast.15), channel_id=1, source_target_pairs={{0,0},{1,1},{2,64},{3,65},{4,128},{5,129},{6,192},{7,193},{8,256},... | collective-permute-start | bytes 98312 | tf_op jit(solution)/shard_map/ppermute | solution.py:31
  3.2 32.4 %collective-permute-start.11 = (bf16[128,512]{1,0:T(8,128)(2,1)S(1)}, bf16[128,512]{1,0:T(8,128)(2,1)S(1)}, u32[]{:S(2)}, u32[]{:S(2)}) collective-permute-start(bf16[128,512]{1,0:T(8,128)(2,1)S(1)} %pad_maximum_fusion.6), channel_id=1, source_target_pairs={{0,192},{1,193},{2,194},{3,195},{4,196},{5,197},{6,198},{7,199},{8... | collective-permute-start | bytes 393224 | tf_op jit(solution)/shard_map/ppermute | solution.py:31
  24.4 13.3 %collective-permute-start.10 = (bf16[128,512]{1,0:T(8,128)(2,1)S(1)}, bf16[128,512]{1,0:T(8,128)(2,1)S(1)}, u32[]{:S(2)}, u32[]{:S(2)}) collective-permute-start(bf16[128,512]{1,0:T(8,128)(2,1)S(1)} %pad_maximum_fusion.6), channel_id=1, source_target_pairs={{0,64},{1,65},{2,66},{3,67},{4,68},{5,69},{6,70},{7,71},{8,72},{9,... | collective-permute-start | bytes 393224 | tf_op jit(solution)/shard_map/ppermute | solution.py:31
  26.4 26.1 %collective-permute-start = (bf16[512,256]{1,0:T(8,128)(2,1)}, bf16[512,256]{1,0:T(8,128)(2,1)S(1)}, u32[]{:S(2)}, u32[]{:S(2)}) collective-permute-start(bf16[512,256]{1,0:T(8,128)(2,1)} %refs_6_.1), channel_id=1, source_target_pairs={{0,8},{1,9},{2,10},{3,11},{4,12},{5,13},{6,14},{7,15},{8,264},{9,2... | collective-permute-start | bytes 786440 | tf_op jit(solution)/shard_map/ppermute | solution.py:31
  30.4 22.1 %collective-permute-start.1 = (bf16[512,256]{1,0:T(8,128)(2,1)}, bf16[512,256]{1,0:T(8,128)(2,1)S(1)}, u32[]{:S(2)}, u32[]{:S(2)}) collective-permute-start(bf16[512,256]{1,0:T(8,128)(2,1)} %refs_6_.1), channel_id=1, source_target_pairs={{8,256},{9,257},{10,258},{11,259},{12,260},{13,261},{14,262},{15,2... | collective-permute-start | bytes 786440 | tf_op jit(solution)/shard_map/ppermute | solution.py:31
  37.8 25.9 %collective-permute-start.12 = (bf16[128,512]{1,0:T(8,128)(2,1)S(1)}, bf16[128,512]{1,0:T(8,128)(2,1)S(1)}, u32[]{:S(2)}, u32[]{:S(2)}) collective-permute-start(bf16[128,512]{1,0:T(8,128)(2,1)S(1)} %broadcast_select_fusion.2), channel_id=1, source_target_pairs={{0,192},{1,65},{2,194},{3,67},{4,196},{5,69},{6,198},{7,71},{8,200... | collective-permute-start | bytes 393224 | tf_op jit(solution)/shard_map/ppermute | solution.py:31
  47.5 18.6 %collective-permute-start.13 = (bf16[256,512]{1,0:T(8,128)(2,1)S(1)}, bf16[256,512]{1,0:T(8,128)(2,1)S(1)}, u32[]{:S(2)}, u32[]{:S(2)}) collective-permute-start(bf16[256,512]{1,0:T(8,128)(2,1)S(1)} %get-tuple-element.24), channel_id=1, source_target_pairs={{0,224},{1,225},{2,226},{3,227},{4,228},{5,229},{6,230},{7,231},{8... | collective-permute-start | bytes 786440 | tf_op jit(solution)/shard_map/ppermute | solution.py:31
  52.6 29.3 %collective-permute-start.2 = (bf16[1024,256]{1,0:T(8,128)(2,1)S(1)}, bf16[1024,256]{1,0:T(8,128)(2,1)S(1)}, u32[]{:S(2)}, u32[]{:S(2)}) collective-permute-start(bf16[1024,256]{1,0:T(8,128)(2,1)S(1)} %pad_maximum_fusion.refs_0_), channel_id=1, source_target_pairs={{0,1},{1,0},{2,3},{3,2},{4,5},{5,4},{6,7},{7,6},{8,9},{9,8},{10,11... | collective-permute-start | bytes 1572872 | tf_op jit(solution)/shard_map/ppermute | solution.py:31
  58.2 27.8 %collective-permute-start.3 = (bf16[1024,256]{1,0:T(8,128)(2,1)S(1)}, bf16[1024,256]{1,0:T(8,128)(2,1)S(1)}, u32[]{:S(2)}, u32[]{:S(2)}) collective-permute-start(bf16[1024,256]{1,0:T(8,128)(2,1)S(1)} %pad_maximum_fusion.refs_0_), channel_id=1, source_target_pairs={{0,6},{1,7},{2,0},{3,1},{4,2},{5,3},{6,4},{7,5},{8,14},{9,15},{10,... | collective-permute-start | bytes 1572872 | tf_op jit(solution)/shard_map/ppermute | solution.py:31
  61.7 31.1 %collective-permute-start.5 = (bf16[1024,256]{1,0:T(8,128)(2,1)S(1)}, bf16[1024,256]{1,0:T(8,128)(2,1)S(1)}, u32[]{:S(2)}, u32[]{:S(2)}) collective-permute-start(bf16[1024,256]{1,0:T(8,128)(2,1)S(1)} %pad_maximum_fusion.refs_0_), channel_id=1, source_target_pairs={{0,4},{1,5},{2,6},{3,7},{4,0},{5,1},{6,2},{7,3},{8,12},{9,13},{10,... | collective-permute-start | bytes 1572872 | tf_op jit(solution)/shard_map/ppermute | solution.py:31
  63.6 31.1 %collective-permute-start.7 = (bf16[1024,256]{1,0:T(8,128)(2,1)S(1)}, bf16[1024,256]{1,0:T(8,128)(2,1)S(1)}, u32[]{:S(2)}, u32[]{:S(2)}) collective-permute-start(bf16[1024,256]{1,0:T(8,128)(2,1)S(1)} %pad_maximum_fusion.refs_0_), channel_id=1, source_target_pairs={{0,2},{1,3},{2,4},{3,5},{4,6},{5,7},{6,0},{7,1},{8,10},{9,11},{10,... | collective-permute-start | bytes 1572872 | tf_op jit(solution)/shard_map/ppermute | solution.py:31
  66.1 9.5 %collective-permute-start.14 = (bf16[256,512]{1,0:T(8,128)(2,1)S(1)}, bf16[256,512]{1,0:T(8,128)(2,1)S(1)}, u32[]{:S(2)}, u32[]{:S(2)}) collective-permute-start(bf16[256,512]{1,0:T(8,128)(2,1)S(1)} %get-tuple-element.23), channel_id=1, source_target_pairs={{0,32},{1,33},{2,34},{3,35},{4,36},{5,37},{6,38},{7,39},{8,40},{9,... | collective-permute-start | bytes 786440 | tf_op jit(solution)/shard_map/ppermute | solution.py:31
  75.7 21.5 %collective-permute-start.15 = (bf16[512,512]{1,0:T(8,128)(2,1)S(1)}, bf16[512,512]{1,0:T(8,128)(2,1)S(1)}, u32[]{:S(2)}, u32[]{:S(2)}) collective-permute-start(bf16[512,512]{1,0:T(8,128)(2,1)S(1)} %pad_maximum_fusion.1.refs_8_), channel_id=1, source_target_pairs={{0,240},{1,241},{2,242},{3,243},{4,244},{5,245},{6,246},{7,247},{8... | collective-permute-start | bytes 1572872 | tf_op jit(solution)/shard_map/ppermute | solution.py:31
  82.0 15.3 %collective-permute-start.16 = (bf16[512,512]{1,0:T(8,128)(2,1)S(1)}, bf16[512,512]{1,0:T(8,128)(2,1)S(1)}, u32[]{:S(2)}, u32[]{:S(2)}) collective-permute-start(bf16[512,512]{1,0:T(8,128)(2,1)S(1)} %pad_maximum_fusion.1.refs_8_), channel_id=1, source_target_pairs={{0,16},{1,17},{2,18},{3,19},{4,20},{5,21},{6,22},{7,23},{8,24},{9,... | collective-permute-start | bytes 1572872 | tf_op jit(solution)/shard_map/ppermute | solution.py:31
  86.0 11.2 %collective-permute-start.4 = (bf16[1024,256]{1,0:T(8,128)(2,1)S(1)}, bf16[1024,256]{1,0:T(8,128)(2,1)S(1)}, u32[]{:S(2)}, u32[]{:S(2)}) collective-permute-start(bf16[1024,256]{1,0:T(8,128)(2,1)S(1)} %collective-permute-done.3.refs_2_), channel_id=1, source_target_pairs={{0,1},{1,0},{2,3},{3,2},{4,5},{5,4},{6,7},{7,6},{8,9},{9,8},{10,11... | collective-permute-start | bytes 1572872 | tf_op jit(solution)/shard_map/ppermute | solution.py:31
  92.8 4.4 %collective-permute-start.6 = (bf16[1024,256]{1,0:T(8,128)(2,1)S(1)}, bf16[1024,256]{1,0:T(8,128)(2,1)S(1)}, u32[]{:S(2)}, u32[]{:S(2)}) collective-permute-start(bf16[1024,256]{1,0:T(8,128)(2,1)S(1)} %collective-permute-done.5.refs_4_), channel_id=1, source_target_pairs={{0,1},{1,0},{2,3},{3,2},{4,5},{5,4},{6,7},{7,6},{8,9},{9,8},{10,11... | collective-permute-start | bytes 1572872 | tf_op jit(solution)/shard_map/ppermute | solution.py:31
  94.7 3.9 %collective-permute-start.8 = (bf16[1024,256]{1,0:T(8,128)(2,1)S(1)}, bf16[1024,256]{1,0:T(8,128)(2,1)S(1)}, u32[]{:S(2)}, u32[]{:S(2)}) collective-permute-start(bf16[1024,256]{1,0:T(8,128)(2,1)S(1)} %collective-permute-done.7.refs_6_), channel_id=1, source_target_pairs={{0,1},{1,0},{2,3},{3,2},{4,5},{5,4},{6,7},{7,6},{8,9},{9,8},{10,11... | collective-permute-start | bytes 1572872 | tf_op jit(solution)/shard_map/ppermute | solution.py:31
  100.7 14.6 %collective-permute-start.19 = (bf16[512,256]{1,0:T(8,128)(2,1)S(1)}, bf16[512,256]{1,0:T(8,128)(2,1)S(1)}, u32[]{:S(2)}, u32[]{:S(2)}) collective-permute-start(bf16[512,256]{1,0:T(8,128)(2,1)S(1)} %get-tuple-element.17), channel_id=1, source_target_pairs={{0,256},{1,257},{2,258},{3,259},{4,260},{5,261},{6,262},{7,263},{8... | collective-permute-start | bytes 786440 | tf_op jit(solution)/shard_map/ppermute | solution.py:31
  109.3 6.0 %collective-permute-start.18 = (f32[8,512]{1,0:T(8,128)S(1)}, f32[8,512]{1,0:T(8,128)S(1)}, u32[]{:S(2)}, u32[]{:S(2)}) collective-permute-start(f32[8,512]{1,0:T(8,128)S(1)} %get-tuple-element.16), channel_id=1, source_target_pairs={{0,256},{1,257},{2,258},{3,259},{4,260},{5,261},{6,262},{7,263},{8... | collective-permute-start | bytes 49160 | tf_op jit(solution)/shard_map/ppermute | solution.py:31
  115.9 13.2 %collective-permute-start.20 = (bf16[512,256]{1,0:T(8,128)(2,1)S(1)}, bf16[512,256]{1,0:T(8,128)(2,1)S(1)}, u32[]{:S(2)}, u32[]{:S(2)}) collective-permute-start(bf16[512,256]{1,0:T(8,128)(2,1)S(1)} %shard_map.50.kv_ref), channel_id=1, source_target_pairs={{0,16},{16,32},{32,48},{48,64},{64,80},{80,96},{96,112},{112,128},... | collective-permute-start | bytes 786440 | tf_op jit(solution)/shard_map/ppermute | solution.py:284
  120.0 8.2 %collective-permute-start.17 = (bf16[512,128]{1,0:T(8,128)(2,1)S(1)}, bf16[512,128]{1,0:T(8,128)(2,1)S(1)}, u32[]{:S(2)}, u32[]{:S(2)}) collective-permute-start(bf16[512,128]{1,0:T(8,128)(2,1)S(1)} %get-tuple-element.14), channel_id=1, source_target_pairs={{0,256},{1,257},{2,258},{3,259},{4,260},{5,261},{6,262},{7,263},{8... | collective-permute-start | bytes 393224 | tf_op jit(solution)/shard_map/ppermute | solution.py:31
  122.7 29.7 %collective-permute-start.25 = (bf16[2048,128]{1,0:T(8,128)(2,1)S(1)}, bf16[2048,128]{1,0:T(8,128)(2,1)S(1)}, u32[]{:S(2)}, u32[]{:S(2)}) collective-permute-start(bf16[2048,128]{1,0:T(8,128)(2,1)S(1)} %get-tuple-element.20.refs_4_), channel_id=1, source_target_pairs={{0,256},{1,257},{2,258},{3,259},{4,260},{5,261},{6,262},{7,263},{8... | collective-permute-start | bytes 1572872 | tf_op jit(solution)/shard_map/ppermute | solution.py:31
  130.9 12.2 %collective-permute-start.21 = (bf16[512,128]{1,0:T(8,128)(2,1)S(1)}, bf16[512,128]{1,0:T(8,128)(2,1)S(1)}, u32[]{:S(2)}, u32[]{:S(2)}) collective-permute-start(bf16[512,128]{1,0:T(8,128)(2,1)S(1)} %shard_map.52), channel_id=1, source_target_pairs={{0,8},{1,9},{2,10},{3,11},{4,12},{5,13},{6,14},{7,15},{8,0},{9,1},... | collective-permute-start | bytes 393224 | tf_op jit(solution)/shard_map/ppermute | solution.py:31
  143.1 9.3 %collective-permute-start.22 = (bf16[512,256]{1,0:T(8,128)(2,1)S(1)}, bf16[512,256]{1,0:T(8,128)(2,1)S(1)}, u32[]{:S(2)}, u32[]{:S(2)}) collective-permute-start(bf16[512,256]{1,0:T(8,128)(2,1)S(1)} %pad_maximum_fusion.5.refs_0_), channel_id=1, source_target_pairs={{0,6},{1,7},{2,0},{3,1},{4,2},{5,3},{6,4},{7,5},{8,14},{9,15},{10,... | collective-permute-start | bytes 786440 | tf_op jit(solution)/shard_map/ppermute | solution.py:31
  147.6 9.4 %collective-permute-start.23 = (bf16[512,256]{1,0:T(8,128)(2,1)S(1)}, bf16[512,256]{1,0:T(8,128)(2,1)S(1)}, u32[]{:S(2)}, u32[]{:S(2)}) collective-permute-start(bf16[512,256]{1,0:T(8,128)(2,1)S(1)} %pad_maximum_fusion.5.refs_0_), channel_id=1, source_target_pairs={{0,4},{1,5},{2,6},{3,7},{4,0},{5,1},{6,2},{7,3},{8,12},{9,13},{10,... | collective-permute-start | bytes 786440 | tf_op jit(solution)/shard_map/ppermute | solution.py:31
  150.4 13.3 %collective-permute-start.24 = (bf16[512,256]{1,0:T(8,128)(2,1)S(1)}, bf16[512,256]{1,0:T(8,128)(2,1)S(1)}, u32[]{:S(2)}, u32[]{:S(2)}) collective-permute-start(bf16[512,256]{1,0:T(8,128)(2,1)S(1)} %pad_maximum_fusion.5.refs_0_), channel_id=1, source_target_pairs={{0,2},{1,3},{2,4},{3,5},{4,6},{5,7},{6,0},{7,1},{8,10},{9,11},{10,... | collective-permute-start | bytes 786440 | tf_op jit(solution)/shard_map/ppermute | solution.py:31
  164.7 4.7 %collective-permute-start.26 = (bf16[512,256]{1,0:T(8,128)(2,1)S(1)}, bf16[512,256]{1,0:T(8,128)(2,1)S(1)}, u32[]{:S(2)}, u32[]{:S(2)}) collective-permute-start(bf16[512,256]{1,0:T(8,128)(2,1)S(1)} %shard_map.54), channel_id=1, source_target_pairs={{0,1},{1,0},{2,3},{3,2},{4,5},{5,4},{6,7},{7,6},{8,9},{9,8},{10,11... | collective-permute-start | bytes 786440 | tf_op jit(solution)/shard_map/ppermute | solution.py:31

commit v6 on v5

--- a/solution.py
+++ b/solution.py
@@ -108,8 +108,13 @@
         yield slice(r, r + tile), acc
 
 
+EXTRA = 16
+
+
 def project_other_body(pos, *refs):
-    blocks, parts, (kv_ref, q_ref, w_ref, out_w_ref) = refs[:8], refs[8:13], refs[13:]
+    blocks, parts, ssq_ref, (kv_ref, q_ref, w_ref, out_w_ref) = (
+        refs[:8], refs[8:13], refs[13], refs[14:],
+    )
     _, z, _, _, _ = place(pos)
     rows = w_ref.shape[0] // 16
     seg, hd = q_ref.shape
@@ -122,6 +127,16 @@
     for at, acc in project_rows(pos, blocks, w_ref, seg, seg):
         q_ref[at, :] = acc[:, :hd].astype(BF)
         kv_ref[at, :] = acc[:, hd:].astype(BF)
+    half = kv_ref.shape[1]
+    ssq = ssq_ref[:1, :]
+    high = ssq.astype(BF).astype(F32)
+    row = lax.broadcasted_iota(jnp.int32, (EXTRA, half), 0)
+    extra = jnp.zeros((EXTRA, half), F32)
+    for i, part in enumerate((high, ssq - high)):
+        for j in range(seg // half):
+            here = jnp.broadcast_to(part[:, j * half : (j + 1) * half], (EXTRA, half))
+            extra = jnp.where(row == i * (seg // half) + j, here, extra)
+    kv_ref[seg:, :] = extra.astype(BF)
 
 
 def project_own_body(pos, *refs):
@@ -130,9 +145,13 @@
         own_ref[at, :] = acc
 
 
-def combine_body(own_ref, got_ref, ssq_ref, ssq_got_ref, out_ref, *, features, first):
-    wide = out_ref.shape[1]
-    scale = lax.rsqrt((ssq_ref[...] + ssq_got_ref[...]) * (1.0 / features) + 1e-06)
+def combine_body(own_ref, got_ref, ssq_ref, extra_ref, out_ref, *, features, first):
+    seg, wide = out_ref.shape
+    extra = extra_ref[seg:, :].astype(F32)
+    parts = seg // extra.shape[1]
+    got = [extra[j : j + 1, :] + extra[parts + j : parts + j + 1, :] for j in range(parts)]
+    total = ssq_ref[...] + jnp.concatenate(got, axis=1)
+    scale = lax.rsqrt(total * (1.0 / features) + 1e-06)
     column = lax.dot_general(
         scale,
         jnp.full((scale.shape[0], wide), 1.0 / scale.shape[0], F32),
@@ -141,7 +160,7 @@
         preferred_element_type=F32,
     )
     own = own_ref[:, first : first + wide]
-    out_ref[...] = ((own + got_ref[...].astype(F32)) * column).astype(BF)
+    out_ref[...] = ((own + got_ref[:seg, :].astype(F32)) * column).astype(BF)
 
 
 def scores_of(q, keys):
@@ -173,34 +192,33 @@
     out_ref[...] = out.astype(BF)
 
 
-def output_of(pos, pieces, w_own, w_other, core):
+def output_of(pos, pieces, w_ref, core):
     a, _, b, y, _ = place(pos)
-    hd = w_own.shape[1]
+    hd = w_ref.shape[1] // 2
     total = None
     for i in range(4):
         yy = (y + i) & 3
         at = pl.multiple_of(((core + 2 * yy + 2 * y) & 7) * 2 * hd, 2 * hd)
-        own = w_own[pl.ds(at, 2 * hd), :]
-        other = w_other[pl.ds(at, 2 * hd), :]
+        both = w_ref[pl.ds(at, 2 * hd), :]
+        own, other = both[:, :hd], both[:, hd:]
         same = jnp.full(own.shape, a == b)
         rows = []
-        for both in (jnp.where(same, own, other), jnp.where(same, other, own)):
-            rows.append(jnp.concatenate([both[:hd], both[hd:]], axis=1))
+        for half in (jnp.where(same, own, other), jnp.where(same, other, own)):
+            rows.append(jnp.concatenate([half[:hd], half[hd:]], axis=1))
         part = jnp.dot(pieces[i][...], jnp.concatenate(rows, axis=0), preferred_element_type=F32)
         total = part if total is None else total + part
     return total
 
 
 def output_other_body(pos, *refs):
-    pieces, (w_own, w_other, send_ref) = refs[:4], refs[4:]
-    core = 1 - place(pos)[4]
-    send_ref[...] = output_of(pos, pieces, w_own, w_other, core).astype(BF)
+    pieces, (w_ref, send_ref) = refs[:4], refs[4:]
+    send_ref[...] = output_of(pos, pieces, w_ref, 1 - place(pos)[4]).astype(BF)
 
 
 def output_own_body(pos, *refs):
-    pieces, (w_own, w_other, hidden_ref, out_ref) = refs[:4], refs[4:]
+    pieces, (w_ref, hidden_ref, out_ref) = refs[:4], refs[4:]
     core = place(pos)[4]
-    out_ref[...] = hidden_ref[...].astype(F32) + output_of(pos, pieces, w_own, w_other, core)
+    out_ref[...] = hidden_ref[...].astype(F32) + output_of(pos, pieces, w_ref, core)
 
 
 def add_body(own_ref, got_ref, out_ref):
@@ -229,9 +247,10 @@
     pos = jnp.stack([ctx, tp]).astype(jnp.int32)
     same = (ctx >> 4) == (tp >> 3)
 
-    piece = permute(w_out[0], lambda a, z, b, y, k: (b, z + 4 * y, a, z // 4, k))
+    piece_a = permute(w_out[0], lambda a, z, b, y, k: (b, z + 4 * y, a, z // 4, k))
+    piece_b = permute(w_out[0], lambda a, z, b, y, k: (1 - b, z + 4 * y, a, z // 4, k))
     folded = (w_qkv[0].astype(F32) * norm_gain[0].astype(F32)[None, :, None]).astype(BF)
-    chunk = jnp.concatenate([folded[0], folded[1], folded[2], piece], axis=1)
+    chunk = jnp.concatenate([folded[0], folded[1], folded[2], piece_a, piece_b], axis=1)
     parts = gather_z(chunk, tp & 1)
 
     corner = {(0, 0): (0, 1), (0, 1): (1, 1), (1, 1): (1, 0), (1, 0): (0, 0)}
@@ -250,18 +269,17 @@
         nbytes=4 << 20,
         scalars=False,
     )(*blocks)
-    ssq_got = permute(ssq_send, swap_hi)
     kv_send, q_send, weights, out_w = call(
         project_other_body,
         (
-            shape((seg, 2 * hd), BF),
+            shape((seg + EXTRA, 2 * hd), BF),
             shape((seg, hd), BF),
             shape((16 * hd, 3 * hd), BF),
-            shape((16 * hd, hd), BF),
+            shape((16 * hd, 2 * hd), BF),
         ),
         flops=2 * seg * 8 * feats * 3 * hd,
         nbytes=8 << 20,
-    )(pos, *blocks, *parts)
+    )(pos, *blocks, *parts, ssq_send)
     kv_got = permute(kv_send, swap_hi)
     q_got = permute(q_send, swap_hi)
     own_part = call(
@@ -274,10 +292,10 @@
     def combine(got, first):
         return call(
             lambda *refs: combine_body(*refs, features=16 * feats, first=first),
-            shape(got.shape, BF),
+            shape((seg, got.shape[1]), BF),
             nbytes=1 << 20,
             scalars=False,
-        )(own_part, got, ssq, ssq_got)
+        )(own_part, got, ssq, kv_got)
 
     kv = combine(kv_got, hd)
     q = combine(q_got, 0)
@@ -294,15 +312,14 @@
     )(pos, q, kv, prev, e_own, sum_own)
 
     facing = permute(attended, lambda a, z, b, y, k: (a, z, 1 - b, y, k))
-    out_w_other = permute(out_w, swap_hi)
     pieces = around(jnp.concatenate([attended, facing], axis=1))
     sizes = dict(flops=2 * seg * feats * 8 * hd, nbytes=3 << 20)
     out_send = call(output_other_body, shape((seg, feats), BF), **sizes)(
-        pos, *pieces, out_w, out_w_other
+        pos, *pieces, out_w
     )
     out_got = permute(out_send, swap_core)
     out_own = call(output_own_body, shape((seg, feats), F32), **sizes)(
-        pos, *pieces, out_w, out_w_other, hidden
+        pos, *pieces, out_w, hidden
     )
     return call(add_body, shape((seg, feats), BF), scalars=False)(out_own, out_got)
 

time: 171 us -> 179 us (1.047)
  the two profiles are of different devices: /device:TPU:1 before, /device:TPU:4 now
where the time goes in v6:
time: 179 us; the launch traced here: 178 us
  starting transfers between devices  103 us (58%)
  waiting for transfers between devices  61.7 us (34%)
  Pallas kernels  11 us (6%)
  other arithmetic  1.96 us (1%)
    ppermute x25, starting transfers between devices, permute(): return lax.ppermute(value, AXES, pairs_of(target))  101 us
    ppermute x25, waiting for transfers between devices, permute(): return lax.ppermute(value, AXES, pairs_of(target))  61.7 us
    pallas_call x10, Pallas kernels, run(): pl.pallas_call(body, out_shape=outs, in_specs=specs, out_specs=jax.tree.m...  11 us
  transfers between devices with their start and end apart: 26, of which 12 were waited for; matrix products, arithmetic and copies ran while one was open for 1% of the time, Pallas kernels for 3%

profile of v6, /device:TPU:4, one launch (start us, length us, event | category | flops | bytes accessed | tf_op | source)
XLA Modules:
  0.0 177.9 jit_solution(6958296515612581840)
XLA Ops:
  0.0 3.1 %collective-permute-start.10 = (bf16[128,128]{1,0:T(8,128)(2,1)}, bf16[128,128]{1,0:T(8,128)(2,1)S(1)}, u32[]{:S(2)}, u32[]{:S(2)}) collective-permute-start(bf16[128,128]{1,0:T(8,128)(2,1)} %bitcast.21), channel_id=1, source_target_pairs={{0,256},{1,257},{2,320},{3,321},{4,384},{5,385},{6,448},{7,449},{8... | collective-permute-start | bytes 98312 | tf_op jit(solution)/shard_map/ppermute | solution.py:31
  3.1 7.1 %collective-permute-start.9 = (bf16[128,128]{1,0:T(8,128)(2,1)}, bf16[128,128]{1,0:T(8,128)(2,1)S(1)}, u32[]{:S(2)}, u32[]{:S(2)}) collective-permute-start(bf16[128,128]{1,0:T(8,128)(2,1)} %bitcast.22), channel_id=1, source_target_pairs={{0,0},{1,1},{2,64},{3,65},{4,128},{5,129},{6,192},{7,193},{8,256},... | collective-permute-start | bytes 98312 | tf_op jit(solution)/shard_map/ppermute | solution.py:31
  10.2 1.9 %collective-permute-start = (bf16[512,256]{1,0:T(8,128)(2,1)}, bf16[512,256]{1,0:T(8,128)(2,1)S(1)}, u32[]{:S(2)}, u32[]{:S(2)}) collective-permute-start(bf16[512,256]{1,0:T(8,128)(2,1)} %refs_5_.1), channel_id=1, source_target_pairs={{0,8},{1,9},{2,10},{3,11},{4,12},{5,13},{6,14},{7,15},{8,264},{9,2... | collective-permute-start | bytes 786440 | tf_op jit(solution)/shard_map/ppermute | solution.py:31
  12.2 1.9 %collective-permute-start.1 = (bf16[512,256]{1,0:T(8,128)(2,1)}, bf16[512,256]{1,0:T(8,128)(2,1)S(1)}, u32[]{:S(2)}, u32[]{:S(2)}) collective-permute-start(bf16[512,256]{1,0:T(8,128)(2,1)} %refs_5_.1), channel_id=1, source_target_pairs={{8,256},{9,257},{10,258},{11,259},{12,260},{13,261},{14,262},{15,2... | collective-permute-start | bytes 786440 | tf_op jit(solution)/shard_map/ppermute | solution.py:31
  15.8 2.9 %collective-permute-done = bf16[512,256]{1,0:T(8,128)(2,1)S(1)} collective-permute-done((bf16[512,256]{1,0:T(8,128)(2,1)}, bf16[512,256]{1,0:T(8,128)(2,1)S(1)}, u32[]{:S(2)}, u32[]{:S(2)}) %collective-permute-start) | collective-permute-done | bytes 262176 | tf_op jit(solution)/shard_map/ppermute | solution.py:31
  18.7 1.9 %collective-permute-done.1 = bf16[512,256]{1,0:T(8,128)(2,1)S(1)} collective-permute-done((bf16[512,256]{1,0:T(8,128)(2,1)}, bf16[512,256]{1,0:T(8,128)(2,1)S(1)}, u32[]{:S(2)}, u32[]{:S(2)}) %collective-permute-start.1) | collective-permute-done | bytes 262176 | tf_op jit(solution)/shard_map/ppermute | solution.py:31
  20.7 10.2 %collective-permute-start.7 = (bf16[1024,256]{1,0:T(8,128)(2,1)S(1)}, bf16[1024,256]{1,0:T(8,128)(2,1)S(1)}, u32[]{:S(2)}, u32[]{:S(2)}) collective-permute-start(bf16[1024,256]{1,0:T(8,128)(2,1)S(1)} %pad_maximum_fusion.1.refs_0_), channel_id=1, source_target_pairs={{0,2},{1,3},{2,4},{3,5},{4,6},{5,7},{6,0},{7,1},{8,10},{9,11},{10,... | collective-permute-start | bytes 1572872 | tf_op jit(solution)/shard_map/ppermute | solution.py:31
  31.0 11.7 %collective-permute-start.5 = (bf16[1024,256]{1,0:T(8,128)(2,1)S(1)}, bf16[1024,256]{1,0:T(8,128)(2,1)S(1)}, u32[]{:S(2)}, u32[]{:S(2)}) collective-permute-start(bf16[1024,256]{1,0:T(8,128)(2,1)S(1)} %pad_maximum_fusion.1.refs_0_), channel_id=1, source_target_pairs={{0,4},{1,5},{2,6},{3,7},{4,0},{5,1},{6,2},{7,3},{8,12},{9,13},{10,... | collective-permute-start | bytes 1572872 | tf_op jit(solution)/shard_map/ppermute | solution.py:31
  44.6 7.8 %collective-permute-start.11 = (bf16[128,640]{1,0:T(8,128)(2,1)S(1)}, bf16[128,640]{1,0:T(8,128)(2,1)S(1)}, u32[]{:S(2)}, u32[]{:S(2)}) collective-permute-start(bf16[128,640]{1,0:T(8,128)(2,1)S(1)} %constant_dynamic-update-slice_fusion), channel_id=1, source_target_pairs={{0,64},{1,65},{2,66},{3,67},{4,68},{5,69},{6,70},{7,71},{8,72},{9,... | collective-permute-start | bytes 491528 | tf_op jit(solution)/shard_map/ppermute | solution.py:31
  52.4 4.5 %collective-permute-start.3 = (bf16[1024,256]{1,0:T(8,128)(2,1)S(1)}, bf16[1024,256]{1,0:T(8,128)(2,1)S(1)}, u32[]{:S(2)}, u32[]{:S(2)}) collective-permute-start(bf16[1024,256]{1,0:T(8,128)(2,1)S(1)} %pad_maximum_fusion.1.refs_0_), channel_id=1, source_target_pairs={{0,6},{1,7},{2,0},{3,1},{4,2},{5,3},{6,4},{7,5},{8,14},{9,15},{10,... | collective-permute-start | bytes 1572872 | tf_op jit(solution)/shard_map/ppermute | solution.py:31
  57.0 6.3 %collective-permute-done.12 = bf16[128,640]{1,0:T(8,128)(2,1)S(1)} collective-permute-done((bf16[128,640]{1,0:T(8,128)(2,1)S(1)}, bf16[128,640]{1,0:T(8,128)(2,1)S(1)}, u32[]{:S(2)}, u32[]{:S(2)}) %collective-permute-start.12) | collective-permute-done | bytes 163872 | tf_op jit(solution)/shard_map/ppermute | solution.py:31
  65.2 7.3 %collective-permute-start.13 = (bf16[128,640]{1,0:T(8,128)(2,1)S(1)}, bf16[128,640]{1,0:T(8,128)(2,1)S(1)}, u32[]{:S(2)}, u32[]{:S(2)}) collective-permute-start(bf16[128,640]{1,0:T(8,128)(2,1)S(1)} %broadcast_select_fusion.2), channel_id=1, source_target_pairs={{0,192},{1,65},{2,194},{3,67},{4,196},{5,69},{6,198},{7,71},{8,200... | collective-permute-start | bytes 491528 | tf_op jit(solution)/shard_map/ppermute | solution.py:31
  72.6 1.9 %collective-permute-start.8 = (bf16[1024,256]{1,0:T(8,128)(2,1)S(1)}, bf16[1024,256]{1,0:T(8,128)(2,1)S(1)}, u32[]{:S(2)}, u32[]{:S(2)}) collective-permute-start(bf16[1024,256]{1,0:T(8,128)(2,1)S(1)} %collective-permute-done.7.refs_6_), channel_id=1, source_target_pairs={{0,1},{1,0},{2,3},{3,2},{4,5},{5,4},{6,7},{7,6},{8,9},{9,8},{10,11... | collective-permute-start | bytes 1572872 | tf_op jit(solution)/shard_map/ppermute | solution.py:31
  74.5 2.4 %collective-permute-start.6 = (bf16[1024,256]{1,0:T(8,128)(2,1)S(1)}, bf16[1024,256]{1,0:T(8,128)(2,1)S(1)}, u32[]{:S(2)}, u32[]{:S(2)}) collective-permute-start(bf16[1024,256]{1,0:T(8,128)(2,1)S(1)} %collective-permute-done.5.refs_4_), channel_id=1, source_target_pairs={{0,1},{1,0},{2,3},{3,2},{4,5},{5,4},{6,7},{7,6},{8,9},{9,8},{10,11... | collective-permute-start | bytes 1572872 | tf_op jit(solution)/shard_map/ppermute | solution.py:31
  79.1 6.7 %collective-permute-start.16 = (bf16[512,640]{1,0:T(8,128)(2,1)S(1)}, bf16[512,640]{1,0:T(8,128)(2,1)S(1)}, u32[]{:S(2)}, u32[]{:S(2)}) collective-permute-start(bf16[512,640]{1,0:T(8,128)(2,1)S(1)} %pad_maximum_fusion.refs_8_), channel_id=1, source_target_pairs={{0,240},{1,241},{2,242},{3,243},{4,244},{5,245},{6,246},{7,247},{8... | collective-permute-start | bytes 1966088 | tf_op jit(solution)/shard_map/ppermute | solution.py:31
  85.8 3.7 %collective-permute-start.4 = (bf16[1024,256]{1,0:T(8,128)(2,1)S(1)}, bf16[1024,256]{1,0:T(8,128)(2,1)S(1)}, u32[]{:S(2)}, u32[]{:S(2)}) collective-permute-start(bf16[1024,256]{1,0:T(8,128)(2,1)S(1)} %collective-permute-done.3.refs_2_), channel_id=1, source_target_pairs={{0,1},{1,0},{2,3},{3,2},{4,5},{5,4},{6,7},{7,6},{8,9},{9,8},{10,11... | collective-permute-start | bytes 1572872 | tf_op jit(solution)/shard_map/ppermute | solution.py:31
  89.5 2.2 %collective-permute-start.15 = (bf16[256,640]{1,0:T(8,128)(2,1)S(1)}, bf16[256,640]{1,0:T(8,128)(2,1)S(1)}, u32[]{:S(2)}, u32[]{:S(2)}) collective-permute-start(bf16[256,640]{1,0:T(8,128)(2,1)S(1)} %get-tuple-element.23), channel_id=1, source_target_pairs={{0,32},{1,33},{2,34},{3,35},{4,36},{5,37},{6,38},{7,39},{8,40},{9,... | collective-permute-start | bytes 983048 | tf_op jit(solution)/shard_map/ppermute | solution.py:31
  91.7 5.8 %collective-permute-start.14 = (bf16[256,640]{1,0:T(8,128)(2,1)S(1)}, bf16[256,640]{1,0:T(8,128)(2,1)S(1)}, u32[]{:S(2)}, u32[]{:S(2)}) collective-permute-start(bf16[256,640]{1,0:T(8,128)(2,1)S(1)} %get-tuple-element.24), channel_id=1, source_target_pairs={{0,224},{1,225},{2,226},{3,227},{4,228},{5,229},{6,230},{7,231},{8... | collective-permute-start | bytes 983048 | tf_op jit(solution)/shard_map/ppermute | solution.py:31
  98.8 15.0 %collective-permute-done.15.refs_10_ = bf16[256,640]{1,0:T(8,128)(2,1)S(1)} collective-permute-done((bf16[256,640]{1,0:T(8,128)(2,1)S(1)}, bf16[256,640]{1,0:T(8,128)(2,1)S(1)}, u32[]{:S(2)}, u32[]{:S(2)}) %collective-permute-start.15) | collective-permute-done | bytes 327712 | tf_op jit(solution)/shard_map/ppermute | solution.py:31
  115.5 2.0 %shard_map.47 = (bf16[528,256]{1,0:T(8,128)(2,1)S(1)}, bf16[512,128]{1,0:T(8,128)(2,1)S(1)}, bf16[2048,384]{1,0:T(8,128)(2,1)S(1)}, bf16[2048,256]{1,0:T(8,128)(2,1)S(1)}) custom-call(s32[2]{0:T(128)S(1)} %pad_add_fusion.pos, bf16[1024,256]{1,0:T(8,128)(2,1)S(1)} %pad_maximum_fusion.1.refs_0_, bf16[1024,256]{1,0:T(8,128)(2,1)S(1)} %collective-permute-done.2.refs_1_, ...), custom_call_target="tpu_custom_call" | custom-call | flops 805306368 | bytes 8388608 | tf_op jit(solution)/shard_map/pallas_call | solution.py:39
  121.3 7.5 %collective-permute-done.19.refs_3_.refs_1_ = bf16[528,256]{1,0:T(8,128)(2,1)S(1)} collective-permute-done((bf16[528,256]{1,0:T(8,128)(2,1)S(1)}, bf16[528,256]{1,0:T(8,128)(2,1)S(1)}, u32[]{:S(2)}, u32[]{:S(2)}) %collective-permute-start.19) | collective-permute-done | bytes 270368 | tf_op jit(solution)/shard_map/ppermute | solution.py:31
  129.4 1.9 %collective-permute-start.20 = (bf16[512,256]{1,0:T(8,128)(2,1)S(1)}, bf16[512,256]{1,0:T(8,128)(2,1)S(1)}, u32[]{:S(2)}, u32[]{:S(2)}) collective-permute-start(bf16[512,256]{1,0:T(8,128)(2,1)S(1)} %shard_map.50.kv_ref), channel_id=1, source_target_pairs={{0,16},{16,32},{32,48},{48,64},{64,80},{80,96},{96,112},{112,128},... | collective-permute-start | bytes 786440 | tf_op jit(solution)/shard_map/ppermute | solution.py:302
  131.3 1.9 %collective-permute-start.18 = (bf16[512,128]{1,0:T(8,128)(2,1)S(1)}, bf16[512,128]{1,0:T(8,128)(2,1)S(1)}, u32[]{:S(2)}, u32[]{:S(2)}) collective-permute-start(bf16[512,128]{1,0:T(8,128)(2,1)S(1)} %get-tuple-element.15), channel_id=1, source_target_pairs={{0,256},{1,257},{2,258},{3,259},{4,260},{5,261},{6,262},{7,263},{8... | collective-permute-start | bytes 393224 | tf_op jit(solution)/shard_map/ppermute | solution.py:31
  133.2 11.1 %collective-permute-done.18.refs_1_ = bf16[512,128]{1,0:T(8,128)(2,1)S(1)} collective-permute-done((bf16[512,128]{1,0:T(8,128)(2,1)S(1)}, bf16[512,128]{1,0:T(8,128)(2,1)S(1)}, u32[]{:S(2)}, u32[]{:S(2)}) %collective-permute-start.18) | collective-permute-done | bytes 131104 | tf_op jit(solution)/shard_map/ppermute | solution.py:31
  147.0 1.9 %collective-permute-start.21 = (bf16[512,128]{1,0:T(8,128)(2,1)S(1)}, bf16[512,128]{1,0:T(8,128)(2,1)S(1)}, u32[]{:S(2)}, u32[]{:S(2)}) collective-permute-start(bf16[512,128]{1,0:T(8,128)(2,1)S(1)} %shard_map.52), channel_id=1, source_target_pairs={{0,8},{1,9},{2,10},{3,11},{4,12},{5,13},{6,14},{7,15},{8,0},{9,1},... | collective-permute-start | bytes 393224 | tf_op jit(solution)/shard_map/ppermute | solution.py:31
  148.9 5.2 %collective-permute-done.21 = bf16[512,128]{1,0:T(8,128)(2,1)S(1)} collective-permute-done((bf16[512,128]{1,0:T(8,128)(2,1)S(1)}, bf16[512,128]{1,0:T(8,128)(2,1)S(1)}, u32[]{:S(2)}, u32[]{:S(2)}) %collective-permute-start.21) | collective-permute-done | bytes 131104 | tf_op jit(solution)/shard_map/ppermute | solution.py:31
  154.2 2.1 %collective-permute-start.24 = (bf16[512,256]{1,0:T(8,128)(2,1)S(1)}, bf16[512,256]{1,0:T(8,128)(2,1)S(1)}, u32[]{:S(2)}, u32[]{:S(2)}) collective-permute-start(bf16[512,256]{1,0:T(8,128)(2,1)S(1)} %pad_maximum_fusion.4.refs_0_), channel_id=1, source_target_pairs={{0,2},{1,3},{2,4},{3,5},{4,6},{5,7},{6,0},{7,1},{8,10},{9,11},{10,... | collective-permute-start | bytes 786440 | tf_op jit(solution)/shard_map/ppermute | solution.py:31
  156.2 3.7 %collective-permute-start.23 = (bf16[512,256]{1,0:T(8,128)(2,1)S(1)}, bf16[512,256]{1,0:T(8,128)(2,1)S(1)}, u32[]{:S(2)}, u32[]{:S(2)}) collective-permute-start(bf16[512,256]{1,0:T(8,128)(2,1)S(1)} %pad_maximum_fusion.4.refs_0_), channel_id=1, source_target_pairs={{0,4},{1,5},{2,6},{3,7},{4,0},{5,1},{6,2},{7,3},{8,12},{9,13},{10,... | collective-permute-start | bytes 786440 | tf_op jit(solution)/shard_map/ppermute | solution.py:31
  160.0 3.3 %collective-permute-start.22 = (bf16[512,256]{1,0:T(8,128)(2,1)S(1)}, bf16[512,256]{1,0:T(8,128)(2,1)S(1)}, u32[]{:S(2)}, u32[]{:S(2)}) collective-permute-start(bf16[512,256]{1,0:T(8,128)(2,1)S(1)} %pad_maximum_fusion.4.refs_0_), channel_id=1, source_target_pairs={{0,6},{1,7},{2,0},{3,1},{4,2},{5,3},{6,4},{7,5},{8,14},{9,15},{10,... | collective-permute-start | bytes 786440 | tf_op jit(solution)/shard_map/ppermute | solution.py:31
  163.3 6.9 %collective-permute-done.24.refs_3_ = bf16[512,256]{1,0:T(8,128)(2,1)S(1)} collective-permute-done((bf16[512,256]{1,0:T(8,128)(2,1)S(1)}, bf16[512,256]{1,0:T(8,128)(2,1)S(1)}, u32[]{:S(2)}, u32[]{:S(2)}) %collective-permute-start.24) | collective-permute-done | bytes 262176 | tf_op jit(solution)/shard_map/ppermute | solution.py:31
  170.2 2.5 %collective-permute-done.22.refs_1_ = bf16[512,256]{1,0:T(8,128)(2,1)S(1)} collective-permute-done((bf16[512,256]{1,0:T(8,128)(2,1)S(1)}, bf16[512,256]{1,0:T(8,128)(2,1)S(1)}, u32[]{:S(2)}, u32[]{:S(2)}) %collective-permute-start.22) | collective-permute-done | bytes 262176 | tf_op jit(solution)/shard_map/ppermute | solution.py:31
  173.7 1.9 %collective-permute-start.25 = (bf16[512,256]{1,0:T(8,128)(2,1)S(1)}, bf16[512,256]{1,0:T(8,128)(2,1)S(1)}, u32[]{:S(2)}, u32[]{:S(2)}) collective-permute-start(bf16[512,256]{1,0:T(8,128)(2,1)S(1)} %shard_map.54), channel_id=1, source_target_pairs={{0,1},{1,0},{2,3},{3,2},{4,5},{5,4},{6,7},{7,6},{8,9},{9,8},{10,11... | collective-permute-start | bytes 786440 | tf_op jit(solution)/shard_map/ppermute | solution.py:31
  (46 shorter events, 21.1 us)
Async XLA Ops:
  0.0 42.6 %collective-permute-start.10 = (bf16[128,128]{1,0:T(8,128)(2,1)}, bf16[128,128]{1,0:T(8,128)(2,1)S(1)}, u32[]{:S(2)}, u32[]{:S(2)}) collective-permute-start(bf16[128,128]{1,0:T(8,128)(2,1)} %bitcast.21), channel_id=1, source_target_pairs={{0,256},{1,257},{2,320},{3,321},{4,384},{5,385},{6,448},{7,449},{8... | collective-permute-start | bytes 98312 | tf_op jit(solution)/shard_map/ppermute | solution.py:31
  3.1 12.7 %collective-permute-start.9 = (bf16[128,128]{1,0:T(8,128)(2,1)}, bf16[128,128]{1,0:T(8,128)(2,1)S(1)}, u32[]{:S(2)}, u32[]{:S(2)}) collective-permute-start(bf16[128,128]{1,0:T(8,128)(2,1)} %bitcast.22), channel_id=1, source_target_pairs={{0,0},{1,1},{2,64},{3,65},{4,128},{5,129},{6,192},{7,193},{8,256},... | collective-permute-start | bytes 98312 | tf_op jit(solution)/shard_map/ppermute | solution.py:31
  10.2 8.5 %collective-permute-start = (bf16[512,256]{1,0:T(8,128)(2,1)}, bf16[512,256]{1,0:T(8,128)(2,1)S(1)}, u32[]{:S(2)}, u32[]{:S(2)}) collective-permute-start(bf16[512,256]{1,0:T(8,128)(2,1)} %refs_5_.1), channel_id=1, source_target_pairs={{0,8},{1,9},{2,10},{3,11},{4,12},{5,13},{6,14},{7,15},{8,264},{9,2... | collective-permute-start | bytes 786440 | tf_op jit(solution)/shard_map/ppermute | solution.py:31
  12.2 8.5 %collective-permute-start.1 = (bf16[512,256]{1,0:T(8,128)(2,1)}, bf16[512,256]{1,0:T(8,128)(2,1)S(1)}, u32[]{:S(2)}, u32[]{:S(2)}) collective-permute-start(bf16[512,256]{1,0:T(8,128)(2,1)} %refs_5_.1), channel_id=1, source_target_pairs={{8,256},{9,257},{10,258},{11,259},{12,260},{13,261},{14,262},{15,2... | collective-permute-start | bytes 786440 | tf_op jit(solution)/shard_map/ppermute | solution.py:31
  20.7 51.8 %collective-permute-start.7 = (bf16[1024,256]{1,0:T(8,128)(2,1)S(1)}, bf16[1024,256]{1,0:T(8,128)(2,1)S(1)}, u32[]{:S(2)}, u32[]{:S(2)}) collective-permute-start(bf16[1024,256]{1,0:T(8,128)(2,1)S(1)} %pad_maximum_fusion.1.refs_0_), channel_id=1, source_target_pairs={{0,2},{1,3},{2,4},{3,5},{4,6},{5,7},{6,0},{7,1},{8,10},{9,11},{10,... | collective-permute-start | bytes 1572872 | tf_op jit(solution)/shard_map/ppermute | solution.py:31
  31.0 43.5 %collective-permute-start.5 = (bf16[1024,256]{1,0:T(8,128)(2,1)S(1)}, bf16[1024,256]{1,0:T(8,128)(2,1)S(1)}, u32[]{:S(2)}, u32[]{:S(2)}) collective-permute-start(bf16[1024,256]{1,0:T(8,128)(2,1)S(1)} %pad_maximum_fusion.1.refs_0_), channel_id=1, source_target_pairs={{0,4},{1,5},{2,6},{3,7},{4,0},{5,1},{6,2},{7,3},{8,12},{9,13},{10,... | collective-permute-start | bytes 1572872 | tf_op jit(solution)/shard_map/ppermute | solution.py:31
  42.7 20.6 %collective-permute-start.12 = (bf16[128,640]{1,0:T(8,128)(2,1)S(1)}, bf16[128,640]{1,0:T(8,128)(2,1)S(1)}, u32[]{:S(2)}, u32[]{:S(2)}) collective-permute-start(bf16[128,640]{1,0:T(8,128)(2,1)S(1)} %constant_dynamic-update-slice_fusion), channel_id=1, source_target_pairs={{0,192},{1,193},{2,194},{3,195},{4,196},{5,197},{6,198},{7,199},{8... | collective-permute-start | bytes 491528 | tf_op jit(solution)/shard_map/ppermute | solution.py:31
  44.6 20.6 %collective-permute-start.11 = (bf16[128,640]{1,0:T(8,128)(2,1)S(1)}, bf16[128,640]{1,0:T(8,128)(2,1)S(1)}, u32[]{:S(2)}, u32[]{:S(2)}) collective-permute-start(bf16[128,640]{1,0:T(8,128)(2,1)S(1)} %constant_dynamic-update-slice_fusion), channel_id=1, source_target_pairs={{0,64},{1,65},{2,66},{3,67},{4,68},{5,69},{6,70},{7,71},{8,72},{9,... | collective-permute-start | bytes 491528 | tf_op jit(solution)/shard_map/ppermute | solution.py:31
  52.4 26.6 %collective-permute-start.3 = (bf16[1024,256]{1,0:T(8,128)(2,1)S(1)}, bf16[1024,256]{1,0:T(8,128)(2,1)S(1)}, u32[]{:S(2)}, u32[]{:S(2)}) collective-permute-start(bf16[1024,256]{1,0:T(8,128)(2,1)S(1)} %pad_maximum_fusion.1.refs_0_), channel_id=1, source_target_pairs={{0,6},{1,7},{2,0},{3,1},{4,2},{5,3},{6,4},{7,5},{8,14},{9,15},{10,... | collective-permute-start | bytes 1572872 | tf_op jit(solution)/shard_map/ppermute | solution.py:31
  63.3 22.5 %collective-permute-start.2 = (bf16[1024,256]{1,0:T(8,128)(2,1)S(1)}, bf16[1024,256]{1,0:T(8,128)(2,1)S(1)}, u32[]{:S(2)}, u32[]{:S(2)}) collective-permute-start(bf16[1024,256]{1,0:T(8,128)(2,1)S(1)} %pad_maximum_fusion.1.refs_0_), channel_id=1, source_target_pairs={{0,1},{1,0},{2,3},{3,2},{4,5},{5,4},{6,7},{7,6},{8,9},{9,8},{10,11... | collective-permute-start | bytes 1572872 | tf_op jit(solution)/shard_map/ppermute | solution.py:31
  65.2 11.8 %collective-permute-start.13 = (bf16[128,640]{1,0:T(8,128)(2,1)S(1)}, bf16[128,640]{1,0:T(8,128)(2,1)S(1)}, u32[]{:S(2)}, u32[]{:S(2)}) collective-permute-start(bf16[128,640]{1,0:T(8,128)(2,1)S(1)} %broadcast_select_fusion.2), channel_id=1, source_target_pairs={{0,192},{1,65},{2,194},{3,67},{4,196},{5,69},{6,198},{7,71},{8,200... | collective-permute-start | bytes 491528 | tf_op jit(solution)/shard_map/ppermute | solution.py:31
  72.6 17.0 %collective-permute-start.8 = (bf16[1024,256]{1,0:T(8,128)(2,1)S(1)}, bf16[1024,256]{1,0:T(8,128)(2,1)S(1)}, u32[]{:S(2)}, u32[]{:S(2)}) collective-permute-start(bf16[1024,256]{1,0:T(8,128)(2,1)S(1)} %collective-permute-done.7.refs_6_), channel_id=1, source_target_pairs={{0,1},{1,0},{2,3},{3,2},{4,5},{5,4},{6,7},{7,6},{8,9},{9,8},{10,11... | collective-permute-start | bytes 1572872 | tf_op jit(solution)/shard_map/ppermute | solution.py:31
  74.5 17.2 %collective-permute-start.6 = (bf16[1024,256]{1,0:T(8,128)(2,1)S(1)}, bf16[1024,256]{1,0:T(8,128)(2,1)S(1)}, u32[]{:S(2)}, u32[]{:S(2)}) collective-permute-start(bf16[1024,256]{1,0:T(8,128)(2,1)S(1)} %collective-permute-done.5.refs_4_), channel_id=1, source_target_pairs={{0,1},{1,0},{2,3},{3,2},{4,5},{5,4},{6,7},{7,6},{8,9},{9,8},{10,11... | collective-permute-start | bytes 1572872 | tf_op jit(solution)/shard_map/ppermute | solution.py:31
  77.1 38.4 %collective-permute-start.17 = (bf16[512,640]{1,0:T(8,128)(2,1)S(1)}, bf16[512,640]{1,0:T(8,128)(2,1)S(1)}, u32[]{:S(2)}, u32[]{:S(2)}) collective-permute-start(bf16[512,640]{1,0:T(8,128)(2,1)S(1)} %pad_maximum_fusion.refs_8_), channel_id=1, source_target_pairs={{0,16},{1,17},{2,18},{3,19},{4,20},{5,21},{6,22},{7,23},{8,24},{9,... | collective-permute-start | bytes 1966088 | tf_op jit(solution)/shard_map/ppermute | solution.py:31
  79.1 36.5 %collective-permute-start.16 = (bf16[512,640]{1,0:T(8,128)(2,1)S(1)}, bf16[512,640]{1,0:T(8,128)(2,1)S(1)}, u32[]{:S(2)}, u32[]{:S(2)}) collective-permute-start(bf16[512,640]{1,0:T(8,128)(2,1)S(1)} %pad_maximum_fusion.refs_8_), channel_id=1, source_target_pairs={{0,240},{1,241},{2,242},{3,243},{4,244},{5,245},{6,246},{7,247},{8... | collective-permute-start | bytes 1966088 | tf_op jit(solution)/shard_map/ppermute | solution.py:31
  85.8 11.9 %collective-permute-start.4 = (bf16[1024,256]{1,0:T(8,128)(2,1)S(1)}, bf16[1024,256]{1,0:T(8,128)(2,1)S(1)}, u32[]{:S(2)}, u32[]{:S(2)}) collective-permute-start(bf16[1024,256]{1,0:T(8,128)(2,1)S(1)} %collective-permute-done.3.refs_2_), channel_id=1, source_target_pairs={{0,1},{1,0},{2,3},{3,2},{4,5},{5,4},{6,7},{7,6},{8,9},{9,8},{10,11... | collective-permute-start | bytes 1572872 | tf_op jit(solution)/shard_map/ppermute | solution.py:31
  89.5 24.2 %collective-permute-start.15 = (bf16[256,640]{1,0:T(8,128)(2,1)S(1)}, bf16[256,640]{1,0:T(8,128)(2,1)S(1)}, u32[]{:S(2)}, u32[]{:S(2)}) collective-permute-start(bf16[256,640]{1,0:T(8,128)(2,1)S(1)} %get-tuple-element.23), channel_id=1, source_target_pairs={{0,32},{1,33},{2,34},{3,35},{4,36},{5,37},{6,38},{7,39},{8,40},{9,... | collective-permute-start | bytes 983048 | tf_op jit(solution)/shard_map/ppermute | solution.py:31
  91.7 23.8 %collective-permute-start.14 = (bf16[256,640]{1,0:T(8,128)(2,1)S(1)}, bf16[256,640]{1,0:T(8,128)(2,1)S(1)}, u32[]{:S(2)}, u32[]{:S(2)}) collective-permute-start(bf16[256,640]{1,0:T(8,128)(2,1)S(1)} %get-tuple-element.24), channel_id=1, source_target_pairs={{0,224},{1,225},{2,226},{3,227},{4,228},{5,229},{6,230},{7,231},{8... | collective-permute-start | bytes 983048 | tf_op jit(solution)/shard_map/ppermute | solution.py:31
  117.6 11.2 %collective-permute-start.19 = (bf16[528,256]{1,0:T(8,128)(2,1)S(1)}, bf16[528,256]{1,0:T(8,128)(2,1)S(1)}, u32[]{:S(2)}, u32[]{:S(2)}) collective-permute-start(bf16[528,256]{1,0:T(8,128)(2,1)S(1)} %get-tuple-element.17), channel_id=1, source_target_pairs={{0,256},{1,257},{2,258},{3,259},{4,260},{5,261},{6,262},{7,263},{8... | collective-permute-start | bytes 811016 | tf_op jit(solution)/shard_map/ppermute | solution.py:31
  129.4 15.8 %collective-permute-start.20 = (bf16[512,256]{1,0:T(8,128)(2,1)S(1)}, bf16[512,256]{1,0:T(8,128)(2,1)S(1)}, u32[]{:S(2)}, u32[]{:S(2)}) collective-permute-start(bf16[512,256]{1,0:T(8,128)(2,1)S(1)} %shard_map.50.kv_ref), channel_id=1, source_target_pairs={{0,16},{16,32},{32,48},{48,64},{64,80},{80,96},{96,112},{112,128},... | collective-permute-start | bytes 786440 | tf_op jit(solution)/shard_map/ppermute | solution.py:302
  131.3 13.0 %collective-permute-start.18 = (bf16[512,128]{1,0:T(8,128)(2,1)S(1)}, bf16[512,128]{1,0:T(8,128)(2,1)S(1)}, u32[]{:S(2)}, u32[]{:S(2)}) collective-permute-start(bf16[512,128]{1,0:T(8,128)(2,1)S(1)} %get-tuple-element.15), channel_id=1, source_target_pairs={{0,256},{1,257},{2,258},{3,259},{4,260},{5,261},{6,262},{7,263},{8... | collective-permute-start | bytes 393224 | tf_op jit(solution)/shard_map/ppermute | solution.py:31
  147.0 7.1 %collective-permute-start.21 = (bf16[512,128]{1,0:T(8,128)(2,1)S(1)}, bf16[512,128]{1,0:T(8,128)(2,1)S(1)}, u32[]{:S(2)}, u32[]{:S(2)}) collective-permute-start(bf16[512,128]{1,0:T(8,128)(2,1)S(1)} %shard_map.52), channel_id=1, source_target_pairs={{0,8},{1,9},{2,10},{3,11},{4,12},{5,13},{6,14},{7,15},{8,0},{9,1},... | collective-permute-start | bytes 393224 | tf_op jit(solution)/shard_map/ppermute | solution.py:31
  154.2 21.5 %copy-start = (bf16[512,256]{1,0:T(8,128)(2,1)S(1)}, bf16[512,256]{1,0:T(8,128)(2,1)}, u32[]{:S(2)}) copy-start(bf16[512,256]{1,0:T(8,128)(2,1)} %refs_5_.1) | copy-start | bytes 786436
  154.2 16.0 %collective-permute-start.24 = (bf16[512,256]{1,0:T(8,128)(2,1)S(1)}, bf16[512,256]{1,0:T(8,128)(2,1)S(1)}, u32[]{:S(2)}, u32[]{:S(2)}) collective-permute-start(bf16[512,256]{1,0:T(8,128)(2,1)S(1)} %pad_maximum_fusion.4.refs_0_), channel_id=1, source_target_pairs={{0,2},{1,3},{2,4},{3,5},{4,6},{5,7},{6,0},{7,1},{8,10},{9,11},{10,... | collective-permute-start | bytes 786440 | tf_op jit(solution)/shard_map/ppermute | solution.py:31
  156.2 14.0 %collective-permute-start.23 = (bf16[512,256]{1,0:T(8,128)(2,1)S(1)}, bf16[512,256]{1,0:T(8,128)(2,1)S(1)}, u32[]{:S(2)}, u32[]{:S(2)}) collective-permute-start(bf16[512,256]{1,0:T(8,128)(2,1)S(1)} %pad_maximum_fusion.4.refs_0_), channel_id=1, source_target_pairs={{0,4},{1,5},{2,6},{3,7},{4,0},{5,1},{6,2},{7,3},{8,12},{9,13},{10,... | collective-permute-start | bytes 786440 | tf_op jit(solution)/shard_map/ppermute | solution.py:31
  160.0 12.8 %collective-permute-start.22 = (bf16[512,256]{1,0:T(8,128)(2,1)S(1)}, bf16[512,256]{1,0:T(8,128)(2,1)S(1)}, u32[]{:S(2)}, u32[]{:S(2)}) collective-permute-start(bf16[512,256]{1,0:T(8,128)(2,1)S(1)} %pad_maximum_fusion.4.refs_0_), channel_id=1, source_target_pairs={{0,6},{1,7},{2,0},{3,1},{4,2},{5,3},{6,4},{7,5},{8,14},{9,15},{10,... | collective-permute-start | bytes 786440 | tf_op jit(solution)/shard_map/ppermute | solution.py:31
  173.7 3.4 %collective-permute-start.25 = (bf16[512,256]{1,0:T(8,128)(2,1)S(1)}, bf16[512,256]{1,0:T(8,128)(2,1)S(1)}, u32[]{:S(2)}, u32[]{:S(2)}) collective-permute-start(bf16[512,256]{1,0:T(8,128)(2,1)S(1)} %shard_map.54), channel_id=1, source_target_pairs={{0,1},{1,0},{2,3},{3,2},{4,5},{5,4},{6,7},{7,6},{8,9},{9,8},{10,11... | collective-permute-start | bytes 786440 | tf_op jit(solution)/shard_map/ppermute | solution.py:31

commit v7 on v6

--- a/solution.py
+++ b/solution.py
@@ -192,33 +192,34 @@
     out_ref[...] = out.astype(BF)
 
 
-def output_of(pos, pieces, w_ref, core):
+def output_of(pos, pieces, w_own, w_other, core):
     a, _, b, y, _ = place(pos)
-    hd = w_ref.shape[1] // 2
+    hd = w_own.shape[1]
     total = None
     for i in range(4):
         yy = (y + i) & 3
         at = pl.multiple_of(((core + 2 * yy + 2 * y) & 7) * 2 * hd, 2 * hd)
-        both = w_ref[pl.ds(at, 2 * hd), :]
-        own, other = both[:, :hd], both[:, hd:]
+        own = w_own[pl.ds(at, 2 * hd), :]
+        other = w_other[pl.ds(at, 2 * hd), :]
         same = jnp.full(own.shape, a == b)
         rows = []
-        for half in (jnp.where(same, own, other), jnp.where(same, other, own)):
-            rows.append(jnp.concatenate([half[:hd], half[hd:]], axis=1))
+        for both in (jnp.where(same, own, other), jnp.where(same, other, own)):
+            rows.append(jnp.concatenate([both[:hd], both[hd:]], axis=1))
         part = jnp.dot(pieces[i][...], jnp.concatenate(rows, axis=0), preferred_element_type=F32)
         total = part if total is None else total + part
     return total
 
 
 def output_other_body(pos, *refs):
-    pieces, (w_ref, send_ref) = refs[:4], refs[4:]
-    send_ref[...] = output_of(pos, pieces, w_ref, 1 - place(pos)[4]).astype(BF)
+    pieces, (w_own, w_other, send_ref) = refs[:4], refs[4:]
+    core = 1 - place(pos)[4]
+    send_ref[...] = output_of(pos, pieces, w_own, w_other, core).astype(BF)
 
 
 def output_own_body(pos, *refs):
-    pieces, (w_ref, hidden_ref, out_ref) = refs[:4], refs[4:]
+    pieces, (w_own, w_other, hidden_ref, out_ref) = refs[:4], refs[4:]
     core = place(pos)[4]
-    out_ref[...] = hidden_ref[...].astype(F32) + output_of(pos, pieces, w_ref, core)
+    out_ref[...] = hidden_ref[...].astype(F32) + output_of(pos, pieces, w_own, w_other, core)
 
 
 def add_body(own_ref, got_ref, out_ref):
@@ -247,10 +248,9 @@
     pos = jnp.stack([ctx, tp]).astype(jnp.int32)
     same = (ctx >> 4) == (tp >> 3)
 
-    piece_a = permute(w_out[0], lambda a, z, b, y, k: (b, z + 4 * y, a, z // 4, k))
-    piece_b = permute(w_out[0], lambda a, z, b, y, k: (1 - b, z + 4 * y, a, z // 4, k))
+    piece = permute(w_out[0], lambda a, z, b, y, k: (b, z + 4 * y, a, z // 4, k))
     folded = (w_qkv[0].astype(F32) * norm_gain[0].astype(F32)[None, :, None]).astype(BF)
-    chunk = jnp.concatenate([folded[0], folded[1], folded[2], piece_a, piece_b], axis=1)
+    chunk = jnp.concatenate([folded[0], folded[1], folded[2], piece], axis=1)
     parts = gather_z(chunk, tp & 1)
 
     corner = {(0, 0): (0, 1), (0, 1): (1, 1), (1, 1): (1, 0), (1, 0): (0, 0)}
@@ -275,7 +275,7 @@
             shape((seg + EXTRA, 2 * hd), BF),
             shape((seg, hd), BF),
             shape((16 * hd, 3 * hd), BF),
-            shape((16 * hd, 2 * hd), BF),
+            shape((16 * hd, hd), BF),
         ),
         flops=2 * seg * 8 * feats * 3 * hd,
         nbytes=8 << 20,
@@ -312,14 +312,15 @@
     )(pos, q, kv, prev, e_own, sum_own)
 
     facing = permute(attended, lambda a, z, b, y, k: (a, z, 1 - b, y, k))
+    out_w_other = permute(out_w, swap_hi)
     pieces = around(jnp.concatenate([attended, facing], axis=1))
     sizes = dict(flops=2 * seg * feats * 8 * hd, nbytes=3 << 20)
     out_send = call(output_other_body, shape((seg, feats), BF), **sizes)(
-        pos, *pieces, out_w
+        pos, *pieces, out_w, out_w_other
     )
     out_got = permute(out_send, swap_core)
     out_own = call(output_own_body, shape((seg, feats), F32), **sizes)(
-        pos, *pieces, out_w, hidden
+        pos, *pieces, out_w, out_w_other, hidden
     )
     return call(add_body, shape((seg, feats), BF), scalars=False)(out_own, out_got)
 

time: 179 us -> 167 us (0.933)
  the two profiles are of different devices: /device:TPU:4 before, /device:TPU:1 now
where the time goes in v7:
time: 167 us; the launch traced here: 166 us
  starting transfers between devices  99.7 us (60%)
  waiting for transfers between devices  53.1 us (32%)
  Pallas kernels  11 us (7%)
  other arithmetic  2 us (1%)
    ppermute x25, starting transfers between devices, permute(): return lax.ppermute(value, AXES, pairs_of(target))  98.4 us
    ppermute x25, waiting for transfers between devices, permute(): return lax.ppermute(value, AXES, pairs_of(target))  53.1 us
    pallas_call x10, Pallas kernels, run(): pl.pallas_call(body, out_shape=outs, in_specs=specs, out_specs=jax.tree.m...  11 us
  transfers between devices with their start and end apart: 26, of which 12 were waited for; matrix products, arithmetic and copies ran while one was open for 1% of the time, Pallas kernels for 4%

profile of v7, /device:TPU:1, one launch (start us, length us, event | category | flops | bytes accessed | tf_op | source)
XLA Modules:
  0.0 166.2 jit_solution(1551684586492718631)
XLA Ops:
  0.0 4.1 %collective-permute-start = (bf16[512,256]{1,0:T(8,128)(2,1)}, bf16[512,256]{1,0:T(8,128)(2,1)S(1)}, u32[]{:S(2)}, u32[]{:S(2)}) collective-permute-start(bf16[512,256]{1,0:T(8,128)(2,1)} %refs_6_.1), channel_id=1, source_target_pairs={{0,8},{1,9},{2,10},{3,11},{4,12},{5,13},{6,14},{7,15},{8,264},{9,2... | collective-permute-start | bytes 786440 | tf_op jit(solution)/shard_map/ppermute | solution.py:31
  6.8 2.7 %collective-permute-done = bf16[512,256]{1,0:T(8,128)(2,1)S(1)} collective-permute-done((bf16[512,256]{1,0:T(8,128)(2,1)}, bf16[512,256]{1,0:T(8,128)(2,1)S(1)}, u32[]{:S(2)}, u32[]{:S(2)}) %collective-permute-start) | collective-permute-done | bytes 262176 | tf_op jit(solution)/shard_map/ppermute | solution.py:31
  10.6 7.8 %collective-permute-start.7 = (bf16[1024,256]{1,0:T(8,128)(2,1)S(1)}, bf16[1024,256]{1,0:T(8,128)(2,1)S(1)}, u32[]{:S(2)}, u32[]{:S(2)}) collective-permute-start(bf16[1024,256]{1,0:T(8,128)(2,1)S(1)} %pad_maximum_fusion.refs_0_), channel_id=1, source_target_pairs={{0,2},{1,3},{2,4},{3,5},{4,6},{5,7},{6,0},{7,1},{8,10},{9,11},{10,... | collective-permute-start | bytes 1572872 | tf_op jit(solution)/shard_map/ppermute | solution.py:31
  18.4 10.1 %collective-permute-start.5 = (bf16[1024,256]{1,0:T(8,128)(2,1)S(1)}, bf16[1024,256]{1,0:T(8,128)(2,1)S(1)}, u32[]{:S(2)}, u32[]{:S(2)}) collective-permute-start(bf16[1024,256]{1,0:T(8,128)(2,1)S(1)} %pad_maximum_fusion.refs_0_), channel_id=1, source_target_pairs={{0,4},{1,5},{2,6},{3,7},{4,0},{5,1},{6,2},{7,3},{8,12},{9,13},{10,... | collective-permute-start | bytes 1572872 | tf_op jit(solution)/shard_map/ppermute | solution.py:31
  28.6 4.5 %collective-permute-start.11 = (bf16[128,512]{1,0:T(8,128)(2,1)S(1)}, bf16[128,512]{1,0:T(8,128)(2,1)S(1)}, u32[]{:S(2)}, u32[]{:S(2)}) collective-permute-start(bf16[128,512]{1,0:T(8,128)(2,1)S(1)} %pad_maximum_fusion.6), channel_id=1, source_target_pairs={{0,192},{1,193},{2,194},{3,195},{4,196},{5,197},{6,198},{7,199},{8... | collective-permute-start | bytes 393224 | tf_op jit(solution)/shard_map/ppermute | solution.py:31
  33.2 3.0 %collective-permute-start.3 = (bf16[1024,256]{1,0:T(8,128)(2,1)S(1)}, bf16[1024,256]{1,0:T(8,128)(2,1)S(1)}, u32[]{:S(2)}, u32[]{:S(2)}) collective-permute-start(bf16[1024,256]{1,0:T(8,128)(2,1)S(1)} %pad_maximum_fusion.refs_0_), channel_id=1, source_target_pairs={{0,6},{1,7},{2,0},{3,1},{4,2},{5,3},{6,4},{7,5},{8,14},{9,15},{10,... | collective-permute-start | bytes 1572872 | tf_op jit(solution)/shard_map/ppermute | solution.py:31
  36.1 5.6 %collective-permute-start.10 = (bf16[128,512]{1,0:T(8,128)(2,1)S(1)}, bf16[128,512]{1,0:T(8,128)(2,1)S(1)}, u32[]{:S(2)}, u32[]{:S(2)}) collective-permute-start(bf16[128,512]{1,0:T(8,128)(2,1)S(1)} %pad_maximum_fusion.6), channel_id=1, source_target_pairs={{0,64},{1,65},{2,66},{3,67},{4,68},{5,69},{6,70},{7,71},{8,72},{9,... | collective-permute-start | bytes 393224 | tf_op jit(solution)/shard_map/ppermute | solution.py:31
  41.8 5.9 %collective-permute-done.11 = bf16[128,512]{1,0:T(8,128)(2,1)S(1)} collective-permute-done((bf16[128,512]{1,0:T(8,128)(2,1)S(1)}, bf16[128,512]{1,0:T(8,128)(2,1)S(1)}, u32[]{:S(2)}, u32[]{:S(2)}) %collective-permute-start.11) | collective-permute-done | bytes 131104 | tf_op jit(solution)/shard_map/ppermute | solution.py:31
  47.7 3.0 %collective-permute-start.2 = (bf16[1024,256]{1,0:T(8,128)(2,1)S(1)}, bf16[1024,256]{1,0:T(8,128)(2,1)S(1)}, u32[]{:S(2)}, u32[]{:S(2)}) collective-permute-start(bf16[1024,256]{1,0:T(8,128)(2,1)S(1)} %pad_maximum_fusion.refs_0_), channel_id=1, source_target_pairs={{0,1},{1,0},{2,3},{3,2},{4,5},{5,4},{6,7},{7,6},{8,9},{9,8},{10,11... | collective-permute-start | bytes 1572872 | tf_op jit(solution)/shard_map/ppermute | solution.py:31
  50.7 1.9 %collective-permute-start.8 = (bf16[1024,256]{1,0:T(8,128)(2,1)S(1)}, bf16[1024,256]{1,0:T(8,128)(2,1)S(1)}, u32[]{:S(2)}, u32[]{:S(2)}) collective-permute-start(bf16[1024,256]{1,0:T(8,128)(2,1)S(1)} %collective-permute-done.7.refs_6_), channel_id=1, source_target_pairs={{0,1},{1,0},{2,3},{3,2},{4,5},{5,4},{6,7},{7,6},{8,9},{9,8},{10,11... | collective-permute-start | bytes 1572872 | tf_op jit(solution)/shard_map/ppermute | solution.py:31
  52.6 2.4 %collective-permute-start.6 = (bf16[1024,256]{1,0:T(8,128)(2,1)S(1)}, bf16[1024,256]{1,0:T(8,128)(2,1)S(1)}, u32[]{:S(2)}, u32[]{:S(2)}) collective-permute-start(bf16[1024,256]{1,0:T(8,128)(2,1)S(1)} %collective-permute-done.5.refs_4_), channel_id=1, source_target_pairs={{0,1},{1,0},{2,3},{3,2},{4,5},{5,4},{6,7},{7,6},{8,9},{9,8},{10,11... | collective-permute-start | bytes 1572872 | tf_op jit(solution)/shard_map/ppermute | solution.py:31
  55.1 4.1 %collective-permute-start.12 = (bf16[128,512]{1,0:T(8,128)(2,1)S(1)}, bf16[128,512]{1,0:T(8,128)(2,1)S(1)}, u32[]{:S(2)}, u32[]{:S(2)}) collective-permute-start(bf16[128,512]{1,0:T(8,128)(2,1)S(1)} %broadcast_select_fusion.2), channel_id=1, source_target_pairs={{0,192},{1,65},{2,194},{3,67},{4,196},{5,69},{6,198},{7,71},{8,200... | collective-permute-start | bytes 393224 | tf_op jit(solution)/shard_map/ppermute | solution.py:31
  59.2 2.6 %collective-permute-start.4 = (bf16[1024,256]{1,0:T(8,128)(2,1)S(1)}, bf16[1024,256]{1,0:T(8,128)(2,1)S(1)}, u32[]{:S(2)}, u32[]{:S(2)}) collective-permute-start(bf16[1024,256]{1,0:T(8,128)(2,1)S(1)} %collective-permute-done.3.refs_2_), channel_id=1, source_target_pairs={{0,1},{1,0},{2,3},{3,2},{4,5},{5,4},{6,7},{7,6},{8,9},{9,8},{10,11... | collective-permute-start | bytes 1572872 | tf_op jit(solution)/shard_map/ppermute | solution.py:31
  61.8 6.5 %collective-permute-done.12 = bf16[128,512]{1,0:T(8,128)(2,1)S(1)} collective-permute-done((bf16[128,512]{1,0:T(8,128)(2,1)S(1)}, bf16[128,512]{1,0:T(8,128)(2,1)S(1)}, u32[]{:S(2)}, u32[]{:S(2)}) %collective-permute-start.12) | collective-permute-done | bytes 131104 | tf_op jit(solution)/shard_map/ppermute | solution.py:31
  68.3 1.9 %collective-permute-start.16 = (bf16[512,512]{1,0:T(8,128)(2,1)S(1)}, bf16[512,512]{1,0:T(8,128)(2,1)S(1)}, u32[]{:S(2)}, u32[]{:S(2)}) collective-permute-start(bf16[512,512]{1,0:T(8,128)(2,1)S(1)} %pad_maximum_fusion.1.refs_8_), channel_id=1, source_target_pairs={{0,16},{1,17},{2,18},{3,19},{4,20},{5,21},{6,22},{7,23},{8,24},{9,... | collective-permute-start | bytes 1572872 | tf_op jit(solution)/shard_map/ppermute | solution.py:31
  70.3 4.6 %collective-permute-start.15 = (bf16[512,512]{1,0:T(8,128)(2,1)S(1)}, bf16[512,512]{1,0:T(8,128)(2,1)S(1)}, u32[]{:S(2)}, u32[]{:S(2)}) collective-permute-start(bf16[512,512]{1,0:T(8,128)(2,1)S(1)} %pad_maximum_fusion.1.refs_8_), channel_id=1, source_target_pairs={{0,240},{1,241},{2,242},{3,243},{4,244},{5,245},{6,246},{7,247},{8... | collective-permute-start | bytes 1572872 | tf_op jit(solution)/shard_map/ppermute | solution.py:31
  76.9 5.5 %collective-permute-start.13 = (bf16[256,512]{1,0:T(8,128)(2,1)S(1)}, bf16[256,512]{1,0:T(8,128)(2,1)S(1)}, u32[]{:S(2)}, u32[]{:S(2)}) collective-permute-start(bf16[256,512]{1,0:T(8,128)(2,1)S(1)} %get-tuple-element.24), channel_id=1, source_target_pairs={{0,224},{1,225},{2,226},{3,227},{4,228},{5,229},{6,230},{7,231},{8... | collective-permute-start | bytes 786440 | tf_op jit(solution)/shard_map/ppermute | solution.py:31
  83.6 8.5 %collective-permute-done.14.refs_10_ = bf16[256,512]{1,0:T(8,128)(2,1)S(1)} collective-permute-done((bf16[256,512]{1,0:T(8,128)(2,1)S(1)}, bf16[256,512]{1,0:T(8,128)(2,1)S(1)}, u32[]{:S(2)}, u32[]{:S(2)}) %collective-permute-start.14) | collective-permute-done | bytes 262176 | tf_op jit(solution)/shard_map/ppermute | solution.py:31
  92.1 4.0 %collective-permute-done.13.refs_9_ = bf16[256,512]{1,0:T(8,128)(2,1)S(1)} collective-permute-done((bf16[256,512]{1,0:T(8,128)(2,1)S(1)}, bf16[256,512]{1,0:T(8,128)(2,1)S(1)}, u32[]{:S(2)}, u32[]{:S(2)}) %collective-permute-start.13) | collective-permute-done | bytes 262176 | tf_op jit(solution)/shard_map/ppermute | solution.py:31
  96.1 2.0 %shard_map.47 = (bf16[528,256]{1,0:T(8,128)(2,1)S(1)}, bf16[512,128]{1,0:T(8,128)(2,1)S(1)}, bf16[2048,384]{1,0:T(8,128)(2,1)S(1)}, bf16[2048,128]{1,0:T(8,128)(2,1)S(1)}) custom-call(s32[2]{0:T(128)S(1)} %pad_add_fusion.pos, bf16[1024,256]{1,0:T(8,128)(2,1)S(1)} %pad_maximum_fusion.refs_0_, bf16[1024,256]{1,0:T(8,128)(2,1)S(1)} %collective-permute-done.2.refs_1_, ...), custom_call_target="tpu_custom_call" | custom-call | flops 805306368 | bytes 8388608 | tf_op jit(solution)/shard_map/pallas_call | solution.py:39
  98.2 5.0 %collective-permute-start.18 = (bf16[528,256]{1,0:T(8,128)(2,1)S(1)}, bf16[528,256]{1,0:T(8,128)(2,1)S(1)}, u32[]{:S(2)}, u32[]{:S(2)}) collective-permute-start(bf16[528,256]{1,0:T(8,128)(2,1)S(1)} %get-tuple-element.17), channel_id=1, source_target_pairs={{0,256},{1,257},{2,258},{3,259},{4,260},{5,261},{6,262},{7,263},{8... | collective-permute-start | bytes 811016 | tf_op jit(solution)/shard_map/ppermute | solution.py:31
  105.0 2.5 %collective-permute-done.18.refs_3_.refs_1_ = bf16[528,256]{1,0:T(8,128)(2,1)S(1)} collective-permute-done((bf16[528,256]{1,0:T(8,128)(2,1)S(1)}, bf16[528,256]{1,0:T(8,128)(2,1)S(1)}, u32[]{:S(2)}, u32[]{:S(2)}) %collective-permute-start.18) | collective-permute-done | bytes 270368 | tf_op jit(solution)/shard_map/ppermute | solution.py:31
  109.4 5.0 %collective-permute-start.17 = (bf16[512,128]{1,0:T(8,128)(2,1)S(1)}, bf16[512,128]{1,0:T(8,128)(2,1)S(1)}, u32[]{:S(2)}, u32[]{:S(2)}) collective-permute-start(bf16[512,128]{1,0:T(8,128)(2,1)S(1)} %get-tuple-element.15), channel_id=1, source_target_pairs={{0,256},{1,257},{2,258},{3,259},{4,260},{5,261},{6,262},{7,263},{8... | collective-permute-start | bytes 393224 | tf_op jit(solution)/shard_map/ppermute | solution.py:31
  116.4 2.8 %collective-permute-done.17.refs_1_ = bf16[512,128]{1,0:T(8,128)(2,1)S(1)} collective-permute-done((bf16[512,128]{1,0:T(8,128)(2,1)S(1)}, bf16[512,128]{1,0:T(8,128)(2,1)S(1)}, u32[]{:S(2)}, u32[]{:S(2)}) %collective-permute-start.17) | collective-permute-done | bytes 131104 | tf_op jit(solution)/shard_map/ppermute | solution.py:31
  121.8 9.5 %collective-permute-start.20 = (bf16[512,128]{1,0:T(8,128)(2,1)S(1)}, bf16[512,128]{1,0:T(8,128)(2,1)S(1)}, u32[]{:S(2)}, u32[]{:S(2)}) collective-permute-start(bf16[512,128]{1,0:T(8,128)(2,1)S(1)} %shard_map.52), channel_id=1, source_target_pairs={{0,8},{1,9},{2,10},{3,11},{4,12},{5,13},{6,14},{7,15},{8,0},{9,1},... | collective-permute-start | bytes 393224 | tf_op jit(solution)/shard_map/ppermute | solution.py:31
  131.3 10.1 %collective-permute-done.20 = bf16[512,128]{1,0:T(8,128)(2,1)S(1)} collective-permute-done((bf16[512,128]{1,0:T(8,128)(2,1)S(1)}, bf16[512,128]{1,0:T(8,128)(2,1)S(1)}, u32[]{:S(2)}, u32[]{:S(2)}) %collective-permute-start.20) | collective-permute-done | bytes 131104 | tf_op jit(solution)/shard_map/ppermute | solution.py:31
  143.3 4.1 %collective-permute-start.22 = (bf16[512,256]{1,0:T(8,128)(2,1)S(1)}, bf16[512,256]{1,0:T(8,128)(2,1)S(1)}, u32[]{:S(2)}, u32[]{:S(2)}) collective-permute-start(bf16[512,256]{1,0:T(8,128)(2,1)S(1)} %pad_maximum_fusion.5.refs_0_), channel_id=1, source_target_pairs={{0,4},{1,5},{2,6},{3,7},{4,0},{5,1},{6,2},{7,3},{8,12},{9,13},{10,... | collective-permute-start | bytes 786440 | tf_op jit(solution)/shard_map/ppermute | solution.py:31
  147.5 2.3 %collective-permute-start.21 = (bf16[512,256]{1,0:T(8,128)(2,1)S(1)}, bf16[512,256]{1,0:T(8,128)(2,1)S(1)}, u32[]{:S(2)}, u32[]{:S(2)}) collective-permute-start(bf16[512,256]{1,0:T(8,128)(2,1)S(1)} %pad_maximum_fusion.5.refs_0_), channel_id=1, source_target_pairs={{0,6},{1,7},{2,0},{3,1},{4,2},{5,3},{6,4},{7,5},{8,14},{9,15},{10,... | collective-permute-start | bytes 786440 | tf_op jit(solution)/shard_map/ppermute | solution.py:31
  149.9 2.4 %collective-permute-done.23.refs_3_ = bf16[512,256]{1,0:T(8,128)(2,1)S(1)} collective-permute-done((bf16[512,256]{1,0:T(8,128)(2,1)S(1)}, bf16[512,256]{1,0:T(8,128)(2,1)S(1)}, u32[]{:S(2)}, u32[]{:S(2)}) %collective-permute-start.23) | collective-permute-done | bytes 262176 | tf_op jit(solution)/shard_map/ppermute | solution.py:31
  152.3 4.9 %collective-permute-done.22.refs_2_ = bf16[512,256]{1,0:T(8,128)(2,1)S(1)} collective-permute-done((bf16[512,256]{1,0:T(8,128)(2,1)S(1)}, bf16[512,256]{1,0:T(8,128)(2,1)S(1)}, u32[]{:S(2)}, u32[]{:S(2)}) %collective-permute-start.22) | collective-permute-done | bytes 262176 | tf_op jit(solution)/shard_map/ppermute | solution.py:31
  157.1 2.7 %collective-permute-done.21.refs_1_ = bf16[512,256]{1,0:T(8,128)(2,1)S(1)} collective-permute-done((bf16[512,256]{1,0:T(8,128)(2,1)S(1)}, bf16[512,256]{1,0:T(8,128)(2,1)S(1)}, u32[]{:S(2)}, u32[]{:S(2)}) %collective-permute-start.21) | collective-permute-done | bytes 262176 | tf_op jit(solution)/shard_map/ppermute | solution.py:31
  160.9 3.5 %collective-permute-start.25 = (bf16[512,256]{1,0:T(8,128)(2,1)S(1)}, bf16[512,256]{1,0:T(8,128)(2,1)S(1)}, u32[]{:S(2)}, u32[]{:S(2)}) collective-permute-start(bf16[512,256]{1,0:T(8,128)(2,1)S(1)} %shard_map.54), channel_id=1, source_target_pairs={{0,1},{1,0},{2,3},{3,2},{4,5},{5,4},{6,7},{7,6},{8,9},{9,8},{10,11... | collective-permute-start | bytes 786440 | tf_op jit(solution)/shard_map/ppermute | solution.py:31
  (45 shorter events, 20.3 us)
Async XLA Ops:
  0.0 28.5 %copy-start.1 = (bf16[1,3,128,128]{3,2,1,0:T(8,128)(2,1)S(1)}, bf16[1,3,128,128]{3,2,1,0:T(8,128)(2,1)}, u32[]{:S(2)}) copy-start(bf16[1,3,128,128]{3,2,1,0:T(8,128)(2,1)} %param.6) | copy-start | bytes 294916
  0.0 9.6 %collective-permute-start = (bf16[512,256]{1,0:T(8,128)(2,1)}, bf16[512,256]{1,0:T(8,128)(2,1)S(1)}, u32[]{:S(2)}, u32[]{:S(2)}) collective-permute-start(bf16[512,256]{1,0:T(8,128)(2,1)} %refs_6_.1), channel_id=1, source_target_pairs={{0,8},{1,9},{2,10},{3,11},{4,12},{5,13},{6,14},{7,15},{8,264},{9,2... | collective-permute-start | bytes 786440 | tf_op jit(solution)/shard_map/ppermute | solution.py:31
  4.1 5.5 %collective-permute-start.1 = (bf16[512,256]{1,0:T(8,128)(2,1)}, bf16[512,256]{1,0:T(8,128)(2,1)S(1)}, u32[]{:S(2)}, u32[]{:S(2)}) collective-permute-start(bf16[512,256]{1,0:T(8,128)(2,1)} %refs_6_.1), channel_id=1, source_target_pairs={{8,256},{9,257},{10,258},{11,259},{12,260},{13,261},{14,262},{15,2... | collective-permute-start | bytes 786440 | tf_op jit(solution)/shard_map/ppermute | solution.py:31
  4.8 23.8 %collective-permute-start.9 = (bf16[128,128]{1,0:T(8,128)(2,1)}, bf16[128,128]{1,0:T(8,128)(2,1)S(1)}, u32[]{:S(2)}, u32[]{:S(2)}) collective-permute-start(bf16[128,128]{1,0:T(8,128)(2,1)} %bitcast.15), channel_id=1, source_target_pairs={{0,0},{1,1},{2,64},{3,65},{4,128},{5,129},{6,192},{7,193},{8,256},... | collective-permute-start | bytes 98312 | tf_op jit(solution)/shard_map/ppermute | solution.py:31
  10.6 40.1 %collective-permute-start.7 = (bf16[1024,256]{1,0:T(8,128)(2,1)S(1)}, bf16[1024,256]{1,0:T(8,128)(2,1)S(1)}, u32[]{:S(2)}, u32[]{:S(2)}) collective-permute-start(bf16[1024,256]{1,0:T(8,128)(2,1)S(1)} %pad_maximum_fusion.refs_0_), channel_id=1, source_target_pairs={{0,2},{1,3},{2,4},{3,5},{4,6},{5,7},{6,0},{7,1},{8,10},{9,11},{10,... | collective-permute-start | bytes 1572872 | tf_op jit(solution)/shard_map/ppermute | solution.py:31
  18.4 34.2 %collective-permute-start.5 = (bf16[1024,256]{1,0:T(8,128)(2,1)S(1)}, bf16[1024,256]{1,0:T(8,128)(2,1)S(1)}, u32[]{:S(2)}, u32[]{:S(2)}) collective-permute-start(bf16[1024,256]{1,0:T(8,128)(2,1)S(1)} %pad_maximum_fusion.refs_0_), channel_id=1, source_target_pairs={{0,4},{1,5},{2,6},{3,7},{4,0},{5,1},{6,2},{7,3},{8,12},{9,13},{10,... | collective-permute-start | bytes 1572872 | tf_op jit(solution)/shard_map/ppermute | solution.py:31
  28.6 19.1 %collective-permute-start.11 = (bf16[128,512]{1,0:T(8,128)(2,1)S(1)}, bf16[128,512]{1,0:T(8,128)(2,1)S(1)}, u32[]{:S(2)}, u32[]{:S(2)}) collective-permute-start(bf16[128,512]{1,0:T(8,128)(2,1)S(1)} %pad_maximum_fusion.6), channel_id=1, source_target_pairs={{0,192},{1,193},{2,194},{3,195},{4,196},{5,197},{6,198},{7,199},{8... | collective-permute-start | bytes 393224 | tf_op jit(solution)/shard_map/ppermute | solution.py:31
  33.2 26.0 %collective-permute-start.3 = (bf16[1024,256]{1,0:T(8,128)(2,1)S(1)}, bf16[1024,256]{1,0:T(8,128)(2,1)S(1)}, u32[]{:S(2)}, u32[]{:S(2)}) collective-permute-start(bf16[1024,256]{1,0:T(8,128)(2,1)S(1)} %pad_maximum_fusion.refs_0_), channel_id=1, source_target_pairs={{0,6},{1,7},{2,0},{3,1},{4,2},{5,3},{6,4},{7,5},{8,14},{9,15},{10,... | collective-permute-start | bytes 1572872 | tf_op jit(solution)/shard_map/ppermute | solution.py:31
  36.1 18.9 %collective-permute-start.10 = (bf16[128,512]{1,0:T(8,128)(2,1)S(1)}, bf16[128,512]{1,0:T(8,128)(2,1)S(1)}, u32[]{:S(2)}, u32[]{:S(2)}) collective-permute-start(bf16[128,512]{1,0:T(8,128)(2,1)S(1)} %pad_maximum_fusion.6), channel_id=1, source_target_pairs={{0,64},{1,65},{2,66},{3,67},{4,68},{5,69},{6,70},{7,71},{8,72},{9,... | collective-permute-start | bytes 393224 | tf_op jit(solution)/shard_map/ppermute | solution.py:31
  47.7 22.6 %collective-permute-start.2 = (bf16[1024,256]{1,0:T(8,128)(2,1)S(1)}, bf16[1024,256]{1,0:T(8,128)(2,1)S(1)}, u32[]{:S(2)}, u32[]{:S(2)}) collective-permute-start(bf16[1024,256]{1,0:T(8,128)(2,1)S(1)} %pad_maximum_fusion.refs_0_), channel_id=1, source_target_pairs={{0,1},{1,0},{2,3},{3,2},{4,5},{5,4},{6,7},{7,6},{8,9},{9,8},{10,11... | collective-permute-start | bytes 1572872 | tf_op jit(solution)/shard_map/ppermute | solution.py:31
  50.7 24.2 %collective-permute-start.8 = (bf16[1024,256]{1,0:T(8,128)(2,1)S(1)}, bf16[1024,256]{1,0:T(8,128)(2,1)S(1)}, u32[]{:S(2)}, u32[]{:S(2)}) collective-permute-start(bf16[1024,256]{1,0:T(8,128)(2,1)S(1)} %collective-permute-done.7.refs_6_), channel_id=1, source_target_pairs={{0,1},{1,0},{2,3},{3,2},{4,5},{5,4},{6,7},{7,6},{8,9},{9,8},{10,11... | collective-permute-start | bytes 1572872 | tf_op jit(solution)/shard_map/ppermute | solution.py:31
  52.6 24.2 %collective-permute-start.6 = (bf16[1024,256]{1,0:T(8,128)(2,1)S(1)}, bf16[1024,256]{1,0:T(8,128)(2,1)S(1)}, u32[]{:S(2)}, u32[]{:S(2)}) collective-permute-start(bf16[1024,256]{1,0:T(8,128)(2,1)S(1)} %collective-permute-done.5.refs_4_), channel_id=1, source_target_pairs={{0,1},{1,0},{2,3},{3,2},{4,5},{5,4},{6,7},{7,6},{8,9},{9,8},{10,11... | collective-permute-start | bytes 1572872 | tf_op jit(solution)/shard_map/ppermute | solution.py:31
  55.1 13.2 %collective-permute-start.12 = (bf16[128,512]{1,0:T(8,128)(2,1)S(1)}, bf16[128,512]{1,0:T(8,128)(2,1)S(1)}, u32[]{:S(2)}, u32[]{:S(2)}) collective-permute-start(bf16[128,512]{1,0:T(8,128)(2,1)S(1)} %broadcast_select_fusion.2), channel_id=1, source_target_pairs={{0,192},{1,65},{2,194},{3,67},{4,196},{5,69},{6,198},{7,71},{8,200... | collective-permute-start | bytes 393224 | tf_op jit(solution)/shard_map/ppermute | solution.py:31
  59.2 23.2 %collective-permute-start.4 = (bf16[1024,256]{1,0:T(8,128)(2,1)S(1)}, bf16[1024,256]{1,0:T(8,128)(2,1)S(1)}, u32[]{:S(2)}, u32[]{:S(2)}) collective-permute-start(bf16[1024,256]{1,0:T(8,128)(2,1)S(1)} %collective-permute-done.3.refs_2_), channel_id=1, source_target_pairs={{0,1},{1,0},{2,3},{3,2},{4,5},{5,4},{6,7},{7,6},{8,9},{9,8},{10,11... | collective-permute-start | bytes 1572872 | tf_op jit(solution)/shard_map/ppermute | solution.py:31
  68.3 27.8 %collective-permute-start.16 = (bf16[512,512]{1,0:T(8,128)(2,1)S(1)}, bf16[512,512]{1,0:T(8,128)(2,1)S(1)}, u32[]{:S(2)}, u32[]{:S(2)}) collective-permute-start(bf16[512,512]{1,0:T(8,128)(2,1)S(1)} %pad_maximum_fusion.1.refs_8_), channel_id=1, source_target_pairs={{0,16},{1,17},{2,18},{3,19},{4,20},{5,21},{6,22},{7,23},{8,24},{9,... | collective-permute-start | bytes 1572872 | tf_op jit(solution)/shard_map/ppermute | solution.py:31
  70.3 25.9 %collective-permute-start.15 = (bf16[512,512]{1,0:T(8,128)(2,1)S(1)}, bf16[512,512]{1,0:T(8,128)(2,1)S(1)}, u32[]{:S(2)}, u32[]{:S(2)}) collective-permute-start(bf16[512,512]{1,0:T(8,128)(2,1)S(1)} %pad_maximum_fusion.1.refs_8_), channel_id=1, source_target_pairs={{0,240},{1,241},{2,242},{3,243},{4,244},{5,245},{6,246},{7,247},{8... | collective-permute-start | bytes 1572872 | tf_op jit(solution)/shard_map/ppermute | solution.py:31
  74.9 17.2 %collective-permute-start.14 = (bf16[256,512]{1,0:T(8,128)(2,1)S(1)}, bf16[256,512]{1,0:T(8,128)(2,1)S(1)}, u32[]{:S(2)}, u32[]{:S(2)}) collective-permute-start(bf16[256,512]{1,0:T(8,128)(2,1)S(1)} %get-tuple-element.23), channel_id=1, source_target_pairs={{0,32},{1,33},{2,34},{3,35},{4,36},{5,37},{6,38},{7,39},{8,40},{9,... | collective-permute-start | bytes 786440 | tf_op jit(solution)/shard_map/ppermute | solution.py:31
  76.9 19.3 %collective-permute-start.13 = (bf16[256,512]{1,0:T(8,128)(2,1)S(1)}, bf16[256,512]{1,0:T(8,128)(2,1)S(1)}, u32[]{:S(2)}, u32[]{:S(2)}) collective-permute-start(bf16[256,512]{1,0:T(8,128)(2,1)S(1)} %get-tuple-element.24), channel_id=1, source_target_pairs={{0,224},{1,225},{2,226},{3,227},{4,228},{5,229},{6,230},{7,231},{8... | collective-permute-start | bytes 786440 | tf_op jit(solution)/shard_map/ppermute | solution.py:31
  98.2 9.3 %collective-permute-start.18 = (bf16[528,256]{1,0:T(8,128)(2,1)S(1)}, bf16[528,256]{1,0:T(8,128)(2,1)S(1)}, u32[]{:S(2)}, u32[]{:S(2)}) collective-permute-start(bf16[528,256]{1,0:T(8,128)(2,1)S(1)} %get-tuple-element.17), channel_id=1, source_target_pairs={{0,256},{1,257},{2,258},{3,259},{4,260},{5,261},{6,262},{7,263},{8... | collective-permute-start | bytes 811016 | tf_op jit(solution)/shard_map/ppermute | solution.py:31
  108.1 11.9 %collective-permute-start.19 = (bf16[512,256]{1,0:T(8,128)(2,1)S(1)}, bf16[512,256]{1,0:T(8,128)(2,1)S(1)}, u32[]{:S(2)}, u32[]{:S(2)}) collective-permute-start(bf16[512,256]{1,0:T(8,128)(2,1)S(1)} %shard_map.50.kv_ref), channel_id=1, source_target_pairs={{0,16},{16,32},{32,48},{48,64},{64,80},{80,96},{96,112},{112,128},... | collective-permute-start | bytes 786440 | tf_op jit(solution)/shard_map/ppermute | solution.py:302
  109.4 9.7 %collective-permute-start.17 = (bf16[512,128]{1,0:T(8,128)(2,1)S(1)}, bf16[512,128]{1,0:T(8,128)(2,1)S(1)}, u32[]{:S(2)}, u32[]{:S(2)}) collective-permute-start(bf16[512,128]{1,0:T(8,128)(2,1)S(1)} %get-tuple-element.15), channel_id=1, source_target_pairs={{0,256},{1,257},{2,258},{3,259},{4,260},{5,261},{6,262},{7,263},{8... | collective-permute-start | bytes 393224 | tf_op jit(solution)/shard_map/ppermute | solution.py:31
  114.4 35.4 %collective-permute-start.24 = (bf16[2048,128]{1,0:T(8,128)(2,1)S(1)}, bf16[2048,128]{1,0:T(8,128)(2,1)S(1)}, u32[]{:S(2)}, u32[]{:S(2)}) collective-permute-start(bf16[2048,128]{1,0:T(8,128)(2,1)S(1)} %get-tuple-element.20.refs_4_), channel_id=1, source_target_pairs={{0,256},{1,257},{2,258},{3,259},{4,260},{5,261},{6,262},{7,263},{8... | collective-permute-start | bytes 1572872 | tf_op jit(solution)/shard_map/ppermute | solution.py:31
  121.8 42.5 %copy-start = (bf16[512,256]{1,0:T(8,128)(2,1)S(1)}, bf16[512,256]{1,0:T(8,128)(2,1)}, u32[]{:S(2)}) copy-start(bf16[512,256]{1,0:T(8,128)(2,1)} %refs_6_.1) | copy-start | bytes 786436
  121.8 19.6 %collective-permute-start.20 = (bf16[512,128]{1,0:T(8,128)(2,1)S(1)}, bf16[512,128]{1,0:T(8,128)(2,1)S(1)}, u32[]{:S(2)}, u32[]{:S(2)}) collective-permute-start(bf16[512,128]{1,0:T(8,128)(2,1)S(1)} %shard_map.52), channel_id=1, source_target_pairs={{0,8},{1,9},{2,10},{3,11},{4,12},{5,13},{6,14},{7,15},{8,0},{9,1},... | collective-permute-start | bytes 393224 | tf_op jit(solution)/shard_map/ppermute | solution.py:31
  141.4 10.8 %collective-permute-start.23 = (bf16[512,256]{1,0:T(8,128)(2,1)S(1)}, bf16[512,256]{1,0:T(8,128)(2,1)S(1)}, u32[]{:S(2)}, u32[]{:S(2)}) collective-permute-start(bf16[512,256]{1,0:T(8,128)(2,1)S(1)} %pad_maximum_fusion.5.refs_0_), channel_id=1, source_target_pairs={{0,2},{1,3},{2,4},{3,5},{4,6},{5,7},{6,0},{7,1},{8,10},{9,11},{10,... | collective-permute-start | bytes 786440 | tf_op jit(solution)/shard_map/ppermute | solution.py:31
  143.3 13.8 %collective-permute-start.22 = (bf16[512,256]{1,0:T(8,128)(2,1)S(1)}, bf16[512,256]{1,0:T(8,128)(2,1)S(1)}, u32[]{:S(2)}, u32[]{:S(2)}) collective-permute-start(bf16[512,256]{1,0:T(8,128)(2,1)S(1)} %pad_maximum_fusion.5.refs_0_), channel_id=1, source_target_pairs={{0,4},{1,5},{2,6},{3,7},{4,0},{5,1},{6,2},{7,3},{8,12},{9,13},{10,... | collective-permute-start | bytes 786440 | tf_op jit(solution)/shard_map/ppermute | solution.py:31
  147.5 12.3 %collective-permute-start.21 = (bf16[512,256]{1,0:T(8,128)(2,1)S(1)}, bf16[512,256]{1,0:T(8,128)(2,1)S(1)}, u32[]{:S(2)}, u32[]{:S(2)}) collective-permute-start(bf16[512,256]{1,0:T(8,128)(2,1)S(1)} %pad_maximum_fusion.5.refs_0_), channel_id=1, source_target_pairs={{0,6},{1,7},{2,0},{3,1},{4,2},{5,3},{6,4},{7,5},{8,14},{9,15},{10,... | collective-permute-start | bytes 786440 | tf_op jit(solution)/shard_map/ppermute | solution.py:31
  160.9 4.6 %collective-permute-start.25 = (bf16[512,256]{1,0:T(8,128)(2,1)S(1)}, bf16[512,256]{1,0:T(8,128)(2,1)S(1)}, u32[]{:S(2)}, u32[]{:S(2)}) collective-permute-start(bf16[512,256]{1,0:T(8,128)(2,1)S(1)} %shard_map.54), channel_id=1, source_target_pairs={{0,1},{1,0},{2,3},{3,2},{4,5},{5,4},{6,7},{7,6},{8,9},{9,8},{10,11... | collective-permute-start | bytes 786440 | tf_op jit(solution)/shard_map/ppermute | solution.py:31

commit v8 on v7

--- a/solution.py
+++ b/solution.py
@@ -12,7 +12,7 @@
 AXES = ("ctx", "tp")
 BF = jnp.bfloat16
 F32 = jnp.float32
-STEPS = ((0, -4, 4, 8), (2, 6), (-2, -6), (1, -3, 5, 9), (-1, -5, 3, 7))
+HELD = (0, -4, 4, 8)
 
 
 def pairs_of(target):
@@ -68,22 +68,27 @@
     relay = permute(
         jnp.where(core == 0, down4, up4), lambda a, z, b, y, k: (a, z + (4 if k else 12), b, y, k)
     )
-    down2 = move(jnp.concatenate([chunk, down4], axis=0), -2)
-    up2 = move(jnp.concatenate([chunk, up4], axis=0), 2)
     held = jnp.concatenate([chunk, up4, down4, relay], axis=0)
-    down1 = move(held, -1)
-    up1 = move(held, 1)
-    return held, down2, up2, down1, up1
+    two = permute(held, lambda a, z, b, y, k: (a, z + (2 if k else 14), b, y, k))
+    return held, two, move(held, -1), move(held, 1)
+
+
+def columns_of(blocks, i, first, size):
+    if i % 2 == 0:
+        return blocks[i // 2][first : first + size, :]
+    if i > 1:
+        first += (i // 2 - 1) * blocks[0].shape[0]
+    return blocks[4 if i == 1 else 5][first : first + size, :]
 
 
 def squares_body(*refs):
-    blocks, (own_ref, other_ref) = refs[:8], refs[8:]
+    blocks, (own_ref, other_ref) = refs[:6], refs[6:]
     seg = own_ref.shape[1]
     ones = jnp.ones((own_ref.shape[0], blocks[0].shape[1]), BF)
     for first, ref in ((0, own_ref), (seg, other_ref)):
         total = jnp.zeros(ref.shape, F32)
-        for block in blocks:
-            wider = block[first : first + seg, :].astype(F32)
+        for i in range(8):
+            wider = columns_of(blocks, i, first, seg).astype(F32)
             total += lax.dot_general(
                 ones,
                 (wider * wider).astype(BF),
@@ -103,7 +108,7 @@
             yy = (y + i // 2) & 3
             kk = k if i % 2 == 0 else 1 - k
             at = pl.multiple_of((yy * 2 + kk) * 2 * rows, 2 * rows)
-            block = blocks[i][first + r : first + r + tile, :]
+            block = columns_of(blocks, i, first + r, tile)
             acc += jnp.dot(block, weights[pl.ds(at, 2 * rows), :], preferred_element_type=F32)
         yield slice(r, r + tile), acc
 
@@ -113,15 +118,15 @@
 
 def project_other_body(pos, *refs):
     blocks, parts, ssq_ref, (kv_ref, q_ref, w_ref, out_w_ref) = (
-        refs[:8], refs[8:13], refs[13], refs[14:],
-    )
-    _, z, _, _, _ = place(pos)
+        refs[:6], refs[6:10], refs[10], refs[11:],
+    )
+    _, z, _, _, k = place(pos)
     rows = w_ref.shape[0] // 16
     seg, hd = q_ref.shape
     wide = w_ref.shape[1]
-    for part, steps in zip(parts, STEPS):
-        for i, step in enumerate(steps):
-            at = pl.multiple_of(((z + step + 16) & 15) * rows, rows)
+    for part, base in zip(parts, (0, 2 - 4 * k, 1, -1)):
+        for i, step in enumerate(HELD):
+            at = pl.multiple_of(((z + base + step + 16) & 15) * rows, rows)
             w_ref[pl.ds(at, rows), :] = part[i * rows : (i + 1) * rows, :wide]
             out_w_ref[pl.ds(at, rows), :] = part[i * rows : (i + 1) * rows, wide:]
     for at, acc in project_rows(pos, blocks, w_ref, seg, seg):
@@ -140,7 +145,7 @@
 
 
 def project_own_body(pos, *refs):
-    blocks, (w_ref, own_ref) = refs[:8], refs[8:]
+    blocks, (w_ref, own_ref) = refs[:6], refs[6:]
     for at, acc in project_rows(pos, blocks, w_ref, 0, own_ref.shape[0]):
         own_ref[at, :] = acc
 
@@ -258,9 +263,10 @@
     cross = permute(hidden, lambda a, z, b, y, k: (b, z, a, y, k) if a != b else None)
     own = jnp.where(same, hidden, turn)
     other = jnp.where(same, turn, cross)
-    blocks = []
-    for block in around(jnp.concatenate([own, other], axis=0)):
-        blocks += [block, permute(block, swap_core)]
+    blocks = around(jnp.concatenate([own, other], axis=0))
+    blocks += [
+        permute(blocks[0], swap_core), permute(jnp.concatenate(blocks[1:], axis=0), swap_core)
+    ]
 
     ssq, ssq_send = call(
         squares_body,

time: 167 us -> 188 us (1.13)
  the two profiles are of different devices: /device:TPU:1 before, /device:TPU:11 now
where the time goes in v8:
time: 188 us; the launch traced here: 187 us
  starting transfers between devices  92.7 us (49%)
  waiting for transfers between devices  80.6 us (43%)
  Pallas kernels  11 us (6%)
  other arithmetic  2.35 us (1%)
    ppermute x22, starting transfers between devices, permute(): return lax.ppermute(value, AXES, pairs_of(target))  90.6 us
    ppermute x22, waiting for transfers between devices, permute(): return lax.ppermute(value, AXES, pairs_of(target))  80.6 us
    pallas_call x10, Pallas kernels, run(): pl.pallas_call(body, out_shape=outs, in_specs=specs, out_specs=jax.tree.m...  11 us
  transfers between devices with their start and end apart: 23, of which 15 were waited for; matrix products, arithmetic and copies ran while one was open for 1% of the time, Pallas kernels for 4%

profile of v8, /device:TPU:11, one launch (start us, length us, event | category | flops | bytes accessed | tf_op | source)
XLA Modules:
  0.0 187.1 jit_solution(8977192639935923484)
XLA Ops:
  0.0 3.9 %collective-permute-start = (bf16[512,256]{1,0:T(8,128)(2,1)}, bf16[512,256]{1,0:T(8,128)(2,1)S(1)}, u32[]{:S(2)}, u32[]{:S(2)}) collective-permute-start(bf16[512,256]{1,0:T(8,128)(2,1)} %refs_6_.1), channel_id=1, source_target_pairs={{0,8},{1,9},{2,10},{3,11},{4,12},{5,13},{6,14},{7,15},{8,264},{9,2... | collective-permute-start | bytes 786440 | tf_op jit(solution)/shard_map/ppermute | solution.py:31
  5.8 3.6 %collective-permute-done = bf16[512,256]{1,0:T(8,128)(2,1)S(1)} collective-permute-done((bf16[512,256]{1,0:T(8,128)(2,1)}, bf16[512,256]{1,0:T(8,128)(2,1)S(1)}, u32[]{:S(2)}, u32[]{:S(2)}) %collective-permute-start) | collective-permute-done | bytes 262176 | tf_op jit(solution)/shard_map/ppermute | solution.py:31
  9.4 3.5 %collective-permute-done.1 = bf16[512,256]{1,0:T(8,128)(2,1)S(1)} collective-permute-done((bf16[512,256]{1,0:T(8,128)(2,1)}, bf16[512,256]{1,0:T(8,128)(2,1)S(1)}, u32[]{:S(2)}, u32[]{:S(2)}) %collective-permute-start.1) | collective-permute-done | bytes 262176 | tf_op jit(solution)/shard_map/ppermute | solution.py:31
  13.0 3.2 %collective-permute-start.4 = (bf16[1024,256]{1,0:T(8,128)(2,1)S(1)}, bf16[1024,256]{1,0:T(8,128)(2,1)S(1)}, u32[]{:S(2)}, u32[]{:S(2)}) collective-permute-start(bf16[1024,256]{1,0:T(8,128)(2,1)S(1)} %pad_maximum_fusion.1.refs_0_), channel_id=1, source_target_pairs={{0,2},{1,3},{2,4},{3,5},{4,6},{5,7},{6,0},{7,1},{8,10},{9,11},{10,... | collective-permute-start | bytes 1572872 | tf_op jit(solution)/shard_map/ppermute | solution.py:31
  16.2 2.6 %collective-permute-start.3 = (bf16[1024,256]{1,0:T(8,128)(2,1)S(1)}, bf16[1024,256]{1,0:T(8,128)(2,1)S(1)}, u32[]{:S(2)}, u32[]{:S(2)}) collective-permute-start(bf16[1024,256]{1,0:T(8,128)(2,1)S(1)} %pad_maximum_fusion.1.refs_0_), channel_id=1, source_target_pairs={{0,4},{1,5},{2,6},{3,7},{4,0},{5,1},{6,2},{7,3},{8,12},{9,13},{10,... | collective-permute-start | bytes 1572872 | tf_op jit(solution)/shard_map/ppermute | solution.py:31
  18.9 4.0 %collective-permute-start.2 = (bf16[1024,256]{1,0:T(8,128)(2,1)S(1)}, bf16[1024,256]{1,0:T(8,128)(2,1)S(1)}, u32[]{:S(2)}, u32[]{:S(2)}) collective-permute-start(bf16[1024,256]{1,0:T(8,128)(2,1)S(1)} %pad_maximum_fusion.1.refs_0_), channel_id=1, source_target_pairs={{0,6},{1,7},{2,0},{3,1},{4,2},{5,3},{6,4},{7,5},{8,14},{9,15},{10,... | collective-permute-start | bytes 1572872 | tf_op jit(solution)/shard_map/ppermute | solution.py:31
  22.8 9.6 %collective-permute-start.7 = (bf16[128,128]{1,0:T(8,128)(2,1)S(1)}, bf16[128,128]{1,0:T(8,128)(2,1)S(1)}, u32[]{:S(2)}, u32[]{:S(2)}) collective-permute-start(bf16[128,128]{1,0:T(8,128)(2,1)S(1)} %bitcast.15), channel_id=1, source_target_pairs={{0,0},{1,1},{2,64},{3,65},{4,128},{5,129},{6,192},{7,193},{8,256},... | collective-permute-start | bytes 98312 | tf_op jit(solution)/shard_map/ppermute | solution.py:31
  32.5 12.9 %collective-permute-done.2.refs_1_ = bf16[1024,256]{1,0:T(8,128)(2,1)S(1)} collective-permute-done((bf16[1024,256]{1,0:T(8,128)(2,1)S(1)}, bf16[1024,256]{1,0:T(8,128)(2,1)S(1)}, u32[]{:S(2)}, u32[]{:S(2)}) %collective-permute-start.2) | collective-permute-done | bytes 524320 | tf_op jit(solution)/shard_map/ppermute | solution.py:31
  46.7 2.4 %collective-permute-start.6 = (bf16[3072,256]{1,0:T(8,128)(2,1)}, bf16[3072,256]{1,0:T(8,128)(2,1)S(1)}, u32[]{:S(2)}, u32[]{:S(2)}) collective-permute-start(bf16[3072,256]{1,0:T(8,128)(2,1)} %pad_maximum_fusion), channel_id=1, source_target_pairs={{0,1},{1,0},{2,3},{3,2},{4,5},{5,4},{6,7},{7,6},{8,9},{9,8},{10,11... | collective-permute-start | bytes 4718600 | tf_op jit(solution)/shard_map/ppermute | solution.py:31
  49.9 12.4 %collective-permute-start.9 = (bf16[128,512]{1,0:T(8,128)(2,1)}, bf16[128,512]{1,0:T(8,128)(2,1)S(1)}, u32[]{:S(2)}, u32[]{:S(2)}) collective-permute-start(bf16[128,512]{1,0:T(8,128)(2,1)} %pad_maximum_fusion.4), channel_id=1, source_target_pairs={{0,192},{1,193},{2,194},{3,195},{4,196},{5,197},{6,198},{7,199},{8... | collective-permute-start | bytes 393224 | tf_op jit(solution)/shard_map/ppermute | solution.py:31
  64.3 9.6 %collective-permute-done.9 = bf16[128,512]{1,0:T(8,128)(2,1)S(1)} collective-permute-done((bf16[128,512]{1,0:T(8,128)(2,1)}, bf16[128,512]{1,0:T(8,128)(2,1)S(1)}, u32[]{:S(2)}, u32[]{:S(2)}) %collective-permute-start.9) | collective-permute-done | bytes 131104 | tf_op jit(solution)/shard_map/ppermute | solution.py:31
  74.9 4.5 %collective-permute-start.10 = (bf16[128,512]{1,0:T(8,128)(2,1)S(1)}, bf16[128,512]{1,0:T(8,128)(2,1)S(1)}, u32[]{:S(2)}, u32[]{:S(2)}) collective-permute-start(bf16[128,512]{1,0:T(8,128)(2,1)S(1)} %broadcast_select_fusion.2), channel_id=1, source_target_pairs={{0,192},{1,65},{2,194},{3,67},{4,196},{5,69},{6,198},{7,71},{8,200... | collective-permute-start | bytes 393224 | tf_op jit(solution)/shard_map/ppermute | solution.py:31
  79.4 6.2 %collective-permute-start.5 = (bf16[1024,256]{1,0:T(8,128)(2,1)S(1)}, bf16[1024,256]{1,0:T(8,128)(2,1)S(1)}, u32[]{:S(2)}, u32[]{:S(2)}) collective-permute-start(bf16[1024,256]{1,0:T(8,128)(2,1)S(1)} %pad_maximum_fusion.1.refs_0_), channel_id=1, source_target_pairs={{0,1},{1,0},{2,3},{3,2},{4,5},{5,4},{6,7},{7,6},{8,9},{9,8},{10,11... | collective-permute-start | bytes 1572872 | tf_op jit(solution)/shard_map/ppermute | solution.py:31
  85.7 5.2 %collective-permute-start.13 = (bf16[512,512]{1,0:T(8,128)(2,1)S(1)}, bf16[512,512]{1,0:T(8,128)(2,1)S(1)}, u32[]{:S(2)}, u32[]{:S(2)}) collective-permute-start(bf16[512,512]{1,0:T(8,128)(2,1)S(1)} %pad_maximum_fusion.2.refs_6_), channel_id=1, source_target_pairs={{0,16},{1,17},{2,18},{3,19},{4,20},{5,21},{6,22},{7,23},{8,24},{9,... | collective-permute-start | bytes 1572872 | tf_op jit(solution)/shard_map/ppermute | solution.py:31
  90.9 6.7 %collective-permute-start.12 = (bf16[512,512]{1,0:T(8,128)(2,1)S(1)}, bf16[512,512]{1,0:T(8,128)(2,1)S(1)}, u32[]{:S(2)}, u32[]{:S(2)}) collective-permute-start(bf16[512,512]{1,0:T(8,128)(2,1)S(1)} %pad_maximum_fusion.2.refs_6_), channel_id=1, source_target_pairs={{0,240},{1,241},{2,242},{3,243},{4,244},{5,245},{6,246},{7,247},{8... | collective-permute-start | bytes 1572872 | tf_op jit(solution)/shard_map/ppermute | solution.py:31
  97.5 2.3 %collective-permute-start.11 = (bf16[512,512]{1,0:T(8,128)(2,1)S(1)}, bf16[512,512]{1,0:T(8,128)(2,1)S(1)}, u32[]{:S(2)}, u32[]{:S(2)}) collective-permute-start(bf16[512,512]{1,0:T(8,128)(2,1)S(1)} %pad_maximum_fusion.2.refs_6_), channel_id=1, source_target_pairs={{0,224},{1,33},{2,226},{3,35},{4,228},{5,37},{6,230},{7,39},{8,232... | collective-permute-start | bytes 1572872 | tf_op jit(solution)/shard_map/ppermute | solution.py:31
  101.1 4.0 %collective-permute-done.13.refs_9_ = bf16[512,512]{1,0:T(8,128)(2,1)S(1)} collective-permute-done((bf16[512,512]{1,0:T(8,128)(2,1)S(1)}, bf16[512,512]{1,0:T(8,128)(2,1)S(1)}, u32[]{:S(2)}, u32[]{:S(2)}) %collective-permute-start.13) | collective-permute-done | bytes 524320 | tf_op jit(solution)/shard_map/ppermute | solution.py:31
  106.1 14.1 %collective-permute-done.11.refs_7_ = bf16[512,512]{1,0:T(8,128)(2,1)S(1)} collective-permute-done((bf16[512,512]{1,0:T(8,128)(2,1)S(1)}, bf16[512,512]{1,0:T(8,128)(2,1)S(1)}, u32[]{:S(2)}, u32[]{:S(2)}) %collective-permute-start.11) | collective-permute-done | bytes 524320 | tf_op jit(solution)/shard_map/ppermute | solution.py:31
  122.2 2.7 %collective-permute-start.15 = (bf16[528,256]{1,0:T(8,128)(2,1)S(1)}, bf16[528,256]{1,0:T(8,128)(2,1)S(1)}, u32[]{:S(2)}, u32[]{:S(2)}) collective-permute-start(bf16[528,256]{1,0:T(8,128)(2,1)S(1)} %get-tuple-element.17), channel_id=1, source_target_pairs={{0,256},{1,257},{2,258},{3,259},{4,260},{5,261},{6,262},{7,263},{8... | collective-permute-start | bytes 811016 | tf_op jit(solution)/shard_map/ppermute | solution.py:31
  126.8 5.0 %collective-permute-done.15.refs_3_.refs_1_ = bf16[528,256]{1,0:T(8,128)(2,1)S(1)} collective-permute-done((bf16[528,256]{1,0:T(8,128)(2,1)S(1)}, bf16[528,256]{1,0:T(8,128)(2,1)S(1)}, u32[]{:S(2)}, u32[]{:S(2)}) %collective-permute-start.15) | collective-permute-done | bytes 270368 | tf_op jit(solution)/shard_map/ppermute | solution.py:31
  132.3 2.2 %collective-permute-start.16 = (bf16[512,256]{1,0:T(8,128)(2,1)S(1)}, bf16[512,256]{1,0:T(8,128)(2,1)S(1)}, u32[]{:S(2)}, u32[]{:S(2)}) collective-permute-start(bf16[512,256]{1,0:T(8,128)(2,1)S(1)} %shard_map.50.kv_ref), channel_id=1, source_target_pairs={{0,16},{16,32},{32,48},{48,64},{64,80},{80,96},{96,112},{112,128},... | collective-permute-start | bytes 786440 | tf_op jit(solution)/shard_map/ppermute | solution.py:308
  134.5 2.7 %collective-permute-start.14 = (bf16[512,128]{1,0:T(8,128)(2,1)S(1)}, bf16[512,128]{1,0:T(8,128)(2,1)S(1)}, u32[]{:S(2)}, u32[]{:S(2)}) collective-permute-start(bf16[512,128]{1,0:T(8,128)(2,1)S(1)} %get-tuple-element.15), channel_id=1, source_target_pairs={{0,256},{1,257},{2,258},{3,259},{4,260},{5,261},{6,262},{7,263},{8... | collective-permute-start | bytes 393224 | tf_op jit(solution)/shard_map/ppermute | solution.py:31
  137.3 4.1 %collective-permute-start.21 = (bf16[2048,128]{1,0:T(8,128)(2,1)S(1)}, bf16[2048,128]{1,0:T(8,128)(2,1)S(1)}, u32[]{:S(2)}, u32[]{:S(2)}) collective-permute-start(bf16[2048,128]{1,0:T(8,128)(2,1)S(1)} %get-tuple-element.20.refs_4_), channel_id=1, source_target_pairs={{0,256},{1,257},{2,258},{3,259},{4,260},{5,261},{6,262},{7,263},{8... | collective-permute-start | bytes 1572872 | tf_op jit(solution)/shard_map/ppermute | solution.py:31
  141.3 4.6 %collective-permute-done.14.refs_1_ = bf16[512,128]{1,0:T(8,128)(2,1)S(1)} collective-permute-done((bf16[512,128]{1,0:T(8,128)(2,1)S(1)}, bf16[512,128]{1,0:T(8,128)(2,1)S(1)}, u32[]{:S(2)}, u32[]{:S(2)}) %collective-permute-start.14) | collective-permute-done | bytes 131104 | tf_op jit(solution)/shard_map/ppermute | solution.py:31
  148.6 3.3 %collective-permute-start.17 = (bf16[512,128]{1,0:T(8,128)(2,1)S(1)}, bf16[512,128]{1,0:T(8,128)(2,1)S(1)}, u32[]{:S(2)}, u32[]{:S(2)}) collective-permute-start(bf16[512,128]{1,0:T(8,128)(2,1)S(1)} %shard_map.52), channel_id=1, source_target_pairs={{0,8},{1,9},{2,10},{3,11},{4,12},{5,13},{6,14},{7,15},{8,0},{9,1},... | collective-permute-start | bytes 393224 | tf_op jit(solution)/shard_map/ppermute | solution.py:31
  151.9 10.1 %collective-permute-done.17 = bf16[512,128]{1,0:T(8,128)(2,1)S(1)} collective-permute-done((bf16[512,128]{1,0:T(8,128)(2,1)S(1)}, bf16[512,128]{1,0:T(8,128)(2,1)S(1)}, u32[]{:S(2)}, u32[]{:S(2)}) %collective-permute-start.17) | collective-permute-done | bytes 131104 | tf_op jit(solution)/shard_map/ppermute | solution.py:31
  162.0 2.6 %collective-permute-start.20 = (bf16[512,256]{1,0:T(8,128)(2,1)S(1)}, bf16[512,256]{1,0:T(8,128)(2,1)S(1)}, u32[]{:S(2)}, u32[]{:S(2)}) collective-permute-start(bf16[512,256]{1,0:T(8,128)(2,1)S(1)} %pad_maximum_fusion.3.refs_0_), channel_id=1, source_target_pairs={{0,2},{1,3},{2,4},{3,5},{4,6},{5,7},{6,0},{7,1},{8,10},{9,11},{10,... | collective-permute-start | bytes 786440 | tf_op jit(solution)/shard_map/ppermute | solution.py:31
  164.5 2.3 %collective-permute-start.19 = (bf16[512,256]{1,0:T(8,128)(2,1)S(1)}, bf16[512,256]{1,0:T(8,128)(2,1)S(1)}, u32[]{:S(2)}, u32[]{:S(2)}) collective-permute-start(bf16[512,256]{1,0:T(8,128)(2,1)S(1)} %pad_maximum_fusion.3.refs_0_), channel_id=1, source_target_pairs={{0,4},{1,5},{2,6},{3,7},{4,0},{5,1},{6,2},{7,3},{8,12},{9,13},{10,... | collective-permute-start | bytes 786440 | tf_op jit(solution)/shard_map/ppermute | solution.py:31
  166.8 3.7 %collective-permute-start.18 = (bf16[512,256]{1,0:T(8,128)(2,1)S(1)}, bf16[512,256]{1,0:T(8,128)(2,1)S(1)}, u32[]{:S(2)}, u32[]{:S(2)}) collective-permute-start(bf16[512,256]{1,0:T(8,128)(2,1)S(1)} %pad_maximum_fusion.3.refs_0_), channel_id=1, source_target_pairs={{0,6},{1,7},{2,0},{3,1},{4,2},{5,3},{6,4},{7,5},{8,14},{9,15},{10,... | collective-permute-start | bytes 786440 | tf_op jit(solution)/shard_map/ppermute | solution.py:31
  171.1 3.8 %collective-permute-done.19.refs_2_ = bf16[512,256]{1,0:T(8,128)(2,1)S(1)} collective-permute-done((bf16[512,256]{1,0:T(8,128)(2,1)S(1)}, bf16[512,256]{1,0:T(8,128)(2,1)S(1)}, u32[]{:S(2)}, u32[]{:S(2)}) %collective-permute-start.19) | collective-permute-done | bytes 262176 | tf_op jit(solution)/shard_map/ppermute | solution.py:31
  174.9 6.9 %collective-permute-done.18.refs_1_ = bf16[512,256]{1,0:T(8,128)(2,1)S(1)} collective-permute-done((bf16[512,256]{1,0:T(8,128)(2,1)S(1)}, bf16[512,256]{1,0:T(8,128)(2,1)S(1)}, u32[]{:S(2)}, u32[]{:S(2)}) %collective-permute-start.18) | collective-permute-done | bytes 262176 | tf_op jit(solution)/shard_map/ppermute | solution.py:31
  182.8 2.4 %collective-permute-start.22 = (bf16[512,256]{1,0:T(8,128)(2,1)S(1)}, bf16[512,256]{1,0:T(8,128)(2,1)S(1)}, u32[]{:S(2)}, u32[]{:S(2)}) collective-permute-start(bf16[512,256]{1,0:T(8,128)(2,1)S(1)} %shard_map.54), channel_id=1, source_target_pairs={{0,1},{1,0},{2,3},{3,2},{4,5},{5,4},{6,7},{7,6},{8,9},{9,8},{10,11... | collective-permute-start | bytes 786440 | tf_op jit(solution)/shard_map/ppermute | solution.py:31
  (47 shorter events, 19.8 us)
Async XLA Ops:
  0.0 22.8 %copy-start.4 = (bf16[1,128,128]{2,1,0:T(8,128)(2,1)S(1)}, bf16[1,128,128]{2,1,0:T(8,128)(2,1)}, u32[]{:S(2)}) copy-start(bf16[1,128,128]{2,1,0:T(8,128)(2,1)} %param.7) | copy-start | bytes 98308
  0.0 32.5 %copy-start.5 = (bf16[1,128]{1,0:T(2,128)(2,1)S(1)}, bf16[1,128]{1,0:T(2,128)(2,1)}, u32[]{:S(2)}) copy-start(bf16[1,128]{1,0:T(2,128)(2,1)} %param.5) | copy-start | bytes 772
  0.0 9.4 %collective-permute-start = (bf16[512,256]{1,0:T(8,128)(2,1)}, bf16[512,256]{1,0:T(8,128)(2,1)S(1)}, u32[]{:S(2)}, u32[]{:S(2)}) collective-permute-start(bf16[512,256]{1,0:T(8,128)(2,1)} %refs_6_.1), channel_id=1, source_target_pairs={{0,8},{1,9},{2,10},{3,11},{4,12},{5,13},{6,14},{7,15},{8,264},{9,2... | collective-permute-start | bytes 786440 | tf_op jit(solution)/shard_map/ppermute | solution.py:31
  3.9 9.0 %collective-permute-start.1 = (bf16[512,256]{1,0:T(8,128)(2,1)}, bf16[512,256]{1,0:T(8,128)(2,1)S(1)}, u32[]{:S(2)}, u32[]{:S(2)}) collective-permute-start(bf16[512,256]{1,0:T(8,128)(2,1)} %refs_6_.1), channel_id=1, source_target_pairs={{8,256},{9,257},{10,258},{11,259},{12,260},{13,261},{14,262},{15,2... | collective-permute-start | bytes 786440 | tf_op jit(solution)/shard_map/ppermute | solution.py:31
  13.0 19.5 %collective-permute-start.4 = (bf16[1024,256]{1,0:T(8,128)(2,1)S(1)}, bf16[1024,256]{1,0:T(8,128)(2,1)S(1)}, u32[]{:S(2)}, u32[]{:S(2)}) collective-permute-start(bf16[1024,256]{1,0:T(8,128)(2,1)S(1)} %pad_maximum_fusion.1.refs_0_), channel_id=1, source_target_pairs={{0,2},{1,3},{2,4},{3,5},{4,6},{5,7},{6,0},{7,1},{8,10},{9,11},{10,... | collective-permute-start | bytes 1572872 | tf_op jit(solution)/shard_map/ppermute | solution.py:31
  16.2 16.3 %collective-permute-start.3 = (bf16[1024,256]{1,0:T(8,128)(2,1)S(1)}, bf16[1024,256]{1,0:T(8,128)(2,1)S(1)}, u32[]{:S(2)}, u32[]{:S(2)}) collective-permute-start(bf16[1024,256]{1,0:T(8,128)(2,1)S(1)} %pad_maximum_fusion.1.refs_0_), channel_id=1, source_target_pairs={{0,4},{1,5},{2,6},{3,7},{4,0},{5,1},{6,2},{7,3},{8,12},{9,13},{10,... | collective-permute-start | bytes 1572872 | tf_op jit(solution)/shard_map/ppermute | solution.py:31
  18.9 26.5 %collective-permute-start.2 = (bf16[1024,256]{1,0:T(8,128)(2,1)S(1)}, bf16[1024,256]{1,0:T(8,128)(2,1)S(1)}, u32[]{:S(2)}, u32[]{:S(2)}) collective-permute-start(bf16[1024,256]{1,0:T(8,128)(2,1)S(1)} %pad_maximum_fusion.1.refs_0_), channel_id=1, source_target_pairs={{0,6},{1,7},{2,0},{3,1},{4,2},{5,3},{6,4},{7,5},{8,14},{9,15},{10,... | collective-permute-start | bytes 1572872 | tf_op jit(solution)/shard_map/ppermute | solution.py:31
  22.8 26.4 %collective-permute-start.7 = (bf16[128,128]{1,0:T(8,128)(2,1)S(1)}, bf16[128,128]{1,0:T(8,128)(2,1)S(1)}, u32[]{:S(2)}, u32[]{:S(2)}) collective-permute-start(bf16[128,128]{1,0:T(8,128)(2,1)S(1)} %bitcast.15), channel_id=1, source_target_pairs={{0,0},{1,1},{2,64},{3,65},{4,128},{5,129},{6,192},{7,193},{8,256},... | collective-permute-start | bytes 98312 | tf_op jit(solution)/shard_map/ppermute | solution.py:31
  32.5 16.7 %copy-start.3 = (bf16[1,3,128,128]{3,2,1,0:T(8,128)(2,1)S(1)}, bf16[1,3,128,128]{3,2,1,0:T(8,128)(2,1)}, u32[]{:S(2)}) copy-start(bf16[1,3,128,128]{3,2,1,0:T(8,128)(2,1)} %param.6) | copy-start | bytes 294916
  45.4 3.8 %copy-start = (bf16[1024,256]{1,0:T(8,128)(2,1)}, bf16[1024,256]{1,0:T(8,128)(2,1)S(1)}, u32[]{:S(2)}) copy-start(bf16[1024,256]{1,0:T(8,128)(2,1)S(1)} %collective-permute-done.2.refs_1_) | copy-start | bytes 1572868
  46.7 53.2 %collective-permute-start.6 = (bf16[3072,256]{1,0:T(8,128)(2,1)}, bf16[3072,256]{1,0:T(8,128)(2,1)S(1)}, u32[]{:S(2)}, u32[]{:S(2)}) collective-permute-start(bf16[3072,256]{1,0:T(8,128)(2,1)} %pad_maximum_fusion), channel_id=1, source_target_pairs={{0,1},{1,0},{2,3},{3,2},{4,5},{5,4},{6,7},{7,6},{8,9},{9,8},{10,11... | collective-permute-start | bytes 4718600 | tf_op jit(solution)/shard_map/ppermute | solution.py:31
  49.9 24.0 %collective-permute-start.9 = (bf16[128,512]{1,0:T(8,128)(2,1)}, bf16[128,512]{1,0:T(8,128)(2,1)S(1)}, u32[]{:S(2)}, u32[]{:S(2)}) collective-permute-start(bf16[128,512]{1,0:T(8,128)(2,1)} %pad_maximum_fusion.4), channel_id=1, source_target_pairs={{0,192},{1,193},{2,194},{3,195},{4,196},{5,197},{6,198},{7,199},{8... | collective-permute-start | bytes 393224 | tf_op jit(solution)/shard_map/ppermute | solution.py:31
  62.4 12.5 %collective-permute-start.8 = (bf16[128,512]{1,0:T(8,128)(2,1)}, bf16[128,512]{1,0:T(8,128)(2,1)S(1)}, u32[]{:S(2)}, u32[]{:S(2)}) collective-permute-start(bf16[128,512]{1,0:T(8,128)(2,1)} %pad_maximum_fusion.4), channel_id=1, source_target_pairs={{0,64},{1,65},{2,66},{3,67},{4,68},{5,69},{6,70},{7,71},{8,72},{9,... | collective-permute-start | bytes 393224 | tf_op jit(solution)/shard_map/ppermute | solution.py:31
  64.3 35.6 %copy-start.1 = (bf16[1024,256]{1,0:T(8,128)(2,1)S(1)}, bf16[1024,256]{1,0:T(8,128)(2,1)}, u32[]{:S(2)}) copy-start(bf16[1024,256]{1,0:T(8,128)(2,1)} %copy-done) | copy-start | bytes 1572868
  74.9 10.7 %collective-permute-start.10 = (bf16[128,512]{1,0:T(8,128)(2,1)S(1)}, bf16[128,512]{1,0:T(8,128)(2,1)S(1)}, u32[]{:S(2)}, u32[]{:S(2)}) collective-permute-start(bf16[128,512]{1,0:T(8,128)(2,1)S(1)} %broadcast_select_fusion.2), channel_id=1, source_target_pairs={{0,192},{1,65},{2,194},{3,67},{4,196},{5,69},{6,198},{7,71},{8,200... | collective-permute-start | bytes 393224 | tf_op jit(solution)/shard_map/ppermute | solution.py:31
  79.4 20.6 %collective-permute-start.5 = (bf16[1024,256]{1,0:T(8,128)(2,1)S(1)}, bf16[1024,256]{1,0:T(8,128)(2,1)S(1)}, u32[]{:S(2)}, u32[]{:S(2)}) collective-permute-start(bf16[1024,256]{1,0:T(8,128)(2,1)S(1)} %pad_maximum_fusion.1.refs_0_), channel_id=1, source_target_pairs={{0,1},{1,0},{2,3},{3,2},{4,5},{5,4},{6,7},{7,6},{8,9},{9,8},{10,11... | collective-permute-start | bytes 1572872 | tf_op jit(solution)/shard_map/ppermute | solution.py:31
  85.7 19.5 %collective-permute-start.13 = (bf16[512,512]{1,0:T(8,128)(2,1)S(1)}, bf16[512,512]{1,0:T(8,128)(2,1)S(1)}, u32[]{:S(2)}, u32[]{:S(2)}) collective-permute-start(bf16[512,512]{1,0:T(8,128)(2,1)S(1)} %pad_maximum_fusion.2.refs_6_), channel_id=1, source_target_pairs={{0,16},{1,17},{2,18},{3,19},{4,20},{5,21},{6,22},{7,23},{8,24},{9,... | collective-permute-start | bytes 1572872 | tf_op jit(solution)/shard_map/ppermute | solution.py:31
  90.9 15.2 %collective-permute-start.12 = (bf16[512,512]{1,0:T(8,128)(2,1)S(1)}, bf16[512,512]{1,0:T(8,128)(2,1)S(1)}, u32[]{:S(2)}, u32[]{:S(2)}) collective-permute-start(bf16[512,512]{1,0:T(8,128)(2,1)S(1)} %pad_maximum_fusion.2.refs_6_), channel_id=1, source_target_pairs={{0,240},{1,241},{2,242},{3,243},{4,244},{5,245},{6,246},{7,247},{8... | collective-permute-start | bytes 1572872 | tf_op jit(solution)/shard_map/ppermute | solution.py:31
  97.5 22.7 %collective-permute-start.11 = (bf16[512,512]{1,0:T(8,128)(2,1)S(1)}, bf16[512,512]{1,0:T(8,128)(2,1)S(1)}, u32[]{:S(2)}, u32[]{:S(2)}) collective-permute-start(bf16[512,512]{1,0:T(8,128)(2,1)S(1)} %pad_maximum_fusion.2.refs_6_), channel_id=1, source_target_pairs={{0,224},{1,33},{2,226},{3,35},{4,228},{5,37},{6,230},{7,39},{8,232... | collective-permute-start | bytes 1572872 | tf_op jit(solution)/shard_map/ppermute | solution.py:31
  122.2 9.6 %collective-permute-start.15 = (bf16[528,256]{1,0:T(8,128)(2,1)S(1)}, bf16[528,256]{1,0:T(8,128)(2,1)S(1)}, u32[]{:S(2)}, u32[]{:S(2)}) collective-permute-start(bf16[528,256]{1,0:T(8,128)(2,1)S(1)} %get-tuple-element.17), channel_id=1, source_target_pairs={{0,256},{1,257},{2,258},{3,259},{4,260},{5,261},{6,262},{7,263},{8... | collective-permute-start | bytes 811016 | tf_op jit(solution)/shard_map/ppermute | solution.py:31
  132.3 14.4 %collective-permute-start.16 = (bf16[512,256]{1,0:T(8,128)(2,1)S(1)}, bf16[512,256]{1,0:T(8,128)(2,1)S(1)}, u32[]{:S(2)}, u32[]{:S(2)}) collective-permute-start(bf16[512,256]{1,0:T(8,128)(2,1)S(1)} %shard_map.50.kv_ref), channel_id=1, source_target_pairs={{0,16},{16,32},{32,48},{48,64},{64,80},{80,96},{96,112},{112,128},... | collective-permute-start | bytes 786440 | tf_op jit(solution)/shard_map/ppermute | solution.py:308
  134.5 11.4 %collective-permute-start.14 = (bf16[512,128]{1,0:T(8,128)(2,1)S(1)}, bf16[512,128]{1,0:T(8,128)(2,1)S(1)}, u32[]{:S(2)}, u32[]{:S(2)}) collective-permute-start(bf16[512,128]{1,0:T(8,128)(2,1)S(1)} %get-tuple-element.15), channel_id=1, source_target_pairs={{0,256},{1,257},{2,258},{3,259},{4,260},{5,261},{6,262},{7,263},{8... | collective-permute-start | bytes 393224 | tf_op jit(solution)/shard_map/ppermute | solution.py:31
  137.3 33.3 %collective-permute-start.21 = (bf16[2048,128]{1,0:T(8,128)(2,1)S(1)}, bf16[2048,128]{1,0:T(8,128)(2,1)S(1)}, u32[]{:S(2)}, u32[]{:S(2)}) collective-permute-start(bf16[2048,128]{1,0:T(8,128)(2,1)S(1)} %get-tuple-element.20.refs_4_), channel_id=1, source_target_pairs={{0,256},{1,257},{2,258},{3,259},{4,260},{5,261},{6,262},{7,263},{8... | collective-permute-start | bytes 1572872 | tf_op jit(solution)/shard_map/ppermute | solution.py:31
  148.6 36.7 %copy-start.2 = (bf16[512,256]{1,0:T(8,128)(2,1)S(1)}, bf16[512,256]{1,0:T(8,128)(2,1)}, u32[]{:S(2)}) copy-start(bf16[512,256]{1,0:T(8,128)(2,1)} %refs_6_.1) | copy-start | bytes 786436
  148.6 13.4 %collective-permute-start.17 = (bf16[512,128]{1,0:T(8,128)(2,1)S(1)}, bf16[512,128]{1,0:T(8,128)(2,1)S(1)}, u32[]{:S(2)}, u32[]{:S(2)}) collective-permute-start(bf16[512,128]{1,0:T(8,128)(2,1)S(1)} %shard_map.52), channel_id=1, source_target_pairs={{0,8},{1,9},{2,10},{3,11},{4,12},{5,13},{6,14},{7,15},{8,0},{9,1},... | collective-permute-start | bytes 393224 | tf_op jit(solution)/shard_map/ppermute | solution.py:31
  162.0 9.2 %collective-permute-start.20 = (bf16[512,256]{1,0:T(8,128)(2,1)S(1)}, bf16[512,256]{1,0:T(8,128)(2,1)S(1)}, u32[]{:S(2)}, u32[]{:S(2)}) collective-permute-start(bf16[512,256]{1,0:T(8,128)(2,1)S(1)} %pad_maximum_fusion.3.refs_0_), channel_id=1, source_target_pairs={{0,2},{1,3},{2,4},{3,5},{4,6},{5,7},{6,0},{7,1},{8,10},{9,11},{10,... | collective-permute-start | bytes 786440 | tf_op jit(solution)/shard_map/ppermute | solution.py:31
  164.5 10.4 %collective-permute-start.19 = (bf16[512,256]{1,0:T(8,128)(2,1)S(1)}, bf16[512,256]{1,0:T(8,128)(2,1)S(1)}, u32[]{:S(2)}, u32[]{:S(2)}) collective-permute-start(bf16[512,256]{1,0:T(8,128)(2,1)S(1)} %pad_maximum_fusion.3.refs_0_), channel_id=1, source_target_pairs={{0,4},{1,5},{2,6},{3,7},{4,0},{5,1},{6,2},{7,3},{8,12},{9,13},{10,... | collective-permute-start | bytes 786440 | tf_op jit(solution)/shard_map/ppermute | solution.py:31
  166.8 15.0 %collective-permute-start.18 = (bf16[512,256]{1,0:T(8,128)(2,1)S(1)}, bf16[512,256]{1,0:T(8,128)(2,1)S(1)}, u32[]{:S(2)}, u32[]{:S(2)}) collective-permute-start(bf16[512,256]{1,0:T(8,128)(2,1)S(1)} %pad_maximum_fusion.3.refs_0_), channel_id=1, source_target_pairs={{0,6},{1,7},{2,0},{3,1},{4,2},{5,3},{6,4},{7,5},{8,14},{9,15},{10,... | collective-permute-start | bytes 786440 | tf_op jit(solution)/shard_map/ppermute | solution.py:31
  182.8 3.6 %collective-permute-start.22 = (bf16[512,256]{1,0:T(8,128)(2,1)S(1)}, bf16[512,256]{1,0:T(8,128)(2,1)S(1)}, u32[]{:S(2)}, u32[]{:S(2)}) collective-permute-start(bf16[512,256]{1,0:T(8,128)(2,1)S(1)} %shard_map.54), channel_id=1, source_target_pairs={{0,1},{1,0},{2,3},{3,2},{4,5},{5,4},{6,7},{7,6},{8,9},{9,8},{10,11... | collective-permute-start | bytes 786440 | tf_op jit(solution)/shard_map/ppermute | solution.py:31
